TPU v7x, 128 devices: a whole 4x4x4 slice. The times are simulated.
128 devices in a mesh: dp: 4 (over x), seq: 32 (over z, y, core).
Axes of the slice: x: 4, y: 4, z: 4, core: 2. Of those that a mesh axis runs over, the one named last changes fastest.
Arguments:
- inputs: bfloat16 [16384, 6144], P('seq'), may hold values from -6 to 6
- qkv_weight: bfloat16 [6144, 12288], P(None, ('dp', 'seq')), may hold values from -0.078125 to 0.078125
- log_decay: float32 [32, 16384], P('dp', 'seq'), may hold values from -1 to 0, as said below
- out_gain: float32 [32, 128], P('dp'), may hold values from 0.1 to 1.9
Outputs:
- attended: bfloat16 [16384, 4096], P('seq', 'dp')
Inputs may be any that keep to these rules, and one draw needn't show every extreme that they name: `log_decay`: log of a decay factor, negative at every position.
All inputs are finite; a program needn't handle non-finite values.
Results may differ from a plain program's by a relative error of at most 0.0055.
Values may be sent and summed in bfloat16 or wider, within the bound.
No kernel may reach another device: no remote copies, remote signals or barrier semaphores. Data moves between devices by JAX's collectives and lax.ppermute only.
A program may use at most 128 MiB of HBM per device.

v0:
```python
import jax
import jax.numpy as jnp
from jax import lax
from jax.experimental import pallas as pl
from jax.experimental.pallas import tpu as pltpu
from jax.sharding import Mesh
from jax.sharding import PartitionSpec as P


F32 = jnp.float32
BF16 = jnp.bfloat16
TOK = 512
DIM = 6144
UNIT = 96
KB = 2048
NK = DIM // KB
SPLIT = 1
GROUP = ("zl", "y", "c")


def ring_pairs(step):
    return [
        (i * 2 + c, ((i + (step if c == 0 else -step)) % 4) * 2 + c) for i in range(4) for c in range(2)
    ]


def y_move(v, step):
    return lax.ppermute(v, ("y", "c"), ring_pairs(step))


def x_move(v, step):
    return lax.ppermute(v, ("x", "c"), ring_pairs(step))


def z_in(v):
    return lax.ppermute(v, "zl", [(0, 1), (1, 0)])


def z_out(v):
    return lax.ppermute(v, ("zh", "zl"), [(i, 3 - i) for i in range(4)])


def core_swap(v):
    return lax.ppermute(v, "c", [(0, 1), (1, 0)])


def project(scalars, tokens, units, jobs, held):
    flat = [a for arrays, _ in tokens for a in arrays]
    sizes = [arrays[0].shape[0] for arrays, _ in tokens]
    copies_of = sum(len(g) * len(u) for g, u in jobs)

    def kernel(s_ref, *refs):
        x_refs, refs = list(refs[: len(flat)]), refs[len(flat) :]
        w_refs, refs = refs[: len(units)], refs[len(units) :]
        if held is not None:
            refs = refs[1:]
        u_ref, sem, refs = refs[0], refs[1], refs[2:]
        accs, stages, bufs = refs[: len(jobs)], refs[len(jobs) : 2 * len(jobs)], list(refs[2 * len(jobs) :])
        k = pl.program_id(0)
        values = []
        for arrays, _ in tokens:
            if len(arrays) == 1:
                values.append(x_refs.pop(0)[...])
                continue
            early, late, buf = x_refs.pop(0), x_refs.pop(0), bufs.pop(0)

            @pl.when(k < SPLIT)
            def _():
                buf[...] = early[...]

            @pl.when(k >= SPLIT)
            def _():
                buf[...] = late[...]

            values.append(buf[...])
        for (groups, members), acc in zip(jobs, accs):
            x = jnp.concatenate([values[g] for g in groups], axis=0)
            w = jnp.concatenate([w_refs[m][...] for m in members], axis=0)
            part = lax.dot_general(w, x, (((1,), (1,)), ((), ())), preferred_element_type=F32)

            @pl.when(k == 0)
            def _():
                acc[...] = part

            @pl.when(k > 0)
            def _():
                acc[...] += part

        @pl.when(k == NK - 1)
        def _():
            copies = []
            for (groups, members), acc, stage in zip(jobs, accs, stages):
                for i, m in enumerate(members):
                    rows = slice(i * UNIT, (i + 1) * UNIT)
                    v = acc[rows, :]
                    stage[rows, :] = (v * jax.nn.sigmoid(v)).astype(BF16)
                    at = pl.multiple_of(s_ref[units[m][1]] * UNIT, UNIT)
                    start = 0
                    for g in groups:
                        lane = tokens[g][1]
                        size = sizes[g]
                        if size == 128:
                            lane = pl.multiple_of(s_ref[lane] * 128, 128)
                        copy = pltpu.make_async_copy(
                            stage.at[rows, start : start + size],
                            u_ref.at[pl.ds(at, UNIT), pl.ds(lane, size)],
                            sem.at[len(copies)],
                        )
                        copy.start()
                        copies.append(copy)
                        start += size
            for copy in copies:
                copy.wait()

    in_specs = []
    for arrays, _ in tokens:
        rows = arrays[0].shape[0]
        if len(arrays) == 1:
            in_specs.append(pl.BlockSpec((rows, KB), lambda k, s: (0, k)))
        else:
            in_specs.append(pl.BlockSpec((rows, KB), lambda k, s: (0, jnp.minimum(k, SPLIT - 1))))
            in_specs.append(pl.BlockSpec((rows, KB), lambda k, s: (0, jnp.maximum(k - SPLIT, 0))))
    in_specs += [pl.BlockSpec((UNIT, KB), lambda k, s: (0, k))] * len(units)
    shapes = [(len(u) * UNIT, sum(sizes[g] for g in gs)) for gs, u in jobs]
    scratch = [pltpu.SemaphoreType.DMA((copies_of,))]
    scratch += [pltpu.VMEM(shape, F32) for shape in shapes]
    scratch += [pltpu.VMEM(shape, BF16) for shape in shapes]
    scratch += [pltpu.VMEM((128, KB), BF16) for arrays, _ in tokens if len(arrays) == 2]
    args = [scalars, *flat, *[w for w, _ in units]]
    aliases = {}
    if held is not None:
        in_specs.append(pl.BlockSpec(memory_space=pl.ANY))
        aliases = {len(args): 0}
        args.append(held)
    products = sum(a * b for a, b in shapes)
    return pl.pallas_call(
        kernel,
        grid_spec=pltpu.PrefetchScalarGridSpec(
            num_scalar_prefetch=1,
            grid=(NK,),
            in_specs=in_specs,
            out_specs=pl.BlockSpec(memory_space=pl.ANY),
            scratch_shapes=scratch,
        ),
        out_shape=jax.ShapeDtypeStruct((16 * UNIT, 2 * TOK), BF16),
        input_output_aliases=aliases,
        cost_estimate=pl.CostEstimate(
            flops=2 * products * DIM,
            bytes_accessed=2 * DIM * (len(units) * UNIT + sum(sizes)),
            transcendentals=products,
        ),
        name="project",
    )(*args)


def heads_of(kind):
    return [pl.BlockSpec((128, 2 * TOK), lambda i, h=h: (h * 3 + kind, 0)) for h in range(4)]


def whole(shape):
    return pl.BlockSpec(shape, lambda i: (0,) * len(shape))


def states(held, cumulated):
    def kernel(*refs):
        k_refs, v_refs, c_ref, o_ref = refs[:4], refs[4:8], refs[8], refs[9]
        dims = (((1,), (1,)), ((), ()))
        for block in range(2):
            lanes = slice(block * TOK, (block + 1) * TOK)
            for h in range(4):
                cum = c_ref[block * 4 + h]
                tail = jnp.exp(cum[:, TOK - 1 :] - cum)
                k = k_refs[h][:, lanes].astype(F32) * tail
                high = k.astype(BF16)
                low = (k - high.astype(F32)).astype(BF16)
                v = v_refs[h][:, lanes]
                update = lax.dot_general(high, v, dims, preferred_element_type=F32)
                update += lax.dot_general(low, v, dims, preferred_element_type=F32)
                o_ref[h * 4 : h * 4 + 4, block] = update.astype(BF16).reshape(4, 32, 128)

    return pl.pallas_call(
        kernel,
        grid=(1,),
        in_specs=heads_of(1) + heads_of(2) + [whole((8, 1, TOK))],
        out_specs=whole((16, 2, 32, 128)),
        out_shape=jax.ShapeDtypeStruct((16, 2, 32, 128), BF16),
        name="states",
    )(*[held] * 8, cumulated)


def intra(held, cumulated, block):
    def kernel(*refs):
        q_refs, k_refs, v_refs, c_ref, o_ref = refs[:4], refs[4:8], refs[8:12], refs[12], refs[13]
        for h in range(4):
            cum = c_ref[h]
            cum_col = jnp.transpose(jnp.broadcast_to(cum, (128, TOK)))
            for j in range(4):
                lanes = slice(j * 128, (j + 1) * 128)
                count = (j + 1) * 128
                scores = lax.dot_general(
                    k_refs[h][:, :count],
                    q_refs[h][:, lanes],
                    (((0,), (0,)), ((), ())),
                    preferred_element_type=F32,
                )
                spread = cum[:, lanes] - cum_col[:count]
                s = lax.broadcasted_iota(jnp.int32, (count, 128), 0)
                t = lax.broadcasted_iota(jnp.int32, (count, 128), 1) + j * 128
                decay = jnp.exp(jnp.where(s <= t, spread, -1e30))
                weights = (scores * decay).astype(BF16)
                o_ref[h, :, lanes] = jnp.dot(v_refs[h][:, :count], weights, preferred_element_type=F32)

    return pl.pallas_call(
        kernel,
        grid=(1,),
        in_specs=[
            pl.BlockSpec((128, TOK), lambda i, h=h, kind=kind: (h * 3 + kind, block))
            for kind in range(3)
            for h in range(4)
        ]
        + [pl.BlockSpec((4, 1, TOK), lambda i: (block, 0, 0))],
        out_specs=whole((4, 128, TOK)),
        out_shape=jax.ShapeDtypeStruct((4, 128, TOK), F32),
        name="intra",
    )(*[held] * 12, cumulated)


def carries(order, decays, pieces):
    def kernel(n_ref, d_ref, s_ref, o_ref):
        state = jnp.zeros((32, 128), F32)
        for b in range(32):
            z, yc = b // 8, b % 8
            source = n_ref[2 * z] * 8 + yc
            block = n_ref[2 * z + 1]
            o_ref[source, block] = state.astype(BF16)
            state = d_ref[source, block] * state + s_ref[source, block].astype(F32)

    return pl.pallas_call(
        kernel,
        in_specs=[
            pl.BlockSpec(memory_space=pltpu.SMEM),
            pl.BlockSpec(memory_space=pltpu.SMEM),
            pl.BlockSpec(memory_space=pltpu.VMEM),
        ],
        out_specs=pl.BlockSpec(memory_space=pltpu.VMEM),
        out_shape=jax.ShapeDtypeStruct((16, 2, 32, 128), BF16),
        name="carries",
    )(order, decays, pieces)


def finish(held, cumulated, inside, carried, gains, block):
    def kernel(*refs):
        q_refs, c_ref, i_ref, s_ref, g_ref, o_ref = refs[:4], *refs[4:]
        for h in range(4):
            carry = s_ref[4 * h : 4 * h + 4, 0].reshape(128, 128)
            outer = lax.dot_general(
                carry, q_refs[h][...], (((0,), (0,)), ((), ())), preferred_element_type=F32
            )
            combined = i_ref[h] + outer * jnp.exp(c_ref[h])
            root = lax.rsqrt(jnp.mean(combined * combined, axis=0, keepdims=True) + 1e-05)
            o_ref[:, h * 128 : (h + 1) * 128] = jnp.transpose(combined * root * g_ref[h]).astype(BF16)

    return pl.pallas_call(
        kernel,
        grid=(1,),
        in_specs=[pl.BlockSpec((128, TOK), lambda i, h=h: (h * 3, block)) for h in range(4)]
        + [
            pl.BlockSpec((4, 1, TOK), lambda i: (block, 0, 0)),
            whole((4, 128, TOK)),
            pl.BlockSpec((16, 1, 32, 128), lambda i: (0, block, 0, 0)),
            whole((4, 128, 1)),
        ],
        out_specs=whole((TOK, 512)),
        out_shape=jax.ShapeDtypeStruct((TOK, 512), BF16),
        name="finish",
    )(*[held] * 4, cumulated, inside, carried, gains)


def shards(inputs, qkv_weight, log_decay, out_gain):
    x = lax.axis_index("x")
    zh = lax.axis_index("zh")
    zl = lax.axis_index("zl")
    y = lax.axis_index("y")
    c = lax.axis_index("c")
    side = 1 - 2 * c

    log_decay_across = z_out(log_decay)
    rates = jnp.stack([log_decay, log_decay_across])
    rates = lax.dynamic_slice(rates, (0, 4 * zh, 0), (2, 4, TOK))
    cumulated = jnp.cumsum(rates, axis=-1)
    totals = cumulated[:, :, -1]
    parts = jnp.repeat(totals.T, 4, axis=0)
    decays = jnp.exp(lax.all_to_all(parts, GROUP, 0, 0, tiled=True))
    cumulated = cumulated.reshape(8, 1, TOK)
    order = jnp.where(zh == 0, jnp.array([0, 0, 1, 0, 1, 1, 0, 1]), jnp.array([1, 1, 0, 1, 0, 0, 1, 0]))
    order = order.astype(jnp.int32)
    gains = lax.dynamic_slice(out_gain, (4 * zh, 0), (4, 128)).reshape(4, 128, 1)

    def unit(row, shift, core):
        return (row * 4 + (y + shift) % 4) * 2 + core

    zi, cs = 1 - zl, 1 - c
    rows = [
        unit(zl, 0, c),
        unit(zl, 0, cs),
        unit(zl, -side, c),
        unit(zl, side, cs),
        unit(zl, side, c),
        unit(zl, -side, cs),
        unit(zi, 0, c),
        unit(zi, 0, cs),
        unit(zl, 2, c),
        unit(zl, 2, cs),
        unit(zi, -side, c),
        unit(zi, side, cs),
        unit(zi, side, c),
        unit(zi, -side, cs),
        unit(zi, 2, c),
        unit(zi, 2, cs),
    ]
    lanes = [4 + q % 4 for q in (x, x - side, x + side, x + 2)]
    scalars = jnp.stack(rows + lanes).astype(jnp.int32)

    own = qkv_weight.T
    quarter = lax.dynamic_slice(inputs, (128 * x, 0), (128, DIM))
    cut = SPLIT * KB
    w_a = y_move(own, 1)
    w_b = y_move(own, -1)
    w_z = z_in(own)
    a0 = z_out(quarter[:, :cut])
    a1 = z_out(quarter[:, cut:])
    s_own = core_swap(own)
    small = (cumulated, decays, order, gains, scalars)
    a0, (cumulated, decays, order, gains, scalars) = lax.optimization_barrier((a0, small))
    xa0 = x_move(a0, 1)
    xb0 = x_move(a0, -1)
    w_c = y_move(w_a, 1)
    w_zb = y_move(w_z, -1)
    w_za = z_in(w_a)
    s_a = core_swap(w_a)
    s_b = core_swap(w_b)
    s_z = core_swap(w_z)
    xc0 = x_move(xa0, 1)
    xa1 = x_move(a1, 1)
    xb1 = x_move(a1, -1)
    w_zbb = y_move(w_zb, -1)
    s_c = core_swap(w_c)
    s_zb = core_swap(w_zb)
    s_za = core_swap(w_za)
    xc1 = x_move(xa1, 1)
    s_zbb = core_swap(w_zbb)

    weights = [own, s_own, w_a, s_a, w_b, s_b, w_z, s_z, w_c, s_c, w_za, s_za, w_zb, s_zb, w_zbb, s_zbb]
    units = [(w, i) for i, w in enumerate(weights)]
    here = ([inputs], 0)
    across = [([a0, a1], 16), ([xa0, xa1], 17), ([xb0, xb1], 18), ([xc0, xc1], 19)]
    held = project(scalars, [here], units[:8], [((0,), range(8))], None)
    jobs = [((0,), range(8, 14)), ((1, 2, 3), range(14))]
    held = project(scalars, [here] + across[:3], units[:14], jobs, held)
    jobs = [((0, 1, 2, 3), (14, 15)), ((4,), range(16))]
    held = project(scalars, [here] + across, units, jobs, held)

    own_states = states(held, cumulated)
    update = lax.all_to_all(own_states, GROUP, 0, 0, tiled=True)
    held, _ = lax.optimization_barrier((held, own_states))
    inside_across = intra(held, cumulated, 1)
    update, inside_across = lax.optimization_barrier((update, inside_across))
    running = carries(order, decays, update)
    carried = lax.all_to_all(running, GROUP, 0, 0, tiled=True)
    held, _ = lax.optimization_barrier((held, running))
    inside = intra(held, cumulated, 0)
    carried, inside = lax.optimization_barrier((carried, inside))
    over = z_out(finish(held, cumulated, inside_across, carried, gains, 1))
    here = finish(held, cumulated, inside, carried, gains, 0)
    return jnp.where(zh == 0, jnp.concatenate([here, over], 1), jnp.concatenate([over, here], 1))


def solution(mesh):
    fine = Mesh(mesh.devices.reshape(4, 2, 2, 4, 2), ("x", "zh", "zl", "y", "c"))
    seq = ("zh", "zl", "y", "c")
    in_specs = (P(seq, None), P(None, ("x",) + seq), P("x", seq), P("x", None))
    return jax.shard_map(shards, mesh=fine, in_specs=in_specs, out_specs=P(seq, "x"), check_vma=False)
```

profile of v0, /device:TPU:0, one launch (start us, length us, event | category | flops | bytes accessed | tf_op | source)
XLA Modules:
  0.0 210.4 jit_solution(4581472275239646596)
XLA Ops:
  0.0 4.1 %collective-permute-start.1 = (f32[8,512]{1,0:T(8,128)}, f32[8,512]{1,0:T(8,128)S(1)}, u32[]{:S(2)}, u32[]{:S(2)}) collective-permute-start(f32[8,512]{1,0:T(8,128)} %param.8), channel_id=1, source_target_pairs={{0,24},{8,16},{16,8},{24,0},{1,25},{9,17},{17,9},{25,1},{2,26},{10... | collective-permute-start | bytes 49160 | tf_op jit(solution)/shard_map/ppermute | solution.py:40
  4.2 1.1 constant_dynamic-slice_fusion
  5.2 0.1 collective-permute-start
  5.3 1.6 collective-permute-start.10
  7.0 1.2 broadcast_select_fusion.n_ref
  8.4 2.4 %reduce-window.6 = f32[2,4,4,128]{3,2,1,0:T(4,128)S(1)} reduce-window(f32[2,4,4,128]{3,2,1,0:T(4,128)S(1)} %reshape.40, f32[]{:T(128)} %constant.99.clone.1), window={size=1x1x1x128 pad=0_0x0_0x0_0x127_0}, to_apply=%region_0.0 | reduce-window | flops 520192 | bytes 32772 | tf_op jit(solution)/shard_map/reduce-window
  10.8 0.2 slice_reduce_fusion
  11.0 0.4 reduce-window.9
  11.3 0.1 broadcast_add_fusion
  11.4 0.3 copy.27
  11.7 0.0 copy-start.1
  11.7 0.1 copy.29
  11.8 0.6 broadcast_in_dim.3.clone
  12.4 4.3 %all-to-all-start = ((f32[16,1,2]{2,1,0:T(1,128)}), f32[16,1,2]{2,1,0:T(1,128)S(1)}, u32[]{:S(2)}, u32[]{:S(2)}) async-start(f32[16,1,2]{2,1,0:T(1,128)} %bitcast.6), calls=%async_computation | async-start | bytes 16384 | tf_op jit(solution)/shard_map/all_to_all | solution.py:293
  16.7 0.6 stack.95.s_ref
  17.3 7.0 %all-to-all-done = f32[16,1,2]{2,1,0:T(1,128)S(1)} async-done(((f32[16,1,2]{2,1,0:T(1,128)}), f32[16,1,2]{2,1,0:T(1,128)S(1)}, u32[]{:S(2)}, u32[]{:S(2)}) %all-to-all-start) | async-done | bytes 160 | tf_op jit(solution)/shard_map/all_to_all | solution.py:293
  24.3 0.1 copy.23
  24.4 1.6 collective-permute-start.3
  26.0 1.3 dynamic-slice.1
  27.3 3.2 %collective-permute-start.2 = (bf16[128,4096]{1,0:T(8,128)(2,1)S(1)}, bf16[128,4096]{1,0:T(8,128)(2,1)S(1)}, u32[]{:S(2)}, u32[]{:S(2)}) collective-permute-start(bf16[128,4096]{1,0:T(8,128)(2,1)S(1)} %dynamic-slice.1), channel_id=1, source_target_pairs={{0,24},{8,16},{16,8},{24,0},{1,25},{9,17},{17,9},{25,1},{2,26},{10... | collective-permute-start | bytes 3145736 | tf_op jit(solution)/shard_map/ppermute | solution.py:40
  30.5 1.7 collective-permute-start.5
  32.3 0.8 collective-permute-start.14
  33.1 2.1 collective-permute-done.3.refs_3_
  35.2 0.7 collective-permute-start.12
  35.9 4.1 %collective-permute-done.5.refs_5_ = bf16[128,2048]{1,0:T(8,128)(2,1)} collective-permute-done((bf16[128,2048]{1,0:T(8,128)(2,1)}, bf16[128,2048]{1,0:T(8,128)(2,1)}, u32[]{:S(2)}, u32[]{:S(2)}) %collective-permute-start.5) | collective-permute-done | bytes 524320 | tf_op jit(solution)/shard_map/ppermute | solution.py:32
  40.0 0.8 collective-permute-start.9
  40.8 13.7 %collective-permute-done.2.refs_2_ = bf16[128,4096]{1,0:T(8,128)(2,1)S(1)} collective-permute-done((bf16[128,4096]{1,0:T(8,128)(2,1)S(1)}, bf16[128,4096]{1,0:T(8,128)(2,1)S(1)}, u32[]{:S(2)}, u32[]{:S(2)}) %collective-permute-start.2) | collective-permute-done | bytes 1048608 | tf_op jit(solution)/shard_map/ppermute | solution.py:40
  54.6 3.2 %collective-permute-start.6 = (bf16[128,4096]{1,0:T(8,128)(2,1)S(1)}, bf16[128,4096]{1,0:T(8,128)(2,1)S(1)}, u32[]{:S(2)}, u32[]{:S(2)}) collective-permute-start(bf16[128,4096]{1,0:T(8,128)(2,1)S(1)} %collective-permute-done.2.refs_2_), channel_id=1, source_target_pairs={{0,96},{1,33},{32,0},{33,65},{64,32},{65,97},{96,64},{97,1},{2,98}... | collective-permute-start | bytes 3145736 | tf_op jit(solution)/shard_map/ppermute | solution.py:32
  57.8 1.2 collective-permute-done.14.refs_7_.refs_13_.refs_15_
  59.0 0.9 collective-permute-start.20
  59.9 1.2 collective-permute-start.16
  61.1 20.1 %collective-permute-done.4.refs_4_ = bf16[128,4096]{1,0:T(8,128)(2,1)} collective-permute-done((bf16[128,4096]{1,0:T(8,128)(2,1)S(1)}, bf16[128,4096]{1,0:T(8,128)(2,1)}, u32[]{:S(2)}, u32[]{:S(2)}) %collective-permute-start.4) | collective-permute-done | bytes 1048608 | tf_op jit(solution)/shard_map/ppermute | solution.py:32
  81.1 0.8 collective-permute-start.18
  82.0 1.0 copy-done.11
  83.0 4.6 %collective-permute-done.20.refs_19_.refs_21_ = bf16[96,6144]{1,0:T(8,128)(2,1)} collective-permute-done((bf16[96,6144]{1,0:T(8,128)(2,1)S(1)}, bf16[96,6144]{1,0:T(8,128)(2,1)}, u32[]{:S(2)}, u32[]{:S(2)}) %collective-permute-start.20) | collective-permute-done | bytes 1179680 | tf_op jit(solution)/shard_map/ppermute | solution.py:28
  87.5 0.9 collective-permute-start.22
  88.4 0.2 collective-permute-done.16.refs_15_.refs_17_
  88.7 18.3 %collective-permute-done.18.refs_17_.refs_19_ = bf16[96,6144]{1,0:T(8,128)(2,1)} collective-permute-done((bf16[96,6144]{1,0:T(8,128)(2,1)S(1)}, bf16[96,6144]{1,0:T(8,128)(2,1)}, u32[]{:S(2)}, u32[]{:S(2)}) %collective-permute-start.18) | collective-permute-done | bytes 1179680 | tf_op jit(solution)/shard_map/ppermute | solution.py:36
  107.0 0.6 collective-permute-start.21
  107.6 0.1 collective-permute-start.8
  107.7 1.0 copy-done.8
  108.7 0.2 collective-permute-start.23
  108.8 10.6 %project.3.refs_21_ = bf16[1536,1024]{1,0:T(8,128)(2,1)} custom-call(s32[20]{0:T(128)} %stack.95.s_ref, bf16[512,6144]{1,0:T(8,128)(2,1)} %refs_0_.5, bf16[96,6144]{1,0:T(8,128)(2,1)} %bitcast.36, bf16[96,6144]{1,0:T(8,128)(2,1)} %copy-done.5, bf16[96,6144]{1,0:T(8,128)(2,1)} %copy-done.2, bf16[96,6144]{1,0:T(8,128)(2,1)} %copy-done.6, ...), custom_call_target="tpu_custom_call" | custom-call | flops 4831838208 | bytes 15728640 | tf_op jit(solution)/shard_map/project/pallas_call | solution.py:136
  119.4 0.9 collective-permute-start.7
  120.4 21.5 %project.4.refs_25_ = bf16[1536,1024]{1,0:T(8,128)(2,1)} custom-call(s32[20]{0:T(128)} %stack.95.s_ref, bf16[512,6144]{1,0:T(8,128)(2,1)} %refs_0_.5, bf16[128,2048]{1,0:T(8,128)(2,1)} %collective-permute-done.refs_1_, bf16[128,4096]{1,0:T(8,128)(2,1)} %copy-done.10, ...), custom_call_target="tpu_custom_call", output_to_operand_aliasing={{}: (22, {})} | custom-call | flops 9965666304 | bytes 27525120 | tf_op jit(solution)/shard_map/project/pallas_call | solution.py:136
  142.0 0.8 copy-done.14
  142.7 17.7 %project.5.refs_0_.refs_1_.refs_2_.refs_3_.refs_4_.refs_5_.refs_6_.refs_7_.refs_8_.refs_9_.refs_10_.refs_11_ = bf16[1536,1024]{1,0:T(8,128)(2,1)} custom-call(s32[20]{0:T(128)} %stack.95.s_ref, bf16[512,6144]{1,0:T(8,128)(2,1)} %refs_0_.5, bf16[128,2048]{1,0:T(8,128)(2,1)} %collective-permute-done.refs_1_, ...), custom_call_target="tpu_custom_call", output_to_operand_aliasing={{}: (26, {})} | custom-call | flops 4529848320 | bytes 31457280 | tf_op jit(solution)/shard_map/project/pallas_call | solution.py:136
  160.5 3.0 %states.1 = bf16[16,2,32,128]{3,2,1,0:T(8,128)(2,1)} custom-call(bf16[1536,1024]{1,0:T(8,128)(2,1)} %project.5.refs_0_.refs_1_.refs_2_.refs_3_.refs_4_.refs_5_.refs_6_.refs_7_.refs_8_.refs_9_.refs_10_.refs_11_, bf16[1536,1024]{1,0:T(8,128)(2,1)} %project.5.refs_0_.refs_1_.refs_2_.refs_3_.refs_4_.refs_5_.refs_6_.refs_7_.refs_8_.refs_9_.refs_10_.refs_11_, ...), custom_call_target="tpu_custom_call" | custom-call | tf_op jit(solution)/shard_map/states/pallas_call | solution.py:181
  163.5 3.8 %all-to-all-start.1 = ((bf16[16,2,32,128]{3,2,1,0:T(8,128)(2,1)}), bf16[16,2,32,128]{3,2,1,0:T(8,128)(2,1)S(1)}, u32[]{:S(2)}, u32[]{:S(2)}) async-start(bf16[16,2,32,128]{3,2,1,0:T(8,128)(2,1)} %states.1), calls=%async_computation.1 | async-start | bytes 524288 | tf_op jit(solution)/shard_map/all_to_all | solution.py:364
  167.3 0.7 copy.24.d_ref
  167.9 3.4 %intra.2.refs_5_ = f32[4,128,512]{2,1,0:T(8,128)} custom-call(bf16[1536,1024]{1,0:T(8,128)(2,1)} %project.5.refs_0_.refs_1_.refs_2_.refs_3_.refs_4_.refs_5_.refs_6_.refs_7_.refs_8_.refs_9_.refs_10_.refs_11_, bf16[1536,1024]{1,0:T(8,128)(2,1)} %project.5.refs_0_.refs_1_.refs_2_.refs_3_.refs_4_.refs_5_.refs_6_.refs_7_.refs_8_.refs_9_.refs_10_.refs_11_, ...), custom_call_target="tpu_custom_call" | custom-call | tf_op jit(solution)/shard_map/intra/pallas_call | solution.py:213
  171.4 3.7 %all-to-all-done.1.s_ref = bf16[16,2,32,128]{3,2,1,0:T(8,128)(2,1)S(1)} async-done(((bf16[16,2,32,128]{3,2,1,0:T(8,128)(2,1)}), bf16[16,2,32,128]{3,2,1,0:T(8,128)(2,1)S(1)}, u32[]{:S(2)}, u32[]{:S(2)}) %all-to-all-start.1) | async-done | bytes 262176 | tf_op jit(solution)/shard_map/all_to_all | solution.py:364
  175.1 0.7 copy-done.12
  175.8 1.8 carries.1
  177.6 3.8 %all-to-all-start.2 = ((bf16[16,2,32,128]{3,2,1,0:T(8,128)(2,1)}), bf16[16,2,32,128]{3,2,1,0:T(8,128)(2,1)S(1)}, u32[]{:S(2)}, u32[]{:S(2)}) async-start(bf16[16,2,32,128]{3,2,1,0:T(8,128)(2,1)} %carries.1), calls=%async_computation.2 | async-start | bytes 524288 | tf_op jit(solution)/shard_map/all_to_all | solution.py:369
  181.3 0.9 copy.25.refs_7_
  182.2 3.5 %intra.3.refs_5_ = f32[4,128,512]{2,1,0:T(8,128)} custom-call(bf16[1536,1024]{1,0:T(8,128)(2,1)} %project.5.refs_0_.refs_1_.refs_2_.refs_3_.refs_4_.refs_5_.refs_6_.refs_7_.refs_8_.refs_9_.refs_10_.refs_11_, bf16[1536,1024]{1,0:T(8,128)(2,1)} %project.5.refs_0_.refs_1_.refs_2_.refs_3_.refs_4_.refs_5_.refs_6_.refs_7_.refs_8_.refs_9_.refs_10_.refs_11_, ...), custom_call_target="tpu_custom_call" | custom-call | tf_op jit(solution)/shard_map/intra/pallas_call | solution.py:213
  185.7 3.3 %all-to-all-done.2.refs_6_ = bf16[16,2,32,128]{3,2,1,0:T(8,128)(2,1)S(1)} async-done(((bf16[16,2,32,128]{3,2,1,0:T(8,128)(2,1)}), bf16[16,2,32,128]{3,2,1,0:T(8,128)(2,1)S(1)}, u32[]{:S(2)}, u32[]{:S(2)}) %all-to-all-start.2) | async-done | bytes 262176 | tf_op jit(solution)/shard_map/all_to_all | solution.py:369
  188.9 0.7 copy-done.9
  189.6 2.9 %finish.3 = bf16[512,512]{1,0:T(8,128)(2,1)} custom-call(bf16[1536,1024]{1,0:T(8,128)(2,1)} %project.5.refs_0_.refs_1_.refs_2_.refs_3_.refs_4_.refs_5_.refs_6_.refs_7_.refs_8_.refs_9_.refs_10_.refs_11_, bf16[1536,1024]{1,0:T(8,128)(2,1)} %project.5.refs_0_.refs_1_.refs_2_.refs_3_.refs_4_.refs_5_.refs_6_.refs_7_.refs_8_.refs_9_.refs_10_.refs_11_, ...), custom_call_target="tpu_custom_call" | custom-call | tf_op jit(solution)/shard_map/finish/pallas_call | solution.py:263
  192.6 2.8 %collective-permute-start.24 = (bf16[512,512]{1,0:T(8,128)(2,1)}, bf16[512,512]{1,0:T(8,128)(2,1)S(1)}, u32[]{:S(2)}, u32[]{:S(2)}) collective-permute-start(bf16[512,512]{1,0:T(8,128)(2,1)} %finish.3), channel_id=1, source_target_pairs={{0,24},{8,16},{16,8},{24,0},{1,25},{9,17},{17,9},{25,1},{2,26},{10... | collective-permute-start | bytes 1572872 | tf_op jit(solution)/shard_map/ppermute | solution.py:40
  195.4 2.9 %finish.2 = bf16[512,512]{1,0:T(8,128)(2,1)} custom-call(bf16[1536,1024]{1,0:T(8,128)(2,1)} %project.5.refs_0_.refs_1_.refs_2_.refs_3_.refs_4_.refs_5_.refs_6_.refs_7_.refs_8_.refs_9_.refs_10_.refs_11_, bf16[1536,1024]{1,0:T(8,128)(2,1)} %project.5.refs_0_.refs_1_.refs_2_.refs_3_.refs_4_.refs_5_.refs_6_.refs_7_.refs_8_.refs_9_.refs_10_.refs_11_, ...), custom_call_target="tpu_custom_call" | custom-call | tf_op jit(solution)/shard_map/finish/pallas_call | solution.py:263
  198.3 9.5 %collective-permute-done.24 = bf16[512,512]{1,0:T(8,128)(2,1)S(1)} collective-permute-done((bf16[512,512]{1,0:T(8,128)(2,1)}, bf16[512,512]{1,0:T(8,128)(2,1)S(1)}, u32[]{:S(2)}, u32[]{:S(2)}) %collective-permute-start.24) | collective-permute-done | bytes 524320 | tf_op jit(solution)/shard_map/ppermute | solution.py:40
  207.8 2.6 %maximum_select_fusion = bf16[512,1024]{1,0:T(8,128)(2,1)} fusion(bf16[512,512]{1,0:T(8,128)(2,1)S(1)} %collective-permute-done.24, bf16[512,512]{1,0:T(8,128)(2,1)} %finish.2, pred[]{:T(512)S(6)} %eq.25), kind=kLoop, calls=%fused_computation | loop fusion | flops 4718592 | bytes 2097153 | tf_op jit(solution)/shard_map/jit(_where)/select_n | solution.py:375
  (53 shorter events, 0.2 us)
Async XLA Ops:
  0.0 8.2 %copy-start = (f32[8,128]{1,0:T(8,128)S(1)}, f32[8,128]{1,0:T(8,128)}, u32[]{:S(2)}) copy-start(f32[8,128]{1,0:T(8,128)} %param.9) | copy-start | bytes 12292
  0.0 8.3 %copy-start.15 = (f32[8,512]{1,0:T(8,128)S(1)}, f32[8,512]{1,0:T(8,128)}, u32[]{:S(2)}) copy-start(f32[8,512]{1,0:T(8,128)} %param.8) | copy-start | bytes 49156
  0.0 8.3 %collective-permute-start.1 = (f32[8,512]{1,0:T(8,128)}, f32[8,512]{1,0:T(8,128)S(1)}, u32[]{:S(2)}, u32[]{:S(2)}) collective-permute-start(f32[8,512]{1,0:T(8,128)} %param.8), channel_id=1, source_target_pairs={{0,24},{8,16},{16,8},{24,0},{1,25},{9,17},{17,9},{25,1},{2,26},{10... | collective-permute-start | bytes 49160 | tf_op jit(solution)/shard_map/ppermute | solution.py:40
  5.2 19.2 %collective-permute-start = (bf16[128,2048]{1,0:T(8,128)(2,1)S(1)}, bf16[128,2048]{1,0:T(8,128)(2,1)}, u32[]{:S(2)}, u32[]{:S(2)}) collective-permute-start(bf16[128,2048]{1,0:T(8,128)(2,1)S(1)} %constant_dynamic-slice_fusion), channel_id=1, source_target_pairs={{0,24},{8,16},{16,8},{24,0},{1,25},{9,17},{17,9},{25,1},{2,26},{10... | collective-permute-start | bytes 1572872 | tf_op jit(solution)/shard_map/ppermute | solution.py:40
  5.3 49.2 %collective-permute-start.10 = (bf16[96,6144]{1,0:T(8,128)(2,1)}, bf16[96,6144]{1,0:T(8,128)(2,1)S(1)}, u32[]{:S(2)}, u32[]{:S(2)}) collective-permute-start(bf16[96,6144]{1,0:T(8,128)(2,1)} %bitcast.35), channel_id=1, source_target_pairs={{0,2},{1,7},{2,4},{3,1},{4,6},{5,3},{6,0},{7,5},{8,10},{9,15},{10,... | collective-permute-start | bytes 3538952 | tf_op jit(solution)/shard_map/ppermute | solution.py:28
  11.4 15.9 %copy-start.13 = (f32[2,4,4,128]{3,2,1,0:T(4,128)}, f32[2,4,4,128]{3,2,1,0:T(4,128)S(1)}, u32[]{:S(2)}) copy-start(f32[2,4,4,128]{3,2,1,0:T(4,128)S(1)} %broadcast_add_fusion) | copy-start | bytes 49156
  11.7 20.6 %copy-start.1 = (bf16[6144,96]{0,1:T(8,128)(2,1)S(1)}, bf16[6144,96]{0,1:T(8,128)(2,1)}, u32[]{:S(2)}) copy-start(bf16[6144,96]{0,1:T(8,128)(2,1)} %param.7) | copy-start | bytes 3538948
  12.4 11.9 %all-to-all-start = ((f32[16,1,2]{2,1,0:T(1,128)}), f32[16,1,2]{2,1,0:T(1,128)S(1)}, u32[]{:S(2)}, u32[]{:S(2)}) async-start(f32[16,1,2]{2,1,0:T(1,128)} %bitcast.6), calls=%async_computation | async-start | bytes 16384 | tf_op jit(solution)/shard_map/all_to_all | solution.py:293
  24.4 10.8 %collective-permute-start.3 = (bf16[128,2048]{1,0:T(8,128)(2,1)}, bf16[128,2048]{1,0:T(8,128)(2,1)}, u32[]{:S(2)}, u32[]{:S(2)}) collective-permute-start(bf16[128,2048]{1,0:T(8,128)(2,1)} %collective-permute-done.refs_1_), channel_id=1, source_target_pairs={{0,32},{1,97},{32,64},{33,1},{64,96},{65,33},{96,0},{97,65},{2,34}... | collective-permute-start | bytes 1572872 | tf_op jit(solution)/shard_map/ppermute | solution.py:32
  27.3 27.3 %collective-permute-start.2 = (bf16[128,4096]{1,0:T(8,128)(2,1)S(1)}, bf16[128,4096]{1,0:T(8,128)(2,1)S(1)}, u32[]{:S(2)}, u32[]{:S(2)}) collective-permute-start(bf16[128,4096]{1,0:T(8,128)(2,1)S(1)} %dynamic-slice.1), channel_id=1, source_target_pairs={{0,24},{8,16},{16,8},{24,0},{1,25},{9,17},{17,9},{25,1},{2,26},{10... | collective-permute-start | bytes 3145736 | tf_op jit(solution)/shard_map/ppermute | solution.py:40
  30.5 9.5 %collective-permute-start.5 = (bf16[128,2048]{1,0:T(8,128)(2,1)}, bf16[128,2048]{1,0:T(8,128)(2,1)}, u32[]{:S(2)}, u32[]{:S(2)}) collective-permute-start(bf16[128,2048]{1,0:T(8,128)(2,1)} %collective-permute-done.refs_1_), channel_id=1, source_target_pairs={{0,96},{1,33},{32,0},{33,65},{64,32},{65,97},{96,64},{97,1},{2,98}... | collective-permute-start | bytes 1572872 | tf_op jit(solution)/shard_map/ppermute | solution.py:32
  32.3 26.7 %collective-permute-start.14 = (bf16[96,6144]{1,0:T(8,128)(2,1)S(1)}, bf16[96,6144]{1,0:T(8,128)(2,1)S(1)}, u32[]{:S(2)}, u32[]{:S(2)}) collective-permute-start(bf16[96,6144]{1,0:T(8,128)(2,1)S(1)} %bitcast.39), channel_id=1, source_target_pairs={{0,8},{8,0},{1,9},{9,1},{2,10},{10,2},{3,11},{11,3},{4,12},{12,4},... | collective-permute-start | bytes 3538952 | tf_op jit(solution)/shard_map/ppermute | solution.py:36
  35.2 23.8 %collective-permute-start.12 = (bf16[96,6144]{1,0:T(8,128)(2,1)S(1)}, bf16[96,6144]{1,0:T(8,128)(2,1)S(1)}, u32[]{:S(2)}, u32[]{:S(2)}) collective-permute-start(bf16[96,6144]{1,0:T(8,128)(2,1)S(1)} %bitcast.40), channel_id=1, source_target_pairs={{0,6},{1,3},{2,0},{3,5},{4,2},{5,7},{6,4},{7,1},{8,14},{9,11},{10,... | collective-permute-start | bytes 3538952 | tf_op jit(solution)/shard_map/ppermute | solution.py:28
  40.0 19.8 %collective-permute-start.9 = (bf16[96,6144]{1,0:T(8,128)(2,1)S(1)}, bf16[96,6144]{1,0:T(8,128)(2,1)S(1)}, u32[]{:S(2)}, u32[]{:S(2)}) collective-permute-start(bf16[96,6144]{1,0:T(8,128)(2,1)S(1)} %bitcast.41), channel_id=1, source_target_pairs={{0,1},{1,0},{2,3},{3,2},{4,5},{5,4},{6,7},{7,6},{8,9},{9,8},{10,11... | collective-permute-start | bytes 3538952 | tf_op jit(solution)/shard_map/ppermute | solution.py:44
  54.5 27.4 %copy-start.10 = (bf16[128,4096]{1,0:T(8,128)(2,1)}, bf16[128,4096]{1,0:T(8,128)(2,1)S(1)}, u32[]{:S(2)}) copy-start(bf16[128,4096]{1,0:T(8,128)(2,1)S(1)} %collective-permute-done.2.refs_2_) | copy-start | bytes 3145732
  54.5 26.6 %collective-permute-start.4 = (bf16[128,4096]{1,0:T(8,128)(2,1)S(1)}, bf16[128,4096]{1,0:T(8,128)(2,1)}, u32[]{:S(2)}, u32[]{:S(2)}) collective-permute-start(bf16[128,4096]{1,0:T(8,128)(2,1)S(1)} %collective-permute-done.2.refs_2_), channel_id=1, source_target_pairs={{0,32},{1,97},{32,64},{33,1},{64,96},{65,33},{96,0},{97,65},{2,34}... | collective-permute-start | bytes 3145736 | tf_op jit(solution)/shard_map/ppermute | solution.py:32
  54.5 54.3 %copy-start.2 = (bf16[96,6144]{1,0:T(8,128)(2,1)}, bf16[96,6144]{1,0:T(8,128)(2,1)S(1)}, u32[]{:S(2)}) copy-start(bf16[96,6144]{1,0:T(8,128)(2,1)S(1)} %collective-permute-done.10.refs_3_.refs_9_.refs_11_) | copy-start | bytes 3538948
  54.6 27.4 %collective-permute-start.6 = (bf16[128,4096]{1,0:T(8,128)(2,1)S(1)}, bf16[128,4096]{1,0:T(8,128)(2,1)S(1)}, u32[]{:S(2)}, u32[]{:S(2)}) collective-permute-start(bf16[128,4096]{1,0:T(8,128)(2,1)S(1)} %collective-permute-done.2.refs_2_), channel_id=1, source_target_pairs={{0,96},{1,33},{32,0},{33,65},{64,32},{65,97},{96,64},{97,1},{2,98}... | collective-permute-start | bytes 3145736 | tf_op jit(solution)/shard_map/ppermute | solution.py:32
  58.9 49.9 %copy-start.3 = (bf16[96,6144]{1,0:T(8,128)(2,1)}, bf16[96,6144]{1,0:T(8,128)(2,1)S(1)}, u32[]{:S(2)}) copy-start(bf16[96,6144]{1,0:T(8,128)(2,1)S(1)} %collective-permute-done.14.refs_7_.refs_13_.refs_15_) | copy-start | bytes 3538948
  58.9 24.0 %collective-permute-start.11 = (bf16[96,6144]{1,0:T(8,128)(2,1)S(1)}, bf16[96,6144]{1,0:T(8,128)(2,1)S(1)}, u32[]{:S(2)}, u32[]{:S(2)}) collective-permute-start(bf16[96,6144]{1,0:T(8,128)(2,1)S(1)} %collective-permute-done.10.refs_3_.refs_9_.refs_11_), channel_id=1, source_target_pairs={{0,1},{1,0},{2,3},{3,2},{4,5},{5,4},{6,7},{7,6},{8,9},{9,8},{10,11... | collective-permute-start | bytes 3538952 | tf_op jit(solution)/shard_map/ppermute | solution.py:44
  59.0 48.0 %copy-start.4 = (bf16[96,6144]{1,0:T(8,128)(2,1)}, bf16[96,6144]{1,0:T(8,128)(2,1)S(1)}, u32[]{:S(2)}) copy-start(bf16[96,6144]{1,0:T(8,128)(2,1)S(1)} %collective-permute-done.12.refs_5_.refs_11_.refs_13_) | copy-start | bytes 3538948
  59.0 28.6 %collective-permute-start.20 = (bf16[96,6144]{1,0:T(8,128)(2,1)S(1)}, bf16[96,6144]{1,0:T(8,128)(2,1)}, u32[]{:S(2)}, u32[]{:S(2)}) collective-permute-start(bf16[96,6144]{1,0:T(8,128)(2,1)S(1)} %collective-permute-done.14.refs_7_.refs_13_.refs_15_), channel_id=1, source_target_pairs={{0,6},{1,3},{2,0},{3,5},{4,2},{5,7},{6,4},{7,1},{8,14},{9,11},{10,... | collective-permute-start | bytes 3538952 | tf_op jit(solution)/shard_map/ppermute | solution.py:28
  59.9 47.7 %copy-start.5 = (bf16[96,6144]{1,0:T(8,128)(2,1)}, bf16[96,6144]{1,0:T(8,128)(2,1)S(1)}, u32[]{:S(2)}) copy-start(bf16[96,6144]{1,0:T(8,128)(2,1)S(1)} %collective-permute-done.9.refs_2_.refs_8_.refs_10_) | copy-start | bytes 3538948
  59.9 28.8 %collective-permute-start.16 = (bf16[96,6144]{1,0:T(8,128)(2,1)S(1)}, bf16[96,6144]{1,0:T(8,128)(2,1)}, u32[]{:S(2)}, u32[]{:S(2)}) collective-permute-start(bf16[96,6144]{1,0:T(8,128)(2,1)S(1)} %collective-permute-done.10.refs_3_.refs_9_.refs_11_), channel_id=1, source_target_pairs={{0,2},{1,7},{2,4},{3,1},{4,6},{5,3},{6,0},{7,5},{8,10},{9,15},{10,... | collective-permute-start | bytes 3538952 | tf_op jit(solution)/shard_map/ppermute | solution.py:28
  81.1 25.9 %collective-permute-start.18 = (bf16[96,6144]{1,0:T(8,128)(2,1)S(1)}, bf16[96,6144]{1,0:T(8,128)(2,1)}, u32[]{:S(2)}, u32[]{:S(2)}) collective-permute-start(bf16[96,6144]{1,0:T(8,128)(2,1)S(1)} %collective-permute-done.10.refs_3_.refs_9_.refs_11_), channel_id=1, source_target_pairs={{0,8},{8,0},{1,9},{9,1},{2,10},{10,2},{3,11},{11,3},{4,12},{12,4},... | collective-permute-start | bytes 3538952 | tf_op jit(solution)/shard_map/ppermute | solution.py:36
  82.0 1.0 copy-start.11
  82.0 25.0 %collective-permute-start.15 = (bf16[96,6144]{1,0:T(8,128)(2,1)S(1)}, bf16[96,6144]{1,0:T(8,128)(2,1)S(1)}, u32[]{:S(2)}, u32[]{:S(2)}) collective-permute-start(bf16[96,6144]{1,0:T(8,128)(2,1)S(1)} %collective-permute-done.14.refs_7_.refs_13_.refs_15_), channel_id=1, source_target_pairs={{0,1},{1,0},{2,3},{3,2},{4,5},{5,4},{6,7},{7,6},{8,9},{9,8},{10,11... | collective-permute-start | bytes 3538952 | tf_op jit(solution)/shard_map/ppermute | solution.py:44
  83.0 24.7 %copy-start.6 = (bf16[96,6144]{1,0:T(8,128)(2,1)}, bf16[96,6144]{1,0:T(8,128)(2,1)S(1)}, u32[]{:S(2)}) copy-start(bf16[96,6144]{1,0:T(8,128)(2,1)S(1)} %collective-permute-done.11.refs_4_.refs_10_.refs_12_) | copy-start | bytes 3538948
  83.0 24.6 %collective-permute-start.13 = (bf16[96,6144]{1,0:T(8,128)(2,1)S(1)}, bf16[96,6144]{1,0:T(8,128)(2,1)S(1)}, u32[]{:S(2)}, u32[]{:S(2)}) collective-permute-start(bf16[96,6144]{1,0:T(8,128)(2,1)S(1)} %collective-permute-done.12.refs_5_.refs_11_.refs_13_), channel_id=1, source_target_pairs={{0,1},{1,0},{2,3},{3,2},{4,5},{5,4},{6,7},{7,6},{8,9},{9,8},{10,11... | collective-permute-start | bytes 3538952 | tf_op jit(solution)/shard_map/ppermute | solution.py:44
  87.5 20.1 %collective-permute-start.22 = (bf16[96,6144]{1,0:T(8,128)(2,1)}, bf16[96,6144]{1,0:T(8,128)(2,1)}, u32[]{:S(2)}, u32[]{:S(2)}) collective-permute-start(bf16[96,6144]{1,0:T(8,128)(2,1)} %collective-permute-done.20.refs_19_.refs_21_), channel_id=1, source_target_pairs={{0,6},{1,3},{2,0},{3,5},{4,2},{5,7},{6,4},{7,1},{8,14},{9,11},{10,... | collective-permute-start | bytes 3538952 | tf_op jit(solution)/shard_map/ppermute | solution.py:28
  88.7 30.8 %collective-permute-start.17 = (bf16[96,6144]{1,0:T(8,128)(2,1)}, bf16[96,6144]{1,0:T(8,128)(2,1)}, u32[]{:S(2)}, u32[]{:S(2)}) collective-permute-start(bf16[96,6144]{1,0:T(8,128)(2,1)} %collective-permute-done.16.refs_15_.refs_17_), channel_id=1, source_target_pairs={{0,1},{1,0},{2,3},{3,2},{4,5},{5,4},{6,7},{7,6},{8,9},{9,8},{10,11... | collective-permute-start | bytes 3538952 | tf_op jit(solution)/shard_map/ppermute | solution.py:44
  107.0 13.4 %collective-permute-start.19 = (bf16[96,6144]{1,0:T(8,128)(2,1)}, bf16[96,6144]{1,0:T(8,128)(2,1)}, u32[]{:S(2)}, u32[]{:S(2)}) collective-permute-start(bf16[96,6144]{1,0:T(8,128)(2,1)} %collective-permute-done.18.refs_17_.refs_19_), channel_id=1, source_target_pairs={{0,1},{1,0},{2,3},{3,2},{4,5},{5,4},{6,7},{7,6},{8,9},{9,8},{10,11... | collective-permute-start | bytes 3538952 | tf_op jit(solution)/shard_map/ppermute | solution.py:44
  107.0 1.9 copy-start.7
  107.0 13.4 %collective-permute-start.21 = (bf16[96,6144]{1,0:T(8,128)(2,1)}, bf16[96,6144]{1,0:T(8,128)(2,1)}, u32[]{:S(2)}, u32[]{:S(2)}) collective-permute-start(bf16[96,6144]{1,0:T(8,128)(2,1)} %collective-permute-done.20.refs_19_.refs_21_), channel_id=1, source_target_pairs={{0,1},{1,0},{2,3},{3,2},{4,5},{5,4},{6,7},{7,6},{8,9},{9,8},{10,11... | collective-permute-start | bytes 3538952 | tf_op jit(solution)/shard_map/ppermute | solution.py:44
  107.6 1.1 copy-start.8
  107.6 34.4 %collective-permute-start.8 = (bf16[128,4096]{1,0:T(8,128)(2,1)}, bf16[128,4096]{1,0:T(8,128)(2,1)}, u32[]{:S(2)}, u32[]{:S(2)}) collective-permute-start(bf16[128,4096]{1,0:T(8,128)(2,1)} %collective-permute-done.4.refs_4_), channel_id=1, source_target_pairs={{0,32},{1,97},{32,64},{33,1},{64,96},{65,33},{96,0},{97,65},{2,34}... | collective-permute-start | bytes 3145736 | tf_op jit(solution)/shard_map/ppermute | solution.py:32
  108.7 33.3 %collective-permute-start.23 = (bf16[96,6144]{1,0:T(8,128)(2,1)}, bf16[96,6144]{1,0:T(8,128)(2,1)}, u32[]{:S(2)}, u32[]{:S(2)}) collective-permute-start(bf16[96,6144]{1,0:T(8,128)(2,1)} %collective-permute-done.22.refs_23_), channel_id=1, source_target_pairs={{0,1},{1,0},{2,3},{3,2},{4,5},{5,4},{6,7},{7,6},{8,9},{9,8},{10,11... | collective-permute-start | bytes 3538952 | tf_op jit(solution)/shard_map/ppermute | solution.py:44
  119.4 22.5 %collective-permute-start.7 = (bf16[128,2048]{1,0:T(8,128)(2,1)}, bf16[128,2048]{1,0:T(8,128)(2,1)S(1)}, u32[]{:S(2)}, u32[]{:S(2)}) collective-permute-start(bf16[128,2048]{1,0:T(8,128)(2,1)} %collective-permute-done.3.refs_3_), channel_id=1, source_target_pairs={{0,32},{1,97},{32,64},{33,1},{64,96},{65,33},{96,0},{97,65},{2,34}... | collective-permute-start | bytes 1572872 | tf_op jit(solution)/shard_map/ppermute | solution.py:32
  141.9 0.8 copy-start.14
  163.5 11.6 %all-to-all-start.1 = ((bf16[16,2,32,128]{3,2,1,0:T(8,128)(2,1)}), bf16[16,2,32,128]{3,2,1,0:T(8,128)(2,1)S(1)}, u32[]{:S(2)}, u32[]{:S(2)}) async-start(bf16[16,2,32,128]{3,2,1,0:T(8,128)(2,1)} %states.1), calls=%async_computation.1 | async-start | bytes 524288 | tf_op jit(solution)/shard_map/all_to_all | solution.py:364
  175.1 0.7 copy-start.12
  177.6 11.4 %all-to-all-start.2 = ((bf16[16,2,32,128]{3,2,1,0:T(8,128)(2,1)}), bf16[16,2,32,128]{3,2,1,0:T(8,128)(2,1)S(1)}, u32[]{:S(2)}, u32[]{:S(2)}) async-start(bf16[16,2,32,128]{3,2,1,0:T(8,128)(2,1)} %carries.1), calls=%async_computation.2 | async-start | bytes 524288 | tf_op jit(solution)/shard_map/all_to_all | solution.py:369
  188.9 0.7 copy-start.9
  192.6 15.3 %collective-permute-start.24 = (bf16[512,512]{1,0:T(8,128)(2,1)}, bf16[512,512]{1,0:T(8,128)(2,1)S(1)}, u32[]{:S(2)}, u32[]{:S(2)}) collective-permute-start(bf16[512,512]{1,0:T(8,128)(2,1)} %finish.3), channel_id=1, source_target_pairs={{0,24},{8,16},{16,8},{24,0},{1,25},{9,17},{17,9},{25,1},{2,26},{10... | collective-permute-start | bytes 1572872 | tf_op jit(solution)/shard_map/ppermute | solution.py:40
where the time goes:
time: 211 us; the launch traced here: 210 us
  waiting for transfers between devices  87.9 us (42%)
  Pallas kernels  67.4 us (32%)
  starting transfers between devices  38.1 us (18%)
  local copies, waits for them, and re-layouts  9.93 us (5%)
  other arithmetic  6.62 us (3%)
    pallas_call x3, Pallas kernels, project(): pl.pallas_call(kernel, grid_spec=pltpu.PrefetchScalarGridSpec(num_scalar_...  49.8 us
    ppermute x6, waiting for transfers between devices, x_move(): return lax.ppermute(v, ('x', 'c'), ring_pairs(step))  26.3 us
    ppermute x4, waiting for transfers between devices, z_out(): return lax.ppermute(v, ('zh', 'zl'), [(i, 3 - i) for i in range(4)])  23.2 us
    ppermute x2, waiting for transfers between devices, z_in(): return lax.ppermute(v, 'zl', [(0, 1), (1, 0)])  19.5 us
    ppermute x4, starting transfers between devices, z_out(): return lax.ppermute(v, ('zh', 'zl'), [(i, 3 - i) for i in range(4)])  10.3 us
    ppermute x6, starting transfers between devices, x_move(): return lax.ppermute(v, ('x', 'c'), ring_pairs(step))  7.53 us
    all_to_all x1, waiting for transfers between devices, shards(): decays = jnp.exp(lax.all_to_all(parts, GROUP, 0, 0, tiled=True))  7.05 us
    pallas_call x2, Pallas kernels, intra(): pl.pallas_call(kernel, grid=(1,), in_specs=[pl.BlockSpec((128, TOK), lamb...  6.9 us
  transfers between devices with their start and end apart: 28, of which 12 were waited for; matrix products, arithmetic and copies ran while one was open for 5% of the time, Pallas kernels for 20%

commit v1 on v0

v1 whole, which is shorter than its diff:
```python
import jax
import jax.numpy as jnp
from jax import lax
from jax.experimental import pallas as pl
from jax.experimental.pallas import tpu as pltpu
from jax.sharding import Mesh
from jax.sharding import PartitionSpec as P


F32 = jnp.float32
BF16 = jnp.bfloat16
TOK = 512
DIM = 6144
UNIT = 96
KB = 1536
NK = DIM // KB
SPLIT = 2
GROUP = ("zl", "y", "c")
SEQ = ("zh", "zl", "y", "c")


def ring_pairs(step):
    return [
        (i * 2 + c, ((i + (step if c == 0 else -step)) % 4) * 2 + c) for i in range(4) for c in range(2)
    ]


def y_move(v, step):
    return lax.ppermute(v, ("y", "c"), ring_pairs(step))


def x_move(v, step):
    return lax.ppermute(v, ("x", "c"), ring_pairs(step))


def z_in(v):
    return lax.ppermute(v, "zl", [(0, 1), (1, 0)])


def z_out(v):
    return lax.ppermute(v, ("zh", "zl"), [(i, 3 - i) for i in range(4)])


def exchange(v, axes):
    return lax.all_to_all(v, axes, 0, 0, tiled=True)


def core_swap(v):
    return lax.ppermute(v, "c", [(0, 1), (1, 0)])


def project(scalars, blocks, units, jobs, held):
    flat = [a for arrays in blocks for a in arrays]
    count = sum(len(u) for _, u in jobs)
    both = len(blocks) == 2

    def kernel(s_ref, *refs):
        x_refs, refs = refs[: len(flat)], refs[len(flat) :]
        w_refs, refs = refs[: len(units)], refs[len(units) :]
        if held is not None:
            refs = refs[1:]
        u_ref, sem, refs = refs[0], refs[1], refs[2:]
        accs, stages, refs = refs[: len(jobs)], refs[len(jobs) : 2 * len(jobs)], refs[2 * len(jobs) :]
        k = pl.program_id(0)
        values = [x_refs[0]]
        if both:
            buf = refs[0]
            for p in range(4):
                row = pl.multiple_of(s_ref[16 + p] * 128, 128)

                @pl.when(k < SPLIT)
                def _():
                    buf[pl.ds(row, 128), :] = x_refs[1 + p][...]

                @pl.when(k >= SPLIT)
                def _():
                    buf[pl.ds(row, 128), :] = x_refs[5 + p][...]

            values.append(buf)
        for (block, members), acc in zip(jobs, accs):
            w = jnp.concatenate([w_refs[m][...] for m in members], axis=0)
            part = lax.dot_general(
                w, values[block][...], (((1,), (1,)), ((), ())), preferred_element_type=F32
            )

            @pl.when(k == 0)
            def _():
                acc[...] = part

            @pl.when(k > 0)
            def _():
                acc[...] += part

        @pl.when(k == NK - 1)
        def _():
            copies = []
            for (block, members), acc, stage in zip(jobs, accs, stages):
                for i, m in enumerate(members):
                    rows = slice(i * UNIT, (i + 1) * UNIT)
                    v = acc[rows, :]
                    stage[rows, :] = (v * jax.nn.sigmoid(v)).astype(BF16)
                    at = pl.multiple_of(s_ref[units[m][1]] * UNIT, UNIT)
                    copy = pltpu.make_async_copy(
                        stage.at[rows, :],
                        u_ref.at[pl.ds(at, UNIT), block * TOK : (block + 1) * TOK],
                        sem.at[len(copies)],
                    )
                    copy.start()
                    copies.append(copy)
            for copy in copies:
                copy.wait()

    in_specs = [pl.BlockSpec((TOK, KB), lambda k, s: (0, k))]
    if both:
        in_specs += [pl.BlockSpec((128, KB), lambda k, s: (0, jnp.minimum(k, SPLIT - 1)))] * 4
        in_specs += [pl.BlockSpec((128, KB), lambda k, s: (0, jnp.maximum(k - SPLIT, 0)))] * 4
    in_specs += [pl.BlockSpec((UNIT, KB), lambda k, s: (0, k))] * len(units)
    scratch = [pltpu.SemaphoreType.DMA((count,))]
    scratch += [pltpu.VMEM((len(u) * UNIT, TOK), F32) for _, u in jobs]
    scratch += [pltpu.VMEM((len(u) * UNIT, TOK), BF16) for _, u in jobs]
    if both:
        scratch.append(pltpu.VMEM((TOK, KB), BF16))
    args = [scalars, *flat, *[w for w, _ in units]]
    aliases = {}
    if held is not None:
        in_specs.append(pl.BlockSpec(memory_space=pl.ANY))
        aliases = {len(args): 0}
        args.append(held)
    return pl.pallas_call(
        kernel,
        grid_spec=pltpu.PrefetchScalarGridSpec(
            num_scalar_prefetch=1,
            grid=(NK,),
            in_specs=in_specs,
            out_specs=pl.BlockSpec(memory_space=pl.ANY),
            scratch_shapes=scratch,
        ),
        out_shape=jax.ShapeDtypeStruct((16 * UNIT, 2 * TOK), BF16),
        input_output_aliases=aliases,
        cost_estimate=pl.CostEstimate(
            flops=2 * count * UNIT * TOK * DIM,
            bytes_accessed=2 * DIM * (len(units) * UNIT + TOK * len(blocks)),
            transcendentals=count * UNIT * TOK,
        ),
        name="project",
    )(*args)


SMEM = pl.BlockSpec(memory_space=pltpu.SMEM)


def running_sum(v):
    lane = lax.broadcasted_iota(jnp.int32, v.shape, 1)
    step = 1
    while step < v.shape[1]:
        v = v + jnp.where(lane >= step, pltpu.roll(v, step, 1), 0.0)
        step *= 2
    return v


def rates(side, log_decay, across):
    def kernel(z_ref, d_ref, a_ref, all_ref, mine_ref, total_ref):
        here, there = running_sum(d_ref[...]), running_sum(a_ref[...])
        for h in range(8):
            all_ref[h] = here[h : h + 1]
        for half in range(2):

            @pl.when(z_ref[0] == half)
            def _():
                for h in range(4):
                    mine_ref[h] = here[half * 4 + h : half * 4 + h + 1]
                    mine_ref[4 + h] = there[half * 4 + h : half * 4 + h + 1]

        last = jnp.broadcast_to(here[:, TOK - 1 :], (8, 128))
        for d in range(32):
            total_ref[d] = last[d // 4 : d // 4 + 1]

    return pl.pallas_call(
        kernel,
        grid=(1,),
        in_specs=[SMEM, whole((8, TOK)), whole((8, TOK))],
        out_specs=[whole((8, 1, TOK)), whole((8, 1, TOK)), whole((32, 1, 128))],
        out_shape=[
            jax.ShapeDtypeStruct((8, 1, TOK), F32),
            jax.ShapeDtypeStruct((8, 1, TOK), F32),
            jax.ShapeDtypeStruct((32, 1, 128), F32),
        ],
        name="rates",
    )(side, log_decay, across)


def heads_of(kind):
    return [pl.BlockSpec((128, 2 * TOK), lambda i, h=h: (h * 3 + kind, 0)) for h in range(4)]


def whole(shape):
    return pl.BlockSpec(shape, lambda i: (0,) * len(shape))


def states(held, cumulated):
    def kernel(*refs):
        k_refs, v_refs, q_refs, c_ref, o_ref, q_out = refs[:4], refs[4:8], refs[8:12], *refs[12:]
        for h in range(4):
            q_out[h] = q_refs[h][...]
        dims = (((1,), (1,)), ((), ()))
        for block in range(2):
            lanes = slice(block * TOK, (block + 1) * TOK)
            for h in range(4):
                cum = c_ref[block * 4 + h]
                tail = jnp.exp(cum[:, TOK - 1 :] - cum)
                k = k_refs[h][:, lanes].astype(F32) * tail
                high = k.astype(BF16)
                low = (k - high.astype(F32)).astype(BF16)
                v = v_refs[h][:, lanes]
                update = lax.dot_general(high, v, dims, preferred_element_type=F32)
                update += lax.dot_general(low, v, dims, preferred_element_type=F32)
                o_ref[h * 4 : h * 4 + 4, block] = update.astype(BF16).reshape(4, 32, 128)

    return pl.pallas_call(
        kernel,
        grid=(1,),
        in_specs=heads_of(1)
        + heads_of(2)
        + [pl.BlockSpec((128, TOK), lambda i, h=h: (h * 3, 1)) for h in range(4)]
        + [whole((8, 1, TOK))],
        out_specs=[whole((16, 2, 32, 128)), whole((4, 128, TOK))],
        out_shape=[
            jax.ShapeDtypeStruct((16, 2, 32, 128), BF16),
            jax.ShapeDtypeStruct((4, 128, TOK), BF16),
        ],
        name="states",
    )(*[held] * 12, cumulated)


def intra(held, cumulated, block, dtype):
    def kernel(*refs):
        q_refs, k_refs, v_refs, c_ref, o_ref = refs[:4], refs[4:8], refs[8:12], refs[12], refs[13]
        for h in range(4):
            cum = c_ref[h]
            cum_col = jnp.transpose(jnp.broadcast_to(cum, (128, TOK)))
            for j in range(4):
                lanes = slice(j * 128, (j + 1) * 128)
                count = (j + 1) * 128
                scores = lax.dot_general(
                    k_refs[h][:, :count],
                    q_refs[h][:, lanes],
                    (((0,), (0,)), ((), ())),
                    preferred_element_type=F32,
                )
                spread = cum[:, lanes] - cum_col[:count]
                s = lax.broadcasted_iota(jnp.int32, (count, 128), 0)
                t = lax.broadcasted_iota(jnp.int32, (count, 128), 1) + j * 128
                decay = jnp.exp(jnp.where(s <= t, spread, -1e30))
                weights = (scores * decay).astype(BF16)
                inside = jnp.dot(v_refs[h][:, :count], weights, preferred_element_type=F32)
                o_ref[h, :, lanes] = inside.astype(dtype)

    return pl.pallas_call(
        kernel,
        grid=(1,),
        in_specs=[
            pl.BlockSpec((128, TOK), lambda i, h=h, kind=kind: (h * 3 + kind, block))
            for kind in range(3)
            for h in range(4)
        ]
        + [pl.BlockSpec((4, 1, TOK), lambda i: (block, 0, 0))],
        out_specs=whole((4, 128, TOK)),
        out_shape=jax.ShapeDtypeStruct((4, 128, TOK), dtype),
        name="intra",
    )(*[held] * 12, cumulated)


def carries(order, totals, pieces):
    def kernel(n_ref, d_ref, s_ref, o_ref):
        state = jnp.zeros((32, 128), F32)
        for b in range(32):
            z, yc = b // 8, b % 8
            o_ref[b] = state.astype(BF16)
            piece = s_ref[n_ref[2 * z] * 8 + yc, n_ref[2 * z + 1]]
            state = jnp.exp(d_ref[b]) * state + piece.astype(F32)

    return pl.pallas_call(
        kernel,
        grid=(1,),
        in_specs=[SMEM, whole((32, 1, 128)), whole((16, 2, 32, 128))],
        out_specs=whole((32, 32, 128)),
        out_shape=jax.ShapeDtypeStruct((32, 32, 128), BF16),
        name="carries",
    )(order, totals, pieces)


def finish(half, queries, cumulated, inside, carried, gains, output):
    def kernel(z_ref, *refs):
        q_refs, (c_ref, i_ref, s_ref, g_ref), o_ref = refs[: len(queries)], refs[len(queries) :][:4], refs[-1]
        for h in range(4):
            q = q_refs[h][...] if len(queries) == 4 else q_refs[0][h]
            carry = s_ref[4 * h : 4 * h + 4].reshape(128, 128)
            outer = lax.dot_general(carry, q, (((0,), (0,)), ((), ())), preferred_element_type=F32)
            combined = i_ref[h].astype(F32) + outer * jnp.exp(c_ref[h])
            root = lax.rsqrt(jnp.mean(combined * combined, axis=0, keepdims=True) + 1e-05)
            gain = g_ref[pl.ds(z_ref[0] * 4 + h, 1), :]
            o_ref[:, h * 128 : (h + 1) * 128] = (jnp.transpose(combined * root) * gain).astype(BF16)

    if len(queries) == 4:
        q_specs = [pl.BlockSpec((128, TOK), lambda i, z, h=h: (h * 3, 0)) for h in range(4)]
    else:
        q_specs = [pl.BlockSpec((4, 128, TOK), lambda i, z: (0, 0, 0))]
    in_specs = q_specs + [
        pl.BlockSpec((4, 1, TOK), lambda i, z: (z[0], 0, 0)),
        pl.BlockSpec((4, 128, TOK), lambda i, z: (0, 0, 0)),
        pl.BlockSpec((16, 32, 128), lambda i, z: (z[0], 0, 0)),
        pl.BlockSpec((8, 128), lambda i, z: (0, 0)),
    ]
    args = [half, *queries, cumulated, inside, carried, gains]
    aliases = {}
    if output is not None:
        in_specs.append(pl.BlockSpec(memory_space=pl.ANY))
        aliases = {len(args): 0}
        args.append(output)
    return pl.pallas_call(
        kernel,
        grid_spec=pltpu.PrefetchScalarGridSpec(
            num_scalar_prefetch=1,
            grid=(1,),
            in_specs=in_specs,
            out_specs=pl.BlockSpec((TOK, 512), lambda i, z: (0, z[0])),
        ),
        out_shape=jax.ShapeDtypeStruct((TOK, 1024), BF16),
        input_output_aliases=aliases,
        name="finish",
    )(*args)


def shards(inputs, qkv_weight, log_decay, out_gain):
    x = lax.axis_index("x")
    zh = lax.axis_index("zh")
    zl = lax.axis_index("zl")
    y = lax.axis_index("y")
    c = lax.axis_index("c")
    side = 1 - 2 * c

    order = jnp.where(zh == 0, jnp.array([0, 0, 1, 0, 1, 1, 0, 1]), jnp.array([1, 1, 0, 1, 0, 0, 1, 0]))
    order = order.astype(jnp.int32)
    mine, other = zh.astype(jnp.int32).reshape(1), (1 - zh).astype(jnp.int32).reshape(1)

    def unit(row, shift, core):
        return (row * 4 + (y + shift) % 4) * 2 + core

    zi, cs = 1 - zl, 1 - c
    rows = [
        unit(zl, 0, c),
        unit(zl, 0, cs),
        unit(zl, -side, c),
        unit(zl, side, cs),
        unit(zl, side, c),
        unit(zl, -side, cs),
        unit(zi, 0, c),
        unit(zi, 0, cs),
        unit(zl, 2, c),
        unit(zl, 2, cs),
        unit(zi, -side, c),
        unit(zi, side, cs),
        unit(zi, side, c),
        unit(zi, -side, cs),
        unit(zi, 2, c),
        unit(zi, 2, cs),
    ]
    quarters = [q % 4 for q in (x, x - side, x + side, x + 2)]
    scalars = jnp.stack(rows + quarters).astype(jnp.int32)

    own = qkv_weight.T
    quarter = lax.dynamic_slice(inputs, (128 * x, 0), (128, DIM))
    cut = SPLIT * KB
    w_a = y_move(own, 1)
    w_b = y_move(own, -1)
    w_z = z_in(own)
    log_decay_across = z_out(log_decay)
    a0 = z_out(quarter[:, :cut])
    a1 = z_out(quarter[:, cut:])
    s_own = core_swap(own)
    xa0 = x_move(a0, 1)
    xb0 = x_move(a0, -1)
    cumulated_here, cumulated, totals = rates(mine, log_decay, log_decay_across)
    totals = exchange(totals, SEQ)
    w_a, totals, scalars, order = lax.optimization_barrier((w_a, totals, scalars, order))
    w_c = y_move(w_a, 1)
    w_zb = y_move(w_z, -1)
    w_za = z_in(w_a)
    s_a = core_swap(w_a)
    s_b = core_swap(w_b)
    s_z = core_swap(w_z)
    xc0 = x_move(xa0, 1)
    xa1 = x_move(a1, 1)
    xb1 = x_move(a1, -1)
    w_zbb = y_move(w_zb, -1)
    s_c = core_swap(w_c)
    s_zb = core_swap(w_zb)
    s_za = core_swap(w_za)
    xc1 = x_move(xa1, 1)
    s_zbb = core_swap(w_zbb)

    weights = [own, s_own, w_a, s_a, w_b, s_b, w_z, s_z, w_c, s_c, w_za, s_za, w_zb, s_zb, w_zbb, s_zbb]
    units = [(w, i) for i, w in enumerate(weights)]
    here, across = [inputs], [a0, xa0, xb0, xc0, a1, xa1, xb1, xc1]
    held = project(scalars, [here], units[:8], [(0, range(8))], None)
    held = project(scalars, [here], units[8:14], [(0, range(6))], held)
    held = project(scalars, [here, across], units, [(1, range(16)), (0, (14, 15))], held)

    own_states, queries = states(held, cumulated)
    update = exchange(own_states, GROUP)
    over_queries = z_out(queries)
    inside_across = intra(held, cumulated, 1, BF16)
    over_inside = z_out(inside_across)
    running = carries(order, totals, update)
    carried = exchange(running, SEQ)
    inside = intra(held, cumulated, 0, F32)
    carried, inside = lax.optimization_barrier((carried, inside))
    output = finish(mine, [held] * 4, cumulated_here, inside, carried, out_gain, None)
    over_queries, over_inside, output = lax.optimization_barrier((over_queries, over_inside, output))
    return finish(other, [over_queries], cumulated_here, over_inside, carried, out_gain, output)


def solution(mesh):
    fine = Mesh(mesh.devices.reshape(4, 2, 2, 4, 2), ("x", "zh", "zl", "y", "c"))
    seq = ("zh", "zl", "y", "c")
    in_specs = (P(seq, None), P(None, ("x",) + seq), P("x", seq), P("x", None))
    return jax.shard_map(shards, mesh=fine, in_specs=in_specs, out_specs=P(seq, "x"), check_vma=False)
```

time: 211 us -> 208 us (0.986)
  blocking collectives: 0 us -> 11.6 us
  Pallas kernels: 67.4 us -> 60.4 us
  other arithmetic: 6.62 us -> 1.21 us
  local copies, waits for them, and re-layouts: 9.93 us -> 6.11 us
  starting transfers between devices: 38.1 us -> 41.9 us
  waiting for transfers between devices: 87.9 us -> 84.9 us
    ppermute x2, waiting for transfers between devices: 19.5 us -> 2.4 us  [z_in(): return lax.ppermute(v, 'zl', [(0, 1), (1, 0)])]
    ppermute x5, waiting for transfers between devices: 4.82 us -> 21.2 us  [y_move(): return lax.ppermute(v, ('y', 'c'), ring_pairs(step))]
    ppermute x6, waiting for transfers between devices: 26.3 us -> 11.1 us  [x_move(): return lax.ppermute(v, ('x', 'c'), ring_pairs(step))]
    all_to_all x0 -> x1, blocking collectives: none -> 11.6 us  [exchange(): return lax.all_to_all(v, axes, 0, 0, tiled=True)]
    pallas_call x3, Pallas kernels: 49.8 us -> 41.1 us  [project(): pl.pallas_call(kernel, grid_spec=pltpu.PrefetchScalarGridSpec(num_scalar_...]
    ppermute x4 -> x5, waiting for transfers between devices: 23.2 us -> 29.9 us  [z_out(): return lax.ppermute(v, ('zh', 'zl'), [(i, 3 - i) for i in range(4)])]
    all_to_all x3 -> x2, waiting for transfers between devices: 14 us -> 20.3 us  [exchange(): return lax.all_to_all(v, axes, 0, 0, tiled=True)]
    ppermute x5, starting transfers between devices: 5.27 us -> 8.54 us  [y_move(): return lax.ppermute(v, ('y', 'c'), ring_pairs(step))]
  transfers between devices with their start and end apart: 28 -> 28, of which waited for: 12 -> 7; matrix products, arithmetic and copies ran while one was open for 5% -> 1% of each run, Pallas kernels for 20% -> 14%
where the time goes in v1:
time: 208 us; the launch traced here: 206 us
  waiting for transfers between devices  84.9 us (41%)
  Pallas kernels  60.4 us (29%)
  starting transfers between devices  41.9 us (20%)
  blocking collectives  11.6 us (6%)
  local copies, waits for them, and re-layouts  6.11 us (3%)
    pallas_call x3, Pallas kernels, project(): pl.pallas_call(kernel, grid_spec=pltpu.PrefetchScalarGridSpec(num_scalar_...  41.1 us
    ppermute x5, waiting for transfers between devices, z_out(): return lax.ppermute(v, ('zh', 'zl'), [(i, 3 - i) for i in range(4)])  29.9 us
    ppermute x5, waiting for transfers between devices, y_move(): return lax.ppermute(v, ('y', 'c'), ring_pairs(step))  21.2 us
    all_to_all x2, waiting for transfers between devices, exchange(): return lax.all_to_all(v, axes, 0, 0, tiled=True)  20.3 us
    all_to_all x1, blocking collectives, exchange(): return lax.all_to_all(v, axes, 0, 0, tiled=True)  11.6 us
    ppermute x6, waiting for transfers between devices, x_move(): return lax.ppermute(v, ('x', 'c'), ring_pairs(step))  11.1 us
    ppermute x5, starting transfers between devices, z_out(): return lax.ppermute(v, ('zh', 'zl'), [(i, 3 - i) for i in range(4)])  10.7 us
    all_to_all x2, starting transfers between devices, exchange(): return lax.all_to_all(v, axes, 0, 0, tiled=True)  10.2 us
  transfers between devices with their start and end apart: 28, of which 7 were waited for; matrix products, arithmetic and copies ran while one was open for 1% of the time, Pallas kernels for 14%

profile of v1, /device:TPU:0, one launch (start us, length us, event | category | flops | bytes accessed | tf_op | source)
XLA Modules:
  0.0 206.4 jit_solution(16285063650600354333)
XLA Ops:
  0.0 1.6 fusion
  1.6 4.2 %collective-permute-start.2 = (bf16[128,3072]{1,0:T(8,128)(2,1)S(1)}, bf16[128,3072]{1,0:T(8,128)(2,1)}, u32[]{:S(2)}, u32[]{:S(2)}) collective-permute-start(bf16[128,3072]{1,0:T(8,128)(2,1)S(1)} %get-tuple-element.34), channel_id=1, source_target_pairs={{0,24},{8,16},{16,8},{24,0},{1,25},{9,17},{17,9},{25,1},{2,26},{10... | collective-permute-start | bytes 2359304 | tf_op jit(solution)/shard_map/ppermute | solution.py:41
  5.8 1.6 collective-permute-start
  7.4 0.1 collective-permute-start.6
  7.5 3.1 %collective-permute-start.1 = (f32[8,512]{1,0:T(8,128)S(1)}, f32[8,512]{1,0:T(8,128)S(1)}, u32[]{:S(2)}, u32[]{:S(2)}) collective-permute-start(f32[8,512]{1,0:T(8,128)S(1)} %copy-done.15), channel_id=1, source_target_pairs={{0,24},{8,16},{16,8},{24,0},{1,25},{9,17},{17,9},{25,1},{2,26},{10... | collective-permute-start | bytes 49160 | tf_op jit(solution)/shard_map/ppermute | solution.py:41
  10.6 29.9 %collective-permute-done.1.a_ref = f32[8,512]{1,0:T(8,128)S(1)} collective-permute-done((f32[8,512]{1,0:T(8,128)S(1)}, f32[8,512]{1,0:T(8,128)S(1)}, u32[]{:S(2)}, u32[]{:S(2)}) %collective-permute-start.1) | collective-permute-done | bytes 16416 | tf_op jit(solution)/shard_map/ppermute | solution.py:41
  40.6 3.0 %collective-permute-start.12 = (bf16[96,6144]{1,0:T(8,128)(2,1)S(1)}, bf16[96,6144]{1,0:T(8,128)(2,1)S(1)}, u32[]{:S(2)}, u32[]{:S(2)}) collective-permute-start(bf16[96,6144]{1,0:T(8,128)(2,1)S(1)} %bitcast.27), channel_id=1, source_target_pairs={{0,6},{1,3},{2,0},{3,5},{4,2},{5,7},{6,4},{7,1},{8,14},{9,11},{10,... | collective-permute-start | bytes 3538952 | tf_op jit(solution)/shard_map/ppermute | solution.py:29
  43.6 0.0 collective-permute-done.2.refs_1_
  43.6 0.0 collective-permute-start.10
  43.6 0.0 collective-permute-done.6.refs_5_
  43.6 1.6 collective-permute-start.3
  45.1 1.5 collective-permute-start.7
  46.6 0.7 collective-permute-start.20
  47.4 1.9 rates.1
  49.3 6.4 %all-to-all-start = ((f32[32,1,128]{2,1,0:T(1,128)}), f32[32,1,128]{2,1,0:T(1,128)S(1)}, u32[]{:S(2)}, u32[]{:S(2)}) async-start(f32[32,1,128]{2,1,0:T(1,128)} %get-tuple-element.19), calls=%async_computation | async-start | bytes 32768 | tf_op jit(solution)/shard_map/all_to_all | solution.py:45
  55.7 1.2 broadcast_select_fusion.n_ref
  56.9 0.7 stack.83.s_ref
  57.6 15.0 %all-to-all-done.d_ref = f32[32,1,128]{2,1,0:T(1,128)S(1)} async-done(((f32[32,1,128]{2,1,0:T(1,128)}), f32[32,1,128]{2,1,0:T(1,128)S(1)}, u32[]{:S(2)}, u32[]{:S(2)}) %all-to-all-start) | async-done | bytes 16416 | tf_op jit(solution)/shard_map/all_to_all | solution.py:45
  72.5 0.0 collective-permute-done.12.refs_5_.refs_13_
  72.5 0.1 collective-permute-start.11
  72.6 0.0 collective-permute-done.10.refs_2_.refs_10_
  72.6 2.0 collective-permute-start.16
  74.7 0.0 collective-permute-done.3.refs_2_
  74.7 0.9 collective-permute-start.18
  75.5 0.0 collective-permute-done.7.refs_6_
  75.5 1.5 collective-permute-start.15
  77.1 0.0 collective-permute-done.20.refs_5_.refs_21_
  77.1 1.2 collective-permute-start.22
  78.2 0.0 collective-permute-done.11.refs_4_.refs_12_
  78.2 0.0 collective-permute-start.13
  78.2 1.1 copy-done.9
  79.3 21.2 %collective-permute-done.16.refs_1_.refs_17_ = bf16[96,6144]{1,0:T(8,128)(2,1)S(1)} collective-permute-done((bf16[96,6144]{1,0:T(8,128)(2,1)}, bf16[96,6144]{1,0:T(8,128)(2,1)S(1)}, u32[]{:S(2)}, u32[]{:S(2)}) %collective-permute-start.16) | collective-permute-done | bytes 1179680 | tf_op jit(solution)/shard_map/ppermute | solution.py:29
  100.5 0.0 collective-permute-start.17
  100.5 2.4 %collective-permute-done.18.refs_3_.refs_19_ = bf16[96,6144]{1,0:T(8,128)(2,1)S(1)} collective-permute-done((bf16[96,6144]{1,0:T(8,128)(2,1)}, bf16[96,6144]{1,0:T(8,128)(2,1)S(1)}, u32[]{:S(2)}, u32[]{:S(2)}) %collective-permute-start.18) | collective-permute-done | bytes 1179680 | tf_op jit(solution)/shard_map/ppermute | solution.py:37
  102.9 0.7 collective-permute-start.19
  103.5 0.0 collective-permute-done.15.refs_8_.refs_16_
  103.5 0.1 collective-permute-start.21
  103.6 0.0 collective-permute-done.22.refs_23_
  103.6 0.4 collective-permute-start.23
  104.1 0.0 collective-permute-done.13.refs_6_.refs_14_
  104.1 2.8 %collective-permute-start.4 = (bf16[128,3072]{1,0:T(8,128)(2,1)}, bf16[128,3072]{1,0:T(8,128)(2,1)}, u32[]{:S(2)}, u32[]{:S(2)}) collective-permute-start(bf16[128,3072]{1,0:T(8,128)(2,1)} %collective-permute-done.2.refs_1_), channel_id=1, source_target_pairs={{0,96},{1,33},{32,0},{33,65},{64,32},{65,97},{96,64},{97,1},{2,98}... | collective-permute-start | bytes 2359304 | tf_op jit(solution)/shard_map/ppermute | solution.py:33
  106.8 0.8 collective-permute-start.8
  107.7 1.2 collective-permute-start.5
  108.9 1.0 copy-done.6
  109.9 1.0 collective-permute-start.9
  110.9 10.7 %project.3.refs_7_ = bf16[1536,1024]{1,0:T(8,128)(2,1)} custom-call(s32[20]{0:T(128)} %stack.83.s_ref, bf16[512,6144]{1,0:T(8,128)(2,1)} %refs_0_.5, bf16[96,6144]{1,0:T(8,128)(2,1)} %bitcast.23, bf16[96,6144]{1,0:T(8,128)(2,1)} %collective-permute-done.10.refs_2_.refs_10_, bf16[96,6144]{1,0:T(8,128)(2,1)} %collective-permute-done.refs_3_.refs_11_, ...), custom_call_target="tpu_custom_call" | custom-call | flops 4831838208 | bytes 15728640 | tf_op jit(solution)/shard_map/project/pallas_call | solution.py:129
  121.7 9.2 %project.4.refs_25_ = bf16[1536,1024]{1,0:T(8,128)(2,1)} custom-call(s32[20]{0:T(128)} %stack.83.s_ref, bf16[512,6144]{1,0:T(8,128)(2,1)} %refs_0_.5, bf16[96,6144]{1,0:T(8,128)(2,1)} %copy-done.2, bf16[96,6144]{1,0:T(8,128)(2,1)} %copy-done.4, bf16[96,6144]{1,0:T(8,128)(2,1)} %copy-done.3, ...), custom_call_target="tpu_custom_call", output_to_operand_aliasing={{}: (8, {})} | custom-call | flops 3623878656 | bytes 13369344 | tf_op jit(solution)/shard_map/project/pallas_call | solution.py:129
  130.9 9.7 %collective-permute-done.8.refs_7_ = bf16[128,3072]{1,0:T(8,128)(2,1)} collective-permute-done((bf16[128,3072]{1,0:T(8,128)(2,1)}, bf16[128,3072]{1,0:T(8,128)(2,1)}, u32[]{:S(2)}, u32[]{:S(2)}) %collective-permute-start.8) | collective-permute-done | bytes 786464 | tf_op jit(solution)/shard_map/ppermute | solution.py:33
  140.6 1.4 collective-permute-done.9.refs_8_
  142.0 21.2 %project.5.refs_0_.refs_1_.refs_2_.refs_3_.refs_4_.refs_5_.refs_6_.refs_7_.refs_8_.refs_9_.refs_10_.refs_11_ = bf16[1536,1024]{1,0:T(8,128)(2,1)} custom-call(s32[20]{0:T(128)} %stack.83.s_ref, bf16[512,6144]{1,0:T(8,128)(2,1)} %refs_0_.5, bf16[128,3072]{1,0:T(8,128)(2,1)} %collective-permute-done.2.refs_1_, ...), custom_call_target="tpu_custom_call", output_to_operand_aliasing={{}: (26, {})} | custom-call | flops 10871635968 | bytes 31457280 | tf_op jit(solution)/shard_map/project/pallas_call | solution.py:129
  163.2 3.2 %states.1 = (bf16[16,2,32,128]{3,2,1,0:T(8,128)(2,1)}, bf16[4,128,512]{2,1,0:T(8,128)(2,1)}) custom-call(bf16[1536,1024]{1,0:T(8,128)(2,1)} %project.5.refs_0_.refs_1_.refs_2_.refs_3_.refs_4_.refs_5_.refs_6_.refs_7_.refs_8_.refs_9_.refs_10_.refs_11_, ...), custom_call_target="tpu_custom_call" | custom-call | tf_op jit(solution)/shard_map/states/pallas_call | solution.py:219
  166.4 3.4 %intra.2 = bf16[4,128,512]{2,1,0:T(8,128)(2,1)} custom-call(bf16[1536,1024]{1,0:T(8,128)(2,1)} %project.5.refs_0_.refs_1_.refs_2_.refs_3_.refs_4_.refs_5_.refs_6_.refs_7_.refs_8_.refs_9_.refs_10_.refs_11_, bf16[1536,1024]{1,0:T(8,128)(2,1)} %project.5.refs_0_.refs_1_.refs_2_.refs_3_.refs_4_.refs_5_.refs_6_.refs_7_.refs_8_.refs_9_.refs_10_.refs_11_, ...), custom_call_target="tpu_custom_call" | custom-call | tf_op jit(solution)/shard_map/intra/pallas_call | solution.py:258
  169.8 0.7 collective-permute-start.24
  170.5 2.6 %collective-permute-start.25 = (bf16[4,128,512]{2,1,0:T(8,128)(2,1)}, bf16[4,128,512]{2,1,0:T(8,128)(2,1)S(1)}, u32[]{:S(2)}, u32[]{:S(2)}) collective-permute-start(bf16[4,128,512]{2,1,0:T(8,128)(2,1)} %intra.2), channel_id=1, source_target_pairs={{0,24},{8,16},{16,8},{24,0},{1,25},{9,17},{17,9},{25,1},{2,26},{10... | collective-permute-start | bytes 1572872 | tf_op jit(solution)/shard_map/ppermute | solution.py:41
  173.0 11.6 %all_to_all.15.s_ref = bf16[16,2,32,128]{3,2,1,0:T(8,128)(2,1)} all-to-all(bf16[16,2,32,128]{3,2,1,0:T(8,128)(2,1)S(1)} %copy-done.13), channel_id=1, replica_groups=mesh['x'=4,'zh'=2,'zl'=2,'y'=4,'c'=2] {'zl','y','c'}, dimensions={0} | all-to-all | bytes 524288 | tf_op jit(solution)/shard_map/all_to_all | solution.py:45
  184.7 1.8 carries.1
  186.4 3.9 %all-to-all-start.2 = ((bf16[32,32,128]{2,1,0:T(8,128)(2,1)}), bf16[32,32,128]{2,1,0:T(8,128)(2,1)S(1)}, u32[]{:S(2)}, u32[]{:S(2)}) async-start(bf16[32,32,128]{2,1,0:T(8,128)(2,1)} %carries.1), calls=%async_computation.2 | async-start | bytes 524288 | tf_op jit(solution)/shard_map/all_to_all | solution.py:45
  190.3 3.5 %intra.3.refs_5_ = f32[4,128,512]{2,1,0:T(8,128)} custom-call(bf16[1536,1024]{1,0:T(8,128)(2,1)} %project.5.refs_0_.refs_1_.refs_2_.refs_3_.refs_4_.refs_5_.refs_6_.refs_7_.refs_8_.refs_9_.refs_10_.refs_11_, bf16[1536,1024]{1,0:T(8,128)(2,1)} %project.5.refs_0_.refs_1_.refs_2_.refs_3_.refs_4_.refs_5_.refs_6_.refs_7_.refs_8_.refs_9_.refs_10_.refs_11_, ...), custom_call_target="tpu_custom_call" | custom-call | tf_op jit(solution)/shard_map/intra/pallas_call | solution.py:258
  193.8 5.3 %all-to-all-done.2.refs_6_.refs_3_ = bf16[32,32,128]{2,1,0:T(8,128)(2,1)S(1)} async-done(((bf16[32,32,128]{2,1,0:T(8,128)(2,1)}), bf16[32,32,128]{2,1,0:T(8,128)(2,1)S(1)}, u32[]{:S(2)}, u32[]{:S(2)}) %all-to-all-start.2) | async-done | bytes 262176 | tf_op jit(solution)/shard_map/all_to_all | solution.py:45
  199.1 0.7 copy-done
  199.8 2.8 %finish.2.refs_5_ = bf16[512,1024]{1,0:T(8,128)(2,1)} custom-call(s32[1]{0:T(128)} %bitcast.2.z_ref, bf16[1536,1024]{1,0:T(8,128)(2,1)} %project.5.refs_0_.refs_1_.refs_2_.refs_3_.refs_4_.refs_5_.refs_6_.refs_7_.refs_8_.refs_9_.refs_10_.refs_11_, ...), custom_call_target="tpu_custom_call" | custom-call | tf_op jit(solution)/shard_map/finish/pallas_call | solution.py:320
  202.7 0.8 copy-done.11
  203.5 0.2 copy-done.12
  203.7 2.7 %finish.3 = bf16[512,1024]{1,0:T(8,128)(2,1)} custom-call(s32[1]{0:T(128)} %bitcast.z_ref, bf16[4,128,512]{2,1,0:T(8,128)(2,1)} %copy-done.11, f32[8,1,512]{2,1,0:T(1,128)} %get-tuple-element.24.refs_4_.refs_1_, bf16[4,128,512]{2,1,0:T(8,128)(2,1)} %copy-done.12, bf16[32,32,128]{2,1,0:T(8,128)(2,1)} %copy-done, ...), custom_call_target="tpu_custom_call", output_to_operand_aliasing={{}: (6, {})} | custom-call | tf_op jit(solution)/shard_map/finish/pallas_call | solution.py:320
  (42 shorter events, 0.1 us)
Async XLA Ops:
  0.0 5.8 %copy-start.7 = (bf16[6144,96]{0,1:T(8,128)(2,1)S(1)}, bf16[6144,96]{0,1:T(8,128)(2,1)}, u32[]{:S(2)}) copy-start(bf16[6144,96]{0,1:T(8,128)(2,1)} %param.7) | copy-start | bytes 3538948
  0.0 7.5 %copy-start.15 = (f32[8,512]{1,0:T(8,128)S(1)}, f32[8,512]{1,0:T(8,128)}, u32[]{:S(2)}) copy-start(f32[8,512]{1,0:T(8,128)} %d_ref.1) | copy-start | bytes 49156
  1.6 42.0 %collective-permute-start.2 = (bf16[128,3072]{1,0:T(8,128)(2,1)S(1)}, bf16[128,3072]{1,0:T(8,128)(2,1)}, u32[]{:S(2)}, u32[]{:S(2)}) collective-permute-start(bf16[128,3072]{1,0:T(8,128)(2,1)S(1)} %get-tuple-element.34), channel_id=1, source_target_pairs={{0,24},{8,16},{16,8},{24,0},{1,25},{9,17},{17,9},{25,1},{2,26},{10... | collective-permute-start | bytes 2359304 | tf_op jit(solution)/shard_map/ppermute | solution.py:41
  5.8 39.3 %collective-permute-start = (bf16[96,6144]{1,0:T(8,128)(2,1)S(1)}, bf16[96,6144]{1,0:T(8,128)(2,1)}, u32[]{:S(2)}, u32[]{:S(2)}) collective-permute-start(bf16[96,6144]{1,0:T(8,128)(2,1)S(1)} %bitcast.25), channel_id=1, source_target_pairs={{0,2},{1,7},{2,4},{3,1},{4,6},{5,3},{6,0},{7,5},{8,10},{9,15},{10,... | collective-permute-start | bytes 3538952 | tf_op jit(solution)/shard_map/ppermute | solution.py:29
  7.4 36.2 %collective-permute-start.6 = (bf16[128,3072]{1,0:T(8,128)(2,1)S(1)}, bf16[128,3072]{1,0:T(8,128)(2,1)}, u32[]{:S(2)}, u32[]{:S(2)}) collective-permute-start(bf16[128,3072]{1,0:T(8,128)(2,1)S(1)} %get-tuple-element.33), channel_id=1, source_target_pairs={{0,24},{8,16},{16,8},{24,0},{1,25},{9,17},{17,9},{25,1},{2,26},{10... | collective-permute-start | bytes 2359304 | tf_op jit(solution)/shard_map/ppermute | solution.py:41
  7.5 39.2 %collective-permute-start.14 = (bf16[96,6144]{1,0:T(8,128)(2,1)S(1)}, bf16[96,6144]{1,0:T(8,128)(2,1)}, u32[]{:S(2)}, u32[]{:S(2)}) collective-permute-start(bf16[96,6144]{1,0:T(8,128)(2,1)S(1)} %bitcast.26), channel_id=1, source_target_pairs={{0,8},{8,0},{1,9},{9,1},{2,10},{10,2},{3,11},{11,3},{4,12},{12,4},... | collective-permute-start | bytes 3538952 | tf_op jit(solution)/shard_map/ppermute | solution.py:37
  7.5 33.1 %collective-permute-start.1 = (f32[8,512]{1,0:T(8,128)S(1)}, f32[8,512]{1,0:T(8,128)S(1)}, u32[]{:S(2)}, u32[]{:S(2)}) collective-permute-start(f32[8,512]{1,0:T(8,128)S(1)} %copy-done.15), channel_id=1, source_target_pairs={{0,24},{8,16},{16,8},{24,0},{1,25},{9,17},{17,9},{25,1},{2,26},{10... | collective-permute-start | bytes 49160 | tf_op jit(solution)/shard_map/ppermute | solution.py:41
  40.6 6.8 %copy-start.16 = (f32[8,512]{1,0:T(8,128)}, f32[8,512]{1,0:T(8,128)S(1)}, u32[]{:S(2)}) copy-start(f32[8,512]{1,0:T(8,128)S(1)} %collective-permute-done.1.a_ref) | copy-start | bytes 49156
  40.6 32.0 %collective-permute-start.12 = (bf16[96,6144]{1,0:T(8,128)(2,1)S(1)}, bf16[96,6144]{1,0:T(8,128)(2,1)S(1)}, u32[]{:S(2)}, u32[]{:S(2)}) collective-permute-start(bf16[96,6144]{1,0:T(8,128)(2,1)S(1)} %bitcast.27), channel_id=1, source_target_pairs={{0,6},{1,3},{2,0},{3,5},{4,2},{5,7},{6,4},{7,1},{8,14},{9,11},{10,... | collective-permute-start | bytes 3538952 | tf_op jit(solution)/shard_map/ppermute | solution.py:29
  43.6 29.1 %collective-permute-start.10 = (bf16[96,6144]{1,0:T(8,128)(2,1)S(1)}, bf16[96,6144]{1,0:T(8,128)(2,1)}, u32[]{:S(2)}, u32[]{:S(2)}) collective-permute-start(bf16[96,6144]{1,0:T(8,128)(2,1)S(1)} %bitcast.28), channel_id=1, source_target_pairs={{0,1},{1,0},{2,3},{3,2},{4,5},{5,4},{6,7},{7,6},{8,9},{9,8},{10,11... | collective-permute-start | bytes 3538952 | tf_op jit(solution)/shard_map/ppermute | solution.py:49
  43.6 31.1 %collective-permute-start.3 = (bf16[128,3072]{1,0:T(8,128)(2,1)}, bf16[128,3072]{1,0:T(8,128)(2,1)}, u32[]{:S(2)}, u32[]{:S(2)}) collective-permute-start(bf16[128,3072]{1,0:T(8,128)(2,1)} %collective-permute-done.2.refs_1_), channel_id=1, source_target_pairs={{0,32},{1,97},{32,64},{33,1},{64,96},{65,33},{96,0},{97,65},{2,34}... | collective-permute-start | bytes 2359304 | tf_op jit(solution)/shard_map/ppermute | solution.py:33
  45.1 30.4 %collective-permute-start.7 = (bf16[128,3072]{1,0:T(8,128)(2,1)}, bf16[128,3072]{1,0:T(8,128)(2,1)}, u32[]{:S(2)}, u32[]{:S(2)}) collective-permute-start(bf16[128,3072]{1,0:T(8,128)(2,1)} %collective-permute-done.6.refs_5_), channel_id=1, source_target_pairs={{0,32},{1,97},{32,64},{33,1},{64,96},{65,33},{96,0},{97,65},{2,34}... | collective-permute-start | bytes 2359304 | tf_op jit(solution)/shard_map/ppermute | solution.py:33
  46.6 30.4 %collective-permute-start.20 = (bf16[96,6144]{1,0:T(8,128)(2,1)}, bf16[96,6144]{1,0:T(8,128)(2,1)S(1)}, u32[]{:S(2)}, u32[]{:S(2)}) collective-permute-start(bf16[96,6144]{1,0:T(8,128)(2,1)} %collective-permute-done.14.refs_7_.refs_15_), channel_id=1, source_target_pairs={{0,6},{1,3},{2,0},{3,5},{4,2},{5,7},{6,4},{7,1},{8,14},{9,11},{10,... | collective-permute-start | bytes 3538952 | tf_op jit(solution)/shard_map/ppermute | solution.py:29
  49.3 23.2 %all-to-all-start = ((f32[32,1,128]{2,1,0:T(1,128)}), f32[32,1,128]{2,1,0:T(1,128)S(1)}, u32[]{:S(2)}, u32[]{:S(2)}) async-start(f32[32,1,128]{2,1,0:T(1,128)} %get-tuple-element.19), calls=%async_computation | async-start | bytes 32768 | tf_op jit(solution)/shard_map/all_to_all | solution.py:45
  72.5 49.1 %copy-start.14 = (f32[32,1,128]{2,1,0:T(1,128)}, f32[32,1,128]{2,1,0:T(1,128)S(1)}, u32[]{:S(2)}) copy-start(f32[32,1,128]{2,1,0:T(1,128)S(1)} %all-to-all-done.d_ref) | copy-start | bytes 49156
  72.5 2.1 %copy-start.8 = (bf16[96,6144]{1,0:T(8,128)(2,1)}, bf16[96,6144]{1,0:T(8,128)(2,1)S(1)}, u32[]{:S(2)}) copy-start(bf16[96,6144]{1,0:T(8,128)(2,1)S(1)} %collective-permute-done.12.refs_5_.refs_13_) | copy-start | bytes 3538948
  72.5 5.7 %collective-permute-start.11 = (bf16[96,6144]{1,0:T(8,128)(2,1)}, bf16[96,6144]{1,0:T(8,128)(2,1)S(1)}, u32[]{:S(2)}, u32[]{:S(2)}) collective-permute-start(bf16[96,6144]{1,0:T(8,128)(2,1)} %collective-permute-done.refs_3_.refs_11_), channel_id=1, source_target_pairs={{0,1},{1,0},{2,3},{3,2},{4,5},{5,4},{6,7},{7,6},{8,9},{9,8},{10,11... | collective-permute-start | bytes 3538952 | tf_op jit(solution)/shard_map/ppermute | solution.py:49
  72.6 27.9 %collective-permute-start.16 = (bf16[96,6144]{1,0:T(8,128)(2,1)}, bf16[96,6144]{1,0:T(8,128)(2,1)S(1)}, u32[]{:S(2)}, u32[]{:S(2)}) collective-permute-start(bf16[96,6144]{1,0:T(8,128)(2,1)} %collective-permute-done.refs_3_.refs_11_), channel_id=1, source_target_pairs={{0,2},{1,7},{2,4},{3,1},{4,6},{5,3},{6,0},{7,5},{8,10},{9,15},{10,... | collective-permute-start | bytes 3538952 | tf_op jit(solution)/shard_map/ppermute | solution.py:29
  74.7 28.2 %collective-permute-start.18 = (bf16[96,6144]{1,0:T(8,128)(2,1)}, bf16[96,6144]{1,0:T(8,128)(2,1)S(1)}, u32[]{:S(2)}, u32[]{:S(2)}) collective-permute-start(bf16[96,6144]{1,0:T(8,128)(2,1)} %collective-permute-done.refs_3_.refs_11_), channel_id=1, source_target_pairs={{0,8},{8,0},{1,9},{9,1},{2,10},{10,2},{3,11},{11,3},{4,12},{12,4},... | collective-permute-start | bytes 3538952 | tf_op jit(solution)/shard_map/ppermute | solution.py:37
  75.5 28.0 %collective-permute-start.15 = (bf16[96,6144]{1,0:T(8,128)(2,1)}, bf16[96,6144]{1,0:T(8,128)(2,1)}, u32[]{:S(2)}, u32[]{:S(2)}) collective-permute-start(bf16[96,6144]{1,0:T(8,128)(2,1)} %collective-permute-done.14.refs_7_.refs_15_), channel_id=1, source_target_pairs={{0,1},{1,0},{2,3},{3,2},{4,5},{5,4},{6,7},{7,6},{8,9},{9,8},{10,11... | collective-permute-start | bytes 3538952 | tf_op jit(solution)/shard_map/ppermute | solution.py:49
  77.1 44.6 %copy-start.1 = (bf16[96,6144]{1,0:T(8,128)(2,1)}, bf16[96,6144]{1,0:T(8,128)(2,1)S(1)}, u32[]{:S(2)}) copy-start(bf16[96,6144]{1,0:T(8,128)(2,1)S(1)} %collective-permute-done.20.refs_5_.refs_21_) | copy-start | bytes 3538948
  77.1 26.6 %collective-permute-start.22 = (bf16[96,6144]{1,0:T(8,128)(2,1)S(1)}, bf16[96,6144]{1,0:T(8,128)(2,1)}, u32[]{:S(2)}, u32[]{:S(2)}) collective-permute-start(bf16[96,6144]{1,0:T(8,128)(2,1)S(1)} %collective-permute-done.20.refs_5_.refs_21_), channel_id=1, source_target_pairs={{0,6},{1,3},{2,0},{3,5},{4,2},{5,7},{6,4},{7,1},{8,14},{9,11},{10,... | collective-permute-start | bytes 3538952 | tf_op jit(solution)/shard_map/ppermute | solution.py:29
  78.2 1.1 copy-start.9
  78.2 25.8 %collective-permute-start.13 = (bf16[96,6144]{1,0:T(8,128)(2,1)}, bf16[96,6144]{1,0:T(8,128)(2,1)S(1)}, u32[]{:S(2)}, u32[]{:S(2)}) collective-permute-start(bf16[96,6144]{1,0:T(8,128)(2,1)} %copy-done.8), channel_id=1, source_target_pairs={{0,1},{1,0},{2,3},{3,2},{4,5},{5,4},{6,7},{7,6},{8,9},{9,8},{10,11... | collective-permute-start | bytes 3538952 | tf_op jit(solution)/shard_map/ppermute | solution.py:49
  100.5 21.2 %copy-start.2 = (bf16[96,6144]{1,0:T(8,128)(2,1)}, bf16[96,6144]{1,0:T(8,128)(2,1)S(1)}, u32[]{:S(2)}) copy-start(bf16[96,6144]{1,0:T(8,128)(2,1)S(1)} %collective-permute-done.16.refs_1_.refs_17_) | copy-start | bytes 3538948
  100.5 6.3 %collective-permute-start.17 = (bf16[96,6144]{1,0:T(8,128)(2,1)S(1)}, bf16[96,6144]{1,0:T(8,128)(2,1)S(1)}, u32[]{:S(2)}, u32[]{:S(2)}) collective-permute-start(bf16[96,6144]{1,0:T(8,128)(2,1)S(1)} %collective-permute-done.16.refs_1_.refs_17_), channel_id=1, source_target_pairs={{0,1},{1,0},{2,3},{3,2},{4,5},{5,4},{6,7},{7,6},{8,9},{9,8},{10,11... | collective-permute-start | bytes 3538952 | tf_op jit(solution)/shard_map/ppermute | solution.py:49
  102.9 18.8 %copy-start.3 = (bf16[96,6144]{1,0:T(8,128)(2,1)}, bf16[96,6144]{1,0:T(8,128)(2,1)S(1)}, u32[]{:S(2)}) copy-start(bf16[96,6144]{1,0:T(8,128)(2,1)S(1)} %collective-permute-done.18.refs_3_.refs_19_) | copy-start | bytes 3538948
  102.9 4.8 %collective-permute-start.19 = (bf16[96,6144]{1,0:T(8,128)(2,1)S(1)}, bf16[96,6144]{1,0:T(8,128)(2,1)S(1)}, u32[]{:S(2)}, u32[]{:S(2)}) collective-permute-start(bf16[96,6144]{1,0:T(8,128)(2,1)S(1)} %collective-permute-done.18.refs_3_.refs_19_), channel_id=1, source_target_pairs={{0,1},{1,0},{2,3},{3,2},{4,5},{5,4},{6,7},{7,6},{8,9},{9,8},{10,11... | collective-permute-start | bytes 3538952 | tf_op jit(solution)/shard_map/ppermute | solution.py:49
  103.5 5.3 %collective-permute-start.21 = (bf16[96,6144]{1,0:T(8,128)(2,1)S(1)}, bf16[96,6144]{1,0:T(8,128)(2,1)S(1)}, u32[]{:S(2)}, u32[]{:S(2)}) collective-permute-start(bf16[96,6144]{1,0:T(8,128)(2,1)S(1)} %collective-permute-done.20.refs_5_.refs_21_), channel_id=1, source_target_pairs={{0,1},{1,0},{2,3},{3,2},{4,5},{5,4},{6,7},{7,6},{8,9},{9,8},{10,11... | collective-permute-start | bytes 3538952 | tf_op jit(solution)/shard_map/ppermute | solution.py:49
  103.6 38.3 %collective-permute-start.23 = (bf16[96,6144]{1,0:T(8,128)(2,1)}, bf16[96,6144]{1,0:T(8,128)(2,1)}, u32[]{:S(2)}, u32[]{:S(2)}) collective-permute-start(bf16[96,6144]{1,0:T(8,128)(2,1)} %collective-permute-done.22.refs_23_), channel_id=1, source_target_pairs={{0,1},{1,0},{2,3},{3,2},{4,5},{5,4},{6,7},{7,6},{8,9},{9,8},{10,11... | collective-permute-start | bytes 3538952 | tf_op jit(solution)/shard_map/ppermute | solution.py:49
  104.1 4.8 %copy-start.10 = (bf16[96,6144]{1,0:T(8,128)(2,1)}, bf16[96,6144]{1,0:T(8,128)(2,1)S(1)}, u32[]{:S(2)}) copy-start(bf16[96,6144]{1,0:T(8,128)(2,1)S(1)} %collective-permute-done.13.refs_6_.refs_14_) | copy-start | bytes 3538948
  104.1 26.8 %collective-permute-start.4 = (bf16[128,3072]{1,0:T(8,128)(2,1)}, bf16[128,3072]{1,0:T(8,128)(2,1)}, u32[]{:S(2)}, u32[]{:S(2)}) collective-permute-start(bf16[128,3072]{1,0:T(8,128)(2,1)} %collective-permute-done.2.refs_1_), channel_id=1, source_target_pairs={{0,96},{1,33},{32,0},{33,65},{64,32},{65,97},{96,64},{97,1},{2,98}... | collective-permute-start | bytes 2359304 | tf_op jit(solution)/shard_map/ppermute | solution.py:33
  106.8 2.0 copy-start.4
  106.8 33.7 %collective-permute-start.8 = (bf16[128,3072]{1,0:T(8,128)(2,1)}, bf16[128,3072]{1,0:T(8,128)(2,1)}, u32[]{:S(2)}, u32[]{:S(2)}) collective-permute-start(bf16[128,3072]{1,0:T(8,128)(2,1)} %collective-permute-done.6.refs_5_), channel_id=1, source_target_pairs={{0,96},{1,33},{32,0},{33,65},{64,32},{65,97},{96,64},{97,1},{2,98}... | collective-permute-start | bytes 2359304 | tf_op jit(solution)/shard_map/ppermute | solution.py:33
  107.7 1.2 copy-start.5
  107.7 32.9 %collective-permute-start.5 = (bf16[128,3072]{1,0:T(8,128)(2,1)}, bf16[128,3072]{1,0:T(8,128)(2,1)}, u32[]{:S(2)}, u32[]{:S(2)}) collective-permute-start(bf16[128,3072]{1,0:T(8,128)(2,1)} %collective-permute-done.3.refs_2_), channel_id=1, source_target_pairs={{0,32},{1,97},{32,64},{33,1},{64,96},{65,33},{96,0},{97,65},{2,34}... | collective-permute-start | bytes 2359304 | tf_op jit(solution)/shard_map/ppermute | solution.py:33
  108.9 1.0 copy-start.6
  109.9 32.1 %collective-permute-start.9 = (bf16[128,3072]{1,0:T(8,128)(2,1)}, bf16[128,3072]{1,0:T(8,128)(2,1)}, u32[]{:S(2)}, u32[]{:S(2)}) collective-permute-start(bf16[128,3072]{1,0:T(8,128)(2,1)} %collective-permute-done.7.refs_6_), channel_id=1, source_target_pairs={{0,32},{1,97},{32,64},{33,1},{64,96},{65,33},{96,0},{97,65},{2,34}... | collective-permute-start | bytes 2359304 | tf_op jit(solution)/shard_map/ppermute | solution.py:33
  166.4 3.4 %copy-start.17 = (bf16[4,128,512]{2,1,0:T(8,128)(2,1)S(1)}, bf16[4,128,512]{2,1,0:T(8,128)(2,1)}, u32[]{:S(2)}) copy-start(bf16[4,128,512]{2,1,0:T(8,128)(2,1)} %get-tuple-element.23) | copy-start | bytes 1572868
  166.4 6.6 %copy-start.13 = (bf16[16,2,32,128]{3,2,1,0:T(8,128)(2,1)S(1)}, bf16[16,2,32,128]{3,2,1,0:T(8,128)(2,1)}, u32[]{:S(2)}) copy-start(bf16[16,2,32,128]{3,2,1,0:T(8,128)(2,1)} %get-tuple-element.27) | copy-start | bytes 786436
  169.8 32.9 %collective-permute-start.24 = (bf16[4,128,512]{2,1,0:T(8,128)(2,1)S(1)}, bf16[4,128,512]{2,1,0:T(8,128)(2,1)S(1)}, u32[]{:S(2)}, u32[]{:S(2)}) collective-permute-start(bf16[4,128,512]{2,1,0:T(8,128)(2,1)S(1)} %copy-done.17), channel_id=1, source_target_pairs={{0,24},{8,16},{16,8},{24,0},{1,25},{9,17},{17,9},{25,1},{2,26},{10... | collective-permute-start | bytes 1572872 | tf_op jit(solution)/shard_map/ppermute | solution.py:41
  170.5 32.2 %collective-permute-start.25 = (bf16[4,128,512]{2,1,0:T(8,128)(2,1)}, bf16[4,128,512]{2,1,0:T(8,128)(2,1)S(1)}, u32[]{:S(2)}, u32[]{:S(2)}) collective-permute-start(bf16[4,128,512]{2,1,0:T(8,128)(2,1)} %intra.2), channel_id=1, source_target_pairs={{0,24},{8,16},{16,8},{24,0},{1,25},{9,17},{17,9},{25,1},{2,26},{10... | collective-permute-start | bytes 1572872 | tf_op jit(solution)/shard_map/ppermute | solution.py:41
  186.4 12.7 %all-to-all-start.2 = ((bf16[32,32,128]{2,1,0:T(8,128)(2,1)}), bf16[32,32,128]{2,1,0:T(8,128)(2,1)S(1)}, u32[]{:S(2)}, u32[]{:S(2)}) async-start(bf16[32,32,128]{2,1,0:T(8,128)(2,1)} %carries.1), calls=%async_computation.2 | async-start | bytes 524288 | tf_op jit(solution)/shard_map/all_to_all | solution.py:45
  199.1 0.7 copy-start
  202.7 0.8 copy-start.11
  202.7 1.0 copy-start.12

commit v2 on v1

--- a/solution.py
+++ b/solution.py
@@ -14,7 +14,7 @@
 UNIT = 96
 KB = 1536
 NK = DIM // KB
-SPLIT = 2
+CUTS = (0, 1, 2, 4)
 GROUP = ("zl", "y", "c")
 SEQ = ("zh", "zl", "y", "c")
 
@@ -59,22 +59,21 @@
         w_refs, refs = refs[: len(units)], refs[len(units) :]
         if held is not None:
             refs = refs[1:]
-        u_ref, sem, refs = refs[0], refs[1], refs[2:]
-        accs, stages, refs = refs[: len(jobs)], refs[len(jobs) : 2 * len(jobs)], refs[2 * len(jobs) :]
+        u_ref, refs = refs[0], refs[1:]
+        if both:
+            across_ref, query_ref, refs = refs[0], refs[1], refs[2:]
+        sem, accs, stage, refs = refs[0], refs[1 : 1 + len(jobs)], refs[1 + len(jobs)], refs[2 + len(jobs) :]
         k = pl.program_id(0)
         values = [x_refs[0]]
         if both:
             buf = refs[0]
-            for p in range(4):
-                row = pl.multiple_of(s_ref[16 + p] * 128, 128)
-
-                @pl.when(k < SPLIT)
+            for n in range(len(CUTS) - 1):
+
+                @pl.when((k >= CUTS[n]) & (k < CUTS[n + 1]))
                 def _():
-                    buf[pl.ds(row, 128), :] = x_refs[1 + p][...]
-
-                @pl.when(k >= SPLIT)
-                def _():
-                    buf[pl.ds(row, 128), :] = x_refs[5 + p][...]
+                    for p in range(4):
+                        row = pl.multiple_of(s_ref[16 + p] * 128, 128)
+                        buf[pl.ds(row, 128), :] = x_refs[1 + 4 * n + p][...]
 
             values.append(buf)
         for (block, members), acc in zip(jobs, accs):
@@ -94,32 +93,45 @@
         @pl.when(k == NK - 1)
         def _():
             copies = []
-            for (block, members), acc, stage in zip(jobs, accs, stages):
+            for (block, members), acc in zip(jobs, accs):
                 for i, m in enumerate(members):
                     rows = slice(i * UNIT, (i + 1) * UNIT)
                     v = acc[rows, :]
-                    stage[rows, :] = (v * jax.nn.sigmoid(v)).astype(BF16)
-                    at = pl.multiple_of(s_ref[units[m][1]] * UNIT, UNIT)
-                    copy = pltpu.make_async_copy(
-                        stage.at[rows, :],
-                        u_ref.at[pl.ds(at, UNIT), block * TOK : (block + 1) * TOK],
-                        sem.at[len(copies)],
-                    )
+                    v = (v * jax.nn.sigmoid(v)).astype(BF16)
+                    at = pl.ds(pl.multiple_of(s_ref[units[m][1]] * UNIT, UNIT), UNIT)
+                    if block == 1:
+                        across_ref[at, :] = v
+                        continue
+                    stage[rows, :] = v
+                    copy = pltpu.make_async_copy(stage.at[rows, :], u_ref.at[at, :], sem.at[i])
                     copy.start()
                     copies.append(copy)
+            if both:
+                for h in range(4):
+                    query_ref[h] = across_ref[h * 384 : h * 384 + 128, :]
             for copy in copies:
                 copy.wait()
 
     in_specs = [pl.BlockSpec((TOK, KB), lambda k, s: (0, k))]
     if both:
-        in_specs += [pl.BlockSpec((128, KB), lambda k, s: (0, jnp.minimum(k, SPLIT - 1)))] * 4
-        in_specs += [pl.BlockSpec((128, KB), lambda k, s: (0, jnp.maximum(k - SPLIT, 0)))] * 4
+        for n in range(len(CUTS) - 1):
+            low, last = CUTS[n], CUTS[n + 1] - CUTS[n] - 1
+            in_specs += [
+                pl.BlockSpec((128, KB), lambda k, s, low=low, last=last: (0, jnp.clip(k - low, 0, last)))
+            ] * 4
     in_specs += [pl.BlockSpec((UNIT, KB), lambda k, s: (0, k))] * len(units)
-    scratch = [pltpu.SemaphoreType.DMA((count,))]
+    own_count = sum(len(u) for block, u in jobs if block == 0)
+    scratch = [pltpu.SemaphoreType.DMA((own_count,))]
     scratch += [pltpu.VMEM((len(u) * UNIT, TOK), F32) for _, u in jobs]
-    scratch += [pltpu.VMEM((len(u) * UNIT, TOK), BF16) for _, u in jobs]
+    scratch += [pltpu.VMEM((own_count * UNIT, TOK), BF16)]
+    out_specs = [pl.BlockSpec(memory_space=pl.ANY)]
+    out_shape = [jax.ShapeDtypeStruct((16 * UNIT, TOK), BF16)]
     if both:
         scratch.append(pltpu.VMEM((TOK, KB), BF16))
+        out_specs.append(pl.BlockSpec((16 * UNIT, TOK), lambda k, s: (0, 0)))
+        out_specs.append(pl.BlockSpec((4, 128, TOK), lambda k, s: (0, 0, 0)))
+        out_shape.append(jax.ShapeDtypeStruct((16 * UNIT, TOK), BF16))
+        out_shape.append(jax.ShapeDtypeStruct((4, 128, TOK), BF16))
     args = [scalars, *flat, *[w for w, _ in units]]
     aliases = {}
     if held is not None:
@@ -132,10 +144,10 @@
             num_scalar_prefetch=1,
             grid=(NK,),
             in_specs=in_specs,
-            out_specs=pl.BlockSpec(memory_space=pl.ANY),
+            out_specs=out_specs,
             scratch_shapes=scratch,
         ),
-        out_shape=jax.ShapeDtypeStruct((16 * UNIT, 2 * TOK), BF16),
+        out_shape=out_shape,
         input_output_aliases=aliases,
         cost_estimate=pl.CostEstimate(
             flops=2 * count * UNIT * TOK * DIM,
@@ -158,19 +170,19 @@
     return v
 
 
-def rates(side, log_decay, across):
-    def kernel(z_ref, d_ref, a_ref, all_ref, mine_ref, total_ref):
-        here, there = running_sum(d_ref[...]), running_sum(a_ref[...])
+def whole(shape):
+    return pl.BlockSpec(shape, lambda i: (0,) * len(shape))
+
+
+def heads_of(kind):
+    return [pl.BlockSpec((128, TOK), lambda i, h=h: (h * 3 + kind, 0)) for h in range(4)]
+
+
+def rates(log_decay):
+    def kernel(d_ref, all_ref, total_ref):
+        here = running_sum(d_ref[...])
         for h in range(8):
             all_ref[h] = here[h : h + 1]
-        for half in range(2):
-
-            @pl.when(z_ref[0] == half)
-            def _():
-                for h in range(4):
-                    mine_ref[h] = here[half * 4 + h : half * 4 + h + 1]
-                    mine_ref[4 + h] = there[half * 4 + h : half * 4 + h + 1]
-
         last = jnp.broadcast_to(here[:, TOK - 1 :], (8, 128))
         for d in range(32):
             total_ref[d] = last[d // 4 : d // 4 + 1]
@@ -178,40 +190,26 @@
     return pl.pallas_call(
         kernel,
         grid=(1,),
-        in_specs=[SMEM, whole((8, TOK)), whole((8, TOK))],
-        out_specs=[whole((8, 1, TOK)), whole((8, 1, TOK)), whole((32, 1, 128))],
-        out_shape=[
-            jax.ShapeDtypeStruct((8, 1, TOK), F32),
-            jax.ShapeDtypeStruct((8, 1, TOK), F32),
-            jax.ShapeDtypeStruct((32, 1, 128), F32),
-        ],
+        in_specs=[whole((8, TOK))],
+        out_specs=[whole((8, 1, TOK)), whole((32, 1, 128))],
+        out_shape=[jax.ShapeDtypeStruct((8, 1, TOK), F32), jax.ShapeDtypeStruct((32, 1, 128), F32)],
         name="rates",
-    )(side, log_decay, across)
-
-
-def heads_of(kind):
-    return [pl.BlockSpec((128, 2 * TOK), lambda i, h=h: (h * 3 + kind, 0)) for h in range(4)]
-
-
-def whole(shape):
-    return pl.BlockSpec(shape, lambda i: (0,) * len(shape))
-
-
-def states(held, cumulated):
-    def kernel(*refs):
-        k_refs, v_refs, q_refs, c_ref, o_ref, q_out = refs[:4], refs[4:8], refs[8:12], *refs[12:]
-        for h in range(4):
-            q_out[h] = q_refs[h][...]
+    )(log_decay)
+
+
+def states(half, pairs):
+    def kernel(z_ref, *refs):
+        o_ref = refs[-1]
         dims = (((1,), (1,)), ((), ()))
         for block in range(2):
-            lanes = slice(block * TOK, (block + 1) * TOK)
+            k_refs, v_refs, c_ref = refs[9 * block :][:4], refs[9 * block + 4 :][:4], refs[9 * block + 8]
             for h in range(4):
-                cum = c_ref[block * 4 + h]
+                cum = c_ref[z_ref[0] * 4 + h]
                 tail = jnp.exp(cum[:, TOK - 1 :] - cum)
-                k = k_refs[h][:, lanes].astype(F32) * tail
+                k = k_refs[h][...].astype(F32) * tail
                 high = k.astype(BF16)
                 low = (k - high.astype(F32)).astype(BF16)
-                v = v_refs[h][:, lanes]
+                v = v_refs[h][...]
                 update = lax.dot_general(high, v, dims, preferred_element_type=F32)
                 update += lax.dot_general(low, v, dims, preferred_element_type=F32)
                 o_ref[h * 4 : h * 4 + 4, block] = update.astype(BF16).reshape(4, 32, 128)
@@ -219,24 +217,18 @@
     return pl.pallas_call(
         kernel,
         grid=(1,),
-        in_specs=heads_of(1)
-        + heads_of(2)
-        + [pl.BlockSpec((128, TOK), lambda i, h=h: (h * 3, 1)) for h in range(4)]
-        + [whole((8, 1, TOK))],
-        out_specs=[whole((16, 2, 32, 128)), whole((4, 128, TOK))],
-        out_shape=[
-            jax.ShapeDtypeStruct((16, 2, 32, 128), BF16),
-            jax.ShapeDtypeStruct((4, 128, TOK), BF16),
-        ],
+        in_specs=[SMEM] + (heads_of(1) + heads_of(2) + [whole((8, 1, TOK))]) * 2,
+        out_specs=whole((16, 2, 32, 128)),
+        out_shape=jax.ShapeDtypeStruct((16, 2, 32, 128), BF16),
         name="states",
-    )(*[held] * 12, cumulated)
-
-
-def intra(held, cumulated, block, dtype):
-    def kernel(*refs):
+    )(half, *[a for projected, sums in pairs for a in [projected] * 8 + [sums]])
+
+
+def intra(half, projected, sums, dtype):
+    def kernel(z_ref, *refs):
         q_refs, k_refs, v_refs, c_ref, o_ref = refs[:4], refs[4:8], refs[8:12], refs[12], refs[13]
         for h in range(4):
-            cum = c_ref[h]
+            cum = c_ref[z_ref[0] * 4 + h]
             cum_col = jnp.transpose(jnp.broadcast_to(cum, (128, TOK)))
             for j in range(4):
                 lanes = slice(j * 128, (j + 1) * 128)
@@ -258,16 +250,11 @@
     return pl.pallas_call(
         kernel,
         grid=(1,),
-        in_specs=[
-            pl.BlockSpec((128, TOK), lambda i, h=h, kind=kind: (h * 3 + kind, block))
-            for kind in range(3)
-            for h in range(4)
-        ]
-        + [pl.BlockSpec((4, 1, TOK), lambda i: (block, 0, 0))],
+        in_specs=[SMEM] + heads_of(0) + heads_of(1) + heads_of(2) + [whole((8, 1, TOK))],
         out_specs=whole((4, 128, TOK)),
         out_shape=jax.ShapeDtypeStruct((4, 128, TOK), dtype),
         name="intra",
-    )(*[held] * 12, cumulated)
+    )(half, *[projected] * 12, sums)
 
 
 def carries(order, totals, pieces):
@@ -369,19 +356,21 @@
     scalars = jnp.stack(rows + quarters).astype(jnp.int32)
 
     own = qkv_weight.T
-    quarter = lax.dynamic_slice(inputs, (128 * x, 0), (128, DIM))
-    cut = SPLIT * KB
+    cuts = [
+        lax.dynamic_slice(inputs, (128 * x, low * KB), (128, (high - low) * KB))
+        for low, high in zip(CUTS, CUTS[1:])
+    ]
     w_a = y_move(own, 1)
     w_b = y_move(own, -1)
     w_z = z_in(own)
-    log_decay_across = z_out(log_decay)
-    a0 = z_out(quarter[:, :cut])
-    a1 = z_out(quarter[:, cut:])
+    a = [z_out(cut) for cut in cuts]
+    sums, totals = rates(log_decay)
+    totals = exchange(totals, SEQ)
+    sums_across = z_out(sums)
     s_own = core_swap(own)
-    xa0 = x_move(a0, 1)
-    xb0 = x_move(a0, -1)
-    cumulated_here, cumulated, totals = rates(mine, log_decay, log_decay_across)
-    totals = exchange(totals, SEQ)
+    xa = [x_move(v, 1) for v in a]
+    xb = [x_move(v, -1) for v in a]
+    xc = [x_move(v, 1) for v in xa]
     w_a, totals, scalars, order = lax.optimization_barrier((w_a, totals, scalars, order))
     w_c = y_move(w_a, 1)
     w_zb = y_move(w_z, -1)
@@ -389,35 +378,32 @@
     s_a = core_swap(w_a)
     s_b = core_swap(w_b)
     s_z = core_swap(w_z)
-    xc0 = x_move(xa0, 1)
-    xa1 = x_move(a1, 1)
-    xb1 = x_move(a1, -1)
     w_zbb = y_move(w_zb, -1)
     s_c = core_swap(w_c)
     s_zb = core_swap(w_zb)
     s_za = core_swap(w_za)
-    xc1 = x_move(xa1, 1)
     s_zbb = core_swap(w_zbb)
 
     weights = [own, s_own, w_a, s_a, w_b, s_b, w_z, s_z, w_c, s_c, w_za, s_za, w_zb, s_zb, w_zbb, s_zbb]
     units = [(w, i) for i, w in enumerate(weights)]
-    here, across = [inputs], [a0, xa0, xb0, xc0, a1, xa1, xb1, xc1]
-    held = project(scalars, [here], units[:8], [(0, range(8))], None)
-    held = project(scalars, [here], units[8:14], [(0, range(6))], held)
-    held = project(scalars, [here, across], units, [(1, range(16)), (0, (14, 15))], held)
-
-    own_states, queries = states(held, cumulated)
+    here, across = [inputs], [v for parts in zip(a, xa, xb, xc) for v in parts]
+    (held,) = project(scalars, [here], units[:8], [(0, range(8))], None)
+    (held,) = project(scalars, [here], units[8:14], [(0, range(6))], held)
+    jobs = [(1, range(16)), (0, (14, 15))]
+    held, held_across, queries = project(scalars, [here, across], units, jobs, held)
+
+    over_queries = z_out(queries)
+    own_states = states(mine, [(held, sums), (held_across, sums_across)])
     update = exchange(own_states, GROUP)
-    over_queries = z_out(queries)
-    inside_across = intra(held, cumulated, 1, BF16)
+    inside_across = intra(mine, held_across, sums_across, BF16)
     over_inside = z_out(inside_across)
     running = carries(order, totals, update)
     carried = exchange(running, SEQ)
-    inside = intra(held, cumulated, 0, F32)
+    inside = intra(mine, held, sums, F32)
     carried, inside = lax.optimization_barrier((carried, inside))
-    output = finish(mine, [held] * 4, cumulated_here, inside, carried, out_gain, None)
+    output = finish(mine, [held] * 4, sums, inside, carried, out_gain, None)
     over_queries, over_inside, output = lax.optimization_barrier((over_queries, over_inside, output))
-    return finish(other, [over_queries], cumulated_here, over_inside, carried, out_gain, output)
+    return finish(other, [over_queries], sums, over_inside, carried, out_gain, output)
 
 
 def solution(mesh):

time: 208 us -> 202 us (0.971)
  waiting for transfers between devices: 84.9 us -> 72.6 us
  starting transfers between devices: 41.9 us -> 45.1 us
    ppermute x5 -> x6, waiting for transfers between devices: 29.9 us -> 17.9 us  [z_out(): return lax.ppermute(v, ('zh', 'zl'), [(i, 3 - i) for i in range(4)])]
    all_to_all x2, waiting for transfers between devices: 20.3 us -> 13.2 us  [exchange(): return lax.all_to_all(v, axes, 0, 0, tiled=True)]
    ppermute x6 -> x9, waiting for transfers between devices: 11.1 us -> 14 us  [x_move(): return lax.ppermute(v, ('x', 'c'), ring_pairs(step))]
    ppermute x6 -> x9, starting transfers between devices: 8.83 us -> 11.6 us  [x_move(): return lax.ppermute(v, ('x', 'c'), ring_pairs(step))]
    ppermute x5, starting transfers between devices: 8.54 us -> 11 us  [y_move(): return lax.ppermute(v, ('y', 'c'), ring_pairs(step))]
    dynamic_slice x0 -> x2, local copies, waits for them, and re-layouts: none -> 2.35 us  [shards(): lax.dynamic_slice(inputs, (128 * x, low * KB), (128, (high - low) * KB))]
    unnamed x36 -> x48, local copies, waits for them, and re-layouts: 3.86 us -> 5.05 us
    ppermute x5 -> x6, starting transfers between devices: 10.7 us -> 11.4 us  [z_out(): return lax.ppermute(v, ('zh', 'zl'), [(i, 3 - i) for i in range(4)])]
  transfers between devices with their start and end apart: 28 -> 32, of which waited for: 7 -> 13; matrix products, arithmetic and copies ran while one was open for 1% -> 1% of each run, Pallas kernels for 14% -> 28%
where the time goes in v2:
time: 202 us; the launch traced here: 200 us
  waiting for transfers between devices  72.6 us (36%)
  Pallas kernels  61.7 us (31%)
  starting transfers between devices  45.1 us (22%)
  blocking collectives  12.1 us (6%)
  local copies, waits for them, and re-layouts  8.08 us (4%)
    pallas_call x3, Pallas kernels, project(): pl.pallas_call(kernel, grid_spec=pltpu.PrefetchScalarGridSpec(num_scalar_...  42.6 us
    ppermute x5, waiting for transfers between devices, y_move(): return lax.ppermute(v, ('y', 'c'), ring_pairs(step))  22.4 us
    ppermute x6, waiting for transfers between devices, z_out(): return lax.ppermute(v, ('zh', 'zl'), [(i, 3 - i) for i in range(4)])  17.9 us
    ppermute x9, waiting for transfers between devices, x_move(): return lax.ppermute(v, ('x', 'c'), ring_pairs(step))  14 us
    all_to_all x2, waiting for transfers between devices, exchange(): return lax.all_to_all(v, axes, 0, 0, tiled=True)  13.2 us
    all_to_all x1, blocking collectives, exchange(): return lax.all_to_all(v, axes, 0, 0, tiled=True)  12.1 us
    ppermute x9, starting transfers between devices, x_move(): return lax.ppermute(v, ('x', 'c'), ring_pairs(step))  11.6 us
    ppermute x6, starting transfers between devices, z_out(): return lax.ppermute(v, ('zh', 'zl'), [(i, 3 - i) for i in range(4)])  11.4 us
  transfers between devices with their start and end apart: 32, of which 13 were waited for; matrix products, arithmetic and copies ran while one was open for 1% of the time, Pallas kernels for 28%

profile of v2, /device:TPU:0, one launch (start us, length us, event | category | flops | bytes accessed | tf_op | source)
XLA Modules:
  0.0 200.3 jit_solution(636358461994976114)
XLA Ops:
  0.0 1.2 constant_dynamic-slice_fusion.1
  1.2 0.0 copy-start.12
  1.2 0.0 copy-start.13
  1.2 4.2 %collective-permute-start.1 = (bf16[128,1536]{1,0:T(8,128)(2,1)S(1)}, bf16[128,1536]{1,0:T(8,128)(2,1)S(1)}, u32[]{:S(2)}, u32[]{:S(2)}) collective-permute-start(bf16[128,1536]{1,0:T(8,128)(2,1)S(1)} %get-tuple-element.34), channel_id=1, source_target_pairs={{0,24},{8,16},{16,8},{24,0},{1,25},{9,17},{17,9},{25,1},{2,26},{10... | collective-permute-start | bytes 1179656 | tf_op jit(solution)/shard_map/ppermute | solution.py:41
  5.4 0.1 collective-permute-start.5
  5.5 1.2 constant_dynamic-slice_fusion
  6.7 3.2 %collective-permute-start.9 = (bf16[128,3072]{1,0:T(8,128)(2,1)S(1)}, bf16[128,3072]{1,0:T(8,128)(2,1)}, u32[]{:S(2)}, u32[]{:S(2)}) collective-permute-start(bf16[128,3072]{1,0:T(8,128)(2,1)S(1)} %constant_dynamic-slice_fusion), channel_id=1, source_target_pairs={{0,24},{8,16},{16,8},{24,0},{1,25},{9,17},{17,9},{25,1},{2,26},{10... | collective-permute-start | bytes 2359304 | tf_op jit(solution)/shard_map/ppermute | solution.py:41
  9.9 1.6 collective-permute-start
  11.5 3.9 %collective-permute-done.1.refs_1_ = bf16[128,1536]{1,0:T(8,128)(2,1)S(1)} collective-permute-done((bf16[128,1536]{1,0:T(8,128)(2,1)S(1)}, bf16[128,1536]{1,0:T(8,128)(2,1)S(1)}, u32[]{:S(2)}, u32[]{:S(2)}) %collective-permute-start.1) | collective-permute-done | bytes 393248 | tf_op jit(solution)/shard_map/ppermute | solution.py:41
  15.4 1.5 collective-permute-start.2
  16.9 6.9 %collective-permute-done.5.refs_5_ = bf16[128,1536]{1,0:T(8,128)(2,1)S(1)} collective-permute-done((bf16[128,1536]{1,0:T(8,128)(2,1)S(1)}, bf16[128,1536]{1,0:T(8,128)(2,1)S(1)}, u32[]{:S(2)}, u32[]{:S(2)}) %collective-permute-start.5) | collective-permute-done | bytes 393248 | tf_op jit(solution)/shard_map/ppermute | solution.py:41
  23.8 1.5 collective-permute-start.6
  25.3 3.1 %collective-permute-start.15 = (bf16[96,6144]{1,0:T(8,128)(2,1)S(1)}, bf16[96,6144]{1,0:T(8,128)(2,1)}, u32[]{:S(2)}, u32[]{:S(2)}) collective-permute-start(bf16[96,6144]{1,0:T(8,128)(2,1)S(1)} %bitcast.27), channel_id=1, source_target_pairs={{0,6},{1,3},{2,0},{3,5},{4,2},{5,7},{6,4},{7,1},{8,14},{9,11},{10,... | collective-permute-start | bytes 3538952 | tf_op jit(solution)/shard_map/ppermute | solution.py:29
  28.4 4.4 %collective-permute-done.6.refs_6_ = bf16[128,1536]{1,0:T(8,128)(2,1)S(1)} collective-permute-done((bf16[128,1536]{1,0:T(8,128)(2,1)S(1)}, bf16[128,1536]{1,0:T(8,128)(2,1)S(1)}, u32[]{:S(2)}, u32[]{:S(2)}) %collective-permute-start.6) | collective-permute-done | bytes 393248 | tf_op jit(solution)/shard_map/ppermute | solution.py:33
  32.8 7.1 %collective-permute-done.9.refs_9_ = bf16[128,3072]{1,0:T(8,128)(2,1)} collective-permute-done((bf16[128,3072]{1,0:T(8,128)(2,1)S(1)}, bf16[128,3072]{1,0:T(8,128)(2,1)}, u32[]{:S(2)}, u32[]{:S(2)}) %collective-permute-start.9) | collective-permute-done | bytes 786464 | tf_op jit(solution)/shard_map/ppermute | solution.py:41
  39.9 2.8 %collective-permute-start.3 = (bf16[128,1536]{1,0:T(8,128)(2,1)S(1)}, bf16[128,1536]{1,0:T(8,128)(2,1)S(1)}, u32[]{:S(2)}, u32[]{:S(2)}) collective-permute-start(bf16[128,1536]{1,0:T(8,128)(2,1)S(1)} %collective-permute-done.1.refs_1_), channel_id=1, source_target_pairs={{0,96},{1,33},{32,0},{33,65},{64,32},{65,97},{96,64},{97,1},{2,98}... | collective-permute-start | bytes 1179656 | tf_op jit(solution)/shard_map/ppermute | solution.py:33
  42.7 5.3 %collective-permute-done.3.refs_3_ = bf16[128,1536]{1,0:T(8,128)(2,1)S(1)} collective-permute-done((bf16[128,1536]{1,0:T(8,128)(2,1)S(1)}, bf16[128,1536]{1,0:T(8,128)(2,1)S(1)}, u32[]{:S(2)}, u32[]{:S(2)}) %collective-permute-start.3) | collective-permute-done | bytes 393248 | tf_op jit(solution)/shard_map/ppermute | solution.py:33
  48.0 1.2 collective-permute-start.10
  49.2 2.6 %collective-permute-start.7 = (bf16[128,1536]{1,0:T(8,128)(2,1)S(1)}, bf16[128,1536]{1,0:T(8,128)(2,1)}, u32[]{:S(2)}, u32[]{:S(2)}) collective-permute-start(bf16[128,1536]{1,0:T(8,128)(2,1)S(1)} %collective-permute-done.5.refs_5_), channel_id=1, source_target_pairs={{0,96},{1,33},{32,0},{33,65},{64,32},{65,97},{96,64},{97,1},{2,98}... | collective-permute-start | bytes 1179656 | tf_op jit(solution)/shard_map/ppermute | solution.py:33
  51.8 0.9 collective-permute-done.17.refs_7_.refs_19_
  52.7 3.0 %collective-permute-start.23 = (bf16[96,6144]{1,0:T(8,128)(2,1)}, bf16[96,6144]{1,0:T(8,128)(2,1)S(1)}, u32[]{:S(2)}, u32[]{:S(2)}) collective-permute-start(bf16[96,6144]{1,0:T(8,128)(2,1)} %collective-permute-done.17.refs_7_.refs_19_), channel_id=1, source_target_pairs={{0,6},{1,3},{2,0},{3,5},{4,2},{5,7},{6,4},{7,1},{8,14},{9,11},{10,... | collective-permute-start | bytes 3538952 | tf_op jit(solution)/shard_map/ppermute | solution.py:29
  55.7 1.9 rates.1
  57.6 4.5 %all-to-all-start = ((f32[32,1,128]{2,1,0:T(1,128)}), f32[32,1,128]{2,1,0:T(1,128)S(1)}, u32[]{:S(2)}, u32[]{:S(2)}) async-start(f32[32,1,128]{2,1,0:T(1,128)} %get-tuple-element.19), calls=%async_computation | async-start | bytes 32768 | tf_op jit(solution)/shard_map/all_to_all | solution.py:45
  62.2 0.6 broadcast_select_fusion.n_ref
  62.7 0.7 stack.83.s_ref
  63.4 7.9 %all-to-all-done.d_ref = f32[32,1,128]{2,1,0:T(1,128)S(1)} async-done(((f32[32,1,128]{2,1,0:T(1,128)}), f32[32,1,128]{2,1,0:T(1,128)S(1)}, u32[]{:S(2)}, u32[]{:S(2)}) %all-to-all-start) | async-done | bytes 16416 | tf_op jit(solution)/shard_map/all_to_all | solution.py:45
  71.4 0.6 copy-done.10
  71.9 2.6 %collective-permute-start.19 = (bf16[96,6144]{1,0:T(8,128)(2,1)}, bf16[96,6144]{1,0:T(8,128)(2,1)S(1)}, u32[]{:S(2)}, u32[]{:S(2)}) collective-permute-start(bf16[96,6144]{1,0:T(8,128)(2,1)} %copy-done.15), channel_id=1, source_target_pairs={{0,2},{1,7},{2,4},{3,1},{4,6},{5,3},{6,0},{7,5},{8,10},{9,15},{10,... | collective-permute-start | bytes 3538952 | tf_op jit(solution)/shard_map/ppermute | solution.py:29
  74.5 0.9 collective-permute-start.21
  75.4 1.1 collective-permute-start.18
  76.5 0.7 collective-permute-start.25
  77.3 1.1 copy-done.16
  78.4 22.4 %collective-permute-done.19.refs_1_.refs_21_ = bf16[96,6144]{1,0:T(8,128)(2,1)S(1)} collective-permute-done((bf16[96,6144]{1,0:T(8,128)(2,1)}, bf16[96,6144]{1,0:T(8,128)(2,1)S(1)}, u32[]{:S(2)}, u32[]{:S(2)}) %collective-permute-start.19) | collective-permute-done | bytes 1179680 | tf_op jit(solution)/shard_map/ppermute | solution.py:29
  100.8 2.4 %collective-permute-done.21.refs_3_.refs_23_ = bf16[96,6144]{1,0:T(8,128)(2,1)S(1)} collective-permute-done((bf16[96,6144]{1,0:T(8,128)(2,1)}, bf16[96,6144]{1,0:T(8,128)(2,1)S(1)}, u32[]{:S(2)}, u32[]{:S(2)}) %collective-permute-start.21) | collective-permute-done | bytes 1179680 | tf_op jit(solution)/shard_map/ppermute | solution.py:37
  103.2 0.2 collective-permute-start.22
  103.4 0.3 collective-permute-start.24
  103.7 0.2 collective-permute-start.26
  103.9 1.4 collective-permute-start.11
  105.3 0.6 collective-permute-start.4
  106.0 0.1 collective-permute-done.22.refs_4_.refs_24_
  106.0 0.0 collective-permute-start.8
  106.1 1.7 collective-permute-done.24.refs_6_.refs_26_
  107.8 1.0 copy-done.6
  108.7 0.0 collective-permute-start.12
  108.8 10.6 %project.3.refs_7_ = bf16[1536,512]{1,0:T(8,128)(2,1)} custom-call(s32[20]{0:T(128)} %stack.83.s_ref, bf16[512,6144]{1,0:T(8,128)(2,1)} %refs_0_.5, bf16[96,6144]{1,0:T(8,128)(2,1)} %bitcast.23, bf16[96,6144]{1,0:T(8,128)(2,1)} %collective-permute-done.13.refs_2_.refs_14_, bf16[96,6144]{1,0:T(8,128)(2,1)} %copy-done.15, bf16[96,6144]{1,0:T(8,128)(2,1)} %copy-done.16, ...), custom_call_target="tpu_custom_call" | custom-call | flops 4831838208 | bytes 15728640 | tf_op jit(solution)/shard_map/project/pallas_call | solution.py:141
  119.4 9.3 %project.4.refs_29_ = bf16[1536,512]{1,0:T(8,128)(2,1)} custom-call(s32[20]{0:T(128)} %stack.83.s_ref, bf16[512,6144]{1,0:T(8,128)(2,1)} %refs_0_.5, bf16[96,6144]{1,0:T(8,128)(2,1)} %copy-done.2, bf16[96,6144]{1,0:T(8,128)(2,1)} %copy-done.4, bf16[96,6144]{1,0:T(8,128)(2,1)} %copy-done.3, ...), custom_call_target="tpu_custom_call", output_to_operand_aliasing={{}: (8, {})} | custom-call | flops 3623878656 | bytes 13369344 | tf_op jit(solution)/shard_map/project/pallas_call | solution.py:141
  128.8 0.6 collective-permute-start.28
  129.4 4.3 %collective-permute-done.12.refs_12_ = bf16[128,3072]{1,0:T(8,128)(2,1)} collective-permute-done((bf16[128,3072]{1,0:T(8,128)(2,1)}, bf16[128,3072]{1,0:T(8,128)(2,1)}, u32[]{:S(2)}, u32[]{:S(2)}) %collective-permute-start.12) | collective-permute-done | bytes 786464 | tf_op jit(solution)/shard_map/ppermute | solution.py:33
  133.6 22.6 %project.5 = (bf16[1536,512]{1,0:T(8,128)(2,1)}, bf16[1536,512]{1,0:T(8,128)(2,1)}, bf16[4,128,512]{2,1,0:T(8,128)(2,1)}) custom-call(s32[20]{0:T(128)} %stack.83.s_ref, bf16[512,6144]{1,0:T(8,128)(2,1)} %refs_0_.5, bf16[128,1536]{1,0:T(8,128)(2,1)} %copy-done.19, bf16[128,1536]{1,0:T(8,128)(2,1)} %copy-done.21, ...), custom_call_target="tpu_custom_call", output_to_operand_aliasing={{0}: (30, {})} | custom-call | flops 10871635968 | bytes 31457280 | tf_op jit(solution)/shard_map/project/pallas_call | solution.py:141
  156.3 0.6 copy-done.11
  156.9 3.3 %intra.2 = bf16[4,128,512]{2,1,0:T(8,128)(2,1)} custom-call(s32[1]{0:T(128)} %bitcast.22.z_ref, bf16[1536,512]{1,0:T(8,128)(2,1)} %get-tuple-element.23.refs_0_.refs_1_.refs_2_.refs_3_.refs_4_.refs_5_.refs_6_.refs_7_.refs_8_.refs_9_.refs_10_.refs_11_.refs_12_.refs_13_.refs_14_.refs_15_.refs_16_, ...), custom_call_target="tpu_custom_call" | custom-call | tf_op jit(solution)/shard_map/intra/pallas_call | solution.py:250
  160.2 0.6 collective-permute-start.29
  160.8 2.7 %collective-permute-start.27 = (bf16[4,128,512]{2,1,0:T(8,128)(2,1)S(1)}, bf16[4,128,512]{2,1,0:T(8,128)(2,1)S(1)}, u32[]{:S(2)}, u32[]{:S(2)}) collective-permute-start(bf16[4,128,512]{2,1,0:T(8,128)(2,1)S(1)} %copy-done.18), channel_id=1, source_target_pairs={{0,24},{8,16},{16,8},{24,0},{1,25},{9,17},{17,9},{25,1},{2,26},{10... | collective-permute-start | bytes 1572872 | tf_op jit(solution)/shard_map/ppermute | solution.py:41
  163.4 3.1 %states.1 = bf16[16,2,32,128]{3,2,1,0:T(8,128)(2,1)} custom-call(s32[1]{0:T(128)} %bitcast.22.z_ref, bf16[1536,512]{1,0:T(8,128)(2,1)} %get-tuple-element.25.refs_0_.refs_1_.refs_2_.refs_3_.refs_4_.refs_5_.refs_6_.refs_7_.refs_8_.refs_9_.refs_10_.refs_11_, ...), custom_call_target="tpu_custom_call" | custom-call | tf_op jit(solution)/shard_map/states/pallas_call | solution.py:217
  166.5 12.1 %all_to_all.15.s_ref = bf16[16,2,32,128]{3,2,1,0:T(8,128)(2,1)} all-to-all(bf16[16,2,32,128]{3,2,1,0:T(8,128)(2,1)} %states.1), channel_id=1, replica_groups=mesh['x'=4,'zh'=2,'zl'=2,'y'=4,'c'=2] {'zl','y','c'}, dimensions={0} | all-to-all | bytes 524288 | tf_op jit(solution)/shard_map/all_to_all | solution.py:45
  178.6 1.8 carries.1
  180.3 3.9 %all-to-all-start.2 = ((bf16[32,32,128]{2,1,0:T(8,128)(2,1)}), bf16[32,32,128]{2,1,0:T(8,128)(2,1)S(1)}, u32[]{:S(2)}, u32[]{:S(2)}) async-start(bf16[32,32,128]{2,1,0:T(8,128)(2,1)} %carries.1), calls=%async_computation.2 | async-start | bytes 524288 | tf_op jit(solution)/shard_map/all_to_all | solution.py:45
  184.2 3.5 %intra.3.refs_5_ = f32[4,128,512]{2,1,0:T(8,128)} custom-call(s32[1]{0:T(128)} %bitcast.22.z_ref, bf16[1536,512]{1,0:T(8,128)(2,1)} %get-tuple-element.25.refs_0_.refs_1_.refs_2_.refs_3_.refs_4_.refs_5_.refs_6_.refs_7_.refs_8_.refs_9_.refs_10_.refs_11_, ...), custom_call_target="tpu_custom_call" | custom-call | tf_op jit(solution)/shard_map/intra/pallas_call | solution.py:250
  187.7 5.3 %all-to-all-done.2.refs_6_.refs_3_ = bf16[32,32,128]{2,1,0:T(8,128)(2,1)S(1)} async-done(((bf16[32,32,128]{2,1,0:T(8,128)(2,1)}), bf16[32,32,128]{2,1,0:T(8,128)(2,1)S(1)}, u32[]{:S(2)}, u32[]{:S(2)}) %all-to-all-start.2) | async-done | bytes 262176 | tf_op jit(solution)/shard_map/all_to_all | solution.py:45
  193.0 0.7 copy-done
  193.7 2.8 %finish.2.refs_5_ = bf16[512,1024]{1,0:T(8,128)(2,1)} custom-call(s32[1]{0:T(128)} %bitcast.22.z_ref, bf16[1536,512]{1,0:T(8,128)(2,1)} %get-tuple-element.25.refs_0_.refs_1_.refs_2_.refs_3_.refs_4_.refs_5_.refs_6_.refs_7_.refs_8_.refs_9_.refs_10_.refs_11_, ...), custom_call_target="tpu_custom_call" | custom-call | tf_op jit(solution)/shard_map/finish/pallas_call | solution.py:307
  196.6 0.8 copy-done.7
  197.4 0.2 copy-done.8
  197.6 2.7 %finish.3 = bf16[512,1024]{1,0:T(8,128)(2,1)} custom-call(s32[1]{0:T(128)} %bitcast.z_ref, bf16[4,128,512]{2,1,0:T(8,128)(2,1)} %copy-done.8, f32[8,1,512]{2,1,0:T(1,128)} %get-tuple-element.24.refs_8_.refs_12_.refs_4_.refs_1_, bf16[4,128,512]{2,1,0:T(8,128)(2,1)} %copy-done.7, bf16[32,32,128]{2,1,0:T(8,128)(2,1)} %copy-done, ...), custom_call_target="tpu_custom_call", output_to_operand_aliasing={{}: (6, {})} | custom-call | tf_op jit(solution)/shard_map/finish/pallas_call | solution.py:307
  (63 shorter events, 0.1 us)
Async XLA Ops:
  1.2 8.8 %copy-start.14 = (bf16[6144,96]{0,1:T(8,128)(2,1)S(1)}, bf16[6144,96]{0,1:T(8,128)(2,1)}, u32[]{:S(2)}) copy-start(bf16[6144,96]{0,1:T(8,128)(2,1)} %param.7) | copy-start | bytes 3538948
  1.2 61.0 %copy-start.12 = (s32[8]{0:T(128)S(1)}, s32[8]{0:T(128)}, u32[]{:S(2)}) copy-start(s32[8]{0:T(128)} %constant.101.clone) | copy-start | bytes 100
  1.2 61.0 %copy-start.13 = (s32[8]{0:T(128)S(1)}, s32[8]{0:T(128)}, u32[]{:S(2)}) copy-start(s32[8]{0:T(128)} %constant.102.clone) | copy-start | bytes 100
  1.2 14.2 %collective-permute-start.1 = (bf16[128,1536]{1,0:T(8,128)(2,1)S(1)}, bf16[128,1536]{1,0:T(8,128)(2,1)S(1)}, u32[]{:S(2)}, u32[]{:S(2)}) collective-permute-start(bf16[128,1536]{1,0:T(8,128)(2,1)S(1)} %get-tuple-element.34), channel_id=1, source_target_pairs={{0,24},{8,16},{16,8},{24,0},{1,25},{9,17},{17,9},{25,1},{2,26},{10... | collective-permute-start | bytes 1179656 | tf_op jit(solution)/shard_map/ppermute | solution.py:41
  5.4 18.4 %collective-permute-start.5 = (bf16[128,1536]{1,0:T(8,128)(2,1)S(1)}, bf16[128,1536]{1,0:T(8,128)(2,1)S(1)}, u32[]{:S(2)}, u32[]{:S(2)}) collective-permute-start(bf16[128,1536]{1,0:T(8,128)(2,1)S(1)} %get-tuple-element.33), channel_id=1, source_target_pairs={{0,24},{8,16},{16,8},{24,0},{1,25},{9,17},{17,9},{25,1},{2,26},{10... | collective-permute-start | bytes 1179656 | tf_op jit(solution)/shard_map/ppermute | solution.py:41
  6.7 33.2 %collective-permute-start.9 = (bf16[128,3072]{1,0:T(8,128)(2,1)S(1)}, bf16[128,3072]{1,0:T(8,128)(2,1)}, u32[]{:S(2)}, u32[]{:S(2)}) collective-permute-start(bf16[128,3072]{1,0:T(8,128)(2,1)S(1)} %constant_dynamic-slice_fusion), channel_id=1, source_target_pairs={{0,24},{8,16},{16,8},{24,0},{1,25},{9,17},{17,9},{25,1},{2,26},{10... | collective-permute-start | bytes 2359304 | tf_op jit(solution)/shard_map/ppermute | solution.py:41
  9.9 39.3 %collective-permute-start = (bf16[96,6144]{1,0:T(8,128)(2,1)S(1)}, bf16[96,6144]{1,0:T(8,128)(2,1)S(1)}, u32[]{:S(2)}, u32[]{:S(2)}) collective-permute-start(bf16[96,6144]{1,0:T(8,128)(2,1)S(1)} %bitcast.25), channel_id=1, source_target_pairs={{0,2},{1,7},{2,4},{3,1},{4,6},{5,3},{6,0},{7,5},{8,10},{9,15},{10,... | collective-permute-start | bytes 3538952 | tf_op jit(solution)/shard_map/ppermute | solution.py:29
  15.4 55.9 %copy-start.19 = (bf16[128,1536]{1,0:T(8,128)(2,1)}, bf16[128,1536]{1,0:T(8,128)(2,1)S(1)}, u32[]{:S(2)}) copy-start(bf16[128,1536]{1,0:T(8,128)(2,1)S(1)} %collective-permute-done.1.refs_1_) | copy-start | bytes 1179652
  15.4 9.9 %collective-permute-start.2 = (bf16[128,1536]{1,0:T(8,128)(2,1)S(1)}, bf16[128,1536]{1,0:T(8,128)(2,1)S(1)}, u32[]{:S(2)}, u32[]{:S(2)}) collective-permute-start(bf16[128,1536]{1,0:T(8,128)(2,1)S(1)} %collective-permute-done.1.refs_1_), channel_id=1, source_target_pairs={{0,32},{1,97},{32,64},{33,1},{64,96},{65,33},{96,0},{97,65},{2,34}... | collective-permute-start | bytes 1179656 | tf_op jit(solution)/shard_map/ppermute | solution.py:33
  23.8 47.5 %copy-start.20 = (bf16[128,1536]{1,0:T(8,128)(2,1)}, bf16[128,1536]{1,0:T(8,128)(2,1)S(1)}, u32[]{:S(2)}) copy-start(bf16[128,1536]{1,0:T(8,128)(2,1)S(1)} %collective-permute-done.5.refs_5_) | copy-start | bytes 1179652
  23.8 9.0 %collective-permute-start.6 = (bf16[128,1536]{1,0:T(8,128)(2,1)S(1)}, bf16[128,1536]{1,0:T(8,128)(2,1)S(1)}, u32[]{:S(2)}, u32[]{:S(2)}) collective-permute-start(bf16[128,1536]{1,0:T(8,128)(2,1)S(1)} %collective-permute-done.5.refs_5_), channel_id=1, source_target_pairs={{0,32},{1,97},{32,64},{33,1},{64,96},{65,33},{96,0},{97,65},{2,34}... | collective-permute-start | bytes 1179656 | tf_op jit(solution)/shard_map/ppermute | solution.py:33
  25.3 27.4 %collective-permute-start.17 = (bf16[96,6144]{1,0:T(8,128)(2,1)S(1)}, bf16[96,6144]{1,0:T(8,128)(2,1)}, u32[]{:S(2)}, u32[]{:S(2)}) collective-permute-start(bf16[96,6144]{1,0:T(8,128)(2,1)S(1)} %bitcast.26), channel_id=1, source_target_pairs={{0,8},{8,0},{1,9},{9,1},{2,10},{10,2},{3,11},{11,3},{4,12},{12,4},... | collective-permute-start | bytes 3538952 | tf_op jit(solution)/shard_map/ppermute | solution.py:37
  25.3 27.4 %copy-start.21 = (bf16[128,1536]{1,0:T(8,128)(2,1)}, bf16[128,1536]{1,0:T(8,128)(2,1)S(1)}, u32[]{:S(2)}) copy-start(bf16[128,1536]{1,0:T(8,128)(2,1)S(1)} %collective-permute-done.2.refs_2_) | copy-start | bytes 1179652
  25.3 46.6 %collective-permute-start.15 = (bf16[96,6144]{1,0:T(8,128)(2,1)S(1)}, bf16[96,6144]{1,0:T(8,128)(2,1)}, u32[]{:S(2)}, u32[]{:S(2)}) collective-permute-start(bf16[96,6144]{1,0:T(8,128)(2,1)S(1)} %bitcast.27), channel_id=1, source_target_pairs={{0,6},{1,3},{2,0},{3,5},{4,2},{5,7},{6,4},{7,1},{8,14},{9,11},{10,... | collective-permute-start | bytes 3538952 | tf_op jit(solution)/shard_map/ppermute | solution.py:29
  32.8 19.0 %copy-start.22 = (bf16[128,1536]{1,0:T(8,128)(2,1)}, bf16[128,1536]{1,0:T(8,128)(2,1)S(1)}, u32[]{:S(2)}) copy-start(bf16[128,1536]{1,0:T(8,128)(2,1)S(1)} %collective-permute-done.6.refs_6_) | copy-start | bytes 1179652
  32.8 41.7 %collective-permute-start.13 = (bf16[96,6144]{1,0:T(8,128)(2,1)S(1)}, bf16[96,6144]{1,0:T(8,128)(2,1)}, u32[]{:S(2)}, u32[]{:S(2)}) collective-permute-start(bf16[96,6144]{1,0:T(8,128)(2,1)S(1)} %bitcast.28), channel_id=1, source_target_pairs={{0,1},{1,0},{2,3},{3,2},{4,5},{5,4},{6,7},{7,6},{8,9},{9,8},{10,11... | collective-permute-start | bytes 3538952 | tf_op jit(solution)/shard_map/ppermute | solution.py:49
  39.9 8.1 %collective-permute-start.3 = (bf16[128,1536]{1,0:T(8,128)(2,1)S(1)}, bf16[128,1536]{1,0:T(8,128)(2,1)S(1)}, u32[]{:S(2)}, u32[]{:S(2)}) collective-permute-start(bf16[128,1536]{1,0:T(8,128)(2,1)S(1)} %collective-permute-done.1.refs_1_), channel_id=1, source_target_pairs={{0,96},{1,33},{32,0},{33,65},{64,32},{65,97},{96,64},{97,1},{2,98}... | collective-permute-start | bytes 1179656 | tf_op jit(solution)/shard_map/ppermute | solution.py:33
  48.0 3.8 %copy-start.23 = (bf16[128,1536]{1,0:T(8,128)(2,1)}, bf16[128,1536]{1,0:T(8,128)(2,1)S(1)}, u32[]{:S(2)}) copy-start(bf16[128,1536]{1,0:T(8,128)(2,1)S(1)} %collective-permute-done.3.refs_3_) | copy-start | bytes 1179652
  48.0 27.4 %collective-permute-start.10 = (bf16[128,3072]{1,0:T(8,128)(2,1)}, bf16[128,3072]{1,0:T(8,128)(2,1)}, u32[]{:S(2)}, u32[]{:S(2)}) collective-permute-start(bf16[128,3072]{1,0:T(8,128)(2,1)} %collective-permute-done.9.refs_9_), channel_id=1, source_target_pairs={{0,32},{1,97},{32,64},{33,1},{64,96},{65,33},{96,0},{97,65},{2,34}... | collective-permute-start | bytes 2359304 | tf_op jit(solution)/shard_map/ppermute | solution.py:33
  49.2 3.5 %copy-start.15 = (bf16[96,6144]{1,0:T(8,128)(2,1)}, bf16[96,6144]{1,0:T(8,128)(2,1)S(1)}, u32[]{:S(2)}) copy-start(bf16[96,6144]{1,0:T(8,128)(2,1)S(1)} %collective-permute-done.refs_3_.refs_15_) | copy-start | bytes 3538948
  49.2 22.1 %collective-permute-start.7 = (bf16[128,1536]{1,0:T(8,128)(2,1)S(1)}, bf16[128,1536]{1,0:T(8,128)(2,1)}, u32[]{:S(2)}, u32[]{:S(2)}) collective-permute-start(bf16[128,1536]{1,0:T(8,128)(2,1)S(1)} %collective-permute-done.5.refs_5_), channel_id=1, source_target_pairs={{0,96},{1,33},{32,0},{33,65},{64,32},{65,97},{96,64},{97,1},{2,98}... | collective-permute-start | bytes 1179656 | tf_op jit(solution)/shard_map/ppermute | solution.py:33
  52.7 23.8 %collective-permute-start.23 = (bf16[96,6144]{1,0:T(8,128)(2,1)}, bf16[96,6144]{1,0:T(8,128)(2,1)S(1)}, u32[]{:S(2)}, u32[]{:S(2)}) collective-permute-start(bf16[96,6144]{1,0:T(8,128)(2,1)} %collective-permute-done.17.refs_7_.refs_19_), channel_id=1, source_target_pairs={{0,6},{1,3},{2,0},{3,5},{4,2},{5,7},{6,4},{7,1},{8,14},{9,11},{10,... | collective-permute-start | bytes 3538952 | tf_op jit(solution)/shard_map/ppermute | solution.py:29
  57.6 13.7 %all-to-all-start = ((f32[32,1,128]{2,1,0:T(1,128)}), f32[32,1,128]{2,1,0:T(1,128)S(1)}, u32[]{:S(2)}, u32[]{:S(2)}) async-start(f32[32,1,128]{2,1,0:T(1,128)} %get-tuple-element.19), calls=%async_computation | async-start | bytes 32768 | tf_op jit(solution)/shard_map/all_to_all | solution.py:45
  71.3 0.6 copy-start.10
  71.3 5.9 %collective-permute-start.14 = (bf16[96,6144]{1,0:T(8,128)(2,1)}, bf16[96,6144]{1,0:T(8,128)(2,1)S(1)}, u32[]{:S(2)}, u32[]{:S(2)}) collective-permute-start(bf16[96,6144]{1,0:T(8,128)(2,1)} %copy-done.15), channel_id=1, source_target_pairs={{0,1},{1,0},{2,3},{3,2},{4,5},{5,4},{6,7},{7,6},{8,9},{9,8},{10,11... | collective-permute-start | bytes 3538952 | tf_op jit(solution)/shard_map/ppermute | solution.py:49
  71.9 28.9 %collective-permute-start.19 = (bf16[96,6144]{1,0:T(8,128)(2,1)}, bf16[96,6144]{1,0:T(8,128)(2,1)S(1)}, u32[]{:S(2)}, u32[]{:S(2)}) collective-permute-start(bf16[96,6144]{1,0:T(8,128)(2,1)} %copy-done.15), channel_id=1, source_target_pairs={{0,2},{1,7},{2,4},{3,1},{4,6},{5,3},{6,0},{7,5},{8,10},{9,15},{10,... | collective-permute-start | bytes 3538952 | tf_op jit(solution)/shard_map/ppermute | solution.py:29
  74.5 28.6 %collective-permute-start.21 = (bf16[96,6144]{1,0:T(8,128)(2,1)}, bf16[96,6144]{1,0:T(8,128)(2,1)S(1)}, u32[]{:S(2)}, u32[]{:S(2)}) collective-permute-start(bf16[96,6144]{1,0:T(8,128)(2,1)} %copy-done.15), channel_id=1, source_target_pairs={{0,8},{8,0},{1,9},{9,1},{2,10},{10,2},{3,11},{11,3},{4,12},{12,4},... | collective-permute-start | bytes 3538952 | tf_op jit(solution)/shard_map/ppermute | solution.py:37
  75.4 28.0 %collective-permute-start.18 = (bf16[96,6144]{1,0:T(8,128)(2,1)}, bf16[96,6144]{1,0:T(8,128)(2,1)}, u32[]{:S(2)}, u32[]{:S(2)}) collective-permute-start(bf16[96,6144]{1,0:T(8,128)(2,1)} %collective-permute-done.17.refs_7_.refs_19_), channel_id=1, source_target_pairs={{0,1},{1,0},{2,3},{3,2},{4,5},{5,4},{6,7},{7,6},{8,9},{9,8},{10,11... | collective-permute-start | bytes 3538952 | tf_op jit(solution)/shard_map/ppermute | solution.py:49
  76.5 42.9 %copy-start.1 = (bf16[96,6144]{1,0:T(8,128)(2,1)}, bf16[96,6144]{1,0:T(8,128)(2,1)S(1)}, u32[]{:S(2)}) copy-start(bf16[96,6144]{1,0:T(8,128)(2,1)S(1)} %collective-permute-done.23.refs_5_.refs_25_) | copy-start | bytes 3538948
  76.5 27.2 %collective-permute-start.25 = (bf16[96,6144]{1,0:T(8,128)(2,1)S(1)}, bf16[96,6144]{1,0:T(8,128)(2,1)}, u32[]{:S(2)}, u32[]{:S(2)}) collective-permute-start(bf16[96,6144]{1,0:T(8,128)(2,1)S(1)} %collective-permute-done.23.refs_5_.refs_25_), channel_id=1, source_target_pairs={{0,6},{1,3},{2,0},{3,5},{4,2},{5,7},{6,4},{7,1},{8,14},{9,11},{10,... | collective-permute-start | bytes 3538952 | tf_op jit(solution)/shard_map/ppermute | solution.py:29
  77.3 1.1 copy-start.16
  77.3 26.7 %collective-permute-start.16 = (bf16[96,6144]{1,0:T(8,128)(2,1)}, bf16[96,6144]{1,0:T(8,128)(2,1)S(1)}, u32[]{:S(2)}, u32[]{:S(2)}) collective-permute-start(bf16[96,6144]{1,0:T(8,128)(2,1)} %collective-permute-done.15.refs_5_.refs_17_), channel_id=1, source_target_pairs={{0,1},{1,0},{2,3},{3,2},{4,5},{5,4},{6,7},{7,6},{8,9},{9,8},{10,11... | collective-permute-start | bytes 3538952 | tf_op jit(solution)/shard_map/ppermute | solution.py:49
  100.8 18.6 %copy-start.2 = (bf16[96,6144]{1,0:T(8,128)(2,1)}, bf16[96,6144]{1,0:T(8,128)(2,1)S(1)}, u32[]{:S(2)}) copy-start(bf16[96,6144]{1,0:T(8,128)(2,1)S(1)} %collective-permute-done.19.refs_1_.refs_21_) | copy-start | bytes 3538948
  100.8 4.5 %collective-permute-start.20 = (bf16[96,6144]{1,0:T(8,128)(2,1)S(1)}, bf16[96,6144]{1,0:T(8,128)(2,1)S(1)}, u32[]{:S(2)}, u32[]{:S(2)}) collective-permute-start(bf16[96,6144]{1,0:T(8,128)(2,1)S(1)} %collective-permute-done.19.refs_1_.refs_21_), channel_id=1, source_target_pairs={{0,1},{1,0},{2,3},{3,2},{4,5},{5,4},{6,7},{7,6},{8,9},{9,8},{10,11... | collective-permute-start | bytes 3538952 | tf_op jit(solution)/shard_map/ppermute | solution.py:49
  103.2 16.2 %copy-start.3 = (bf16[96,6144]{1,0:T(8,128)(2,1)}, bf16[96,6144]{1,0:T(8,128)(2,1)S(1)}, u32[]{:S(2)}) copy-start(bf16[96,6144]{1,0:T(8,128)(2,1)S(1)} %collective-permute-done.21.refs_3_.refs_23_) | copy-start | bytes 3538948
  103.2 2.8 %collective-permute-start.22 = (bf16[96,6144]{1,0:T(8,128)(2,1)S(1)}, bf16[96,6144]{1,0:T(8,128)(2,1)S(1)}, u32[]{:S(2)}, u32[]{:S(2)}) collective-permute-start(bf16[96,6144]{1,0:T(8,128)(2,1)S(1)} %collective-permute-done.21.refs_3_.refs_23_), channel_id=1, source_target_pairs={{0,1},{1,0},{2,3},{3,2},{4,5},{5,4},{6,7},{7,6},{8,9},{9,8},{10,11... | collective-permute-start | bytes 3538952 | tf_op jit(solution)/shard_map/ppermute | solution.py:49
  103.4 4.3 %collective-permute-start.24 = (bf16[96,6144]{1,0:T(8,128)(2,1)S(1)}, bf16[96,6144]{1,0:T(8,128)(2,1)S(1)}, u32[]{:S(2)}, u32[]{:S(2)}) collective-permute-start(bf16[96,6144]{1,0:T(8,128)(2,1)S(1)} %collective-permute-done.23.refs_5_.refs_25_), channel_id=1, source_target_pairs={{0,1},{1,0},{2,3},{3,2},{4,5},{5,4},{6,7},{7,6},{8,9},{9,8},{10,11... | collective-permute-start | bytes 3538952 | tf_op jit(solution)/shard_map/ppermute | solution.py:49
  103.7 29.9 %collective-permute-start.26 = (bf16[96,6144]{1,0:T(8,128)(2,1)}, bf16[96,6144]{1,0:T(8,128)(2,1)}, u32[]{:S(2)}, u32[]{:S(2)}) collective-permute-start(bf16[96,6144]{1,0:T(8,128)(2,1)} %collective-permute-done.25.refs_27_), channel_id=1, source_target_pairs={{0,1},{1,0},{2,3},{3,2},{4,5},{5,4},{6,7},{7,6},{8,9},{9,8},{10,11... | collective-permute-start | bytes 3538952 | tf_op jit(solution)/shard_map/ppermute | solution.py:49
  103.9 3.8 %copy-start.17 = (bf16[96,6144]{1,0:T(8,128)(2,1)}, bf16[96,6144]{1,0:T(8,128)(2,1)S(1)}, u32[]{:S(2)}) copy-start(bf16[96,6144]{1,0:T(8,128)(2,1)S(1)} %collective-permute-done.16.refs_6_.refs_18_) | copy-start | bytes 3538948
  103.9 25.4 %collective-permute-start.11 = (bf16[128,3072]{1,0:T(8,128)(2,1)}, bf16[128,3072]{1,0:T(8,128)(2,1)}, u32[]{:S(2)}, u32[]{:S(2)}) collective-permute-start(bf16[128,3072]{1,0:T(8,128)(2,1)} %collective-permute-done.9.refs_9_), channel_id=1, source_target_pairs={{0,96},{1,33},{32,0},{33,65},{64,32},{65,97},{96,64},{97,1},{2,98}... | collective-permute-start | bytes 2359304 | tf_op jit(solution)/shard_map/ppermute | solution.py:33
  105.3 2.4 %copy-start.4 = (bf16[96,6144]{1,0:T(8,128)(2,1)}, bf16[96,6144]{1,0:T(8,128)(2,1)S(1)}, u32[]{:S(2)}) copy-start(bf16[96,6144]{1,0:T(8,128)(2,1)S(1)} %collective-permute-done.20.refs_2_.refs_22_) | copy-start | bytes 3538948
  105.3 23.4 %collective-permute-start.4 = (bf16[128,1536]{1,0:T(8,128)(2,1)}, bf16[128,1536]{1,0:T(8,128)(2,1)}, u32[]{:S(2)}, u32[]{:S(2)}) collective-permute-start(bf16[128,1536]{1,0:T(8,128)(2,1)} %copy-done.21), channel_id=1, source_target_pairs={{0,32},{1,97},{32,64},{33,1},{64,96},{65,33},{96,0},{97,65},{2,34}... | collective-permute-start | bytes 1179656 | tf_op jit(solution)/shard_map/ppermute | solution.py:33
  106.0 1.7 copy-start.5
  106.0 23.3 %collective-permute-start.8 = (bf16[128,1536]{1,0:T(8,128)(2,1)}, bf16[128,1536]{1,0:T(8,128)(2,1)}, u32[]{:S(2)}, u32[]{:S(2)}) collective-permute-start(bf16[128,1536]{1,0:T(8,128)(2,1)} %copy-done.22), channel_id=1, source_target_pairs={{0,32},{1,97},{32,64},{33,1},{64,96},{65,33},{96,0},{97,65},{2,34}... | collective-permute-start | bytes 1179656 | tf_op jit(solution)/shard_map/ppermute | solution.py:33
  107.7 1.0 copy-start.6
  108.7 24.9 %collective-permute-start.12 = (bf16[128,3072]{1,0:T(8,128)(2,1)}, bf16[128,3072]{1,0:T(8,128)(2,1)}, u32[]{:S(2)}, u32[]{:S(2)}) collective-permute-start(bf16[128,3072]{1,0:T(8,128)(2,1)} %collective-permute-done.10.refs_10_), channel_id=1, source_target_pairs={{0,32},{1,97},{32,64},{33,1},{64,96},{65,33},{96,0},{97,65},{2,34}... | collective-permute-start | bytes 2359304 | tf_op jit(solution)/shard_map/ppermute | solution.py:33
  119.4 9.4 %copy-start.9 = (f32[8,1,512]{2,1,0:T(1,128)S(1)}, f32[8,1,512]{2,1,0:T(1,128)}, u32[]{:S(2)}) copy-start(f32[8,1,512]{2,1,0:T(1,128)} %get-tuple-element.24.refs_8_.refs_12_.refs_4_.refs_1_) | copy-start | bytes 49156
  128.8 27.5 %collective-permute-start.28 = (f32[8,1,512]{2,1,0:T(1,128)S(1)}, f32[8,1,512]{2,1,0:T(1,128)S(1)}, u32[]{:S(2)}, u32[]{:S(2)}) collective-permute-start(f32[8,1,512]{2,1,0:T(1,128)S(1)} %copy-done.9), channel_id=1, source_target_pairs={{0,24},{8,16},{16,8},{24,0},{1,25},{9,17},{17,9},{25,1},{2,26},{10... | collective-permute-start | bytes 49160 | tf_op jit(solution)/shard_map/ppermute | solution.py:41
  156.3 0.6 copy-start.11
  156.9 3.9 %copy-start.18 = (bf16[4,128,512]{2,1,0:T(8,128)(2,1)S(1)}, bf16[4,128,512]{2,1,0:T(8,128)(2,1)}, u32[]{:S(2)}) copy-start(bf16[4,128,512]{2,1,0:T(8,128)(2,1)} %get-tuple-element.22) | copy-start | bytes 1572868
  160.2 36.4 %collective-permute-start.29 = (bf16[4,128,512]{2,1,0:T(8,128)(2,1)}, bf16[4,128,512]{2,1,0:T(8,128)(2,1)S(1)}, u32[]{:S(2)}, u32[]{:S(2)}) collective-permute-start(bf16[4,128,512]{2,1,0:T(8,128)(2,1)} %intra.2), channel_id=1, source_target_pairs={{0,24},{8,16},{16,8},{24,0},{1,25},{9,17},{17,9},{25,1},{2,26},{10... | collective-permute-start | bytes 1572872 | tf_op jit(solution)/shard_map/ppermute | solution.py:41
  160.8 35.8 %collective-permute-start.27 = (bf16[4,128,512]{2,1,0:T(8,128)(2,1)S(1)}, bf16[4,128,512]{2,1,0:T(8,128)(2,1)S(1)}, u32[]{:S(2)}, u32[]{:S(2)}) collective-permute-start(bf16[4,128,512]{2,1,0:T(8,128)(2,1)S(1)} %copy-done.18), channel_id=1, source_target_pairs={{0,24},{8,16},{16,8},{24,0},{1,25},{9,17},{17,9},{25,1},{2,26},{10... | collective-permute-start | bytes 1572872 | tf_op jit(solution)/shard_map/ppermute | solution.py:41
  180.3 12.7 %all-to-all-start.2 = ((bf16[32,32,128]{2,1,0:T(8,128)(2,1)}), bf16[32,32,128]{2,1,0:T(8,128)(2,1)S(1)}, u32[]{:S(2)}, u32[]{:S(2)}) async-start(bf16[32,32,128]{2,1,0:T(8,128)(2,1)} %carries.1), calls=%async_computation.2 | async-start | bytes 524288 | tf_op jit(solution)/shard_map/all_to_all | solution.py:45
  193.0 0.7 copy-start
  196.6 0.8 copy-start.7
  196.6 1.0 copy-start.8

commit v3 on v2

--- a/solution.py
+++ b/solution.py
@@ -49,95 +49,110 @@
     return lax.ppermute(v, "c", [(0, 1), (1, 0)])
 
 
-def project(scalars, blocks, units, jobs, held):
-    flat = [a for arrays in blocks for a in arrays]
-    count = sum(len(u) for _, u in jobs)
-    both = len(blocks) == 2
-
-    def kernel(s_ref, *refs):
-        x_refs, refs = refs[: len(flat)], refs[len(flat) :]
+def grouped(members):
+    parts = -(-len(members) // 7)
+    size = -(-len(members) // parts)
+    return [range(g, min(g + size, len(members))) for g in range(0, len(members), size)]
+
+
+def project(scalars, here, cuts, units, jobs, held, partial):
+    kinds = [job[0] for job in jobs]
+    after = "across" in kinds
+
+    def kernel(s_ref, x_ref, *refs):
+        cut_refs, refs = refs[: 4 * len(cuts)], refs[4 * len(cuts) :]
         w_refs, refs = refs[: len(units)], refs[len(units) :]
+        if partial is not None:
+            partial_ref, refs = refs[0], refs[1:]
         if held is not None:
             refs = refs[1:]
         u_ref, refs = refs[0], refs[1:]
-        if both:
+        if "start" in kinds:
+            start_ref, refs = refs[0], refs[1:]
+        if after:
             across_ref, query_ref, refs = refs[0], refs[1], refs[2:]
-        sem, accs, stage, refs = refs[0], refs[1 : 1 + len(jobs)], refs[1 + len(jobs)], refs[2 + len(jobs) :]
+        sem, stage, accs = refs[0], refs[1], refs[2:]
         k = pl.program_id(0)
-        values = [x_refs[0]]
-        if both:
-            buf = refs[0]
-            for n in range(len(CUTS) - 1):
-
-                @pl.when((k >= CUTS[n]) & (k < CUTS[n + 1]))
-                def _():
-                    for p in range(4):
-                        row = pl.multiple_of(s_ref[16 + p] * 128, 128)
-                        buf[pl.ds(row, 128), :] = x_refs[1 + 4 * n + p][...]
-
-            values.append(buf)
-        for (block, members), acc in zip(jobs, accs):
-            w = jnp.concatenate([w_refs[m][...] for m in members], axis=0)
-            part = lax.dot_general(
-                w, values[block][...], (((1,), (1,)), ((), ())), preferred_element_type=F32
-            )
-
-            @pl.when(k == 0)
-            def _():
-                acc[...] = part
-
-            @pl.when(k > 0)
-            def _():
-                acc[...] += part
-
-        @pl.when(k == NK - 1)
-        def _():
+
+        def run(step):
             copies = []
-            for (block, members), acc in zip(jobs, accs):
-                for i, m in enumerate(members):
-                    rows = slice(i * UNIT, (i + 1) * UNIT)
-                    v = acc[rows, :]
+            cut = max(n for n in range(len(CUTS) - 1) if CUTS[n] <= step)
+            for (kind, members, first, last), acc in zip(jobs, accs):
+                if not first <= step <= last:
+                    continue
+                if kind == "start":
+                    acc = start_ref
+                for group in grouped(members):
+                    rows = slice(group[0] * UNIT, (group[-1] + 1) * UNIT)
+                    w = jnp.concatenate([w_refs[members[g]][...] for g in group], axis=0)
+                    if kind == "own":
+                        x = x_ref[...]
+                    else:
+                        x = jnp.concatenate([r[...] for r in cut_refs[4 * cut : 4 * cut + 4]], axis=0)
+                    v = lax.dot_general(w, x, (((1,), (1,)), ((), ())), preferred_element_type=F32)
+                    if step > first:
+                        v += acc[rows, :]
+                    elif kind == "resume":
+                        v += partial_ref[rows, :]
+                    if step < last or kind == "start":
+                        acc[rows, :] = v
+                        continue
                     v = (v * jax.nn.sigmoid(v)).astype(BF16)
-                    at = pl.ds(pl.multiple_of(s_ref[units[m][1]] * UNIT, UNIT), UNIT)
-                    if block == 1:
-                        across_ref[at, :] = v
-                        continue
-                    stage[rows, :] = v
-                    copy = pltpu.make_async_copy(stage.at[rows, :], u_ref.at[at, :], sem.at[i])
-                    copy.start()
-                    copies.append(copy)
-            if both:
+                    for n, g in enumerate(group):
+                        place = s_ref[units[members[g]][1]]
+                        at = pl.ds(pl.multiple_of(place * UNIT, UNIT), UNIT)
+                        one = v[n * UNIT : (n + 1) * UNIT, :]
+                        if kind == "own":
+                            own_rows = slice(g * UNIT, (g + 1) * UNIT)
+                            stage[own_rows, :] = one
+                            copies.append(pltpu.make_async_copy(stage.at[own_rows, :], u_ref.at[at, :], sem.at[g]))
+                            copies[-1].start()
+                            continue
+                        for p in range(4):
+                            lane = pl.multiple_of(s_ref[16 + p] * 128, 128)
+                            across_ref[at, pl.ds(lane, 128)] = one[:, p * 128 : (p + 1) * 128]
+            if after and step == NK - 1:
                 for h in range(4):
                     query_ref[h] = across_ref[h * 384 : h * 384 + 128, :]
             for copy in copies:
                 copy.wait()
 
+        for step in range(NK):
+            pl.when(k == step)(lambda step=step: run(step))
+
     in_specs = [pl.BlockSpec((TOK, KB), lambda k, s: (0, k))]
-    if both:
-        for n in range(len(CUTS) - 1):
-            low, last = CUTS[n], CUTS[n + 1] - CUTS[n] - 1
-            in_specs += [
-                pl.BlockSpec((128, KB), lambda k, s, low=low, last=last: (0, jnp.clip(k - low, 0, last)))
-            ] * 4
-    in_specs += [pl.BlockSpec((UNIT, KB), lambda k, s: (0, k))] * len(units)
-    own_count = sum(len(u) for block, u in jobs if block == 0)
-    scratch = [pltpu.SemaphoreType.DMA((own_count,))]
-    scratch += [pltpu.VMEM((len(u) * UNIT, TOK), F32) for _, u in jobs]
-    scratch += [pltpu.VMEM((own_count * UNIT, TOK), BF16)]
+    for n in range(len(cuts)):
+        low, top = CUTS[n], CUTS[n + 1] - CUTS[n] - 1
+        in_specs += [pl.BlockSpec((128, KB), lambda k, s, low=low, top=top: (0, jnp.clip(k - low, 0, top)))] * 4
+    for m in range(len(units)):
+        low = min(first for _, members, first, _ in jobs if m in members)
+        top = max(last for _, members, _, last in jobs if m in members)
+        in_specs.append(pl.BlockSpec((UNIT, KB), lambda k, s, low=low, top=top: (0, jnp.clip(k, low, top))))
+    own_count = sum(len(members) for kind, members, _, _ in jobs if kind == "own")
+    scratch = [pltpu.SemaphoreType.DMA((own_count,)), pltpu.VMEM((own_count * UNIT, TOK), BF16)]
     out_specs = [pl.BlockSpec(memory_space=pl.ANY)]
     out_shape = [jax.ShapeDtypeStruct((16 * UNIT, TOK), BF16)]
-    if both:
-        scratch.append(pltpu.VMEM((TOK, KB), BF16))
+    for kind, members, _, _ in jobs:
+        rows = len(members) * UNIT
+        scratch.append(pltpu.VMEM((rows if kind != "start" else 8, TOK), F32))
+        if kind == "start":
+            out_specs.append(pl.BlockSpec((rows, TOK), lambda k, s: (0, 0)))
+            out_shape.append(jax.ShapeDtypeStruct((rows, TOK), F32))
+    if after:
         out_specs.append(pl.BlockSpec((16 * UNIT, TOK), lambda k, s: (0, 0)))
         out_specs.append(pl.BlockSpec((4, 128, TOK), lambda k, s: (0, 0, 0)))
         out_shape.append(jax.ShapeDtypeStruct((16 * UNIT, TOK), BF16))
         out_shape.append(jax.ShapeDtypeStruct((4, 128, TOK), BF16))
-    args = [scalars, *flat, *[w for w, _ in units]]
+    args = [scalars, here, *[v for quarters in cuts for v in quarters], *[w for w, _ in units]]
+    if partial is not None:
+        in_specs.append(pl.BlockSpec(partial.shape, lambda k, s: (0, 0)))
+        args.append(partial)
     aliases = {}
     if held is not None:
         in_specs.append(pl.BlockSpec(memory_space=pl.ANY))
         aliases = {len(args): 0}
         args.append(held)
+    products = sum(len(members) * (last + 1 - first) for _, members, first, last in jobs) * UNIT * TOK
     return pl.pallas_call(
         kernel,
         grid_spec=pltpu.PrefetchScalarGridSpec(
@@ -150,9 +165,9 @@
         out_shape=out_shape,
         input_output_aliases=aliases,
         cost_estimate=pl.CostEstimate(
-            flops=2 * count * UNIT * TOK * DIM,
-            bytes_accessed=2 * DIM * (len(units) * UNIT + TOK * len(blocks)),
-            transcendentals=count * UNIT * TOK,
+            flops=2 * products * KB,
+            bytes_accessed=2 * DIM * len(units) * UNIT,
+            transcendentals=products // NK,
         ),
         name="project",
     )(*args)
@@ -276,46 +291,31 @@
     )(order, totals, pieces)
 
 
-def finish(half, queries, cumulated, inside, carried, gains, output):
+def finish(half, held, over_queries, sums, inside, over_inside, carried, gains):
     def kernel(z_ref, *refs):
-        q_refs, (c_ref, i_ref, s_ref, g_ref), o_ref = refs[: len(queries)], refs[len(queries) :][:4], refs[-1]
-        for h in range(4):
-            q = q_refs[h][...] if len(queries) == 4 else q_refs[0][h]
-            carry = s_ref[4 * h : 4 * h + 4].reshape(128, 128)
-            outer = lax.dot_general(carry, q, (((0,), (0,)), ((), ())), preferred_element_type=F32)
-            combined = i_ref[h].astype(F32) + outer * jnp.exp(c_ref[h])
-            root = lax.rsqrt(jnp.mean(combined * combined, axis=0, keepdims=True) + 1e-05)
-            gain = g_ref[pl.ds(z_ref[0] * 4 + h, 1), :]
-            o_ref[:, h * 128 : (h + 1) * 128] = (jnp.transpose(combined * root) * gain).astype(BF16)
-
-    if len(queries) == 4:
-        q_specs = [pl.BlockSpec((128, TOK), lambda i, z, h=h: (h * 3, 0)) for h in range(4)]
-    else:
-        q_specs = [pl.BlockSpec((4, 128, TOK), lambda i, z: (0, 0, 0))]
-    in_specs = q_specs + [
-        pl.BlockSpec((4, 1, TOK), lambda i, z: (z[0], 0, 0)),
-        pl.BlockSpec((4, 128, TOK), lambda i, z: (0, 0, 0)),
-        pl.BlockSpec((16, 32, 128), lambda i, z: (z[0], 0, 0)),
-        pl.BlockSpec((8, 128), lambda i, z: (0, 0)),
-    ]
-    args = [half, *queries, cumulated, inside, carried, gains]
-    aliases = {}
-    if output is not None:
-        in_specs.append(pl.BlockSpec(memory_space=pl.ANY))
-        aliases = {len(args): 0}
-        args.append(output)
-    return pl.pallas_call(
-        kernel,
-        grid_spec=pltpu.PrefetchScalarGridSpec(
-            num_scalar_prefetch=1,
-            grid=(1,),
-            in_specs=in_specs,
-            out_specs=pl.BlockSpec((TOK, 512), lambda i, z: (0, z[0])),
-        ),
+        q_refs, (over_ref, c_ref, in_ref, over_in_ref, s_ref, g_ref, o_ref) = refs[:4], refs[4:]
+        for side in range(2):
+            for h in range(4):
+                head = (z_ref[0] if side == 0 else 1 - z_ref[0]) * 4 + h
+                q = q_refs[h][...] if side == 0 else over_ref[h]
+                within = in_ref[h] if side == 0 else over_in_ref[h].astype(F32)
+                carry = s_ref[pl.ds(4 * head, 4)].reshape(128, 128)
+                outer = lax.dot_general(carry, q, (((0,), (0,)), ((), ())), preferred_element_type=F32)
+                combined = within + outer * jnp.exp(c_ref[head])
+                root = lax.rsqrt(jnp.mean(combined * combined, axis=0, keepdims=True) + 1e-05)
+                result = jnp.transpose(combined * root) * g_ref[pl.ds(head, 1), :]
+                o_ref[:, pl.ds(pl.multiple_of(head * 128, 128), 128)] = result.astype(BF16)
+
+    return pl.pallas_call(
+        kernel,
+        grid=(1,),
+        in_specs=[SMEM]
+        + heads_of(0)
+        + [whole(a.shape) for a in (over_queries, sums, inside, over_inside, carried, gains)],
+        out_specs=whole((TOK, 1024)),
         out_shape=jax.ShapeDtypeStruct((TOK, 1024), BF16),
-        input_output_aliases=aliases,
         name="finish",
-    )(*args)
+    )(half, *[held] * 4, over_queries, sums, inside, over_inside, carried, gains)
 
 
 def shards(inputs, qkv_weight, log_decay, out_gain):
@@ -371,7 +371,7 @@
     xa = [x_move(v, 1) for v in a]
     xb = [x_move(v, -1) for v in a]
     xc = [x_move(v, 1) for v in xa]
-    w_a, totals, scalars, order = lax.optimization_barrier((w_a, totals, scalars, order))
+    w_a, scalars, order = lax.optimization_barrier((w_a, scalars, order))
     w_c = y_move(w_a, 1)
     w_zb = y_move(w_z, -1)
     w_za = z_in(w_a)
@@ -386,11 +386,14 @@
 
     weights = [own, s_own, w_a, s_a, w_b, s_b, w_z, s_z, w_c, s_c, w_za, s_za, w_zb, s_zb, w_zbb, s_zbb]
     units = [(w, i) for i, w in enumerate(weights)]
-    here, across = [inputs], [v for parts in zip(a, xa, xb, xc) for v in parts]
-    (held,) = project(scalars, [here], units[:8], [(0, range(8))], None)
-    (held,) = project(scalars, [here], units[8:14], [(0, range(6))], held)
-    jobs = [(1, range(16)), (0, (14, 15))]
-    held, held_across, queries = project(scalars, [here, across], units, jobs, held)
+    cuts = list(zip(a, xa, xb, xc))
+    late = NK // 2
+    jobs = [("own", range(8), 0, NK - 1)]
+    (held,) = project(scalars, inputs, [], units[:8], jobs, None, None)
+    jobs = [("own", range(8, 14), 0, NK - 1), ("start", range(14), 0, late - 1)]
+    held, partial = project(scalars, inputs, cuts[:-1], units[:14], jobs, held, None)
+    jobs = [("across", (14, 15), 0, NK - 1), ("own", (14, 15), 0, NK - 1), ("resume", range(14), late, NK - 1)]
+    held, held_across, queries = project(scalars, inputs, cuts, units, jobs, held, partial)
 
     over_queries = z_out(queries)
     own_states = states(mine, [(held, sums), (held_across, sums_across)])
@@ -400,10 +403,7 @@
     running = carries(order, totals, update)
     carried = exchange(running, SEQ)
     inside = intra(mine, held, sums, F32)
-    carried, inside = lax.optimization_barrier((carried, inside))
-    output = finish(mine, [held] * 4, sums, inside, carried, out_gain, None)
-    over_queries, over_inside, output = lax.optimization_barrier((over_queries, over_inside, output))
-    return finish(other, [over_queries], sums, over_inside, carried, out_gain, output)
+    return finish(mine, held, over_queries, sums, inside, over_inside, carried, out_gain)
 
 
 def solution(mesh):

time: 202 us -> 229 us (1.13)
  waiting for transfers between devices: 72.6 us -> 102 us
  starting transfers between devices: 45.1 us -> 42.5 us
    ppermute x6, waiting for transfers between devices: 17.9 us -> 34.3 us  [z_out(): return lax.ppermute(v, ('zh', 'zl'), [(i, 3 - i) for i in range(4)])]
    ppermute x5, waiting for transfers between devices: 22.4 us -> 10.6 us  [y_move(): return lax.ppermute(v, ('y', 'c'), ring_pairs(step))]
    ppermute x2, waiting for transfers between devices: 3.31 us -> 13.9 us  [z_in(): return lax.ppermute(v, 'zl', [(0, 1), (1, 0)])]
    all_to_all x2, waiting for transfers between devices: 13.2 us -> 22.1 us  [exchange(): return lax.all_to_all(v, axes, 0, 0, tiled=True)]
    ppermute x9, waiting for transfers between devices: 14 us -> 21.1 us  [x_move(): return lax.ppermute(v, ('x', 'c'), ring_pairs(step))]
    ppermute x5, starting transfers between devices: 11 us -> 8.04 us  [y_move(): return lax.ppermute(v, ('y', 'c'), ring_pairs(step))]
    ppermute x6, starting transfers between devices: 11.4 us -> 13.9 us  [z_out(): return lax.ppermute(v, ('zh', 'zl'), [(i, 3 - i) for i in range(4)])]
    pallas_call x2 -> x1, Pallas kernels: 5.55 us -> 3.95 us  [finish(): pl.pallas_call(kernel, grid=(1,), in_specs=[SMEM] + heads_of(0) + [whole(...]
  transfers between devices with their start and end apart: 32 -> 32, of which waited for: 13 -> 10; matrix products, arithmetic and copies ran while one was open for 1% -> 1% of each run, Pallas kernels for 28% -> 24%
where the time goes in v3:
time: 229 us; the launch traced here: 227 us
  waiting for transfers between devices  102 us (45%)
  Pallas kernels  61.4 us (27%)
  starting transfers between devices  42.5 us (19%)
  blocking collectives  12 us (5%)
  local copies, waits for them, and re-layouts  7.94 us (3%)
    pallas_call x3, Pallas kernels, project(): pl.pallas_call(kernel, grid_spec=pltpu.PrefetchScalarGridSpec(num_scalar_...  43.9 us
    ppermute x6, waiting for transfers between devices, z_out(): return lax.ppermute(v, ('zh', 'zl'), [(i, 3 - i) for i in range(4)])  34.3 us
    all_to_all x2, waiting for transfers between devices, exchange(): return lax.all_to_all(v, axes, 0, 0, tiled=True)  22.1 us
    ppermute x9, waiting for transfers between devices, x_move(): return lax.ppermute(v, ('x', 'c'), ring_pairs(step))  21.1 us
    ppermute x2, waiting for transfers between devices, z_in(): return lax.ppermute(v, 'zl', [(0, 1), (1, 0)])  13.9 us
    ppermute x6, starting transfers between devices, z_out(): return lax.ppermute(v, ('zh', 'zl'), [(i, 3 - i) for i in range(4)])  13.9 us
    all_to_all x1, blocking collectives, exchange(): return lax.all_to_all(v, axes, 0, 0, tiled=True)  12 us
    ppermute x9, starting transfers between devices, x_move(): return lax.ppermute(v, ('x', 'c'), ring_pairs(step))  11.6 us
  transfers between devices with their start and end apart: 32, of which 10 were waited for; matrix products, arithmetic and copies ran while one was open for 1% of the time, Pallas kernels for 24%

profile of v3, /device:TPU:0, one launch (start us, length us, event | category | flops | bytes accessed | tf_op | source)
XLA Modules:
  0.0 226.6 jit_solution(14891068128992882682)
XLA Ops:
  0.0 1.3 constant_dynamic-slice_fusion.1
  1.3 0.0 copy-start.18
  1.3 0.0 copy-start.19
  1.3 4.2 %collective-permute-start.1 = (bf16[128,1536]{1,0:T(8,128)(2,1)S(1)}, bf16[128,1536]{1,0:T(8,128)(2,1)S(1)}, u32[]{:S(2)}, u32[]{:S(2)}) collective-permute-start(bf16[128,1536]{1,0:T(8,128)(2,1)S(1)} %get-tuple-element.26), channel_id=1, source_target_pairs={{0,24},{8,16},{16,8},{24,0},{1,25},{9,17},{17,9},{25,1},{2,26},{10... | collective-permute-start | bytes 1179656 | tf_op jit(solution)/shard_map/ppermute | solution.py:41
  5.5 0.1 collective-permute-start.5
  5.6 9.9 %collective-permute-done.1.refs_0_ = bf16[128,1536]{1,0:T(8,128)(2,1)S(1)} collective-permute-done((bf16[128,1536]{1,0:T(8,128)(2,1)S(1)}, bf16[128,1536]{1,0:T(8,128)(2,1)S(1)}, u32[]{:S(2)}, u32[]{:S(2)}) %collective-permute-start.1) | collective-permute-done | bytes 393248 | tf_op jit(solution)/shard_map/ppermute | solution.py:41
  15.5 1.5 collective-permute-start.2
  17.0 6.1 %collective-permute-done.5.refs_4_ = bf16[128,1536]{1,0:T(8,128)(2,1)S(1)} collective-permute-done((bf16[128,1536]{1,0:T(8,128)(2,1)S(1)}, bf16[128,1536]{1,0:T(8,128)(2,1)S(1)}, u32[]{:S(2)}, u32[]{:S(2)}) %collective-permute-start.5) | collective-permute-done | bytes 393248 | tf_op jit(solution)/shard_map/ppermute | solution.py:41
  23.1 1.5 collective-permute-start.6
  24.6 1.7 collective-permute-start.3
  26.3 1.5 collective-permute-start.7
  27.9 1.6 collective-permute-start
  29.4 0.0 collective-permute-done.2.refs_1_
  29.4 0.0 collective-permute-start.17
  29.4 6.1 %collective-permute-done.6.refs_5_ = bf16[128,1536]{1,0:T(8,128)(2,1)S(1)} collective-permute-done((bf16[128,1536]{1,0:T(8,128)(2,1)S(1)}, bf16[128,1536]{1,0:T(8,128)(2,1)S(1)}, u32[]{:S(2)}, u32[]{:S(2)}) %collective-permute-start.6) | collective-permute-done | bytes 393248 | tf_op jit(solution)/shard_map/ppermute | solution.py:33
  35.5 3.0 %collective-permute-start.15 = (bf16[96,6144]{1,0:T(8,128)(2,1)S(1)}, bf16[96,6144]{1,0:T(8,128)(2,1)}, u32[]{:S(2)}, u32[]{:S(2)}) collective-permute-start(bf16[96,6144]{1,0:T(8,128)(2,1)S(1)} %bitcast.27), channel_id=1, source_target_pairs={{0,6},{1,3},{2,0},{3,5},{4,2},{5,7},{6,4},{7,1},{8,14},{9,11},{10,... | collective-permute-start | bytes 3538952 | tf_op jit(solution)/shard_map/ppermute | solution.py:29
  38.5 0.7 copy-done.12
  39.3 0.0 collective-permute-start.13
  39.3 1.2 constant_dynamic-slice_fusion
  40.5 0.0 collective-permute-done.7.refs_6_
  40.5 3.3 %collective-permute-start.9 = (bf16[128,3072]{1,0:T(8,128)(2,1)S(1)}, bf16[128,3072]{1,0:T(8,128)(2,1)}, u32[]{:S(2)}, u32[]{:S(2)}) collective-permute-start(bf16[128,3072]{1,0:T(8,128)(2,1)S(1)} %constant_dynamic-slice_fusion), channel_id=1, source_target_pairs={{0,24},{8,16},{16,8},{24,0},{1,25},{9,17},{17,9},{25,1},{2,26},{10... | collective-permute-start | bytes 2359304 | tf_op jit(solution)/shard_map/ppermute | solution.py:41
  43.8 18.3 %collective-permute-done.9.refs_8_ = bf16[128,3072]{1,0:T(8,128)(2,1)} collective-permute-done((bf16[128,3072]{1,0:T(8,128)(2,1)S(1)}, bf16[128,3072]{1,0:T(8,128)(2,1)}, u32[]{:S(2)}, u32[]{:S(2)}) %collective-permute-start.9) | collective-permute-done | bytes 786464 | tf_op jit(solution)/shard_map/ppermute | solution.py:41
  62.1 0.8 collective-permute-start.4
  62.9 1.6 collective-permute-start.10
  64.5 0.7 stack.83.s_ref
  65.2 0.5 broadcast_select_fusion.n_ref
  65.6 0.0 collective-permute-done.15.refs_4_.refs_12_.refs_16_
  65.7 0.1 collective-permute-start.19
  65.8 3.2 %collective-permute-start.23 = (bf16[96,6144]{1,0:T(8,128)(2,1)S(1)}, bf16[96,6144]{1,0:T(8,128)(2,1)S(1)}, u32[]{:S(2)}, u32[]{:S(2)}) collective-permute-start(bf16[96,6144]{1,0:T(8,128)(2,1)S(1)} %collective-permute-done.17.refs_6_.refs_14_.refs_18_), channel_id=1, source_target_pairs={{0,6},{1,3},{2,0},{3,5},{4,2},{5,7},{6,4},{7,1},{8,14},{9,11},{10,... | collective-permute-start | bytes 3538952 | tf_op jit(solution)/shard_map/ppermute | solution.py:29
  69.0 2.5 %collective-permute-done.4.refs_3_ = bf16[128,1536]{1,0:T(8,128)(2,1)} collective-permute-done((bf16[128,1536]{1,0:T(8,128)(2,1)}, bf16[128,1536]{1,0:T(8,128)(2,1)}, u32[]{:S(2)}, u32[]{:S(2)}) %collective-permute-start.4) | collective-permute-done | bytes 393248 | tf_op jit(solution)/shard_map/ppermute | solution.py:33
  71.4 12.5 %collective-permute-done.8.refs_7_ = bf16[128,1536]{1,0:T(8,128)(2,1)S(1)} collective-permute-done((bf16[128,1536]{1,0:T(8,128)(2,1)}, bf16[128,1536]{1,0:T(8,128)(2,1)S(1)}, u32[]{:S(2)}, u32[]{:S(2)}) %collective-permute-start.8) | collective-permute-done | bytes 393248 | tf_op jit(solution)/shard_map/ppermute | solution.py:33
  84.0 0.7 copy-done.14
  84.7 0.0 collective-permute-done.10.refs_9_
  84.7 0.0 collective-permute-start.18
  84.7 0.0 collective-permute-done.14.refs_3_.refs_11_.refs_15_
  84.7 0.5 collective-permute-start.16
  85.2 10.6 %collective-permute-done.19.refs_16_.refs_20_ = bf16[96,6144]{1,0:T(8,128)(2,1)} collective-permute-done((bf16[96,6144]{1,0:T(8,128)(2,1)S(1)}, bf16[96,6144]{1,0:T(8,128)(2,1)}, u32[]{:S(2)}, u32[]{:S(2)}) %collective-permute-start.19) | collective-permute-done | bytes 1179680 | tf_op jit(solution)/shard_map/ppermute | solution.py:29
  95.8 0.2 collective-permute-start.25
  96.0 13.9 %collective-permute-done.21.refs_18_.refs_22_ = bf16[96,6144]{1,0:T(8,128)(2,1)} collective-permute-done((bf16[96,6144]{1,0:T(8,128)(2,1)S(1)}, bf16[96,6144]{1,0:T(8,128)(2,1)}, u32[]{:S(2)}, u32[]{:S(2)}) %collective-permute-start.21) | collective-permute-done | bytes 1179680 | tf_op jit(solution)/shard_map/ppermute | solution.py:37
  109.9 1.0 copy-done.5
  110.9 0.5 collective-permute-start.24
  111.4 1.9 rates.1
  113.3 3.0 %collective-permute-start.11 = (bf16[128,3072]{1,0:T(8,128)(2,1)}, bf16[128,3072]{1,0:T(8,128)(2,1)}, u32[]{:S(2)}, u32[]{:S(2)}) collective-permute-start(bf16[128,3072]{1,0:T(8,128)(2,1)} %collective-permute-done.9.refs_8_), channel_id=1, source_target_pairs={{0,96},{1,33},{32,0},{33,65},{64,32},{65,97},{96,64},{97,1},{2,98}... | collective-permute-start | bytes 2359304 | tf_op jit(solution)/shard_map/ppermute | solution.py:33
  116.3 0.3 collective-permute-start.26
  116.6 10.0 %project.3.refs_22_ = bf16[1536,512]{1,0:T(8,128)(2,1)} custom-call(s32[20]{0:T(128)} %stack.83.s_ref, bf16[512,6144]{1,0:T(8,128)(2,1)} %x_ref.5, bf16[96,6144]{1,0:T(8,128)(2,1)} %bitcast.22, bf16[96,6144]{1,0:T(8,128)(2,1)} %collective-permute-done.13.refs_1_.refs_9_.refs_13_, bf16[96,6144]{1,0:T(8,128)(2,1)} %copy-done.1, bf16[96,6144]{1,0:T(8,128)(2,1)} %copy-done.3, ...), custom_call_target="tpu_custom_call" | custom-call | flops 4831838208 | bytes 9437184 | tf_op jit(solution)/shard_map/project/pallas_call | solution.py:156
  126.7 3.0 %collective-permute-start.28 = (f32[8,1,512]{2,1,0:T(1,128)S(1)}, f32[8,1,512]{2,1,0:T(1,128)S(1)}, u32[]{:S(2)}, u32[]{:S(2)}) collective-permute-start(f32[8,1,512]{2,1,0:T(1,128)S(1)} %copy-done.15), channel_id=1, source_target_pairs={{0,24},{8,16},{16,8},{24,0},{1,25},{9,17},{17,9},{25,1},{2,26},{10... | collective-permute-start | bytes 49160 | tf_op jit(solution)/shard_map/ppermute | solution.py:41
  129.7 16.4 %project.4 = (bf16[1536,512]{1,0:T(8,128)(2,1)}, f32[1344,512]{1,0:T(8,128)}) custom-call(s32[20]{0:T(128)} %stack.83.s_ref, bf16[512,6144]{1,0:T(8,128)(2,1)} %x_ref.5, bf16[128,1536]{1,0:T(8,128)(2,1)} %copy-done.9, bf16[128,1536]{1,0:T(8,128)(2,1)} %collective-permute-done.2.refs_1_, ...), custom_call_target="tpu_custom_call", output_to_operand_aliasing={{0}: (24, {})} | custom-call | flops 7851737088 | bytes 16515072 | tf_op jit(solution)/shard_map/project/pallas_call | solution.py:156
  146.1 17.5 %project.5 = (bf16[1536,512]{1,0:T(8,128)(2,1)}, bf16[1536,512]{1,0:T(8,128)(2,1)}, bf16[4,128,512]{2,1,0:T(8,128)(2,1)}) custom-call(s32[20]{0:T(128)} %stack.83.s_ref, bf16[512,6144]{1,0:T(8,128)(2,1)} %x_ref.5, bf16[128,1536]{1,0:T(8,128)(2,1)} %copy-done.9, bf16[128,1536]{1,0:T(8,128)(2,1)} %collective-permute-done.2.refs_1_, ...), custom_call_target="tpu_custom_call", output_to_operand_aliasing={{0}: (31, {})} | custom-call | flops 6643777536 | bytes 18874368 | tf_op jit(solution)/shard_map/project/pallas_call | solution.py:156
  163.6 0.6 copy-done.17
  164.2 3.3 %intra.3 = bf16[4,128,512]{2,1,0:T(8,128)(2,1)} custom-call(s32[1]{0:T(128)} %bitcast.z_ref, bf16[1536,512]{1,0:T(8,128)(2,1)} %get-tuple-element.22.refs_0_.refs_1_.refs_2_.refs_3_.refs_4_.refs_5_.refs_6_.refs_7_.refs_8_.refs_9_.refs_10_.refs_11_.refs_12_.refs_13_.refs_14_.refs_15_.refs_16_, ...), custom_call_target="tpu_custom_call" | custom-call | tf_op jit(solution)/shard_map/intra/pallas_call | solution.py:265
  167.5 0.4 collective-permute-start.29
  167.9 2.9 %collective-permute-start.27 = (bf16[4,128,512]{2,1,0:T(8,128)(2,1)S(1)}, bf16[4,128,512]{2,1,0:T(8,128)(2,1)S(1)}, u32[]{:S(2)}, u32[]{:S(2)}) collective-permute-start(bf16[4,128,512]{2,1,0:T(8,128)(2,1)S(1)} %copy-done.20), channel_id=1, source_target_pairs={{0,24},{8,16},{16,8},{24,0},{1,25},{9,17},{17,9},{25,1},{2,26},{10... | collective-permute-start | bytes 1572872 | tf_op jit(solution)/shard_map/ppermute | solution.py:41
  170.8 3.8 %all-to-all-start = ((f32[32,1,128]{2,1,0:T(1,128)}), f32[32,1,128]{2,1,0:T(1,128)S(1)}, u32[]{:S(2)}, u32[]{:S(2)}) async-start(f32[32,1,128]{2,1,0:T(1,128)} %get-tuple-element.24), calls=%async_computation | async-start | bytes 32768 | tf_op jit(solution)/shard_map/all_to_all | solution.py:45
  174.6 3.1 %states.1 = bf16[16,2,32,128]{3,2,1,0:T(8,128)(2,1)} custom-call(s32[1]{0:T(128)} %bitcast.z_ref, bf16[1536,512]{1,0:T(8,128)(2,1)} %get-tuple-element.19.refs_0_.refs_1_.refs_2_.refs_3_.refs_4_.refs_5_.refs_6_.refs_7_.refs_8_.refs_9_.refs_10_.refs_11_, ...), custom_call_target="tpu_custom_call" | custom-call | tf_op jit(solution)/shard_map/states/pallas_call | solution.py:232
  177.7 16.8 %all-to-all-done.d_ref = f32[32,1,128]{2,1,0:T(1,128)S(1)} async-done(((f32[32,1,128]{2,1,0:T(1,128)}), f32[32,1,128]{2,1,0:T(1,128)S(1)}, u32[]{:S(2)}, u32[]{:S(2)}) %all-to-all-start) | async-done | bytes 16416 | tf_op jit(solution)/shard_map/all_to_all | solution.py:45
  194.5 12.0 %all_to_all.15.s_ref = bf16[16,2,32,128]{3,2,1,0:T(8,128)(2,1)} all-to-all(bf16[16,2,32,128]{3,2,1,0:T(8,128)(2,1)} %states.1), channel_id=1, replica_groups=mesh['x'=4,'zh'=2,'zl'=2,'y'=4,'c'=2] {'zl','y','c'}, dimensions={0} | all-to-all | bytes 524288 | tf_op jit(solution)/shard_map/all_to_all | solution.py:45
  206.6 1.8 carries.1
  208.3 3.9 %all-to-all-start.2 = ((bf16[32,32,128]{2,1,0:T(8,128)(2,1)}), bf16[32,32,128]{2,1,0:T(8,128)(2,1)S(1)}, u32[]{:S(2)}, u32[]{:S(2)}) async-start(bf16[32,32,128]{2,1,0:T(8,128)(2,1)} %carries.1), calls=%async_computation.2 | async-start | bytes 524288 | tf_op jit(solution)/shard_map/all_to_all | solution.py:45
  212.2 3.5 %intra.2.refs_6_ = f32[4,128,512]{2,1,0:T(8,128)} custom-call(s32[1]{0:T(128)} %bitcast.z_ref, bf16[1536,512]{1,0:T(8,128)(2,1)} %get-tuple-element.19.refs_0_.refs_1_.refs_2_.refs_3_.refs_4_.refs_5_.refs_6_.refs_7_.refs_8_.refs_9_.refs_10_.refs_11_, ...), custom_call_target="tpu_custom_call" | custom-call | tf_op jit(solution)/shard_map/intra/pallas_call | solution.py:265
  215.7 5.3 %all-to-all-done.2.refs_8_ = bf16[32,32,128]{2,1,0:T(8,128)(2,1)S(1)} async-done(((bf16[32,32,128]{2,1,0:T(8,128)(2,1)}), bf16[32,32,128]{2,1,0:T(8,128)(2,1)S(1)}, u32[]{:S(2)}, u32[]{:S(2)}) %all-to-all-start.2) | async-done | bytes 262176 | tf_op jit(solution)/shard_map/all_to_all | solution.py:45
  221.0 0.7 copy-done.6
  221.7 0.2 copy-done.7
  221.9 0.8 copy-done.8
  222.7 3.9 %finish.1 = bf16[512,1024]{1,0:T(8,128)(2,1)} custom-call(s32[1]{0:T(128)} %bitcast.z_ref, bf16[1536,512]{1,0:T(8,128)(2,1)} %get-tuple-element.19.refs_0_.refs_1_.refs_2_.refs_3_.refs_4_.refs_5_.refs_6_.refs_7_.refs_8_.refs_9_.refs_10_.refs_11_, ...), custom_call_target="tpu_custom_call" | custom-call | tf_op jit(solution)/shard_map/finish/pallas_call | solution.py:309
  (56 shorter events, 0.1 us)
Async XLA Ops:
  0.0 27.9 %copy-start = (bf16[6144,96]{0,1:T(8,128)(2,1)S(1)}, bf16[6144,96]{0,1:T(8,128)(2,1)}, u32[]{:S(2)}) copy-start(bf16[6144,96]{0,1:T(8,128)(2,1)} %param.7) | copy-start | bytes 3538948
  1.3 63.9 %copy-start.18 = (s32[8]{0:T(128)S(1)}, s32[8]{0:T(128)}, u32[]{:S(2)}) copy-start(s32[8]{0:T(128)} %constant.101.clone) | copy-start | bytes 100
  1.3 63.9 %copy-start.19 = (s32[8]{0:T(128)S(1)}, s32[8]{0:T(128)}, u32[]{:S(2)}) copy-start(s32[8]{0:T(128)} %constant.102.clone) | copy-start | bytes 100
  1.3 14.2 %collective-permute-start.1 = (bf16[128,1536]{1,0:T(8,128)(2,1)S(1)}, bf16[128,1536]{1,0:T(8,128)(2,1)S(1)}, u32[]{:S(2)}, u32[]{:S(2)}) collective-permute-start(bf16[128,1536]{1,0:T(8,128)(2,1)S(1)} %get-tuple-element.26), channel_id=1, source_target_pairs={{0,24},{8,16},{16,8},{24,0},{1,25},{9,17},{17,9},{25,1},{2,26},{10... | collective-permute-start | bytes 1179656 | tf_op jit(solution)/shard_map/ppermute | solution.py:41
  5.5 17.5 %collective-permute-start.5 = (bf16[128,1536]{1,0:T(8,128)(2,1)S(1)}, bf16[128,1536]{1,0:T(8,128)(2,1)S(1)}, u32[]{:S(2)}, u32[]{:S(2)}) collective-permute-start(bf16[128,1536]{1,0:T(8,128)(2,1)S(1)} %get-tuple-element.25), channel_id=1, source_target_pairs={{0,24},{8,16},{16,8},{24,0},{1,25},{9,17},{17,9},{25,1},{2,26},{10... | collective-permute-start | bytes 1179656 | tf_op jit(solution)/shard_map/ppermute | solution.py:41
  15.5 23.0 %copy-start.9 = (bf16[128,1536]{1,0:T(8,128)(2,1)}, bf16[128,1536]{1,0:T(8,128)(2,1)S(1)}, u32[]{:S(2)}) copy-start(bf16[128,1536]{1,0:T(8,128)(2,1)S(1)} %collective-permute-done.1.refs_0_) | copy-start | bytes 1179652
  15.5 13.9 %collective-permute-start.2 = (bf16[128,1536]{1,0:T(8,128)(2,1)S(1)}, bf16[128,1536]{1,0:T(8,128)(2,1)}, u32[]{:S(2)}, u32[]{:S(2)}) collective-permute-start(bf16[128,1536]{1,0:T(8,128)(2,1)S(1)} %collective-permute-done.1.refs_0_), channel_id=1, source_target_pairs={{0,32},{1,97},{32,64},{33,1},{64,96},{65,33},{96,0},{97,65},{2,34}... | collective-permute-start | bytes 1179656 | tf_op jit(solution)/shard_map/ppermute | solution.py:33
  23.1 39.8 %copy-start.10 = (bf16[128,1536]{1,0:T(8,128)(2,1)}, bf16[128,1536]{1,0:T(8,128)(2,1)S(1)}, u32[]{:S(2)}) copy-start(bf16[128,1536]{1,0:T(8,128)(2,1)S(1)} %collective-permute-done.5.refs_4_) | copy-start | bytes 1179652
  23.1 12.4 %collective-permute-start.6 = (bf16[128,1536]{1,0:T(8,128)(2,1)S(1)}, bf16[128,1536]{1,0:T(8,128)(2,1)S(1)}, u32[]{:S(2)}, u32[]{:S(2)}) collective-permute-start(bf16[128,1536]{1,0:T(8,128)(2,1)S(1)} %collective-permute-done.5.refs_4_), channel_id=1, source_target_pairs={{0,32},{1,97},{32,64},{33,1},{64,96},{65,33},{96,0},{97,65},{2,34}... | collective-permute-start | bytes 1179656 | tf_op jit(solution)/shard_map/ppermute | solution.py:33
  24.6 14.0 %collective-permute-start.3 = (bf16[128,1536]{1,0:T(8,128)(2,1)S(1)}, bf16[128,1536]{1,0:T(8,128)(2,1)S(1)}, u32[]{:S(2)}, u32[]{:S(2)}) collective-permute-start(bf16[128,1536]{1,0:T(8,128)(2,1)S(1)} %collective-permute-done.1.refs_0_), channel_id=1, source_target_pairs={{0,96},{1,33},{32,0},{33,65},{64,32},{65,97},{96,64},{97,1},{2,98}... | collective-permute-start | bytes 1179656 | tf_op jit(solution)/shard_map/ppermute | solution.py:33
  26.3 14.2 %collective-permute-start.7 = (bf16[128,1536]{1,0:T(8,128)(2,1)S(1)}, bf16[128,1536]{1,0:T(8,128)(2,1)S(1)}, u32[]{:S(2)}, u32[]{:S(2)}) collective-permute-start(bf16[128,1536]{1,0:T(8,128)(2,1)S(1)} %collective-permute-done.5.refs_4_), channel_id=1, source_target_pairs={{0,96},{1,33},{32,0},{33,65},{64,32},{65,97},{96,64},{97,1},{2,98}... | collective-permute-start | bytes 1179656 | tf_op jit(solution)/shard_map/ppermute | solution.py:33
  27.9 35.0 %collective-permute-start = (bf16[96,6144]{1,0:T(8,128)(2,1)S(1)}, bf16[96,6144]{1,0:T(8,128)(2,1)S(1)}, u32[]{:S(2)}, u32[]{:S(2)}) collective-permute-start(bf16[96,6144]{1,0:T(8,128)(2,1)S(1)} %bitcast.25), channel_id=1, source_target_pairs={{0,2},{1,7},{2,4},{3,1},{4,6},{5,3},{6,0},{7,5},{8,10},{9,15},{10,... | collective-permute-start | bytes 3538952 | tf_op jit(solution)/shard_map/ppermute | solution.py:29
  29.4 36.2 %collective-permute-start.17 = (bf16[96,6144]{1,0:T(8,128)(2,1)S(1)}, bf16[96,6144]{1,0:T(8,128)(2,1)S(1)}, u32[]{:S(2)}, u32[]{:S(2)}) collective-permute-start(bf16[96,6144]{1,0:T(8,128)(2,1)S(1)} %bitcast.26), channel_id=1, source_target_pairs={{0,8},{8,0},{1,9},{9,1},{2,10},{10,2},{3,11},{11,3},{4,12},{12,4},... | collective-permute-start | bytes 3538952 | tf_op jit(solution)/shard_map/ppermute | solution.py:37
  35.5 3.0 %copy-start.11 = (bf16[128,1536]{1,0:T(8,128)(2,1)}, bf16[128,1536]{1,0:T(8,128)(2,1)S(1)}, u32[]{:S(2)}) copy-start(bf16[128,1536]{1,0:T(8,128)(2,1)S(1)} %collective-permute-done.6.refs_5_) | copy-start | bytes 1179652
  35.5 30.2 %collective-permute-start.15 = (bf16[96,6144]{1,0:T(8,128)(2,1)S(1)}, bf16[96,6144]{1,0:T(8,128)(2,1)}, u32[]{:S(2)}, u32[]{:S(2)}) collective-permute-start(bf16[96,6144]{1,0:T(8,128)(2,1)S(1)} %bitcast.27), channel_id=1, source_target_pairs={{0,6},{1,3},{2,0},{3,5},{4,2},{5,7},{6,4},{7,1},{8,14},{9,11},{10,... | collective-permute-start | bytes 3538952 | tf_op jit(solution)/shard_map/ppermute | solution.py:29
  38.5 0.8 copy-start.12
  39.3 26.5 %collective-permute-start.13 = (bf16[96,6144]{1,0:T(8,128)(2,1)S(1)}, bf16[96,6144]{1,0:T(8,128)(2,1)}, u32[]{:S(2)}, u32[]{:S(2)}) collective-permute-start(bf16[96,6144]{1,0:T(8,128)(2,1)S(1)} %bitcast.28), channel_id=1, source_target_pairs={{0,1},{1,0},{2,3},{3,2},{4,5},{5,4},{6,7},{7,6},{8,9},{9,8},{10,11... | collective-permute-start | bytes 3538952 | tf_op jit(solution)/shard_map/ppermute | solution.py:49
  40.5 22.4 %copy-start.13 = (bf16[128,1536]{1,0:T(8,128)(2,1)}, bf16[128,1536]{1,0:T(8,128)(2,1)S(1)}, u32[]{:S(2)}) copy-start(bf16[128,1536]{1,0:T(8,128)(2,1)S(1)} %collective-permute-done.7.refs_6_) | copy-start | bytes 1179652
  40.5 21.6 %collective-permute-start.9 = (bf16[128,3072]{1,0:T(8,128)(2,1)S(1)}, bf16[128,3072]{1,0:T(8,128)(2,1)}, u32[]{:S(2)}, u32[]{:S(2)}) collective-permute-start(bf16[128,3072]{1,0:T(8,128)(2,1)S(1)} %constant_dynamic-slice_fusion), channel_id=1, source_target_pairs={{0,24},{8,16},{16,8},{24,0},{1,25},{9,17},{17,9},{25,1},{2,26},{10... | collective-permute-start | bytes 2359304 | tf_op jit(solution)/shard_map/ppermute | solution.py:41
  62.1 9.3 %collective-permute-start.4 = (bf16[128,1536]{1,0:T(8,128)(2,1)}, bf16[128,1536]{1,0:T(8,128)(2,1)}, u32[]{:S(2)}, u32[]{:S(2)}) collective-permute-start(bf16[128,1536]{1,0:T(8,128)(2,1)} %collective-permute-done.2.refs_1_), channel_id=1, source_target_pairs={{0,32},{1,97},{32,64},{33,1},{64,96},{65,33},{96,0},{97,65},{2,34}... | collective-permute-start | bytes 1179656 | tf_op jit(solution)/shard_map/ppermute | solution.py:33
  62.9 53.7 %copy-start.1 = (bf16[96,6144]{1,0:T(8,128)(2,1)}, bf16[96,6144]{1,0:T(8,128)(2,1)S(1)}, u32[]{:S(2)}) copy-start(bf16[96,6144]{1,0:T(8,128)(2,1)S(1)} %collective-permute-done.refs_2_.refs_10_.refs_14_) | copy-start | bytes 3538948
  62.9 21.8 %collective-permute-start.10 = (bf16[128,3072]{1,0:T(8,128)(2,1)}, bf16[128,3072]{1,0:T(8,128)(2,1)}, u32[]{:S(2)}, u32[]{:S(2)}) collective-permute-start(bf16[128,3072]{1,0:T(8,128)(2,1)} %collective-permute-done.9.refs_8_), channel_id=1, source_target_pairs={{0,32},{1,97},{32,64},{33,1},{64,96},{65,33},{96,0},{97,65},{2,34}... | collective-permute-start | bytes 2359304 | tf_op jit(solution)/shard_map/ppermute | solution.py:33
  65.6 51.0 %copy-start.2 = (bf16[96,6144]{1,0:T(8,128)(2,1)}, bf16[96,6144]{1,0:T(8,128)(2,1)S(1)}, u32[]{:S(2)}) copy-start(bf16[96,6144]{1,0:T(8,128)(2,1)S(1)} %collective-permute-done.17.refs_6_.refs_14_.refs_18_) | copy-start | bytes 3538948
  65.6 19.1 %collective-permute-start.14 = (bf16[96,6144]{1,0:T(8,128)(2,1)S(1)}, bf16[96,6144]{1,0:T(8,128)(2,1)S(1)}, u32[]{:S(2)}, u32[]{:S(2)}) collective-permute-start(bf16[96,6144]{1,0:T(8,128)(2,1)S(1)} %collective-permute-done.refs_2_.refs_10_.refs_14_), channel_id=1, source_target_pairs={{0,1},{1,0},{2,3},{3,2},{4,5},{5,4},{6,7},{7,6},{8,9},{9,8},{10,11... | collective-permute-start | bytes 3538952 | tf_op jit(solution)/shard_map/ppermute | solution.py:49
  65.7 30.2 %collective-permute-start.19 = (bf16[96,6144]{1,0:T(8,128)(2,1)S(1)}, bf16[96,6144]{1,0:T(8,128)(2,1)}, u32[]{:S(2)}, u32[]{:S(2)}) collective-permute-start(bf16[96,6144]{1,0:T(8,128)(2,1)S(1)} %collective-permute-done.refs_2_.refs_10_.refs_14_), channel_id=1, source_target_pairs={{0,2},{1,7},{2,4},{3,1},{4,6},{5,3},{6,0},{7,5},{8,10},{9,15},{10,... | collective-permute-start | bytes 3538952 | tf_op jit(solution)/shard_map/ppermute | solution.py:29
  65.8 30.1 %collective-permute-start.23 = (bf16[96,6144]{1,0:T(8,128)(2,1)S(1)}, bf16[96,6144]{1,0:T(8,128)(2,1)S(1)}, u32[]{:S(2)}, u32[]{:S(2)}) collective-permute-start(bf16[96,6144]{1,0:T(8,128)(2,1)S(1)} %collective-permute-done.17.refs_6_.refs_14_.refs_18_), channel_id=1, source_target_pairs={{0,6},{1,3},{2,0},{3,5},{4,2},{5,7},{6,4},{7,1},{8,14},{9,11},{10,... | collective-permute-start | bytes 3538952 | tf_op jit(solution)/shard_map/ppermute | solution.py:29
  71.4 12.5 %collective-permute-start.8 = (bf16[128,1536]{1,0:T(8,128)(2,1)}, bf16[128,1536]{1,0:T(8,128)(2,1)S(1)}, u32[]{:S(2)}, u32[]{:S(2)}) collective-permute-start(bf16[128,1536]{1,0:T(8,128)(2,1)} %copy-done.11), channel_id=1, source_target_pairs={{0,32},{1,97},{32,64},{33,1},{64,96},{65,33},{96,0},{97,65},{2,34}... | collective-permute-start | bytes 1179656 | tf_op jit(solution)/shard_map/ppermute | solution.py:33
  84.0 0.7 copy-start.14
  84.0 25.9 %collective-permute-start.21 = (bf16[96,6144]{1,0:T(8,128)(2,1)S(1)}, bf16[96,6144]{1,0:T(8,128)(2,1)}, u32[]{:S(2)}, u32[]{:S(2)}) collective-permute-start(bf16[96,6144]{1,0:T(8,128)(2,1)S(1)} %collective-permute-done.refs_2_.refs_10_.refs_14_), channel_id=1, source_target_pairs={{0,8},{8,0},{1,9},{9,1},{2,10},{10,2},{3,11},{11,3},{4,12},{12,4},... | collective-permute-start | bytes 3538952 | tf_op jit(solution)/shard_map/ppermute | solution.py:37
  84.7 25.2 %collective-permute-start.18 = (bf16[96,6144]{1,0:T(8,128)(2,1)S(1)}, bf16[96,6144]{1,0:T(8,128)(2,1)S(1)}, u32[]{:S(2)}, u32[]{:S(2)}) collective-permute-start(bf16[96,6144]{1,0:T(8,128)(2,1)S(1)} %collective-permute-done.17.refs_6_.refs_14_.refs_18_), channel_id=1, source_target_pairs={{0,1},{1,0},{2,3},{3,2},{4,5},{5,4},{6,7},{7,6},{8,9},{9,8},{10,11... | collective-permute-start | bytes 3538952 | tf_op jit(solution)/shard_map/ppermute | solution.py:49
  84.7 25.2 %copy-start.3 = (bf16[96,6144]{1,0:T(8,128)(2,1)}, bf16[96,6144]{1,0:T(8,128)(2,1)S(1)}, u32[]{:S(2)}) copy-start(bf16[96,6144]{1,0:T(8,128)(2,1)S(1)} %collective-permute-done.14.refs_3_.refs_11_.refs_15_) | copy-start | bytes 3538948
  84.7 28.6 %collective-permute-start.16 = (bf16[96,6144]{1,0:T(8,128)(2,1)}, bf16[96,6144]{1,0:T(8,128)(2,1)}, u32[]{:S(2)}, u32[]{:S(2)}) collective-permute-start(bf16[96,6144]{1,0:T(8,128)(2,1)} %collective-permute-done.15.refs_4_.refs_12_.refs_16_), channel_id=1, source_target_pairs={{0,1},{1,0},{2,3},{3,2},{4,5},{5,4},{6,7},{7,6},{8,9},{9,8},{10,11... | collective-permute-start | bytes 3538952 | tf_op jit(solution)/shard_map/ppermute | solution.py:49
  95.8 20.5 %collective-permute-start.20 = (bf16[96,6144]{1,0:T(8,128)(2,1)}, bf16[96,6144]{1,0:T(8,128)(2,1)}, u32[]{:S(2)}, u32[]{:S(2)}) collective-permute-start(bf16[96,6144]{1,0:T(8,128)(2,1)} %collective-permute-done.19.refs_16_.refs_20_), channel_id=1, source_target_pairs={{0,1},{1,0},{2,3},{3,2},{4,5},{5,4},{6,7},{7,6},{8,9},{9,8},{10,11... | collective-permute-start | bytes 3538952 | tf_op jit(solution)/shard_map/ppermute | solution.py:49
  95.8 30.8 %copy-start.4 = (bf16[96,6144]{1,0:T(8,128)(2,1)}, bf16[96,6144]{1,0:T(8,128)(2,1)S(1)}, u32[]{:S(2)}) copy-start(bf16[96,6144]{1,0:T(8,128)(2,1)S(1)} %collective-permute-done.23.refs_20_.refs_24_) | copy-start | bytes 3538948
  95.8 20.5 %collective-permute-start.25 = (bf16[96,6144]{1,0:T(8,128)(2,1)S(1)}, bf16[96,6144]{1,0:T(8,128)(2,1)}, u32[]{:S(2)}, u32[]{:S(2)}) collective-permute-start(bf16[96,6144]{1,0:T(8,128)(2,1)S(1)} %collective-permute-done.23.refs_20_.refs_24_), channel_id=1, source_target_pairs={{0,6},{1,3},{2,0},{3,5},{4,2},{5,7},{6,4},{7,1},{8,14},{9,11},{10,... | collective-permute-start | bytes 3538952 | tf_op jit(solution)/shard_map/ppermute | solution.py:29
  109.9 16.8 %collective-permute-start.22 = (bf16[96,6144]{1,0:T(8,128)(2,1)}, bf16[96,6144]{1,0:T(8,128)(2,1)}, u32[]{:S(2)}, u32[]{:S(2)}) collective-permute-start(bf16[96,6144]{1,0:T(8,128)(2,1)} %collective-permute-done.21.refs_18_.refs_22_), channel_id=1, source_target_pairs={{0,1},{1,0},{2,3},{3,2},{4,5},{5,4},{6,7},{7,6},{8,9},{9,8},{10,11... | collective-permute-start | bytes 3538952 | tf_op jit(solution)/shard_map/ppermute | solution.py:49
  109.9 1.0 copy-start.5
  110.9 18.8 %collective-permute-start.24 = (bf16[96,6144]{1,0:T(8,128)(2,1)S(1)}, bf16[96,6144]{1,0:T(8,128)(2,1)}, u32[]{:S(2)}, u32[]{:S(2)}) collective-permute-start(bf16[96,6144]{1,0:T(8,128)(2,1)S(1)} %collective-permute-done.23.refs_20_.refs_24_), channel_id=1, source_target_pairs={{0,1},{1,0},{2,3},{3,2},{4,5},{5,4},{6,7},{7,6},{8,9},{9,8},{10,11... | collective-permute-start | bytes 3538952 | tf_op jit(solution)/shard_map/ppermute | solution.py:49
  113.3 13.4 %copy-start.15 = (f32[8,1,512]{2,1,0:T(1,128)S(1)}, f32[8,1,512]{2,1,0:T(1,128)}, u32[]{:S(2)}) copy-start(f32[8,1,512]{2,1,0:T(1,128)} %get-tuple-element.21.refs_12_.refs_8_.refs_5_) | copy-start | bytes 49156
  113.3 32.8 %collective-permute-start.11 = (bf16[128,3072]{1,0:T(8,128)(2,1)}, bf16[128,3072]{1,0:T(8,128)(2,1)}, u32[]{:S(2)}, u32[]{:S(2)}) collective-permute-start(bf16[128,3072]{1,0:T(8,128)(2,1)} %collective-permute-done.9.refs_8_), channel_id=1, source_target_pairs={{0,96},{1,33},{32,0},{33,65},{64,32},{65,97},{96,64},{97,1},{2,98}... | collective-permute-start | bytes 2359304 | tf_op jit(solution)/shard_map/ppermute | solution.py:33
  116.3 29.8 %collective-permute-start.12 = (bf16[128,3072]{1,0:T(8,128)(2,1)}, bf16[128,3072]{1,0:T(8,128)(2,1)}, u32[]{:S(2)}, u32[]{:S(2)}) collective-permute-start(bf16[128,3072]{1,0:T(8,128)(2,1)} %collective-permute-done.10.refs_9_), channel_id=1, source_target_pairs={{0,32},{1,97},{32,64},{33,1},{64,96},{65,33},{96,0},{97,65},{2,34}... | collective-permute-start | bytes 2359304 | tf_op jit(solution)/shard_map/ppermute | solution.py:33
  116.3 29.8 %collective-permute-start.26 = (bf16[96,6144]{1,0:T(8,128)(2,1)}, bf16[96,6144]{1,0:T(8,128)(2,1)}, u32[]{:S(2)}, u32[]{:S(2)}) collective-permute-start(bf16[96,6144]{1,0:T(8,128)(2,1)} %collective-permute-done.25.refs_26_), channel_id=1, source_target_pairs={{0,1},{1,0},{2,3},{3,2},{4,5},{5,4},{6,7},{7,6},{8,9},{9,8},{10,11... | collective-permute-start | bytes 3538952 | tf_op jit(solution)/shard_map/ppermute | solution.py:49
  126.7 36.9 %collective-permute-start.28 = (f32[8,1,512]{2,1,0:T(1,128)S(1)}, f32[8,1,512]{2,1,0:T(1,128)S(1)}, u32[]{:S(2)}, u32[]{:S(2)}) collective-permute-start(f32[8,1,512]{2,1,0:T(1,128)S(1)} %copy-done.15), channel_id=1, source_target_pairs={{0,24},{8,16},{16,8},{24,0},{1,25},{9,17},{17,9},{25,1},{2,26},{10... | collective-permute-start | bytes 49160 | tf_op jit(solution)/shard_map/ppermute | solution.py:41
  163.6 0.6 copy-start.17
  164.2 3.7 %copy-start.20 = (bf16[4,128,512]{2,1,0:T(8,128)(2,1)S(1)}, bf16[4,128,512]{2,1,0:T(8,128)(2,1)}, u32[]{:S(2)}) copy-start(bf16[4,128,512]{2,1,0:T(8,128)(2,1)} %get-tuple-element.20) | copy-start | bytes 1572868
  167.5 53.4 %collective-permute-start.29 = (bf16[4,128,512]{2,1,0:T(8,128)(2,1)}, bf16[4,128,512]{2,1,0:T(8,128)(2,1)S(1)}, u32[]{:S(2)}, u32[]{:S(2)}) collective-permute-start(bf16[4,128,512]{2,1,0:T(8,128)(2,1)} %intra.3), channel_id=1, source_target_pairs={{0,24},{8,16},{16,8},{24,0},{1,25},{9,17},{17,9},{25,1},{2,26},{10... | collective-permute-start | bytes 1572872 | tf_op jit(solution)/shard_map/ppermute | solution.py:41
  167.9 53.1 %collective-permute-start.27 = (bf16[4,128,512]{2,1,0:T(8,128)(2,1)S(1)}, bf16[4,128,512]{2,1,0:T(8,128)(2,1)S(1)}, u32[]{:S(2)}, u32[]{:S(2)}) collective-permute-start(bf16[4,128,512]{2,1,0:T(8,128)(2,1)S(1)} %copy-done.20), channel_id=1, source_target_pairs={{0,24},{8,16},{16,8},{24,0},{1,25},{9,17},{17,9},{25,1},{2,26},{10... | collective-permute-start | bytes 1572872 | tf_op jit(solution)/shard_map/ppermute | solution.py:41
  170.8 23.7 %all-to-all-start = ((f32[32,1,128]{2,1,0:T(1,128)}), f32[32,1,128]{2,1,0:T(1,128)S(1)}, u32[]{:S(2)}, u32[]{:S(2)}) async-start(f32[32,1,128]{2,1,0:T(1,128)} %get-tuple-element.24), calls=%async_computation | async-start | bytes 32768 | tf_op jit(solution)/shard_map/all_to_all | solution.py:45
  194.5 12.0 %copy-start.16 = (f32[32,1,128]{2,1,0:T(1,128)}, f32[32,1,128]{2,1,0:T(1,128)S(1)}, u32[]{:S(2)}) copy-start(f32[32,1,128]{2,1,0:T(1,128)S(1)} %all-to-all-done.d_ref) | copy-start | bytes 49156
  208.3 12.7 %all-to-all-start.2 = ((bf16[32,32,128]{2,1,0:T(8,128)(2,1)}), bf16[32,32,128]{2,1,0:T(8,128)(2,1)S(1)}, u32[]{:S(2)}, u32[]{:S(2)}) async-start(bf16[32,32,128]{2,1,0:T(8,128)(2,1)} %carries.1), calls=%async_computation.2 | async-start | bytes 524288 | tf_op jit(solution)/shard_map/all_to_all | solution.py:45
  221.0 0.7 copy-start.6
  221.0 0.9 copy-start.7
  221.9 0.8 copy-start.8

commit v4 on v3

--- a/solution.py
+++ b/solution.py
@@ -55,15 +55,14 @@
     return [range(g, min(g + size, len(members))) for g in range(0, len(members), size)]
 
 
-def project(scalars, here, cuts, units, jobs, held, partial):
+def project(scalars, here, cuts, units, jobs, held, partials):
     kinds = [job[0] for job in jobs]
     after = "across" in kinds
 
     def kernel(s_ref, x_ref, *refs):
         cut_refs, refs = refs[: 4 * len(cuts)], refs[4 * len(cuts) :]
         w_refs, refs = refs[: len(units)], refs[len(units) :]
-        if partial is not None:
-            partial_ref, refs = refs[0], refs[1:]
+        partial_refs, refs = list(refs[: len(partials)]), refs[len(partials) :]
         if held is not None:
             refs = refs[1:]
         u_ref, refs = refs[0], refs[1:]
@@ -73,11 +72,12 @@
             across_ref, query_ref, refs = refs[0], refs[1], refs[2:]
         sem, stage, accs = refs[0], refs[1], refs[2:]
         k = pl.program_id(0)
+        sums_of = [partial_refs.pop(0) if kind == "resume" else None for kind in kinds]
 
         def run(step):
             copies = []
             cut = max(n for n in range(len(CUTS) - 1) if CUTS[n] <= step)
-            for (kind, members, first, last), acc in zip(jobs, accs):
+            for (kind, members, first, last), acc, before in zip(jobs, accs, sums_of):
                 if not first <= step <= last:
                     continue
                 if kind == "start":
@@ -93,7 +93,7 @@
                     if step > first:
                         v += acc[rows, :]
                     elif kind == "resume":
-                        v += partial_ref[rows, :]
+                        v += before[rows, :]
                     if step < last or kind == "start":
                         acc[rows, :] = v
                         continue
@@ -144,9 +144,8 @@
         out_shape.append(jax.ShapeDtypeStruct((16 * UNIT, TOK), BF16))
         out_shape.append(jax.ShapeDtypeStruct((4, 128, TOK), BF16))
     args = [scalars, here, *[v for quarters in cuts for v in quarters], *[w for w, _ in units]]
-    if partial is not None:
-        in_specs.append(pl.BlockSpec(partial.shape, lambda k, s: (0, 0)))
-        args.append(partial)
+    in_specs += [pl.BlockSpec(v.shape, lambda k, s: (0, 0)) for v in partials]
+    args += partials
     aliases = {}
     if held is not None:
         in_specs.append(pl.BlockSpec(memory_space=pl.ANY))
@@ -388,12 +387,14 @@
     units = [(w, i) for i, w in enumerate(weights)]
     cuts = list(zip(a, xa, xb, xc))
     late = NK // 2
-    jobs = [("own", range(8), 0, NK - 1)]
-    (held,) = project(scalars, inputs, [], units[:8], jobs, None, None)
-    jobs = [("own", range(8, 14), 0, NK - 1), ("start", range(14), 0, late - 1)]
-    held, partial = project(scalars, inputs, cuts[:-1], units[:14], jobs, held, None)
-    jobs = [("across", (14, 15), 0, NK - 1), ("own", (14, 15), 0, NK - 1), ("resume", range(14), late, NK - 1)]
-    held, held_across, queries = project(scalars, inputs, cuts, units, jobs, held, partial)
+    jobs = [("own", range(8), 0, NK - 1), ("start", range(8), 0, late - 1)]
+    held, early = project(scalars, inputs, cuts[:-1], units[:8], jobs, None, [])
+    jobs = [("own", range(6), 0, NK - 1), ("start", range(6), 0, late - 1)]
+    held, middle = project(scalars, inputs, cuts[:-1], units[8:14], jobs, held, [])
+    jobs = [("across", (14, 15), 0, NK - 1), ("own", (14, 15), 0, NK - 1)]
+    jobs += [("resume", range(8), late, NK - 1), ("resume", range(8, 14), late, NK - 1)]
+    args = (scalars, inputs, cuts, units, jobs, held, [early, middle])
+    held, held_across, queries = project(*args)
 
     over_queries = z_out(queries)
     own_states = states(mine, [(held, sums), (held_across, sums_across)])

time: 229 us -> 217 us (0.948)
  waiting for transfers between devices: 102 us -> 92.8 us
  starting transfers between devices: 42.5 us -> 40.2 us
    ppermute x6, waiting for transfers between devices: 34.3 us -> 14.4 us  [z_out(): return lax.ppermute(v, ('zh', 'zl'), [(i, 3 - i) for i in range(4)])]
    ppermute x5, waiting for transfers between devices: 10.6 us -> 29.2 us  [y_move(): return lax.ppermute(v, ('y', 'c'), ring_pairs(step))]
    ppermute x2, waiting for transfers between devices: 13.9 us -> 0.01 us  [z_in(): return lax.ppermute(v, 'zl', [(0, 1), (1, 0)])]
    ppermute x9, waiting for transfers between devices: 21.1 us -> 27.9 us  [x_move(): return lax.ppermute(v, ('x', 'c'), ring_pairs(step))]
    ppermute x9, starting transfers between devices: 11.6 us -> 7.53 us  [x_move(): return lax.ppermute(v, ('x', 'c'), ring_pairs(step))]
    unnamed x42 -> x40, local copies, waits for them, and re-layouts: 4.81 us -> 4.25 us
  transfers between devices with their start and end apart: 32 -> 32, of which waited for: 10 -> 12; matrix products, arithmetic and copies ran while one was open for 1% -> 1% of each run, Pallas kernels for 24% -> 25%
where the time goes in v4:
time: 217 us; the launch traced here: 215 us
  waiting for transfers between devices  92.8 us (43%)
  Pallas kernels  62.1 us (29%)
  starting transfers between devices  40.2 us (19%)
  blocking collectives  12 us (6%)
  local copies, waits for them, and re-layouts  7.39 us (3%)
    pallas_call x3, Pallas kernels, project(): pl.pallas_call(kernel, grid_spec=pltpu.PrefetchScalarGridSpec(num_scalar_...  44.6 us
    ppermute x5, waiting for transfers between devices, y_move(): return lax.ppermute(v, ('y', 'c'), ring_pairs(step))  29.2 us
    ppermute x9, waiting for transfers between devices, x_move(): return lax.ppermute(v, ('x', 'c'), ring_pairs(step))  27.9 us
    all_to_all x2, waiting for transfers between devices, exchange(): return lax.all_to_all(v, axes, 0, 0, tiled=True)  21.3 us
    ppermute x6, waiting for transfers between devices, z_out(): return lax.ppermute(v, ('zh', 'zl'), [(i, 3 - i) for i in range(4)])  14.4 us
    ppermute x6, starting transfers between devices, z_out(): return lax.ppermute(v, ('zh', 'zl'), [(i, 3 - i) for i in range(4)])  13.4 us
    all_to_all x1, blocking collectives, exchange(): return lax.all_to_all(v, axes, 0, 0, tiled=True)  12 us
    ppermute x5, starting transfers between devices, y_move(): return lax.ppermute(v, ('y', 'c'), ring_pairs(step))  9.48 us
  transfers between devices with their start and end apart: 32, of which 12 were waited for; matrix products, arithmetic and copies ran while one was open for 1% of the time, Pallas kernels for 25%

profile of v4, /device:TPU:0, one launch (start us, length us, event | category | flops | bytes accessed | tf_op | source)
XLA Modules:
  0.0 215.4 jit_solution(3063119814407819041)
XLA Ops:
  0.0 1.3 constant_dynamic-slice_fusion.1
  1.3 0.0 copy-start.17
  1.3 0.0 copy-start.18
  1.3 4.2 %collective-permute-start.1 = (bf16[128,1536]{1,0:T(8,128)(2,1)S(1)}, bf16[128,1536]{1,0:T(8,128)(2,1)S(1)}, u32[]{:S(2)}, u32[]{:S(2)}) collective-permute-start(bf16[128,1536]{1,0:T(8,128)(2,1)S(1)} %get-tuple-element.30), channel_id=1, source_target_pairs={{0,24},{8,16},{16,8},{24,0},{1,25},{9,17},{17,9},{25,1},{2,26},{10... | collective-permute-start | bytes 1179656 | tf_op jit(solution)/shard_map/ppermute | solution.py:41
  5.5 0.1 collective-permute-start.5
  5.6 1.6 collective-permute-start
  7.2 8.3 %collective-permute-done.1.refs_0_ = bf16[128,1536]{1,0:T(8,128)(2,1)S(1)} collective-permute-done((bf16[128,1536]{1,0:T(8,128)(2,1)S(1)}, bf16[128,1536]{1,0:T(8,128)(2,1)S(1)}, u32[]{:S(2)}, u32[]{:S(2)}) %collective-permute-start.1) | collective-permute-done | bytes 393248 | tf_op jit(solution)/shard_map/ppermute | solution.py:41
  15.5 1.5 collective-permute-start.2
  17.0 1.7 collective-permute-start.3
  18.7 4.3 %collective-permute-done.5.refs_4_ = bf16[128,1536]{1,0:T(8,128)(2,1)S(1)} collective-permute-done((bf16[128,1536]{1,0:T(8,128)(2,1)S(1)}, bf16[128,1536]{1,0:T(8,128)(2,1)S(1)}, u32[]{:S(2)}, u32[]{:S(2)}) %collective-permute-start.5) | collective-permute-done | bytes 393248 | tf_op jit(solution)/shard_map/ppermute | solution.py:41
  23.1 1.5 collective-permute-start.6
  24.6 1.2 constant_dynamic-slice_fusion
  25.7 3.0 %collective-permute-start.9 = (bf16[128,3072]{1,0:T(8,128)(2,1)S(1)}, bf16[128,3072]{1,0:T(8,128)(2,1)S(1)}, u32[]{:S(2)}, u32[]{:S(2)}) collective-permute-start(bf16[128,3072]{1,0:T(8,128)(2,1)S(1)} %constant_dynamic-slice_fusion), channel_id=1, source_target_pairs={{0,24},{8,16},{16,8},{24,0},{1,25},{9,17},{17,9},{25,1},{2,26},{10... | collective-permute-start | bytes 2359304 | tf_op jit(solution)/shard_map/ppermute | solution.py:41
  28.8 0.0 collective-permute-start.17
  28.8 4.1 %collective-permute-done.6.refs_5_ = bf16[128,1536]{1,0:T(8,128)(2,1)} collective-permute-done((bf16[128,1536]{1,0:T(8,128)(2,1)S(1)}, bf16[128,1536]{1,0:T(8,128)(2,1)}, u32[]{:S(2)}, u32[]{:S(2)}) %collective-permute-start.6) | collective-permute-done | bytes 393248 | tf_op jit(solution)/shard_map/ppermute | solution.py:33
  32.9 3.0 %collective-permute-start.15 = (bf16[96,6144]{1,0:T(8,128)(2,1)S(1)}, bf16[96,6144]{1,0:T(8,128)(2,1)}, u32[]{:S(2)}, u32[]{:S(2)}) collective-permute-start(bf16[96,6144]{1,0:T(8,128)(2,1)S(1)} %bitcast.26), channel_id=1, source_target_pairs={{0,6},{1,3},{2,0},{3,5},{4,2},{5,7},{6,4},{7,1},{8,14},{9,11},{10,... | collective-permute-start | bytes 3538952 | tf_op jit(solution)/shard_map/ppermute | solution.py:29
  35.9 0.0 collective-permute-done.3.refs_2_
  35.9 0.8 collective-permute-start.7
  36.7 8.2 %collective-permute-done.7.refs_6_ = bf16[128,1536]{1,0:T(8,128)(2,1)S(1)} collective-permute-done((bf16[128,1536]{1,0:T(8,128)(2,1)S(1)}, bf16[128,1536]{1,0:T(8,128)(2,1)S(1)}, u32[]{:S(2)}, u32[]{:S(2)}) %collective-permute-start.7) | collective-permute-done | bytes 393248 | tf_op jit(solution)/shard_map/ppermute | solution.py:33
  44.9 1.8 collective-permute-done.9.refs_8_
  46.7 0.0 collective-permute-start.13
  46.7 0.0 collective-permute-done.refs_10_.refs_14_
  46.8 0.8 copy-done.7
  47.6 0.0 collective-permute-start.8
  47.6 6.6 %collective-permute-done.4.refs_3_ = bf16[128,1536]{1,0:T(8,128)(2,1)} collective-permute-done((bf16[128,1536]{1,0:T(8,128)(2,1)}, bf16[128,1536]{1,0:T(8,128)(2,1)}, u32[]{:S(2)}, u32[]{:S(2)}) %collective-permute-start.4) | collective-permute-done | bytes 393248 | tf_op jit(solution)/shard_map/ppermute | solution.py:33
  54.2 0.0 collective-permute-start.10
  54.3 0.6 broadcast_select_fusion.n_ref
  54.9 0.7 stack.83.s_ref
  55.5 2.9 %collective-permute-done.8.refs_7_ = bf16[128,1536]{1,0:T(8,128)(2,1)} collective-permute-done((bf16[128,1536]{1,0:T(8,128)(2,1)}, bf16[128,1536]{1,0:T(8,128)(2,1)}, u32[]{:S(2)}, u32[]{:S(2)}) %collective-permute-start.8) | collective-permute-done | bytes 393248 | tf_op jit(solution)/shard_map/ppermute | solution.py:33
  58.5 0.0 collective-permute-start.14
  58.5 0.1 collective-permute-start.19
  58.6 0.0 collective-permute-done.15.refs_12_.refs_16_
  58.6 3.2 %collective-permute-start.23 = (bf16[96,6144]{1,0:T(8,128)(2,1)S(1)}, bf16[96,6144]{1,0:T(8,128)(2,1)}, u32[]{:S(2)}, u32[]{:S(2)}) collective-permute-start(bf16[96,6144]{1,0:T(8,128)(2,1)S(1)} %collective-permute-done.17.refs_14_.refs_18_), channel_id=1, source_target_pairs={{0,6},{1,3},{2,0},{3,5},{4,2},{5,7},{6,4},{7,1},{8,14},{9,11},{10,... | collective-permute-start | bytes 3538952 | tf_op jit(solution)/shard_map/ppermute | solution.py:29
  61.8 6.0 %collective-permute-done.10.refs_9_ = bf16[128,3072]{1,0:T(8,128)(2,1)} collective-permute-done((bf16[128,3072]{1,0:T(8,128)(2,1)}, bf16[128,3072]{1,0:T(8,128)(2,1)}, u32[]{:S(2)}, u32[]{:S(2)}) %collective-permute-start.10) | collective-permute-done | bytes 786464 | tf_op jit(solution)/shard_map/ppermute | solution.py:33
  67.8 0.0 collective-permute-start.18
  67.8 0.5 collective-permute-start.16
  68.3 19.8 %collective-permute-done.19.refs_8_.refs_20_ = bf16[96,6144]{1,0:T(8,128)(2,1)} collective-permute-done((bf16[96,6144]{1,0:T(8,128)(2,1)S(1)}, bf16[96,6144]{1,0:T(8,128)(2,1)}, u32[]{:S(2)}, u32[]{:S(2)}) %collective-permute-start.19) | collective-permute-done | bytes 1179680 | tf_op jit(solution)/shard_map/ppermute | solution.py:29
  88.0 1.6 collective-permute-start.25
  89.7 1.1 copy-done.5
  90.8 0.5 collective-permute-start.24
  91.2 1.9 rates.1
  93.1 2.0 collective-permute-start.12
  95.2 9.4 %collective-permute-done.25.refs_26_ = bf16[96,6144]{1,0:T(8,128)(2,1)} collective-permute-done((bf16[96,6144]{1,0:T(8,128)(2,1)}, bf16[96,6144]{1,0:T(8,128)(2,1)}, u32[]{:S(2)}, u32[]{:S(2)}) %collective-permute-start.25) | collective-permute-done | bytes 1179680 | tf_op jit(solution)/shard_map/ppermute | solution.py:29
  104.6 0.9 collective-permute-start.26
  105.4 14.6 %project.3 = (bf16[1536,512]{1,0:T(8,128)(2,1)}, f32[768,512]{1,0:T(8,128)}) custom-call(s32[20]{0:T(128)} %stack.83.s_ref, bf16[512,6144]{1,0:T(8,128)(2,1)} %x_ref.5, bf16[128,1536]{1,0:T(8,128)(2,1)} %copy-done.10, bf16[128,1536]{1,0:T(8,128)(2,1)} %collective-permute-done.2.refs_1_, bf16[128,1536]{1,0:T(8,128)(2,1)} %copy-done.12, ...), custom_call_target="tpu_custom_call" | custom-call | flops 7247757312 | bytes 9437184 | tf_op jit(solution)/shard_map/project/pallas_call | solution.py:155
  120.1 2.8 %collective-permute-start.28 = (f32[8,1,512]{2,1,0:T(1,128)S(1)}, f32[8,1,512]{2,1,0:T(1,128)S(1)}, u32[]{:S(2)}, u32[]{:S(2)}) collective-permute-start(f32[8,1,512]{2,1,0:T(1,128)S(1)} %copy-done.14), channel_id=1, source_target_pairs={{0,24},{8,16},{16,8},{24,0},{1,25},{9,17},{17,9},{25,1},{2,26},{10... | collective-permute-start | bytes 49160 | tf_op jit(solution)/shard_map/ppermute | solution.py:41
  122.9 12.5 %project.4 = (bf16[1536,512]{1,0:T(8,128)(2,1)}, f32[576,512]{1,0:T(8,128)}) custom-call(s32[20]{0:T(128)} %stack.83.s_ref, bf16[512,6144]{1,0:T(8,128)(2,1)} %x_ref.5, bf16[128,1536]{1,0:T(8,128)(2,1)} %copy-done.10, bf16[128,1536]{1,0:T(8,128)(2,1)} %collective-permute-done.2.refs_1_, ...), custom_call_target="tpu_custom_call", output_to_operand_aliasing={{0}: (16, {})} | custom-call | flops 5435817984 | bytes 7077888 | tf_op jit(solution)/shard_map/project/pallas_call | solution.py:155
  135.4 17.4 %project.5 = (bf16[1536,512]{1,0:T(8,128)(2,1)}, bf16[1536,512]{1,0:T(8,128)(2,1)}, bf16[4,128,512]{2,1,0:T(8,128)(2,1)}) custom-call(s32[20]{0:T(128)} %stack.83.s_ref, bf16[512,6144]{1,0:T(8,128)(2,1)} %x_ref.5, bf16[128,1536]{1,0:T(8,128)(2,1)} %copy-done.10, bf16[128,1536]{1,0:T(8,128)(2,1)} %collective-permute-done.2.refs_1_, ...), custom_call_target="tpu_custom_call", output_to_operand_aliasing={{0}: (32, {})} | custom-call | flops 6643777536 | bytes 18874368 | tf_op jit(solution)/shard_map/project/pallas_call | solution.py:155
  152.9 0.6 copy-done.16
  153.5 3.3 %intra.3 = bf16[4,128,512]{2,1,0:T(8,128)(2,1)} custom-call(s32[1]{0:T(128)} %bitcast.z_ref, bf16[1536,512]{1,0:T(8,128)(2,1)} %get-tuple-element.26.refs_0_.refs_1_.refs_2_.refs_3_.refs_4_.refs_5_.refs_6_.refs_7_.refs_8_.refs_9_.refs_10_.refs_11_.refs_12_.refs_13_.refs_14_.refs_15_.refs_16_, ...), custom_call_target="tpu_custom_call" | custom-call | tf_op jit(solution)/shard_map/intra/pallas_call | solution.py:264
  156.8 0.5 collective-permute-start.29
  157.3 2.7 %collective-permute-start.27 = (bf16[4,128,512]{2,1,0:T(8,128)(2,1)S(1)}, bf16[4,128,512]{2,1,0:T(8,128)(2,1)S(1)}, u32[]{:S(2)}, u32[]{:S(2)}) collective-permute-start(bf16[4,128,512]{2,1,0:T(8,128)(2,1)S(1)} %copy-done.19), channel_id=1, source_target_pairs={{0,24},{8,16},{16,8},{24,0},{1,25},{9,17},{17,9},{25,1},{2,26},{10... | collective-permute-start | bytes 1572872 | tf_op jit(solution)/shard_map/ppermute | solution.py:41
  160.1 4.1 %all-to-all-start = ((f32[32,1,128]{2,1,0:T(1,128)}), f32[32,1,128]{2,1,0:T(1,128)S(1)}, u32[]{:S(2)}, u32[]{:S(2)}) async-start(f32[32,1,128]{2,1,0:T(1,128)} %get-tuple-element.28), calls=%async_computation | async-start | bytes 32768 | tf_op jit(solution)/shard_map/all_to_all | solution.py:45
  164.1 3.1 %states.1 = bf16[16,2,32,128]{3,2,1,0:T(8,128)(2,1)} custom-call(s32[1]{0:T(128)} %bitcast.z_ref, bf16[1536,512]{1,0:T(8,128)(2,1)} %get-tuple-element.23.refs_0_.refs_1_.refs_2_.refs_3_.refs_4_.refs_5_.refs_6_.refs_7_.refs_8_.refs_9_.refs_10_.refs_11_, ...), custom_call_target="tpu_custom_call" | custom-call | tf_op jit(solution)/shard_map/states/pallas_call | solution.py:231
  167.2 16.1 %all-to-all-done.d_ref = f32[32,1,128]{2,1,0:T(1,128)S(1)} async-done(((f32[32,1,128]{2,1,0:T(1,128)}), f32[32,1,128]{2,1,0:T(1,128)S(1)}, u32[]{:S(2)}, u32[]{:S(2)}) %all-to-all-start) | async-done | bytes 16416 | tf_op jit(solution)/shard_map/all_to_all | solution.py:45
  183.3 12.0 %all_to_all.15.s_ref = bf16[16,2,32,128]{3,2,1,0:T(8,128)(2,1)} all-to-all(bf16[16,2,32,128]{3,2,1,0:T(8,128)(2,1)} %states.1), channel_id=1, replica_groups=mesh['x'=4,'zh'=2,'zl'=2,'y'=4,'c'=2] {'zl','y','c'}, dimensions={0} | all-to-all | bytes 524288 | tf_op jit(solution)/shard_map/all_to_all | solution.py:45
  195.3 1.8 carries.1
  197.1 3.9 %all-to-all-start.2 = ((bf16[32,32,128]{2,1,0:T(8,128)(2,1)}), bf16[32,32,128]{2,1,0:T(8,128)(2,1)S(1)}, u32[]{:S(2)}, u32[]{:S(2)}) async-start(bf16[32,32,128]{2,1,0:T(8,128)(2,1)} %carries.1), calls=%async_computation.2 | async-start | bytes 524288 | tf_op jit(solution)/shard_map/all_to_all | solution.py:45
  201.0 3.5 %intra.2.refs_6_ = f32[4,128,512]{2,1,0:T(8,128)} custom-call(s32[1]{0:T(128)} %bitcast.z_ref, bf16[1536,512]{1,0:T(8,128)(2,1)} %get-tuple-element.23.refs_0_.refs_1_.refs_2_.refs_3_.refs_4_.refs_5_.refs_6_.refs_7_.refs_8_.refs_9_.refs_10_.refs_11_, ...), custom_call_target="tpu_custom_call" | custom-call | tf_op jit(solution)/shard_map/intra/pallas_call | solution.py:264
  204.5 5.3 %all-to-all-done.2.refs_8_ = bf16[32,32,128]{2,1,0:T(8,128)(2,1)S(1)} async-done(((bf16[32,32,128]{2,1,0:T(8,128)(2,1)}), bf16[32,32,128]{2,1,0:T(8,128)(2,1)S(1)}, u32[]{:S(2)}, u32[]{:S(2)}) %all-to-all-start.2) | async-done | bytes 262176 | tf_op jit(solution)/shard_map/all_to_all | solution.py:45
  209.8 0.7 copy-done.6
  210.5 0.2 copy-done.8
  210.7 0.8 copy-done.9
  211.5 3.9 %finish.1 = bf16[512,1024]{1,0:T(8,128)(2,1)} custom-call(s32[1]{0:T(128)} %bitcast.z_ref, bf16[1536,512]{1,0:T(8,128)(2,1)} %get-tuple-element.23.refs_0_.refs_1_.refs_2_.refs_3_.refs_4_.refs_5_.refs_6_.refs_7_.refs_8_.refs_9_.refs_10_.refs_11_, ...), custom_call_target="tpu_custom_call" | custom-call | tf_op jit(solution)/shard_map/finish/pallas_call | solution.py:308
  (54 shorter events, 0.1 us)
Async XLA Ops:
  0.0 5.6 %copy-start = (bf16[6144,96]{0,1:T(8,128)(2,1)S(1)}, bf16[6144,96]{0,1:T(8,128)(2,1)}, u32[]{:S(2)}) copy-start(bf16[6144,96]{0,1:T(8,128)(2,1)} %param.7) | copy-start | bytes 3538948
  1.3 53.0 %copy-start.17 = (s32[8]{0:T(128)S(1)}, s32[8]{0:T(128)}, u32[]{:S(2)}) copy-start(s32[8]{0:T(128)} %constant.101.clone) | copy-start | bytes 100
  1.3 53.0 %copy-start.18 = (s32[8]{0:T(128)S(1)}, s32[8]{0:T(128)}, u32[]{:S(2)}) copy-start(s32[8]{0:T(128)} %constant.102.clone) | copy-start | bytes 100
  1.3 14.2 %collective-permute-start.1 = (bf16[128,1536]{1,0:T(8,128)(2,1)S(1)}, bf16[128,1536]{1,0:T(8,128)(2,1)S(1)}, u32[]{:S(2)}, u32[]{:S(2)}) collective-permute-start(bf16[128,1536]{1,0:T(8,128)(2,1)S(1)} %get-tuple-element.30), channel_id=1, source_target_pairs={{0,24},{8,16},{16,8},{24,0},{1,25},{9,17},{17,9},{25,1},{2,26},{10... | collective-permute-start | bytes 1179656 | tf_op jit(solution)/shard_map/ppermute | solution.py:41
  5.5 17.5 %collective-permute-start.5 = (bf16[128,1536]{1,0:T(8,128)(2,1)S(1)}, bf16[128,1536]{1,0:T(8,128)(2,1)S(1)}, u32[]{:S(2)}, u32[]{:S(2)}) collective-permute-start(bf16[128,1536]{1,0:T(8,128)(2,1)S(1)} %get-tuple-element.29), channel_id=1, source_target_pairs={{0,24},{8,16},{16,8},{24,0},{1,25},{9,17},{17,9},{25,1},{2,26},{10... | collective-permute-start | bytes 1179656 | tf_op jit(solution)/shard_map/ppermute | solution.py:41
  5.6 41.1 %collective-permute-start = (bf16[96,6144]{1,0:T(8,128)(2,1)S(1)}, bf16[96,6144]{1,0:T(8,128)(2,1)S(1)}, u32[]{:S(2)}, u32[]{:S(2)}) collective-permute-start(bf16[96,6144]{1,0:T(8,128)(2,1)S(1)} %bitcast.24), channel_id=1, source_target_pairs={{0,2},{1,7},{2,4},{3,1},{4,6},{5,3},{6,0},{7,5},{8,10},{9,15},{10,... | collective-permute-start | bytes 3538952 | tf_op jit(solution)/shard_map/ppermute | solution.py:29
  15.5 31.3 %copy-start.10 = (bf16[128,1536]{1,0:T(8,128)(2,1)}, bf16[128,1536]{1,0:T(8,128)(2,1)S(1)}, u32[]{:S(2)}) copy-start(bf16[128,1536]{1,0:T(8,128)(2,1)S(1)} %collective-permute-done.1.refs_0_) | copy-start | bytes 1179652
  15.5 13.3 %collective-permute-start.2 = (bf16[128,1536]{1,0:T(8,128)(2,1)S(1)}, bf16[128,1536]{1,0:T(8,128)(2,1)}, u32[]{:S(2)}, u32[]{:S(2)}) collective-permute-start(bf16[128,1536]{1,0:T(8,128)(2,1)S(1)} %collective-permute-done.1.refs_0_), channel_id=1, source_target_pairs={{0,32},{1,97},{32,64},{33,1},{64,96},{65,33},{96,0},{97,65},{2,34}... | collective-permute-start | bytes 1179656 | tf_op jit(solution)/shard_map/ppermute | solution.py:33
  17.0 19.0 %collective-permute-start.3 = (bf16[128,1536]{1,0:T(8,128)(2,1)S(1)}, bf16[128,1536]{1,0:T(8,128)(2,1)S(1)}, u32[]{:S(2)}, u32[]{:S(2)}) collective-permute-start(bf16[128,1536]{1,0:T(8,128)(2,1)S(1)} %collective-permute-done.1.refs_0_), channel_id=1, source_target_pairs={{0,96},{1,33},{32,0},{33,65},{64,32},{65,97},{96,64},{97,1},{2,98}... | collective-permute-start | bytes 1179656 | tf_op jit(solution)/shard_map/ppermute | solution.py:33
  23.1 23.7 %copy-start.11 = (bf16[128,1536]{1,0:T(8,128)(2,1)}, bf16[128,1536]{1,0:T(8,128)(2,1)S(1)}, u32[]{:S(2)}) copy-start(bf16[128,1536]{1,0:T(8,128)(2,1)S(1)} %collective-permute-done.5.refs_4_) | copy-start | bytes 1179652
  23.1 9.9 %collective-permute-start.6 = (bf16[128,1536]{1,0:T(8,128)(2,1)S(1)}, bf16[128,1536]{1,0:T(8,128)(2,1)}, u32[]{:S(2)}, u32[]{:S(2)}) collective-permute-start(bf16[128,1536]{1,0:T(8,128)(2,1)S(1)} %collective-permute-done.5.refs_4_), channel_id=1, source_target_pairs={{0,32},{1,97},{32,64},{33,1},{64,96},{65,33},{96,0},{97,65},{2,34}... | collective-permute-start | bytes 1179656 | tf_op jit(solution)/shard_map/ppermute | solution.py:33
  25.7 21.0 %collective-permute-start.9 = (bf16[128,3072]{1,0:T(8,128)(2,1)S(1)}, bf16[128,3072]{1,0:T(8,128)(2,1)S(1)}, u32[]{:S(2)}, u32[]{:S(2)}) collective-permute-start(bf16[128,3072]{1,0:T(8,128)(2,1)S(1)} %constant_dynamic-slice_fusion), channel_id=1, source_target_pairs={{0,24},{8,16},{16,8},{24,0},{1,25},{9,17},{17,9},{25,1},{2,26},{10... | collective-permute-start | bytes 2359304 | tf_op jit(solution)/shard_map/ppermute | solution.py:41
  28.8 29.7 %collective-permute-start.17 = (bf16[96,6144]{1,0:T(8,128)(2,1)S(1)}, bf16[96,6144]{1,0:T(8,128)(2,1)S(1)}, u32[]{:S(2)}, u32[]{:S(2)}) collective-permute-start(bf16[96,6144]{1,0:T(8,128)(2,1)S(1)} %bitcast.25), channel_id=1, source_target_pairs={{0,8},{8,0},{1,9},{9,1},{2,10},{10,2},{3,11},{11,3},{4,12},{12,4},... | collective-permute-start | bytes 3538952 | tf_op jit(solution)/shard_map/ppermute | solution.py:37
  32.9 25.6 %collective-permute-start.15 = (bf16[96,6144]{1,0:T(8,128)(2,1)S(1)}, bf16[96,6144]{1,0:T(8,128)(2,1)}, u32[]{:S(2)}, u32[]{:S(2)}) collective-permute-start(bf16[96,6144]{1,0:T(8,128)(2,1)S(1)} %bitcast.26), channel_id=1, source_target_pairs={{0,6},{1,3},{2,0},{3,5},{4,2},{5,7},{6,4},{7,1},{8,14},{9,11},{10,... | collective-permute-start | bytes 3538952 | tf_op jit(solution)/shard_map/ppermute | solution.py:29
  35.9 10.8 %copy-start.12 = (bf16[128,1536]{1,0:T(8,128)(2,1)}, bf16[128,1536]{1,0:T(8,128)(2,1)S(1)}, u32[]{:S(2)}) copy-start(bf16[128,1536]{1,0:T(8,128)(2,1)S(1)} %collective-permute-done.3.refs_2_) | copy-start | bytes 1179652
  35.9 9.0 %collective-permute-start.7 = (bf16[128,1536]{1,0:T(8,128)(2,1)S(1)}, bf16[128,1536]{1,0:T(8,128)(2,1)S(1)}, u32[]{:S(2)}, u32[]{:S(2)}) collective-permute-start(bf16[128,1536]{1,0:T(8,128)(2,1)S(1)} %collective-permute-done.5.refs_4_), channel_id=1, source_target_pairs={{0,96},{1,33},{32,0},{33,65},{64,32},{65,97},{96,64},{97,1},{2,98}... | collective-permute-start | bytes 1179656 | tf_op jit(solution)/shard_map/ppermute | solution.py:33
  44.9 1.8 copy-start.13
  44.9 9.3 %collective-permute-start.4 = (bf16[128,1536]{1,0:T(8,128)(2,1)}, bf16[128,1536]{1,0:T(8,128)(2,1)}, u32[]{:S(2)}, u32[]{:S(2)}) collective-permute-start(bf16[128,1536]{1,0:T(8,128)(2,1)} %collective-permute-done.2.refs_1_), channel_id=1, source_target_pairs={{0,32},{1,97},{32,64},{33,1},{64,96},{65,33},{96,0},{97,65},{2,34}... | collective-permute-start | bytes 1179656 | tf_op jit(solution)/shard_map/ppermute | solution.py:33
  46.7 0.9 copy-start.7
  46.7 15.1 %collective-permute-start.13 = (bf16[96,6144]{1,0:T(8,128)(2,1)S(1)}, bf16[96,6144]{1,0:T(8,128)(2,1)}, u32[]{:S(2)}, u32[]{:S(2)}) collective-permute-start(bf16[96,6144]{1,0:T(8,128)(2,1)S(1)} %bitcast.27), channel_id=1, source_target_pairs={{0,1},{1,0},{2,3},{3,2},{4,5},{5,4},{6,7},{7,6},{8,9},{9,8},{10,11... | collective-permute-start | bytes 3538952 | tf_op jit(solution)/shard_map/ppermute | solution.py:49
  47.6 57.8 %copy-start.1 = (bf16[96,6144]{1,0:T(8,128)(2,1)}, bf16[96,6144]{1,0:T(8,128)(2,1)S(1)}, u32[]{:S(2)}) copy-start(bf16[96,6144]{1,0:T(8,128)(2,1)S(1)} %collective-permute-done.refs_10_.refs_14_) | copy-start | bytes 3538948
  47.6 10.9 %collective-permute-start.8 = (bf16[128,1536]{1,0:T(8,128)(2,1)}, bf16[128,1536]{1,0:T(8,128)(2,1)}, u32[]{:S(2)}, u32[]{:S(2)}) collective-permute-start(bf16[128,1536]{1,0:T(8,128)(2,1)} %collective-permute-done.6.refs_5_), channel_id=1, source_target_pairs={{0,32},{1,97},{32,64},{33,1},{64,96},{65,33},{96,0},{97,65},{2,34}... | collective-permute-start | bytes 1179656 | tf_op jit(solution)/shard_map/ppermute | solution.py:33
  54.2 13.5 %collective-permute-start.10 = (bf16[128,3072]{1,0:T(8,128)(2,1)}, bf16[128,3072]{1,0:T(8,128)(2,1)}, u32[]{:S(2)}, u32[]{:S(2)}) collective-permute-start(bf16[128,3072]{1,0:T(8,128)(2,1)} %copy-done.7), channel_id=1, source_target_pairs={{0,32},{1,97},{32,64},{33,1},{64,96},{65,33},{96,0},{97,65},{2,34}... | collective-permute-start | bytes 2359304 | tf_op jit(solution)/shard_map/ppermute | solution.py:33
  58.5 9.3 %collective-permute-start.14 = (bf16[96,6144]{1,0:T(8,128)(2,1)S(1)}, bf16[96,6144]{1,0:T(8,128)(2,1)S(1)}, u32[]{:S(2)}, u32[]{:S(2)}) collective-permute-start(bf16[96,6144]{1,0:T(8,128)(2,1)S(1)} %collective-permute-done.refs_10_.refs_14_), channel_id=1, source_target_pairs={{0,1},{1,0},{2,3},{3,2},{4,5},{5,4},{6,7},{7,6},{8,9},{9,8},{10,11... | collective-permute-start | bytes 3538952 | tf_op jit(solution)/shard_map/ppermute | solution.py:49
  58.5 47.0 %copy-start.2 = (bf16[96,6144]{1,0:T(8,128)(2,1)}, bf16[96,6144]{1,0:T(8,128)(2,1)S(1)}, u32[]{:S(2)}) copy-start(bf16[96,6144]{1,0:T(8,128)(2,1)S(1)} %collective-permute-done.17.refs_14_.refs_18_) | copy-start | bytes 3538948
  58.5 29.6 %collective-permute-start.19 = (bf16[96,6144]{1,0:T(8,128)(2,1)S(1)}, bf16[96,6144]{1,0:T(8,128)(2,1)}, u32[]{:S(2)}, u32[]{:S(2)}) collective-permute-start(bf16[96,6144]{1,0:T(8,128)(2,1)S(1)} %collective-permute-done.refs_10_.refs_14_), channel_id=1, source_target_pairs={{0,2},{1,7},{2,4},{3,1},{4,6},{5,3},{6,0},{7,5},{8,10},{9,15},{10,... | collective-permute-start | bytes 3538952 | tf_op jit(solution)/shard_map/ppermute | solution.py:29
  58.6 29.5 %collective-permute-start.23 = (bf16[96,6144]{1,0:T(8,128)(2,1)S(1)}, bf16[96,6144]{1,0:T(8,128)(2,1)}, u32[]{:S(2)}, u32[]{:S(2)}) collective-permute-start(bf16[96,6144]{1,0:T(8,128)(2,1)S(1)} %collective-permute-done.17.refs_14_.refs_18_), channel_id=1, source_target_pairs={{0,6},{1,3},{2,0},{3,5},{4,2},{5,7},{6,4},{7,1},{8,14},{9,11},{10,... | collective-permute-start | bytes 3538952 | tf_op jit(solution)/shard_map/ppermute | solution.py:29
  61.8 27.9 %collective-permute-start.21 = (bf16[96,6144]{1,0:T(8,128)(2,1)S(1)}, bf16[96,6144]{1,0:T(8,128)(2,1)S(1)}, u32[]{:S(2)}, u32[]{:S(2)}) collective-permute-start(bf16[96,6144]{1,0:T(8,128)(2,1)S(1)} %collective-permute-done.refs_10_.refs_14_), channel_id=1, source_target_pairs={{0,8},{8,0},{1,9},{9,1},{2,10},{10,2},{3,11},{11,3},{4,12},{12,4},... | collective-permute-start | bytes 3538952 | tf_op jit(solution)/shard_map/ppermute | solution.py:37
  67.8 21.9 %collective-permute-start.18 = (bf16[96,6144]{1,0:T(8,128)(2,1)S(1)}, bf16[96,6144]{1,0:T(8,128)(2,1)S(1)}, u32[]{:S(2)}, u32[]{:S(2)}) collective-permute-start(bf16[96,6144]{1,0:T(8,128)(2,1)S(1)} %collective-permute-done.17.refs_14_.refs_18_), channel_id=1, source_target_pairs={{0,1},{1,0},{2,3},{3,2},{4,5},{5,4},{6,7},{7,6},{8,9},{9,8},{10,11... | collective-permute-start | bytes 3538952 | tf_op jit(solution)/shard_map/ppermute | solution.py:49
  67.8 21.9 %copy-start.3 = (bf16[96,6144]{1,0:T(8,128)(2,1)}, bf16[96,6144]{1,0:T(8,128)(2,1)S(1)}, u32[]{:S(2)}) copy-start(bf16[96,6144]{1,0:T(8,128)(2,1)S(1)} %collective-permute-done.14.refs_11_.refs_15_) | copy-start | bytes 3538948
  67.8 25.3 %collective-permute-start.16 = (bf16[96,6144]{1,0:T(8,128)(2,1)}, bf16[96,6144]{1,0:T(8,128)(2,1)}, u32[]{:S(2)}, u32[]{:S(2)}) collective-permute-start(bf16[96,6144]{1,0:T(8,128)(2,1)} %collective-permute-done.15.refs_12_.refs_16_), channel_id=1, source_target_pairs={{0,1},{1,0},{2,3},{3,2},{4,5},{5,4},{6,7},{7,6},{8,9},{9,8},{10,11... | collective-permute-start | bytes 3538952 | tf_op jit(solution)/shard_map/ppermute | solution.py:49
  88.0 5.1 %collective-permute-start.20 = (bf16[96,6144]{1,0:T(8,128)(2,1)}, bf16[96,6144]{1,0:T(8,128)(2,1)}, u32[]{:S(2)}, u32[]{:S(2)}) collective-permute-start(bf16[96,6144]{1,0:T(8,128)(2,1)} %collective-permute-done.19.refs_8_.refs_20_), channel_id=1, source_target_pairs={{0,1},{1,0},{2,3},{3,2},{4,5},{5,4},{6,7},{7,6},{8,9},{9,8},{10,11... | collective-permute-start | bytes 3538952 | tf_op jit(solution)/shard_map/ppermute | solution.py:49
  88.0 16.5 %collective-permute-start.25 = (bf16[96,6144]{1,0:T(8,128)(2,1)}, bf16[96,6144]{1,0:T(8,128)(2,1)}, u32[]{:S(2)}, u32[]{:S(2)}) collective-permute-start(bf16[96,6144]{1,0:T(8,128)(2,1)} %collective-permute-done.23.refs_12_.refs_24_), channel_id=1, source_target_pairs={{0,6},{1,3},{2,0},{3,5},{4,2},{5,7},{6,4},{7,1},{8,14},{9,11},{10,... | collective-permute-start | bytes 3538952 | tf_op jit(solution)/shard_map/ppermute | solution.py:29
  89.6 30.4 %copy-start.4 = (bf16[96,6144]{1,0:T(8,128)(2,1)}, bf16[96,6144]{1,0:T(8,128)(2,1)S(1)}, u32[]{:S(2)}) copy-start(bf16[96,6144]{1,0:T(8,128)(2,1)S(1)} %collective-permute-done.21.refs_10_.refs_22_) | copy-start | bytes 3538948
  89.6 30.4 %collective-permute-start.22 = (bf16[96,6144]{1,0:T(8,128)(2,1)S(1)}, bf16[96,6144]{1,0:T(8,128)(2,1)}, u32[]{:S(2)}, u32[]{:S(2)}) collective-permute-start(bf16[96,6144]{1,0:T(8,128)(2,1)S(1)} %collective-permute-done.21.refs_10_.refs_22_), channel_id=1, source_target_pairs={{0,1},{1,0},{2,3},{3,2},{4,5},{5,4},{6,7},{7,6},{8,9},{9,8},{10,11... | collective-permute-start | bytes 3538952 | tf_op jit(solution)/shard_map/ppermute | solution.py:49
  89.7 1.1 copy-start.5
  90.8 32.1 %collective-permute-start.24 = (bf16[96,6144]{1,0:T(8,128)(2,1)}, bf16[96,6144]{1,0:T(8,128)(2,1)}, u32[]{:S(2)}, u32[]{:S(2)}) collective-permute-start(bf16[96,6144]{1,0:T(8,128)(2,1)} %collective-permute-done.23.refs_12_.refs_24_), channel_id=1, source_target_pairs={{0,1},{1,0},{2,3},{3,2},{4,5},{5,4},{6,7},{7,6},{8,9},{9,8},{10,11... | collective-permute-start | bytes 3538952 | tf_op jit(solution)/shard_map/ppermute | solution.py:49
  93.1 26.9 %copy-start.14 = (f32[8,1,512]{2,1,0:T(1,128)S(1)}, f32[8,1,512]{2,1,0:T(1,128)}, u32[]{:S(2)}) copy-start(f32[8,1,512]{2,1,0:T(1,128)} %get-tuple-element.25.refs_12_.refs_8_.refs_5_) | copy-start | bytes 49156
  93.1 42.3 %collective-permute-start.11 = (bf16[128,3072]{1,0:T(8,128)(2,1)}, bf16[128,3072]{1,0:T(8,128)(2,1)}, u32[]{:S(2)}, u32[]{:S(2)}) collective-permute-start(bf16[128,3072]{1,0:T(8,128)(2,1)} %copy-done.7), channel_id=1, source_target_pairs={{0,96},{1,33},{32,0},{33,65},{64,32},{65,97},{96,64},{97,1},{2,98}... | collective-permute-start | bytes 2359304 | tf_op jit(solution)/shard_map/ppermute | solution.py:33
  93.1 42.3 %collective-permute-start.12 = (bf16[128,3072]{1,0:T(8,128)(2,1)}, bf16[128,3072]{1,0:T(8,128)(2,1)}, u32[]{:S(2)}, u32[]{:S(2)}) collective-permute-start(bf16[128,3072]{1,0:T(8,128)(2,1)} %collective-permute-done.10.refs_9_), channel_id=1, source_target_pairs={{0,32},{1,97},{32,64},{33,1},{64,96},{65,33},{96,0},{97,65},{2,34}... | collective-permute-start | bytes 2359304 | tf_op jit(solution)/shard_map/ppermute | solution.py:33
  104.6 30.9 %collective-permute-start.26 = (bf16[96,6144]{1,0:T(8,128)(2,1)}, bf16[96,6144]{1,0:T(8,128)(2,1)}, u32[]{:S(2)}, u32[]{:S(2)}) collective-permute-start(bf16[96,6144]{1,0:T(8,128)(2,1)} %collective-permute-done.25.refs_26_), channel_id=1, source_target_pairs={{0,1},{1,0},{2,3},{3,2},{4,5},{5,4},{6,7},{7,6},{8,9},{9,8},{10,11... | collective-permute-start | bytes 3538952 | tf_op jit(solution)/shard_map/ppermute | solution.py:49
  120.1 32.8 %collective-permute-start.28 = (f32[8,1,512]{2,1,0:T(1,128)S(1)}, f32[8,1,512]{2,1,0:T(1,128)S(1)}, u32[]{:S(2)}, u32[]{:S(2)}) collective-permute-start(f32[8,1,512]{2,1,0:T(1,128)S(1)} %copy-done.14), channel_id=1, source_target_pairs={{0,24},{8,16},{16,8},{24,0},{1,25},{9,17},{17,9},{25,1},{2,26},{10... | collective-permute-start | bytes 49160 | tf_op jit(solution)/shard_map/ppermute | solution.py:41
  152.9 0.6 copy-start.16
  153.5 3.8 %copy-start.19 = (bf16[4,128,512]{2,1,0:T(8,128)(2,1)S(1)}, bf16[4,128,512]{2,1,0:T(8,128)(2,1)}, u32[]{:S(2)}) copy-start(bf16[4,128,512]{2,1,0:T(8,128)(2,1)} %get-tuple-element.24) | copy-start | bytes 1572868
  156.8 53.0 %collective-permute-start.29 = (bf16[4,128,512]{2,1,0:T(8,128)(2,1)}, bf16[4,128,512]{2,1,0:T(8,128)(2,1)S(1)}, u32[]{:S(2)}, u32[]{:S(2)}) collective-permute-start(bf16[4,128,512]{2,1,0:T(8,128)(2,1)} %intra.3), channel_id=1, source_target_pairs={{0,24},{8,16},{16,8},{24,0},{1,25},{9,17},{17,9},{25,1},{2,26},{10... | collective-permute-start | bytes 1572872 | tf_op jit(solution)/shard_map/ppermute | solution.py:41
  157.3 52.4 %collective-permute-start.27 = (bf16[4,128,512]{2,1,0:T(8,128)(2,1)S(1)}, bf16[4,128,512]{2,1,0:T(8,128)(2,1)S(1)}, u32[]{:S(2)}, u32[]{:S(2)}) collective-permute-start(bf16[4,128,512]{2,1,0:T(8,128)(2,1)S(1)} %copy-done.19), channel_id=1, source_target_pairs={{0,24},{8,16},{16,8},{24,0},{1,25},{9,17},{17,9},{25,1},{2,26},{10... | collective-permute-start | bytes 1572872 | tf_op jit(solution)/shard_map/ppermute | solution.py:41
  160.1 23.2 %all-to-all-start = ((f32[32,1,128]{2,1,0:T(1,128)}), f32[32,1,128]{2,1,0:T(1,128)S(1)}, u32[]{:S(2)}, u32[]{:S(2)}) async-start(f32[32,1,128]{2,1,0:T(1,128)} %get-tuple-element.28), calls=%async_computation | async-start | bytes 32768 | tf_op jit(solution)/shard_map/all_to_all | solution.py:45
  183.3 12.0 %copy-start.15 = (f32[32,1,128]{2,1,0:T(1,128)}, f32[32,1,128]{2,1,0:T(1,128)S(1)}, u32[]{:S(2)}) copy-start(f32[32,1,128]{2,1,0:T(1,128)S(1)} %all-to-all-done.d_ref) | copy-start | bytes 49156
  197.1 12.7 %all-to-all-start.2 = ((bf16[32,32,128]{2,1,0:T(8,128)(2,1)}), bf16[32,32,128]{2,1,0:T(8,128)(2,1)S(1)}, u32[]{:S(2)}, u32[]{:S(2)}) async-start(bf16[32,32,128]{2,1,0:T(8,128)(2,1)} %carries.1), calls=%async_computation.2 | async-start | bytes 524288 | tf_op jit(solution)/shard_map/all_to_all | solution.py:45
  209.8 0.7 copy-start.6
  209.8 0.9 copy-start.8
  210.7 0.8 copy-start.9

commit v5 on v4

--- a/solution.py
+++ b/solution.py
@@ -49,6 +49,10 @@
     return lax.ppermute(v, "c", [(0, 1), (1, 0)])
 
 
+def near(v):
+    return pltpu.with_memory_space_constraint(v, pltpu.VMEM)
+
+
 def grouped(members):
     parts = -(-len(members) // 7)
     size = -(-len(members) // parts)
@@ -68,11 +72,13 @@
         u_ref, refs = refs[0], refs[1:]
         if "start" in kinds:
             start_ref, refs = refs[0], refs[1:]
+        if "go" in kinds:
+            go_ref, refs = refs[0], refs[1:]
         if after:
             across_ref, query_ref, refs = refs[0], refs[1], refs[2:]
         sem, stage, accs = refs[0], refs[1], refs[2:]
         k = pl.program_id(0)
-        sums_of = [partial_refs.pop(0) if kind == "resume" else None for kind in kinds]
+        sums_of = [partial_refs.pop(0) if kind in ("resume", "go") else None for kind in kinds]
 
         def run(step):
             copies = []
@@ -80,8 +86,8 @@
             for (kind, members, first, last), acc, before in zip(jobs, accs, sums_of):
                 if not first <= step <= last:
                     continue
-                if kind == "start":
-                    acc = start_ref
+                if kind in ("start", "go"):
+                    acc = start_ref if kind == "start" else go_ref
                 for group in grouped(members):
                     rows = slice(group[0] * UNIT, (group[-1] + 1) * UNIT)
                     w = jnp.concatenate([w_refs[members[g]][...] for g in group], axis=0)
@@ -92,9 +98,9 @@
                     v = lax.dot_general(w, x, (((1,), (1,)), ((), ())), preferred_element_type=F32)
                     if step > first:
                         v += acc[rows, :]
-                    elif kind == "resume":
+                    elif before is not None:
                         v += before[rows, :]
-                    if step < last or kind == "start":
+                    if step < last or kind in ("start", "go"):
                         acc[rows, :] = v
                         continue
                     v = (v * jax.nn.sigmoid(v)).astype(BF16)
@@ -134,8 +140,8 @@
     out_shape = [jax.ShapeDtypeStruct((16 * UNIT, TOK), BF16)]
     for kind, members, _, _ in jobs:
         rows = len(members) * UNIT
-        scratch.append(pltpu.VMEM((rows if kind != "start" else 8, TOK), F32))
-        if kind == "start":
+        scratch.append(pltpu.VMEM((8 if kind in ("start", "go") else rows, TOK), F32))
+        if kind in ("start", "go"):
             out_specs.append(pl.BlockSpec((rows, TOK), lambda k, s: (0, 0)))
             out_shape.append(jax.ShapeDtypeStruct((rows, TOK), F32))
     if after:
@@ -173,6 +179,7 @@
 
 
 SMEM = pl.BlockSpec(memory_space=pltpu.SMEM)
+VMEM = pl.BlockSpec(memory_space=pltpu.VMEM)
 
 
 def running_sum(v):
@@ -283,11 +290,11 @@
     return pl.pallas_call(
         kernel,
         grid=(1,),
-        in_specs=[SMEM, whole((32, 1, 128)), whole((16, 2, 32, 128))],
+        in_specs=[SMEM, VMEM, VMEM],
         out_specs=whole((32, 32, 128)),
         out_shape=jax.ShapeDtypeStruct((32, 32, 128), BF16),
         name="carries",
-    )(order, totals, pieces)
+    )(order, near(totals), near(pieces))
 
 
 def finish(half, held, over_queries, sums, inside, over_inside, carried, gains):
@@ -310,11 +317,11 @@
         grid=(1,),
         in_specs=[SMEM]
         + heads_of(0)
-        + [whole(a.shape) for a in (over_queries, sums, inside, over_inside, carried, gains)],
+        + [VMEM, whole((8, 1, TOK)), whole((4, 128, TOK)), VMEM, VMEM, whole((8, 128))],
         out_specs=whole((TOK, 1024)),
         out_shape=jax.ShapeDtypeStruct((TOK, 1024), BF16),
         name="finish",
-    )(half, *[held] * 4, over_queries, sums, inside, over_inside, carried, gains)
+    )(half, *[held] * 4, near(over_queries), sums, inside, near(over_inside), near(carried), gains)
 
 
 def shards(inputs, qkv_weight, log_decay, out_gain):
@@ -387,10 +394,11 @@
     units = [(w, i) for i, w in enumerate(weights)]
     cuts = list(zip(a, xa, xb, xc))
     late = NK // 2
-    jobs = [("own", range(8), 0, NK - 1), ("start", range(8), 0, late - 1)]
-    held, early = project(scalars, inputs, cuts[:-1], units[:8], jobs, None, [])
-    jobs = [("own", range(6), 0, NK - 1), ("start", range(6), 0, late - 1)]
-    held, middle = project(scalars, inputs, cuts[:-1], units[8:14], jobs, held, [])
+    jobs = [("own", range(8), 0, NK - 1), ("start", range(8), 0, 0)]
+    held, early = project(scalars, inputs, cuts[:1], units[:8], jobs, None, [])
+    jobs = [("own", range(8, 14), 0, NK - 1), ("start", range(8, 14), 0, late - 1), ("go", range(8), 1, late - 1)]
+    args = (scalars, inputs, cuts[:2], units[:14], jobs, held, [early])
+    held, middle, early = project(*args)
     jobs = [("across", (14, 15), 0, NK - 1), ("own", (14, 15), 0, NK - 1)]
     jobs += [("resume", range(8), late, NK - 1), ("resume", range(8, 14), late, NK - 1)]
     args = (scalars, inputs, cuts, units, jobs, held, [early, middle])

time: 217 us -> 217 us (level)
  starting transfers between devices: 40.2 us -> 45.4 us
  waiting for transfers between devices: 92.8 us -> 89.1 us
    ppermute x5, waiting for transfers between devices: 29.2 us -> 17.6 us  [y_move(): return lax.ppermute(v, ('y', 'c'), ring_pairs(step))]
    ppermute x9, waiting for transfers between devices: 27.9 us -> 17.6 us  [x_move(): return lax.ppermute(v, ('x', 'c'), ring_pairs(step))]
    ppermute x6, waiting for transfers between devices: 14.4 us -> 24.1 us  [z_out(): return lax.ppermute(v, ('zh', 'zl'), [(i, 3 - i) for i in range(4)])]
    ppermute x2, waiting for transfers between devices: 0.01 us -> 8.39 us  [z_in(): return lax.ppermute(v, 'zl', [(0, 1), (1, 0)])]
    ppermute x9, starting transfers between devices: 7.53 us -> 12.1 us  [x_move(): return lax.ppermute(v, ('x', 'c'), ring_pairs(step))]
  transfers between devices with their start and end apart: 32 -> 32, of which waited for: 12 -> 11; matrix products, arithmetic and copies ran while one was open for 1% -> 1% of each run, Pallas kernels for 25% -> 26%
where the time goes in v5:
time: 217 us; the launch traced here: 215 us
  waiting for transfers between devices  89.1 us (41%)
  Pallas kernels  62.8 us (29%)
  starting transfers between devices  45.4 us (21%)
  blocking collectives  11.3 us (5%)
  local copies, waits for them, and re-layouts  5.71 us (3%)
    pallas_call x3, Pallas kernels, project(): pl.pallas_call(kernel, grid_spec=pltpu.PrefetchScalarGridSpec(num_scalar_...  46 us
    ppermute x6, waiting for transfers between devices, z_out(): return lax.ppermute(v, ('zh', 'zl'), [(i, 3 - i) for i in range(4)])  24.1 us
    all_to_all x2, waiting for transfers between devices, exchange(): return lax.all_to_all(v, axes, 0, 0, tiled=True)  21.4 us
    ppermute x9, waiting for transfers between devices, x_move(): return lax.ppermute(v, ('x', 'c'), ring_pairs(step))  17.6 us
    ppermute x5, waiting for transfers between devices, y_move(): return lax.ppermute(v, ('y', 'c'), ring_pairs(step))  17.6 us
    ppermute x6, starting transfers between devices, z_out(): return lax.ppermute(v, ('zh', 'zl'), [(i, 3 - i) for i in range(4)])  13.4 us
    ppermute x9, starting transfers between devices, x_move(): return lax.ppermute(v, ('x', 'c'), ring_pairs(step))  12.1 us
    all_to_all x1, blocking collectives, exchange(): return lax.all_to_all(v, axes, 0, 0, tiled=True)  11.3 us
  transfers between devices with their start and end apart: 32, of which 11 were waited for; matrix products, arithmetic and copies ran while one was open for 1% of the time, Pallas kernels for 26%

profile of v5, /device:TPU:0, one launch (start us, length us, event | category | flops | bytes accessed | tf_op | source)
XLA Modules:
  0.0 215.2 jit_solution(7484423043715395287)
XLA Ops:
  0.0 1.3 constant_dynamic-slice_fusion.1
  1.3 0.0 copy-start.15
  1.3 0.0 copy-start.16
  1.3 4.2 %collective-permute-start.1 = (bf16[128,1536]{1,0:T(8,128)(2,1)S(1)}, bf16[128,1536]{1,0:T(8,128)(2,1)S(1)}, u32[]{:S(2)}, u32[]{:S(2)}) collective-permute-start(bf16[128,1536]{1,0:T(8,128)(2,1)S(1)} %get-tuple-element.32), channel_id=1, source_target_pairs={{0,24},{8,16},{16,8},{24,0},{1,25},{9,17},{17,9},{25,1},{2,26},{10... | collective-permute-start | bytes 1179656 | tf_op jit(solution)/shard_map/ppermute | solution.py:41
  5.5 0.1 collective-permute-start.5
  5.6 9.9 %collective-permute-done.1.refs_0_ = bf16[128,1536]{1,0:T(8,128)(2,1)S(1)} collective-permute-done((bf16[128,1536]{1,0:T(8,128)(2,1)S(1)}, bf16[128,1536]{1,0:T(8,128)(2,1)S(1)}, u32[]{:S(2)}, u32[]{:S(2)}) %collective-permute-start.1) | collective-permute-done | bytes 393248 | tf_op jit(solution)/shard_map/ppermute | solution.py:41
  15.5 1.5 collective-permute-start.2
  17.0 1.7 collective-permute-start.3
  18.7 4.3 %collective-permute-done.5.refs_4_ = bf16[128,1536]{1,0:T(8,128)(2,1)S(1)} collective-permute-done((bf16[128,1536]{1,0:T(8,128)(2,1)S(1)}, bf16[128,1536]{1,0:T(8,128)(2,1)S(1)}, u32[]{:S(2)}, u32[]{:S(2)}) %collective-permute-start.5) | collective-permute-done | bytes 393248 | tf_op jit(solution)/shard_map/ppermute | solution.py:41
  23.1 1.5 collective-permute-start.6
  24.6 1.6 collective-permute-start
  26.1 1.7 collective-permute-start.7
  27.9 1.2 constant_dynamic-slice_fusion
  29.1 0.0 collective-permute-done.2.refs_1_
  29.1 3.0 %collective-permute-start.9 = (bf16[128,3072]{1,0:T(8,128)(2,1)S(1)}, bf16[128,3072]{1,0:T(8,128)(2,1)S(1)}, u32[]{:S(2)}, u32[]{:S(2)}) collective-permute-start(bf16[128,3072]{1,0:T(8,128)(2,1)S(1)} %constant_dynamic-slice_fusion), channel_id=1, source_target_pairs={{0,24},{8,16},{16,8},{24,0},{1,25},{9,17},{17,9},{25,1},{2,26},{10... | collective-permute-start | bytes 2359304 | tf_op jit(solution)/shard_map/ppermute | solution.py:41
  32.1 0.0 collective-permute-done.3.refs_2_
  32.1 0.0 collective-permute-start.17
  32.1 2.2 %collective-permute-done.6.refs_5_ = bf16[128,1536]{1,0:T(8,128)(2,1)S(1)} collective-permute-done((bf16[128,1536]{1,0:T(8,128)(2,1)S(1)}, bf16[128,1536]{1,0:T(8,128)(2,1)S(1)}, u32[]{:S(2)}, u32[]{:S(2)}) %collective-permute-start.6) | collective-permute-done | bytes 393248 | tf_op jit(solution)/shard_map/ppermute | solution.py:33
  34.3 5.3 %collective-permute-start.15 = (bf16[96,6144]{1,0:T(8,128)(2,1)S(1)}, bf16[96,6144]{1,0:T(8,128)(2,1)}, u32[]{:S(2)}, u32[]{:S(2)}) collective-permute-start(bf16[96,6144]{1,0:T(8,128)(2,1)S(1)} %bitcast.27), channel_id=1, source_target_pairs={{0,6},{1,3},{2,0},{3,5},{4,2},{5,7},{6,4},{7,1},{8,14},{9,11},{10,... | collective-permute-start | bytes 3538952 | tf_op jit(solution)/shard_map/ppermute | solution.py:29
  39.6 0.0 collective-permute-done.7.refs_6_
  39.6 0.0 collective-permute-start.13
  39.6 9.9 %collective-permute-done.9.refs_8_ = bf16[128,3072]{1,0:T(8,128)(2,1)S(1)} collective-permute-done((bf16[128,3072]{1,0:T(8,128)(2,1)S(1)}, bf16[128,3072]{1,0:T(8,128)(2,1)S(1)}, u32[]{:S(2)}, u32[]{:S(2)}) %collective-permute-start.9) | collective-permute-done | bytes 786464 | tf_op jit(solution)/shard_map/ppermute | solution.py:41
  49.5 0.0 copy-start.11
  49.5 0.9 copy-done.11
  50.4 0.5 collective-permute-start.4
  50.9 0.6 stack.83.s_ref
  51.5 0.0 collective-permute-done.refs_6_.refs_10_.refs_14_
  51.5 1.5 collective-permute-start.10
  53.0 0.6 broadcast_select_fusion.n_ref
  53.6 6.1 %collective-permute-done.4.refs_3_ = bf16[128,1536]{1,0:T(8,128)(2,1)} collective-permute-done((bf16[128,1536]{1,0:T(8,128)(2,1)}, bf16[128,1536]{1,0:T(8,128)(2,1)}, u32[]{:S(2)}, u32[]{:S(2)}) %collective-permute-start.4) | collective-permute-done | bytes 393248 | tf_op jit(solution)/shard_map/ppermute | solution.py:33
  59.7 0.1 collective-permute-start.19
  59.8 3.2 %collective-permute-start.23 = (bf16[96,6144]{1,0:T(8,128)(2,1)S(1)}, bf16[96,6144]{1,0:T(8,128)(2,1)}, u32[]{:S(2)}, u32[]{:S(2)}) collective-permute-start(bf16[96,6144]{1,0:T(8,128)(2,1)S(1)} %collective-permute-done.17.refs_10_.refs_14_.refs_18_), channel_id=1, source_target_pairs={{0,6},{1,3},{2,0},{3,5},{4,2},{5,7},{6,4},{7,1},{8,14},{9,11},{10,... | collective-permute-start | bytes 3538952 | tf_op jit(solution)/shard_map/ppermute | solution.py:29
  63.0 0.0 collective-permute-done.13.refs_5_.refs_9_.refs_13_
  63.0 0.0 collective-permute-start.8
  63.0 9.3 %collective-permute-done.8.refs_7_ = bf16[128,1536]{1,0:T(8,128)(2,1)} collective-permute-done((bf16[128,1536]{1,0:T(8,128)(2,1)}, bf16[128,1536]{1,0:T(8,128)(2,1)}, u32[]{:S(2)}, u32[]{:S(2)}) %collective-permute-start.8) | collective-permute-done | bytes 393248 | tf_op jit(solution)/shard_map/ppermute | solution.py:33
  72.3 0.0 collective-permute-done.10.refs_9_
  72.3 0.1 collective-permute-start.18
  72.5 0.5 collective-permute-start.16
  72.9 16.9 %collective-permute-done.19.refs_16_.refs_20_ = bf16[96,6144]{1,0:T(8,128)(2,1)} collective-permute-done((bf16[96,6144]{1,0:T(8,128)(2,1)S(1)}, bf16[96,6144]{1,0:T(8,128)(2,1)}, u32[]{:S(2)}, u32[]{:S(2)}) %collective-permute-start.19) | collective-permute-done | bytes 1179680 | tf_op jit(solution)/shard_map/ppermute | solution.py:29
  89.9 0.3 collective-permute-start.25
  90.1 8.4 %collective-permute-done.21.refs_18_.refs_22_ = bf16[96,6144]{1,0:T(8,128)(2,1)S(1)} collective-permute-done((bf16[96,6144]{1,0:T(8,128)(2,1)S(1)}, bf16[96,6144]{1,0:T(8,128)(2,1)S(1)}, u32[]{:S(2)}, u32[]{:S(2)}) %collective-permute-start.21) | collective-permute-done | bytes 1179680 | tf_op jit(solution)/shard_map/ppermute | solution.py:37
  98.6 1.1 copy-done.5
  99.7 0.4 collective-permute-start.24
  100.1 1.9 rates.1
  102.0 3.7 %collective-permute-start.11 = (bf16[128,3072]{1,0:T(8,128)(2,1)}, bf16[128,3072]{1,0:T(8,128)(2,1)}, u32[]{:S(2)}, u32[]{:S(2)}) collective-permute-start(bf16[128,3072]{1,0:T(8,128)(2,1)} %copy-done.11), channel_id=1, source_target_pairs={{0,96},{1,33},{32,0},{33,65},{64,32},{65,97},{96,64},{97,1},{2,98}... | collective-permute-start | bytes 2359304 | tf_op jit(solution)/shard_map/ppermute | solution.py:33
  105.7 0.7 collective-permute-done.25.refs_26_
  106.4 0.6 collective-permute-start.26
  107.0 12.9 %project.3 = (bf16[1536,512]{1,0:T(8,128)(2,1)}, f32[768,512]{1,0:T(8,128)}) custom-call(s32[20]{0:T(128)} %stack.83.s_ref, bf16[512,6144]{1,0:T(8,128)(2,1)} %x_ref.5, bf16[128,1536]{1,0:T(8,128)(2,1)} %copy-done.6, bf16[128,1536]{1,0:T(8,128)(2,1)} %collective-permute-done.2.refs_1_, bf16[128,1536]{1,0:T(8,128)(2,1)} %copy-done.8, ...), custom_call_target="tpu_custom_call" | custom-call | flops 6039797760 | bytes 9437184 | tf_op jit(solution)/shard_map/project/pallas_call | solution.py:161
  119.9 2.8 %collective-permute-start.28 = (f32[8,1,512]{2,1,0:T(1,128)S(1)}, f32[8,1,512]{2,1,0:T(1,128)S(1)}, u32[]{:S(2)}, u32[]{:S(2)}) collective-permute-start(f32[8,1,512]{2,1,0:T(1,128)S(1)} %copy-done.13), channel_id=1, source_target_pairs={{0,24},{8,16},{16,8},{24,0},{1,25},{9,17},{17,9},{25,1},{2,26},{10... | collective-permute-start | bytes 49160 | tf_op jit(solution)/shard_map/ppermute | solution.py:41
  122.7 15.6 %project.4 = (bf16[1536,512]{1,0:T(8,128)(2,1)}, f32[576,512]{1,0:T(8,128)}, f32[768,512]{1,0:T(8,128)}) custom-call(s32[20]{0:T(128)} %stack.83.s_ref, bf16[512,6144]{1,0:T(8,128)(2,1)} %x_ref.5, bf16[128,1536]{1,0:T(8,128)(2,1)} %copy-done.6, bf16[128,1536]{1,0:T(8,128)(2,1)} %collective-permute-done.2.refs_1_, ...), custom_call_target="tpu_custom_call", output_to_operand_aliasing={{0}: (25, {})} | custom-call | flops 6643777536 | bytes 16515072 | tf_op jit(solution)/shard_map/project/pallas_call | solution.py:161
  138.3 17.5 %project.5 = (bf16[1536,512]{1,0:T(8,128)(2,1)}, bf16[1536,512]{1,0:T(8,128)(2,1)}, bf16[4,128,512]{2,1,0:T(8,128)(2,1)}) custom-call(s32[20]{0:T(128)} %stack.83.s_ref, bf16[512,6144]{1,0:T(8,128)(2,1)} %x_ref.5, bf16[128,1536]{1,0:T(8,128)(2,1)} %copy-done.6, bf16[128,1536]{1,0:T(8,128)(2,1)} %collective-permute-done.2.refs_1_, ...), custom_call_target="tpu_custom_call", output_to_operand_aliasing={{0}: (32, {})} | custom-call | flops 6643777536 | bytes 18874368 | tf_op jit(solution)/shard_map/project/pallas_call | solution.py:161
  155.9 0.6 copy-done.14
  156.5 3.3 %intra.3 = bf16[4,128,512]{2,1,0:T(8,128)(2,1)} custom-call(s32[1]{0:T(128)} %bitcast.z_ref, bf16[1536,512]{1,0:T(8,128)(2,1)} %get-tuple-element.28.refs_0_.refs_1_.refs_2_.refs_3_.refs_4_.refs_5_.refs_6_.refs_7_.refs_8_.refs_9_.refs_10_.refs_11_.refs_12_.refs_13_.refs_14_.refs_15_.refs_16_, ...), custom_call_target="tpu_custom_call" | custom-call | tf_op jit(solution)/shard_map/intra/pallas_call | solution.py:271
  159.8 0.5 collective-permute-start.29
  160.3 2.7 %collective-permute-start.27 = (bf16[4,128,512]{2,1,0:T(8,128)(2,1)S(1)}, bf16[4,128,512]{2,1,0:T(8,128)(2,1)S(1)}, u32[]{:S(2)}, u32[]{:S(2)}) collective-permute-start(bf16[4,128,512]{2,1,0:T(8,128)(2,1)S(1)} %copy-done.17), channel_id=1, source_target_pairs={{0,24},{8,16},{16,8},{24,0},{1,25},{9,17},{17,9},{25,1},{2,26},{10... | collective-permute-start | bytes 1572872 | tf_op jit(solution)/shard_map/ppermute | solution.py:41
  163.0 4.0 %all-to-all-start = ((f32[32,1,128]{2,1,0:T(1,128)}), f32[32,1,128]{2,1,0:T(1,128)S(1)}, u32[]{:S(2)}, u32[]{:S(2)}) async-start(f32[32,1,128]{2,1,0:T(1,128)} %get-tuple-element.30), calls=%async_computation | async-start | bytes 32768 | tf_op jit(solution)/shard_map/all_to_all | solution.py:45
  167.1 3.1 %states.1 = bf16[16,2,32,128]{3,2,1,0:T(8,128)(2,1)} custom-call(s32[1]{0:T(128)} %bitcast.z_ref, bf16[1536,512]{1,0:T(8,128)(2,1)} %get-tuple-element.25.refs_0_.refs_1_.refs_2_.refs_3_.refs_4_.refs_5_.refs_6_.refs_7_.refs_8_.refs_9_.refs_10_.refs_11_, ...), custom_call_target="tpu_custom_call" | custom-call | tf_op jit(solution)/shard_map/states/pallas_call | solution.py:238
  170.2 16.1 %all-to-all-done.d_ref = f32[32,1,128]{2,1,0:T(1,128)S(1)} async-done(((f32[32,1,128]{2,1,0:T(1,128)}), f32[32,1,128]{2,1,0:T(1,128)S(1)}, u32[]{:S(2)}, u32[]{:S(2)}) %all-to-all-start) | async-done | bytes 16416 | tf_op jit(solution)/shard_map/all_to_all | solution.py:45
  186.3 11.3 %all_to_all.15.s_ref = bf16[16,2,32,128]{3,2,1,0:T(8,128)(2,1)S(1)} all-to-all(bf16[16,2,32,128]{3,2,1,0:T(8,128)(2,1)} %states.1), channel_id=1, replica_groups=mesh['x'=4,'zh'=2,'zl'=2,'y'=4,'c'=2] {'zl','y','c'}, dimensions={0} | all-to-all | bytes 524288 | tf_op jit(solution)/shard_map/all_to_all | solution.py:45
  197.6 1.5 carries.1
  199.0 3.9 %all-to-all-start.2 = ((bf16[32,32,128]{2,1,0:T(8,128)(2,1)}), bf16[32,32,128]{2,1,0:T(8,128)(2,1)S(1)}, u32[]{:S(2)}, u32[]{:S(2)}) async-start(bf16[32,32,128]{2,1,0:T(8,128)(2,1)} %carries.1), calls=%async_computation.2 | async-start | bytes 524288 | tf_op jit(solution)/shard_map/all_to_all | solution.py:45
  202.9 3.5 %intra.2.refs_6_ = f32[4,128,512]{2,1,0:T(8,128)} custom-call(s32[1]{0:T(128)} %bitcast.z_ref, bf16[1536,512]{1,0:T(8,128)(2,1)} %get-tuple-element.25.refs_0_.refs_1_.refs_2_.refs_3_.refs_4_.refs_5_.refs_6_.refs_7_.refs_8_.refs_9_.refs_10_.refs_11_, ...), custom_call_target="tpu_custom_call" | custom-call | tf_op jit(solution)/shard_map/intra/pallas_call | solution.py:271
  206.4 5.3 %all-to-all-done.2.refs_8_ = bf16[32,32,128]{2,1,0:T(8,128)(2,1)S(1)} async-done(((bf16[32,32,128]{2,1,0:T(8,128)(2,1)}), bf16[32,32,128]{2,1,0:T(8,128)(2,1)S(1)}, u32[]{:S(2)}, u32[]{:S(2)}) %all-to-all-start.2) | async-done | bytes 262176 | tf_op jit(solution)/shard_map/all_to_all | solution.py:45
  211.7 3.5 %finish.1 = bf16[512,1024]{1,0:T(8,128)(2,1)} custom-call(s32[1]{0:T(128)} %bitcast.z_ref, bf16[1536,512]{1,0:T(8,128)(2,1)} %get-tuple-element.25.refs_0_.refs_1_.refs_2_.refs_3_.refs_4_.refs_5_.refs_6_.refs_7_.refs_8_.refs_9_.refs_10_.refs_11_, ...), custom_call_target="tpu_custom_call" | custom-call | tf_op jit(solution)/shard_map/finish/pallas_call | solution.py:315
  (50 shorter events, 0.1 us)
Async XLA Ops:
  0.0 24.6 %copy-start = (bf16[6144,96]{0,1:T(8,128)(2,1)S(1)}, bf16[6144,96]{0,1:T(8,128)(2,1)}, u32[]{:S(2)}) copy-start(bf16[6144,96]{0,1:T(8,128)(2,1)} %param.7) | copy-start | bytes 3538948
  1.3 51.7 %copy-start.15 = (s32[8]{0:T(128)S(1)}, s32[8]{0:T(128)}, u32[]{:S(2)}) copy-start(s32[8]{0:T(128)} %constant.101.clone) | copy-start | bytes 100
  1.3 51.7 %copy-start.16 = (s32[8]{0:T(128)S(1)}, s32[8]{0:T(128)}, u32[]{:S(2)}) copy-start(s32[8]{0:T(128)} %constant.102.clone) | copy-start | bytes 100
  1.3 14.2 %collective-permute-start.1 = (bf16[128,1536]{1,0:T(8,128)(2,1)S(1)}, bf16[128,1536]{1,0:T(8,128)(2,1)S(1)}, u32[]{:S(2)}, u32[]{:S(2)}) collective-permute-start(bf16[128,1536]{1,0:T(8,128)(2,1)S(1)} %get-tuple-element.32), channel_id=1, source_target_pairs={{0,24},{8,16},{16,8},{24,0},{1,25},{9,17},{17,9},{25,1},{2,26},{10... | collective-permute-start | bytes 1179656 | tf_op jit(solution)/shard_map/ppermute | solution.py:41
  5.5 17.5 %collective-permute-start.5 = (bf16[128,1536]{1,0:T(8,128)(2,1)S(1)}, bf16[128,1536]{1,0:T(8,128)(2,1)S(1)}, u32[]{:S(2)}, u32[]{:S(2)}) collective-permute-start(bf16[128,1536]{1,0:T(8,128)(2,1)S(1)} %get-tuple-element.31), channel_id=1, source_target_pairs={{0,24},{8,16},{16,8},{24,0},{1,25},{9,17},{17,9},{25,1},{2,26},{10... | collective-permute-start | bytes 1179656 | tf_op jit(solution)/shard_map/ppermute | solution.py:41
  15.5 24.1 %copy-start.6 = (bf16[128,1536]{1,0:T(8,128)(2,1)}, bf16[128,1536]{1,0:T(8,128)(2,1)S(1)}, u32[]{:S(2)}) copy-start(bf16[128,1536]{1,0:T(8,128)(2,1)S(1)} %collective-permute-done.1.refs_0_) | copy-start | bytes 1179652
  15.5 13.6 %collective-permute-start.2 = (bf16[128,1536]{1,0:T(8,128)(2,1)S(1)}, bf16[128,1536]{1,0:T(8,128)(2,1)}, u32[]{:S(2)}, u32[]{:S(2)}) collective-permute-start(bf16[128,1536]{1,0:T(8,128)(2,1)S(1)} %collective-permute-done.1.refs_0_), channel_id=1, source_target_pairs={{0,32},{1,97},{32,64},{33,1},{64,96},{65,33},{96,0},{97,65},{2,34}... | collective-permute-start | bytes 1179656 | tf_op jit(solution)/shard_map/ppermute | solution.py:33
  17.0 15.1 %collective-permute-start.3 = (bf16[128,1536]{1,0:T(8,128)(2,1)S(1)}, bf16[128,1536]{1,0:T(8,128)(2,1)S(1)}, u32[]{:S(2)}, u32[]{:S(2)}) collective-permute-start(bf16[128,1536]{1,0:T(8,128)(2,1)S(1)} %collective-permute-done.1.refs_0_), channel_id=1, source_target_pairs={{0,96},{1,33},{32,0},{33,65},{64,32},{65,97},{96,64},{97,1},{2,98}... | collective-permute-start | bytes 1179656 | tf_op jit(solution)/shard_map/ppermute | solution.py:33
  23.1 26.4 %copy-start.7 = (bf16[128,1536]{1,0:T(8,128)(2,1)}, bf16[128,1536]{1,0:T(8,128)(2,1)S(1)}, u32[]{:S(2)}) copy-start(bf16[128,1536]{1,0:T(8,128)(2,1)S(1)} %collective-permute-done.5.refs_4_) | copy-start | bytes 1179652
  23.1 11.2 %collective-permute-start.6 = (bf16[128,1536]{1,0:T(8,128)(2,1)S(1)}, bf16[128,1536]{1,0:T(8,128)(2,1)S(1)}, u32[]{:S(2)}, u32[]{:S(2)}) collective-permute-start(bf16[128,1536]{1,0:T(8,128)(2,1)S(1)} %collective-permute-done.5.refs_4_), channel_id=1, source_target_pairs={{0,32},{1,97},{32,64},{33,1},{64,96},{65,33},{96,0},{97,65},{2,34}... | collective-permute-start | bytes 1179656 | tf_op jit(solution)/shard_map/ppermute | solution.py:33
  24.6 26.9 %collective-permute-start = (bf16[96,6144]{1,0:T(8,128)(2,1)S(1)}, bf16[96,6144]{1,0:T(8,128)(2,1)S(1)}, u32[]{:S(2)}, u32[]{:S(2)}) collective-permute-start(bf16[96,6144]{1,0:T(8,128)(2,1)S(1)} %bitcast.25), channel_id=1, source_target_pairs={{0,2},{1,7},{2,4},{3,1},{4,6},{5,3},{6,0},{7,5},{8,10},{9,15},{10,... | collective-permute-start | bytes 3538952 | tf_op jit(solution)/shard_map/ppermute | solution.py:29
  26.1 13.5 %collective-permute-start.7 = (bf16[128,1536]{1,0:T(8,128)(2,1)S(1)}, bf16[128,1536]{1,0:T(8,128)(2,1)S(1)}, u32[]{:S(2)}, u32[]{:S(2)}) collective-permute-start(bf16[128,1536]{1,0:T(8,128)(2,1)S(1)} %collective-permute-done.5.refs_4_), channel_id=1, source_target_pairs={{0,96},{1,33},{32,0},{33,65},{64,32},{65,97},{96,64},{97,1},{2,98}... | collective-permute-start | bytes 1179656 | tf_op jit(solution)/shard_map/ppermute | solution.py:33
  29.1 20.4 %collective-permute-start.9 = (bf16[128,3072]{1,0:T(8,128)(2,1)S(1)}, bf16[128,3072]{1,0:T(8,128)(2,1)S(1)}, u32[]{:S(2)}, u32[]{:S(2)}) collective-permute-start(bf16[128,3072]{1,0:T(8,128)(2,1)S(1)} %constant_dynamic-slice_fusion), channel_id=1, source_target_pairs={{0,24},{8,16},{16,8},{24,0},{1,25},{9,17},{17,9},{25,1},{2,26},{10... | collective-permute-start | bytes 2359304 | tf_op jit(solution)/shard_map/ppermute | solution.py:41
  32.1 17.4 %copy-start.8 = (bf16[128,1536]{1,0:T(8,128)(2,1)}, bf16[128,1536]{1,0:T(8,128)(2,1)S(1)}, u32[]{:S(2)}) copy-start(bf16[128,1536]{1,0:T(8,128)(2,1)S(1)} %collective-permute-done.3.refs_2_) | copy-start | bytes 1179652
  32.1 27.6 %collective-permute-start.17 = (bf16[96,6144]{1,0:T(8,128)(2,1)S(1)}, bf16[96,6144]{1,0:T(8,128)(2,1)S(1)}, u32[]{:S(2)}, u32[]{:S(2)}) collective-permute-start(bf16[96,6144]{1,0:T(8,128)(2,1)S(1)} %bitcast.26), channel_id=1, source_target_pairs={{0,8},{8,0},{1,9},{9,1},{2,10},{10,2},{3,11},{11,3},{4,12},{12,4},... | collective-permute-start | bytes 3538952 | tf_op jit(solution)/shard_map/ppermute | solution.py:37
  34.3 15.2 %copy-start.9 = (bf16[128,1536]{1,0:T(8,128)(2,1)}, bf16[128,1536]{1,0:T(8,128)(2,1)S(1)}, u32[]{:S(2)}) copy-start(bf16[128,1536]{1,0:T(8,128)(2,1)S(1)} %collective-permute-done.6.refs_5_) | copy-start | bytes 1179652
  34.3 25.5 %collective-permute-start.15 = (bf16[96,6144]{1,0:T(8,128)(2,1)S(1)}, bf16[96,6144]{1,0:T(8,128)(2,1)}, u32[]{:S(2)}, u32[]{:S(2)}) collective-permute-start(bf16[96,6144]{1,0:T(8,128)(2,1)S(1)} %bitcast.27), channel_id=1, source_target_pairs={{0,6},{1,3},{2,0},{3,5},{4,2},{5,7},{6,4},{7,1},{8,14},{9,11},{10,... | collective-permute-start | bytes 3538952 | tf_op jit(solution)/shard_map/ppermute | solution.py:29
  39.6 9.9 %copy-start.10 = (bf16[128,1536]{1,0:T(8,128)(2,1)}, bf16[128,1536]{1,0:T(8,128)(2,1)S(1)}, u32[]{:S(2)}) copy-start(bf16[128,1536]{1,0:T(8,128)(2,1)S(1)} %collective-permute-done.7.refs_6_) | copy-start | bytes 1179652
  39.6 23.4 %collective-permute-start.13 = (bf16[96,6144]{1,0:T(8,128)(2,1)S(1)}, bf16[96,6144]{1,0:T(8,128)(2,1)}, u32[]{:S(2)}, u32[]{:S(2)}) collective-permute-start(bf16[96,6144]{1,0:T(8,128)(2,1)S(1)} %bitcast.28), channel_id=1, source_target_pairs={{0,1},{1,0},{2,3},{3,2},{4,5},{5,4},{6,7},{7,6},{8,9},{9,8},{10,11... | collective-permute-start | bytes 3538952 | tf_op jit(solution)/shard_map/ppermute | solution.py:49
  49.5 0.9 copy-start.11
  50.4 9.3 %collective-permute-start.4 = (bf16[128,1536]{1,0:T(8,128)(2,1)}, bf16[128,1536]{1,0:T(8,128)(2,1)}, u32[]{:S(2)}, u32[]{:S(2)}) collective-permute-start(bf16[128,1536]{1,0:T(8,128)(2,1)} %collective-permute-done.2.refs_1_), channel_id=1, source_target_pairs={{0,32},{1,97},{32,64},{33,1},{64,96},{65,33},{96,0},{97,65},{2,34}... | collective-permute-start | bytes 1179656 | tf_op jit(solution)/shard_map/ppermute | solution.py:33
  51.5 55.5 %copy-start.1 = (bf16[96,6144]{1,0:T(8,128)(2,1)}, bf16[96,6144]{1,0:T(8,128)(2,1)S(1)}, u32[]{:S(2)}) copy-start(bf16[96,6144]{1,0:T(8,128)(2,1)S(1)} %collective-permute-done.refs_6_.refs_10_.refs_14_) | copy-start | bytes 3538948
  51.5 20.8 %collective-permute-start.10 = (bf16[128,3072]{1,0:T(8,128)(2,1)}, bf16[128,3072]{1,0:T(8,128)(2,1)S(1)}, u32[]{:S(2)}, u32[]{:S(2)}) collective-permute-start(bf16[128,3072]{1,0:T(8,128)(2,1)} %copy-done.11), channel_id=1, source_target_pairs={{0,32},{1,97},{32,64},{33,1},{64,96},{65,33},{96,0},{97,65},{2,34}... | collective-permute-start | bytes 2359304 | tf_op jit(solution)/shard_map/ppermute | solution.py:33
  59.7 12.7 %collective-permute-start.14 = (bf16[96,6144]{1,0:T(8,128)(2,1)S(1)}, bf16[96,6144]{1,0:T(8,128)(2,1)S(1)}, u32[]{:S(2)}, u32[]{:S(2)}) collective-permute-start(bf16[96,6144]{1,0:T(8,128)(2,1)S(1)} %collective-permute-done.refs_6_.refs_10_.refs_14_), channel_id=1, source_target_pairs={{0,1},{1,0},{2,3},{3,2},{4,5},{5,4},{6,7},{7,6},{8,9},{9,8},{10,11... | collective-permute-start | bytes 3538952 | tf_op jit(solution)/shard_map/ppermute | solution.py:49
  59.7 47.3 %copy-start.2 = (bf16[96,6144]{1,0:T(8,128)(2,1)}, bf16[96,6144]{1,0:T(8,128)(2,1)S(1)}, u32[]{:S(2)}) copy-start(bf16[96,6144]{1,0:T(8,128)(2,1)S(1)} %collective-permute-done.17.refs_10_.refs_14_.refs_18_) | copy-start | bytes 3538948
  59.7 30.2 %collective-permute-start.19 = (bf16[96,6144]{1,0:T(8,128)(2,1)S(1)}, bf16[96,6144]{1,0:T(8,128)(2,1)}, u32[]{:S(2)}, u32[]{:S(2)}) collective-permute-start(bf16[96,6144]{1,0:T(8,128)(2,1)S(1)} %collective-permute-done.refs_6_.refs_10_.refs_14_), channel_id=1, source_target_pairs={{0,2},{1,7},{2,4},{3,1},{4,6},{5,3},{6,0},{7,5},{8,10},{9,15},{10,... | collective-permute-start | bytes 3538952 | tf_op jit(solution)/shard_map/ppermute | solution.py:29
  59.8 30.1 %collective-permute-start.23 = (bf16[96,6144]{1,0:T(8,128)(2,1)S(1)}, bf16[96,6144]{1,0:T(8,128)(2,1)}, u32[]{:S(2)}, u32[]{:S(2)}) collective-permute-start(bf16[96,6144]{1,0:T(8,128)(2,1)S(1)} %collective-permute-done.17.refs_10_.refs_14_.refs_18_), channel_id=1, source_target_pairs={{0,6},{1,3},{2,0},{3,5},{4,2},{5,7},{6,4},{7,1},{8,14},{9,11},{10,... | collective-permute-start | bytes 3538952 | tf_op jit(solution)/shard_map/ppermute | solution.py:29
  63.0 9.3 %collective-permute-start.8 = (bf16[128,1536]{1,0:T(8,128)(2,1)}, bf16[128,1536]{1,0:T(8,128)(2,1)}, u32[]{:S(2)}, u32[]{:S(2)}) collective-permute-start(bf16[128,1536]{1,0:T(8,128)(2,1)} %copy-done.9), channel_id=1, source_target_pairs={{0,32},{1,97},{32,64},{33,1},{64,96},{65,33},{96,0},{97,65},{2,34}... | collective-permute-start | bytes 1179656 | tf_op jit(solution)/shard_map/ppermute | solution.py:33
  72.3 26.2 %collective-permute-start.21 = (bf16[96,6144]{1,0:T(8,128)(2,1)S(1)}, bf16[96,6144]{1,0:T(8,128)(2,1)S(1)}, u32[]{:S(2)}, u32[]{:S(2)}) collective-permute-start(bf16[96,6144]{1,0:T(8,128)(2,1)S(1)} %collective-permute-done.refs_6_.refs_10_.refs_14_), channel_id=1, source_target_pairs={{0,8},{8,0},{1,9},{9,1},{2,10},{10,2},{3,11},{11,3},{4,12},{12,4},... | collective-permute-start | bytes 3538952 | tf_op jit(solution)/shard_map/ppermute | solution.py:37
  72.3 26.2 %copy-start.12 = (bf16[128,3072]{1,0:T(8,128)(2,1)}, bf16[128,3072]{1,0:T(8,128)(2,1)S(1)}, u32[]{:S(2)}) copy-start(bf16[128,3072]{1,0:T(8,128)(2,1)S(1)} %collective-permute-done.10.refs_9_) | copy-start | bytes 2359300
  72.3 26.2 %collective-permute-start.18 = (bf16[96,6144]{1,0:T(8,128)(2,1)S(1)}, bf16[96,6144]{1,0:T(8,128)(2,1)S(1)}, u32[]{:S(2)}, u32[]{:S(2)}) collective-permute-start(bf16[96,6144]{1,0:T(8,128)(2,1)S(1)} %collective-permute-done.17.refs_10_.refs_14_.refs_18_), channel_id=1, source_target_pairs={{0,1},{1,0},{2,3},{3,2},{4,5},{5,4},{6,7},{7,6},{8,9},{9,8},{10,11... | collective-permute-start | bytes 3538952 | tf_op jit(solution)/shard_map/ppermute | solution.py:49
  72.4 26.1 %copy-start.3 = (bf16[96,6144]{1,0:T(8,128)(2,1)}, bf16[96,6144]{1,0:T(8,128)(2,1)S(1)}, u32[]{:S(2)}) copy-start(bf16[96,6144]{1,0:T(8,128)(2,1)S(1)} %collective-permute-done.14.refs_7_.refs_11_.refs_15_) | copy-start | bytes 3538948
  72.5 29.6 %collective-permute-start.16 = (bf16[96,6144]{1,0:T(8,128)(2,1)}, bf16[96,6144]{1,0:T(8,128)(2,1)}, u32[]{:S(2)}, u32[]{:S(2)}) collective-permute-start(bf16[96,6144]{1,0:T(8,128)(2,1)} %collective-permute-done.15.refs_8_.refs_12_.refs_16_), channel_id=1, source_target_pairs={{0,1},{1,0},{2,3},{3,2},{4,5},{5,4},{6,7},{7,6},{8,9},{9,8},{10,11... | collective-permute-start | bytes 3538952 | tf_op jit(solution)/shard_map/ppermute | solution.py:49
  89.9 15.9 %collective-permute-start.20 = (bf16[96,6144]{1,0:T(8,128)(2,1)}, bf16[96,6144]{1,0:T(8,128)(2,1)}, u32[]{:S(2)}, u32[]{:S(2)}) collective-permute-start(bf16[96,6144]{1,0:T(8,128)(2,1)} %collective-permute-done.19.refs_16_.refs_20_), channel_id=1, source_target_pairs={{0,1},{1,0},{2,3},{3,2},{4,5},{5,4},{6,7},{7,6},{8,9},{9,8},{10,11... | collective-permute-start | bytes 3538952 | tf_op jit(solution)/shard_map/ppermute | solution.py:49
  89.9 16.5 %collective-permute-start.25 = (bf16[96,6144]{1,0:T(8,128)(2,1)}, bf16[96,6144]{1,0:T(8,128)(2,1)}, u32[]{:S(2)}, u32[]{:S(2)}) collective-permute-start(bf16[96,6144]{1,0:T(8,128)(2,1)} %collective-permute-done.23.refs_20_.refs_24_), channel_id=1, source_target_pairs={{0,6},{1,3},{2,0},{3,5},{4,2},{5,7},{6,4},{7,1},{8,14},{9,11},{10,... | collective-permute-start | bytes 3538952 | tf_op jit(solution)/shard_map/ppermute | solution.py:29
  98.5 21.3 %copy-start.4 = (bf16[96,6144]{1,0:T(8,128)(2,1)}, bf16[96,6144]{1,0:T(8,128)(2,1)S(1)}, u32[]{:S(2)}) copy-start(bf16[96,6144]{1,0:T(8,128)(2,1)S(1)} %collective-permute-done.21.refs_18_.refs_22_) | copy-start | bytes 3538948
  98.5 21.3 %collective-permute-start.22 = (bf16[96,6144]{1,0:T(8,128)(2,1)S(1)}, bf16[96,6144]{1,0:T(8,128)(2,1)}, u32[]{:S(2)}, u32[]{:S(2)}) collective-permute-start(bf16[96,6144]{1,0:T(8,128)(2,1)S(1)} %collective-permute-done.21.refs_18_.refs_22_), channel_id=1, source_target_pairs={{0,1},{1,0},{2,3},{3,2},{4,5},{5,4},{6,7},{7,6},{8,9},{9,8},{10,11... | collective-permute-start | bytes 3538952 | tf_op jit(solution)/shard_map/ppermute | solution.py:49
  98.6 1.1 copy-start.5
  99.7 23.0 %collective-permute-start.24 = (bf16[96,6144]{1,0:T(8,128)(2,1)}, bf16[96,6144]{1,0:T(8,128)(2,1)}, u32[]{:S(2)}, u32[]{:S(2)}) collective-permute-start(bf16[96,6144]{1,0:T(8,128)(2,1)} %collective-permute-done.23.refs_20_.refs_24_), channel_id=1, source_target_pairs={{0,1},{1,0},{2,3},{3,2},{4,5},{5,4},{6,7},{7,6},{8,9},{9,8},{10,11... | collective-permute-start | bytes 3538952 | tf_op jit(solution)/shard_map/ppermute | solution.py:49
  102.0 17.8 %copy-start.13 = (f32[8,1,512]{2,1,0:T(1,128)S(1)}, f32[8,1,512]{2,1,0:T(1,128)}, u32[]{:S(2)}) copy-start(f32[8,1,512]{2,1,0:T(1,128)} %get-tuple-element.27.refs_12_.refs_8_.refs_5_) | copy-start | bytes 49156
  102.0 36.2 %collective-permute-start.11 = (bf16[128,3072]{1,0:T(8,128)(2,1)}, bf16[128,3072]{1,0:T(8,128)(2,1)}, u32[]{:S(2)}, u32[]{:S(2)}) collective-permute-start(bf16[128,3072]{1,0:T(8,128)(2,1)} %copy-done.11), channel_id=1, source_target_pairs={{0,96},{1,33},{32,0},{33,65},{64,32},{65,97},{96,64},{97,1},{2,98}... | collective-permute-start | bytes 2359304 | tf_op jit(solution)/shard_map/ppermute | solution.py:33
  105.7 32.6 %collective-permute-start.12 = (bf16[128,3072]{1,0:T(8,128)(2,1)}, bf16[128,3072]{1,0:T(8,128)(2,1)}, u32[]{:S(2)}, u32[]{:S(2)}) collective-permute-start(bf16[128,3072]{1,0:T(8,128)(2,1)} %copy-done.12), channel_id=1, source_target_pairs={{0,32},{1,97},{32,64},{33,1},{64,96},{65,33},{96,0},{97,65},{2,34}... | collective-permute-start | bytes 2359304 | tf_op jit(solution)/shard_map/ppermute | solution.py:33
  106.4 31.9 %collective-permute-start.26 = (bf16[96,6144]{1,0:T(8,128)(2,1)}, bf16[96,6144]{1,0:T(8,128)(2,1)}, u32[]{:S(2)}, u32[]{:S(2)}) collective-permute-start(bf16[96,6144]{1,0:T(8,128)(2,1)} %collective-permute-done.25.refs_26_), channel_id=1, source_target_pairs={{0,1},{1,0},{2,3},{3,2},{4,5},{5,4},{6,7},{7,6},{8,9},{9,8},{10,11... | collective-permute-start | bytes 3538952 | tf_op jit(solution)/shard_map/ppermute | solution.py:49
  119.9 36.0 %collective-permute-start.28 = (f32[8,1,512]{2,1,0:T(1,128)S(1)}, f32[8,1,512]{2,1,0:T(1,128)S(1)}, u32[]{:S(2)}, u32[]{:S(2)}) collective-permute-start(f32[8,1,512]{2,1,0:T(1,128)S(1)} %copy-done.13), channel_id=1, source_target_pairs={{0,24},{8,16},{16,8},{24,0},{1,25},{9,17},{17,9},{25,1},{2,26},{10... | collective-permute-start | bytes 49160 | tf_op jit(solution)/shard_map/ppermute | solution.py:41
  155.9 0.6 copy-start.14
  156.5 3.8 %copy-start.17 = (bf16[4,128,512]{2,1,0:T(8,128)(2,1)S(1)}, bf16[4,128,512]{2,1,0:T(8,128)(2,1)}, u32[]{:S(2)}) copy-start(bf16[4,128,512]{2,1,0:T(8,128)(2,1)} %get-tuple-element.26) | copy-start | bytes 1572868
  159.8 51.9 %collective-permute-start.29 = (bf16[4,128,512]{2,1,0:T(8,128)(2,1)}, bf16[4,128,512]{2,1,0:T(8,128)(2,1)S(1)}, u32[]{:S(2)}, u32[]{:S(2)}) collective-permute-start(bf16[4,128,512]{2,1,0:T(8,128)(2,1)} %intra.3), channel_id=1, source_target_pairs={{0,24},{8,16},{16,8},{24,0},{1,25},{9,17},{17,9},{25,1},{2,26},{10... | collective-permute-start | bytes 1572872 | tf_op jit(solution)/shard_map/ppermute | solution.py:41
  160.3 51.4 %collective-permute-start.27 = (bf16[4,128,512]{2,1,0:T(8,128)(2,1)S(1)}, bf16[4,128,512]{2,1,0:T(8,128)(2,1)S(1)}, u32[]{:S(2)}, u32[]{:S(2)}) collective-permute-start(bf16[4,128,512]{2,1,0:T(8,128)(2,1)S(1)} %copy-done.17), channel_id=1, source_target_pairs={{0,24},{8,16},{16,8},{24,0},{1,25},{9,17},{17,9},{25,1},{2,26},{10... | collective-permute-start | bytes 1572872 | tf_op jit(solution)/shard_map/ppermute | solution.py:41
  163.0 23.2 %all-to-all-start = ((f32[32,1,128]{2,1,0:T(1,128)}), f32[32,1,128]{2,1,0:T(1,128)S(1)}, u32[]{:S(2)}, u32[]{:S(2)}) async-start(f32[32,1,128]{2,1,0:T(1,128)} %get-tuple-element.30), calls=%async_computation | async-start | bytes 32768 | tf_op jit(solution)/shard_map/all_to_all | solution.py:45
  199.0 12.7 %all-to-all-start.2 = ((bf16[32,32,128]{2,1,0:T(8,128)(2,1)}), bf16[32,32,128]{2,1,0:T(8,128)(2,1)S(1)}, u32[]{:S(2)}, u32[]{:S(2)}) async-start(bf16[32,32,128]{2,1,0:T(8,128)(2,1)} %carries.1), calls=%async_computation.2 | async-start | bytes 524288 | tf_op jit(solution)/shard_map/all_to_all | solution.py:45

commit v6 on v5

--- a/solution.py
+++ b/solution.py
@@ -142,16 +142,16 @@
         rows = len(members) * UNIT
         scratch.append(pltpu.VMEM((8 if kind in ("start", "go") else rows, TOK), F32))
         if kind in ("start", "go"):
-            out_specs.append(pl.BlockSpec((rows, TOK), lambda k, s: (0, 0)))
-            out_shape.append(jax.ShapeDtypeStruct((rows, TOK), F32))
+            out_specs.append(pl.BlockSpec(memory_space=pltpu.VMEM))
+            out_shape.append(pltpu.VMEM((rows, TOK), F32))
     if after:
         out_specs.append(pl.BlockSpec((16 * UNIT, TOK), lambda k, s: (0, 0)))
         out_specs.append(pl.BlockSpec((4, 128, TOK), lambda k, s: (0, 0, 0)))
         out_shape.append(jax.ShapeDtypeStruct((16 * UNIT, TOK), BF16))
         out_shape.append(jax.ShapeDtypeStruct((4, 128, TOK), BF16))
     args = [scalars, here, *[v for quarters in cuts for v in quarters], *[w for w, _ in units]]
-    in_specs += [pl.BlockSpec(v.shape, lambda k, s: (0, 0)) for v in partials]
-    args += partials
+    in_specs += [pl.BlockSpec(memory_space=pltpu.VMEM)] * len(partials)
+    args += [near(v) for v in partials]
     aliases = {}
     if held is not None:
         in_specs.append(pl.BlockSpec(memory_space=pl.ANY))
@@ -169,6 +169,7 @@
         ),
         out_shape=out_shape,
         input_output_aliases=aliases,
+        compiler_params=pltpu.CompilerParams(vmem_limit_bytes=44 * 2**20),
         cost_estimate=pl.CostEstimate(
             flops=2 * products * KB,
             bytes_accessed=2 * DIM * len(units) * UNIT,

time: 217 us -> 213 us (0.982)
  Pallas kernels: 62.8 us -> 55.5 us
  local copies, waits for them, and re-layouts: 5.71 us -> 10.8 us
    pallas_call x3, Pallas kernels: 46 us -> 38.8 us  [project(): pl.pallas_call(kernel, grid_spec=pltpu.PrefetchScalarGridSpec(num_scalar_...]
    unnamed x36 -> x44, local copies, waits for them, and re-layouts: 2.65 us -> 8.22 us
    ppermute x5, waiting for transfers between devices: 17.6 us -> 15.4 us  [y_move(): return lax.ppermute(v, ('y', 'c'), ring_pairs(step))]
  transfers between devices with their start and end apart: 32 -> 32, of which waited for: 11 -> 12; matrix products, arithmetic and copies ran while one was open for 1% -> 1% of each run, Pallas kernels for 26% -> 23%
where the time goes in v6:
time: 213 us; the launch traced here: 211 us
  waiting for transfers between devices  87.5 us (41%)
  Pallas kernels  55.5 us (26%)
  starting transfers between devices  45.3 us (21%)
  blocking collectives  11.3 us (5%)
  local copies, waits for them, and re-layouts  10.8 us (5%)
    pallas_call x3, Pallas kernels, project(): pl.pallas_call(kernel, grid_spec=pltpu.PrefetchScalarGridSpec(num_scalar_...  38.8 us
    ppermute x6, waiting for transfers between devices, z_out(): return lax.ppermute(v, ('zh', 'zl'), [(i, 3 - i) for i in range(4)])  23.3 us
    all_to_all x2, waiting for transfers between devices, exchange(): return lax.all_to_all(v, axes, 0, 0, tiled=True)  21.5 us
    ppermute x9, waiting for transfers between devices, x_move(): return lax.ppermute(v, ('x', 'c'), ring_pairs(step))  16.9 us
    ppermute x5, waiting for transfers between devices, y_move(): return lax.ppermute(v, ('y', 'c'), ring_pairs(step))  15.4 us
    ppermute x6, starting transfers between devices, z_out(): return lax.ppermute(v, ('zh', 'zl'), [(i, 3 - i) for i in range(4)])  12.9 us
    ppermute x9, starting transfers between devices, x_move(): return lax.ppermute(v, ('x', 'c'), ring_pairs(step))  12.7 us
    all_to_all x1, blocking collectives, exchange(): return lax.all_to_all(v, axes, 0, 0, tiled=True)  11.3 us
  transfers between devices with their start and end apart: 32, of which 12 were waited for; matrix products, arithmetic and copies ran while one was open for 1% of the time, Pallas kernels for 23%

profile of v6, /device:TPU:0, one launch (start us, length us, event | category | flops | bytes accessed | tf_op | source)
XLA Modules:
  0.0 211.2 jit_solution(11277117994101545327)
XLA Ops:
  0.0 1.3 constant_dynamic-slice_fusion.1
  1.3 0.0 copy-start.20
  1.3 0.0 copy-start.21
  1.3 4.2 %collective-permute-start.1 = (bf16[128,1536]{1,0:T(8,128)(2,1)S(1)}, bf16[128,1536]{1,0:T(8,128)(2,1)S(1)}, u32[]{:S(2)}, u32[]{:S(2)}) collective-permute-start(bf16[128,1536]{1,0:T(8,128)(2,1)S(1)} %get-tuple-element.32), channel_id=1, source_target_pairs={{0,24},{8,16},{16,8},{24,0},{1,25},{9,17},{17,9},{25,1},{2,26},{10... | collective-permute-start | bytes 1179656 | tf_op jit(solution)/shard_map/ppermute | solution.py:41
  5.5 0.1 collective-permute-start.5
  5.6 9.9 %collective-permute-done.1.refs_0_ = bf16[128,1536]{1,0:T(8,128)(2,1)S(1)} collective-permute-done((bf16[128,1536]{1,0:T(8,128)(2,1)S(1)}, bf16[128,1536]{1,0:T(8,128)(2,1)S(1)}, u32[]{:S(2)}, u32[]{:S(2)}) %collective-permute-start.1) | collective-permute-done | bytes 393248 | tf_op jit(solution)/shard_map/ppermute | solution.py:41
  15.5 1.5 collective-permute-start.2
  17.0 1.7 collective-permute-start.3
  18.7 4.3 %collective-permute-done.5.refs_4_ = bf16[128,1536]{1,0:T(8,128)(2,1)S(1)} collective-permute-done((bf16[128,1536]{1,0:T(8,128)(2,1)S(1)}, bf16[128,1536]{1,0:T(8,128)(2,1)S(1)}, u32[]{:S(2)}, u32[]{:S(2)}) %collective-permute-start.5) | collective-permute-done | bytes 393248 | tf_op jit(solution)/shard_map/ppermute | solution.py:41
  23.1 1.5 collective-permute-start.6
  24.6 1.6 collective-permute-start
  26.1 1.7 collective-permute-start.7
  27.9 1.2 constant_dynamic-slice_fusion
  29.1 0.0 collective-permute-done.2.refs_1_
  29.1 3.0 %collective-permute-start.9 = (bf16[128,3072]{1,0:T(8,128)(2,1)S(1)}, bf16[128,3072]{1,0:T(8,128)(2,1)}, u32[]{:S(2)}, u32[]{:S(2)}) collective-permute-start(bf16[128,3072]{1,0:T(8,128)(2,1)S(1)} %constant_dynamic-slice_fusion), channel_id=1, source_target_pairs={{0,24},{8,16},{16,8},{24,0},{1,25},{9,17},{17,9},{25,1},{2,26},{10... | collective-permute-start | bytes 2359304 | tf_op jit(solution)/shard_map/ppermute | solution.py:41
  32.1 0.0 collective-permute-done.3.refs_2_
  32.1 0.7 copy-done.9
  32.9 1.5 collective-permute-done.6.refs_5_
  34.4 5.3 %collective-permute-start.15 = (bf16[96,6144]{1,0:T(8,128)(2,1)S(1)}, bf16[96,6144]{1,0:T(8,128)(2,1)S(1)}, u32[]{:S(2)}, u32[]{:S(2)}) collective-permute-start(bf16[96,6144]{1,0:T(8,128)(2,1)S(1)} %bitcast.25), channel_id=1, source_target_pairs={{0,6},{1,3},{2,0},{3,5},{4,2},{5,7},{6,4},{7,1},{8,14},{9,11},{10,... | collective-permute-start | bytes 3538952 | tf_op jit(solution)/shard_map/ppermute | solution.py:29
  39.7 0.8 copy-done.11
  40.5 9.1 %collective-permute-done.9.refs_8_ = bf16[128,3072]{1,0:T(8,128)(2,1)} collective-permute-done((bf16[128,3072]{1,0:T(8,128)(2,1)S(1)}, bf16[128,3072]{1,0:T(8,128)(2,1)}, u32[]{:S(2)}, u32[]{:S(2)}) %collective-permute-start.9) | collective-permute-done | bytes 786464 | tf_op jit(solution)/shard_map/ppermute | solution.py:41
  49.6 0.5 collective-permute-start.4
  50.1 0.1 stack.83.s_ref
  50.2 1.6 collective-permute-start.10
  51.7 0.5 broadcast_select_fusion.n_ref
  52.3 6.6 %collective-permute-done.4.refs_3_ = bf16[128,1536]{1,0:T(8,128)(2,1)} collective-permute-done((bf16[128,1536]{1,0:T(8,128)(2,1)}, bf16[128,1536]{1,0:T(8,128)(2,1)}, u32[]{:S(2)}, u32[]{:S(2)}) %collective-permute-start.4) | collective-permute-done | bytes 393248 | tf_op jit(solution)/shard_map/ppermute | solution.py:33
  58.9 1.1 collective-permute-done.17.refs_10_.refs_14_.refs_18_
  60.0 3.2 %collective-permute-start.23 = (bf16[96,6144]{1,0:T(8,128)(2,1)}, bf16[96,6144]{1,0:T(8,128)(2,1)}, u32[]{:S(2)}, u32[]{:S(2)}) collective-permute-start(bf16[96,6144]{1,0:T(8,128)(2,1)} %collective-permute-done.17.refs_10_.refs_14_.refs_18_), channel_id=1, source_target_pairs={{0,6},{1,3},{2,0},{3,5},{4,2},{5,7},{6,4},{7,1},{8,14},{9,11},{10,... | collective-permute-start | bytes 3538952 | tf_op jit(solution)/shard_map/ppermute | solution.py:29
  63.2 0.5 collective-permute-start.8
  63.7 8.7 %collective-permute-done.8.refs_7_ = bf16[128,1536]{1,0:T(8,128)(2,1)S(1)} collective-permute-done((bf16[128,1536]{1,0:T(8,128)(2,1)}, bf16[128,1536]{1,0:T(8,128)(2,1)S(1)}, u32[]{:S(2)}, u32[]{:S(2)}) %collective-permute-start.8) | collective-permute-done | bytes 393248 | tf_op jit(solution)/shard_map/ppermute | solution.py:33
  72.4 0.8 copy-done.13
  73.2 0.3 collective-permute-start.21
  73.5 1.0 copy-done.3
  74.5 0.5 collective-permute-start.16
  75.0 14.3 %collective-permute-done.19.refs_16_.refs_20_ = bf16[96,6144]{1,0:T(8,128)(2,1)} collective-permute-done((bf16[96,6144]{1,0:T(8,128)(2,1)S(1)}, bf16[96,6144]{1,0:T(8,128)(2,1)}, u32[]{:S(2)}, u32[]{:S(2)}) %collective-permute-start.19) | collective-permute-done | bytes 1179680 | tf_op jit(solution)/shard_map/ppermute | solution.py:29
  89.3 0.1 collective-permute-start.25
  89.3 9.3 %collective-permute-done.21.refs_18_.refs_22_ = bf16[96,6144]{1,0:T(8,128)(2,1)} collective-permute-done((bf16[96,6144]{1,0:T(8,128)(2,1)S(1)}, bf16[96,6144]{1,0:T(8,128)(2,1)}, u32[]{:S(2)}, u32[]{:S(2)}) %collective-permute-start.21) | collective-permute-done | bytes 1179680 | tf_op jit(solution)/shard_map/ppermute | solution.py:37
  98.6 0.5 collective-permute-start.24
  99.1 1.9 rates.1
  101.0 3.7 %collective-permute-start.11 = (bf16[128,3072]{1,0:T(8,128)(2,1)}, bf16[128,3072]{1,0:T(8,128)(2,1)S(1)}, u32[]{:S(2)}, u32[]{:S(2)}) collective-permute-start(bf16[128,3072]{1,0:T(8,128)(2,1)} %collective-permute-done.9.refs_8_), channel_id=1, source_target_pairs={{0,96},{1,33},{32,0},{33,65},{64,32},{65,97},{96,64},{97,1},{2,98}... | collective-permute-start | bytes 2359304 | tf_op jit(solution)/shard_map/ppermute | solution.py:33
  104.7 1.1 collective-permute-done.25.refs_26_
  105.8 0.6 collective-permute-start.26
  106.4 1.3 copy-done.4
  107.6 1.0 copy-done.6
  108.6 1.0 copy-done.10
  109.6 10.7 %project.3 = (bf16[1536,512]{1,0:T(8,128)(2,1)}, f32[768,512]{1,0:T(8,128)S(1)}) custom-call(s32[20]{0:T(128)S(1)} %stack.83.s_ref, bf16[512,6144]{1,0:T(8,128)(2,1)} %x_ref.5, bf16[128,1536]{1,0:T(8,128)(2,1)S(1)} %copy-done.6, bf16[128,1536]{1,0:T(8,128)(2,1)} %collective-permute-done.2.refs_1_, bf16[128,1536]{1,0:T(8,128)(2,1)S(1)} %copy-done.10, ...), custom_call_target="tpu_custom_call" | custom-call | flops 6039797760 | bytes 9437184 | tf_op jit(solution)/shard_map/project/pallas_call | solution.py:161
  120.4 2.3 %collective-permute-start.28 = (f32[8,1,512]{2,1,0:T(1,128)S(1)}, f32[8,1,512]{2,1,0:T(1,128)S(1)}, u32[]{:S(2)}, u32[]{:S(2)}) collective-permute-start(f32[8,1,512]{2,1,0:T(1,128)S(1)} %copy-done.18), channel_id=1, source_target_pairs={{0,24},{8,16},{16,8},{24,0},{1,25},{9,17},{17,9},{25,1},{2,26},{10... | collective-permute-start | bytes 49160 | tf_op jit(solution)/shard_map/ppermute | solution.py:41
  122.7 0.0 copy-start.16
  122.7 12.7 %project.4 = (bf16[1536,512]{1,0:T(8,128)(2,1)}, f32[576,512]{1,0:T(8,128)S(1)}, f32[768,512]{1,0:T(8,128)S(1)}) custom-call(s32[20]{0:T(128)S(1)} %stack.83.s_ref, bf16[512,6144]{1,0:T(8,128)(2,1)} %x_ref.5, bf16[128,1536]{1,0:T(8,128)(2,1)S(1)} %copy-done.6, bf16[128,1536]{1,0:T(8,128)(2,1)} %collective-permute-done.2.refs_1_, ...), custom_call_target="tpu_custom_call", output_to_operand_aliasing={{0}: (25, {})} | custom-call | flops 6643777536 | bytes 16515072 | tf_op jit(solution)/shard_map/project/pallas_call | solution.py:161
  135.4 1.0 copy-done.17
  136.4 15.4 %project.5 = (bf16[1536,512]{1,0:T(8,128)(2,1)}, bf16[1536,512]{1,0:T(8,128)(2,1)}, bf16[4,128,512]{2,1,0:T(8,128)(2,1)}) custom-call(s32[20]{0:T(128)S(1)} %stack.83.s_ref, bf16[512,6144]{1,0:T(8,128)(2,1)} %x_ref.5, bf16[128,1536]{1,0:T(8,128)(2,1)S(1)} %copy-done.6, ...), custom_call_target="tpu_custom_call", output_to_operand_aliasing={{0}: (32, {})} | custom-call | flops 6643777536 | bytes 18874368 | tf_op jit(solution)/shard_map/project/pallas_call | solution.py:161
  151.9 0.6 copy-done.19
  152.5 3.3 %intra.3 = bf16[4,128,512]{2,1,0:T(8,128)(2,1)} custom-call(s32[1]{0:T(128)} %bitcast.z_ref, bf16[1536,512]{1,0:T(8,128)(2,1)} %get-tuple-element.28.refs_0_.refs_1_.refs_2_.refs_3_.refs_4_.refs_5_.refs_6_.refs_7_.refs_8_.refs_9_.refs_10_.refs_11_.refs_12_.refs_13_.refs_14_.refs_15_.refs_16_, ...), custom_call_target="tpu_custom_call" | custom-call | tf_op jit(solution)/shard_map/intra/pallas_call | solution.py:272
  155.7 1.0 collective-permute-start.29
  156.8 2.2 %collective-permute-start.27 = (bf16[4,128,512]{2,1,0:T(8,128)(2,1)}, bf16[4,128,512]{2,1,0:T(8,128)(2,1)S(1)}, u32[]{:S(2)}, u32[]{:S(2)}) collective-permute-start(bf16[4,128,512]{2,1,0:T(8,128)(2,1)} %get-tuple-element.26), channel_id=1, source_target_pairs={{0,24},{8,16},{16,8},{24,0},{1,25},{9,17},{17,9},{25,1},{2,26},{10... | collective-permute-start | bytes 1572872 | tf_op jit(solution)/shard_map/ppermute | solution.py:41
  159.0 3.9 %all-to-all-start = ((f32[32,1,128]{2,1,0:T(1,128)}), f32[32,1,128]{2,1,0:T(1,128)S(1)}, u32[]{:S(2)}, u32[]{:S(2)}) async-start(f32[32,1,128]{2,1,0:T(1,128)} %get-tuple-element.30), calls=%async_computation | async-start | bytes 32768 | tf_op jit(solution)/shard_map/all_to_all | solution.py:45
  162.8 3.1 %states.1 = bf16[16,2,32,128]{3,2,1,0:T(8,128)(2,1)} custom-call(s32[1]{0:T(128)} %bitcast.z_ref, bf16[1536,512]{1,0:T(8,128)(2,1)} %get-tuple-element.25.refs_0_.refs_1_.refs_2_.refs_3_.refs_4_.refs_5_.refs_6_.refs_7_.refs_8_.refs_9_.refs_10_.refs_11_, ...), custom_call_target="tpu_custom_call" | custom-call | tf_op jit(solution)/shard_map/states/pallas_call | solution.py:239
  166.0 16.3 %all-to-all-done.d_ref = f32[32,1,128]{2,1,0:T(1,128)S(1)} async-done(((f32[32,1,128]{2,1,0:T(1,128)}), f32[32,1,128]{2,1,0:T(1,128)S(1)}, u32[]{:S(2)}, u32[]{:S(2)}) %all-to-all-start) | async-done | bytes 16416 | tf_op jit(solution)/shard_map/all_to_all | solution.py:45
  182.2 11.3 %all_to_all.15.s_ref = bf16[16,2,32,128]{3,2,1,0:T(8,128)(2,1)S(1)} all-to-all(bf16[16,2,32,128]{3,2,1,0:T(8,128)(2,1)} %states.1), channel_id=1, replica_groups=mesh['x'=4,'zh'=2,'zl'=2,'y'=4,'c'=2] {'zl','y','c'}, dimensions={0} | all-to-all | bytes 524288 | tf_op jit(solution)/shard_map/all_to_all | solution.py:45
  193.5 1.5 carries.1
  195.0 3.9 %all-to-all-start.2 = ((bf16[32,32,128]{2,1,0:T(8,128)(2,1)}), bf16[32,32,128]{2,1,0:T(8,128)(2,1)S(1)}, u32[]{:S(2)}, u32[]{:S(2)}) async-start(bf16[32,32,128]{2,1,0:T(8,128)(2,1)} %carries.1), calls=%async_computation.2 | async-start | bytes 524288 | tf_op jit(solution)/shard_map/all_to_all | solution.py:45
  198.9 3.5 %intra.2.refs_6_ = f32[4,128,512]{2,1,0:T(8,128)} custom-call(s32[1]{0:T(128)} %bitcast.z_ref, bf16[1536,512]{1,0:T(8,128)(2,1)} %get-tuple-element.25.refs_0_.refs_1_.refs_2_.refs_3_.refs_4_.refs_5_.refs_6_.refs_7_.refs_8_.refs_9_.refs_10_.refs_11_, ...), custom_call_target="tpu_custom_call" | custom-call | tf_op jit(solution)/shard_map/intra/pallas_call | solution.py:272
  202.4 5.3 %all-to-all-done.2.refs_8_ = bf16[32,32,128]{2,1,0:T(8,128)(2,1)S(1)} async-done(((bf16[32,32,128]{2,1,0:T(8,128)(2,1)}), bf16[32,32,128]{2,1,0:T(8,128)(2,1)S(1)}, u32[]{:S(2)}, u32[]{:S(2)}) %all-to-all-start.2) | async-done | bytes 262176 | tf_op jit(solution)/shard_map/all_to_all | solution.py:45
  207.7 3.5 %finish.1 = bf16[512,1024]{1,0:T(8,128)(2,1)} custom-call(s32[1]{0:T(128)} %bitcast.z_ref, bf16[1536,512]{1,0:T(8,128)(2,1)} %get-tuple-element.25.refs_0_.refs_1_.refs_2_.refs_3_.refs_4_.refs_5_.refs_6_.refs_7_.refs_8_.refs_9_.refs_10_.refs_11_, ...), custom_call_target="tpu_custom_call" | custom-call | tf_op jit(solution)/shard_map/finish/pallas_call | solution.py:316
  (58 shorter events, 0.1 us)
Async XLA Ops:
  0.0 24.6 %copy-start = (bf16[6144,96]{0,1:T(8,128)(2,1)S(1)}, bf16[6144,96]{0,1:T(8,128)(2,1)}, u32[]{:S(2)}) copy-start(bf16[6144,96]{0,1:T(8,128)(2,1)} %param.7) | copy-start | bytes 3538948
  1.3 50.5 %copy-start.20 = (s32[8]{0:T(128)S(1)}, s32[8]{0:T(128)}, u32[]{:S(2)}) copy-start(s32[8]{0:T(128)} %constant.101.clone) | copy-start | bytes 100
  1.3 50.5 %copy-start.21 = (s32[8]{0:T(128)S(1)}, s32[8]{0:T(128)}, u32[]{:S(2)}) copy-start(s32[8]{0:T(128)} %constant.102.clone) | copy-start | bytes 100
  1.3 14.2 %collective-permute-start.1 = (bf16[128,1536]{1,0:T(8,128)(2,1)S(1)}, bf16[128,1536]{1,0:T(8,128)(2,1)S(1)}, u32[]{:S(2)}, u32[]{:S(2)}) collective-permute-start(bf16[128,1536]{1,0:T(8,128)(2,1)S(1)} %get-tuple-element.32), channel_id=1, source_target_pairs={{0,24},{8,16},{16,8},{24,0},{1,25},{9,17},{17,9},{25,1},{2,26},{10... | collective-permute-start | bytes 1179656 | tf_op jit(solution)/shard_map/ppermute | solution.py:41
  5.5 17.5 %collective-permute-start.5 = (bf16[128,1536]{1,0:T(8,128)(2,1)S(1)}, bf16[128,1536]{1,0:T(8,128)(2,1)S(1)}, u32[]{:S(2)}, u32[]{:S(2)}) collective-permute-start(bf16[128,1536]{1,0:T(8,128)(2,1)S(1)} %get-tuple-element.31), channel_id=1, source_target_pairs={{0,24},{8,16},{16,8},{24,0},{1,25},{9,17},{17,9},{25,1},{2,26},{10... | collective-permute-start | bytes 1179656 | tf_op jit(solution)/shard_map/ppermute | solution.py:41
  15.5 24.2 %copy-start.5 = (bf16[128,1536]{1,0:T(8,128)(2,1)}, bf16[128,1536]{1,0:T(8,128)(2,1)S(1)}, u32[]{:S(2)}) copy-start(bf16[128,1536]{1,0:T(8,128)(2,1)S(1)} %collective-permute-done.1.refs_0_) | copy-start | bytes 1179652
  15.5 13.6 %collective-permute-start.2 = (bf16[128,1536]{1,0:T(8,128)(2,1)S(1)}, bf16[128,1536]{1,0:T(8,128)(2,1)}, u32[]{:S(2)}, u32[]{:S(2)}) collective-permute-start(bf16[128,1536]{1,0:T(8,128)(2,1)S(1)} %collective-permute-done.1.refs_0_), channel_id=1, source_target_pairs={{0,32},{1,97},{32,64},{33,1},{64,96},{65,33},{96,0},{97,65},{2,34}... | collective-permute-start | bytes 1179656 | tf_op jit(solution)/shard_map/ppermute | solution.py:33
  17.0 15.1 %collective-permute-start.3 = (bf16[128,1536]{1,0:T(8,128)(2,1)S(1)}, bf16[128,1536]{1,0:T(8,128)(2,1)S(1)}, u32[]{:S(2)}, u32[]{:S(2)}) collective-permute-start(bf16[128,1536]{1,0:T(8,128)(2,1)S(1)} %collective-permute-done.1.refs_0_), channel_id=1, source_target_pairs={{0,96},{1,33},{32,0},{33,65},{64,32},{65,97},{96,64},{97,1},{2,98}... | collective-permute-start | bytes 1179656 | tf_op jit(solution)/shard_map/ppermute | solution.py:33
  23.1 16.6 %copy-start.7 = (bf16[128,1536]{1,0:T(8,128)(2,1)}, bf16[128,1536]{1,0:T(8,128)(2,1)S(1)}, u32[]{:S(2)}) copy-start(bf16[128,1536]{1,0:T(8,128)(2,1)S(1)} %collective-permute-done.5.refs_4_) | copy-start | bytes 1179652
  23.1 11.3 %collective-permute-start.6 = (bf16[128,1536]{1,0:T(8,128)(2,1)S(1)}, bf16[128,1536]{1,0:T(8,128)(2,1)}, u32[]{:S(2)}, u32[]{:S(2)}) collective-permute-start(bf16[128,1536]{1,0:T(8,128)(2,1)S(1)} %collective-permute-done.5.refs_4_), channel_id=1, source_target_pairs={{0,32},{1,97},{32,64},{33,1},{64,96},{65,33},{96,0},{97,65},{2,34}... | collective-permute-start | bytes 1179656 | tf_op jit(solution)/shard_map/ppermute | solution.py:33
  24.6 25.6 %collective-permute-start = (bf16[96,6144]{1,0:T(8,128)(2,1)S(1)}, bf16[96,6144]{1,0:T(8,128)(2,1)S(1)}, u32[]{:S(2)}, u32[]{:S(2)}) collective-permute-start(bf16[96,6144]{1,0:T(8,128)(2,1)S(1)} %bitcast.23), channel_id=1, source_target_pairs={{0,2},{1,7},{2,4},{3,1},{4,6},{5,3},{6,0},{7,5},{8,10},{9,15},{10,... | collective-permute-start | bytes 3538952 | tf_op jit(solution)/shard_map/ppermute | solution.py:29
  26.1 13.6 %collective-permute-start.7 = (bf16[128,1536]{1,0:T(8,128)(2,1)S(1)}, bf16[128,1536]{1,0:T(8,128)(2,1)S(1)}, u32[]{:S(2)}, u32[]{:S(2)}) collective-permute-start(bf16[128,1536]{1,0:T(8,128)(2,1)S(1)} %collective-permute-done.5.refs_4_), channel_id=1, source_target_pairs={{0,96},{1,33},{32,0},{33,65},{64,32},{65,97},{96,64},{97,1},{2,98}... | collective-permute-start | bytes 1179656 | tf_op jit(solution)/shard_map/ppermute | solution.py:33
  29.1 20.5 %collective-permute-start.9 = (bf16[128,3072]{1,0:T(8,128)(2,1)S(1)}, bf16[128,3072]{1,0:T(8,128)(2,1)}, u32[]{:S(2)}, u32[]{:S(2)}) collective-permute-start(bf16[128,3072]{1,0:T(8,128)(2,1)S(1)} %constant_dynamic-slice_fusion), channel_id=1, source_target_pairs={{0,24},{8,16},{16,8},{24,0},{1,25},{9,17},{17,9},{25,1},{2,26},{10... | collective-permute-start | bytes 2359304 | tf_op jit(solution)/shard_map/ppermute | solution.py:41
  32.1 0.8 copy-start.9
  32.9 27.1 %collective-permute-start.17 = (bf16[96,6144]{1,0:T(8,128)(2,1)S(1)}, bf16[96,6144]{1,0:T(8,128)(2,1)}, u32[]{:S(2)}, u32[]{:S(2)}) collective-permute-start(bf16[96,6144]{1,0:T(8,128)(2,1)S(1)} %bitcast.24), channel_id=1, source_target_pairs={{0,8},{8,0},{1,9},{9,1},{2,10},{10,2},{3,11},{11,3},{4,12},{12,4},... | collective-permute-start | bytes 3538952 | tf_op jit(solution)/shard_map/ppermute | solution.py:37
  34.4 25.5 %collective-permute-start.15 = (bf16[96,6144]{1,0:T(8,128)(2,1)S(1)}, bf16[96,6144]{1,0:T(8,128)(2,1)S(1)}, u32[]{:S(2)}, u32[]{:S(2)}) collective-permute-start(bf16[96,6144]{1,0:T(8,128)(2,1)S(1)} %bitcast.25), channel_id=1, source_target_pairs={{0,6},{1,3},{2,0},{3,5},{4,2},{5,7},{6,4},{7,1},{8,14},{9,11},{10,... | collective-permute-start | bytes 3538952 | tf_op jit(solution)/shard_map/ppermute | solution.py:29
  39.7 0.8 copy-start.11
  40.5 22.7 %collective-permute-start.13 = (bf16[96,6144]{1,0:T(8,128)(2,1)S(1)}, bf16[96,6144]{1,0:T(8,128)(2,1)}, u32[]{:S(2)}, u32[]{:S(2)}) collective-permute-start(bf16[96,6144]{1,0:T(8,128)(2,1)S(1)} %bitcast.26), channel_id=1, source_target_pairs={{0,1},{1,0},{2,3},{3,2},{4,5},{5,4},{6,7},{7,6},{8,9},{9,8},{10,11... | collective-permute-start | bytes 3538952 | tf_op jit(solution)/shard_map/ppermute | solution.py:49
  49.6 9.3 %collective-permute-start.4 = (bf16[128,1536]{1,0:T(8,128)(2,1)}, bf16[128,1536]{1,0:T(8,128)(2,1)}, u32[]{:S(2)}, u32[]{:S(2)}) collective-permute-start(bf16[128,1536]{1,0:T(8,128)(2,1)} %collective-permute-done.2.refs_1_), channel_id=1, source_target_pairs={{0,32},{1,97},{32,64},{33,1},{64,96},{65,33},{96,0},{97,65},{2,34}... | collective-permute-start | bytes 1179656 | tf_op jit(solution)/shard_map/ppermute | solution.py:33
  50.2 70.2 %copy-start.1 = (bf16[96,6144]{1,0:T(8,128)(2,1)}, bf16[96,6144]{1,0:T(8,128)(2,1)S(1)}, u32[]{:S(2)}) copy-start(bf16[96,6144]{1,0:T(8,128)(2,1)S(1)} %collective-permute-done.refs_6_.refs_10_.refs_14_) | copy-start | bytes 3538948
  50.2 23.3 %collective-permute-start.10 = (bf16[128,3072]{1,0:T(8,128)(2,1)}, bf16[128,3072]{1,0:T(8,128)(2,1)S(1)}, u32[]{:S(2)}, u32[]{:S(2)}) collective-permute-start(bf16[128,3072]{1,0:T(8,128)(2,1)} %collective-permute-done.9.refs_8_), channel_id=1, source_target_pairs={{0,32},{1,97},{32,64},{33,1},{64,96},{65,33},{96,0},{97,65},{2,34}... | collective-permute-start | bytes 2359304 | tf_op jit(solution)/shard_map/ppermute | solution.py:33
  58.9 14.6 %collective-permute-start.14 = (bf16[96,6144]{1,0:T(8,128)(2,1)S(1)}, bf16[96,6144]{1,0:T(8,128)(2,1)S(1)}, u32[]{:S(2)}, u32[]{:S(2)}) collective-permute-start(bf16[96,6144]{1,0:T(8,128)(2,1)S(1)} %collective-permute-done.refs_6_.refs_10_.refs_14_), channel_id=1, source_target_pairs={{0,1},{1,0},{2,3},{3,2},{4,5},{5,4},{6,7},{7,6},{8,9},{9,8},{10,11... | collective-permute-start | bytes 3538952 | tf_op jit(solution)/shard_map/ppermute | solution.py:49
  59.9 29.3 %collective-permute-start.19 = (bf16[96,6144]{1,0:T(8,128)(2,1)S(1)}, bf16[96,6144]{1,0:T(8,128)(2,1)}, u32[]{:S(2)}, u32[]{:S(2)}) collective-permute-start(bf16[96,6144]{1,0:T(8,128)(2,1)S(1)} %collective-permute-done.refs_6_.refs_10_.refs_14_), channel_id=1, source_target_pairs={{0,2},{1,7},{2,4},{3,1},{4,6},{5,3},{6,0},{7,5},{8,10},{9,15},{10,... | collective-permute-start | bytes 3538952 | tf_op jit(solution)/shard_map/ppermute | solution.py:29
  60.0 60.4 %copy-start.2 = (bf16[96,6144]{1,0:T(8,128)(2,1)}, bf16[96,6144]{1,0:T(8,128)(2,1)S(1)}, u32[]{:S(2)}) copy-start(bf16[96,6144]{1,0:T(8,128)(2,1)S(1)} %collective-permute-done.15.refs_8_.refs_12_.refs_16_) | copy-start | bytes 3538948
  60.0 29.3 %collective-permute-start.23 = (bf16[96,6144]{1,0:T(8,128)(2,1)}, bf16[96,6144]{1,0:T(8,128)(2,1)}, u32[]{:S(2)}, u32[]{:S(2)}) collective-permute-start(bf16[96,6144]{1,0:T(8,128)(2,1)} %collective-permute-done.17.refs_10_.refs_14_.refs_18_), channel_id=1, source_target_pairs={{0,6},{1,3},{2,0},{3,5},{4,2},{5,7},{6,4},{7,1},{8,14},{9,11},{10,... | collective-permute-start | bytes 3538952 | tf_op jit(solution)/shard_map/ppermute | solution.py:29
  63.2 9.2 %collective-permute-start.8 = (bf16[128,1536]{1,0:T(8,128)(2,1)}, bf16[128,1536]{1,0:T(8,128)(2,1)S(1)}, u32[]{:S(2)}, u32[]{:S(2)}) collective-permute-start(bf16[128,1536]{1,0:T(8,128)(2,1)} %collective-permute-done.6.refs_5_), channel_id=1, source_target_pairs={{0,32},{1,97},{32,64},{33,1},{64,96},{65,33},{96,0},{97,65},{2,34}... | collective-permute-start | bytes 1179656 | tf_op jit(solution)/shard_map/ppermute | solution.py:33
  72.4 0.8 copy-start.13
  73.2 25.4 %collective-permute-start.21 = (bf16[96,6144]{1,0:T(8,128)(2,1)S(1)}, bf16[96,6144]{1,0:T(8,128)(2,1)}, u32[]{:S(2)}, u32[]{:S(2)}) collective-permute-start(bf16[96,6144]{1,0:T(8,128)(2,1)S(1)} %collective-permute-done.refs_6_.refs_10_.refs_14_), channel_id=1, source_target_pairs={{0,8},{8,0},{1,9},{9,1},{2,10},{10,2},{3,11},{11,3},{4,12},{12,4},... | collective-permute-start | bytes 3538952 | tf_op jit(solution)/shard_map/ppermute | solution.py:37
  73.4 25.2 %copy-start.15 = (bf16[128,3072]{1,0:T(8,128)(2,1)}, bf16[128,3072]{1,0:T(8,128)(2,1)S(1)}, u32[]{:S(2)}) copy-start(bf16[128,3072]{1,0:T(8,128)(2,1)S(1)} %collective-permute-done.10.refs_9_) | copy-start | bytes 2359300
  73.4 25.2 %collective-permute-start.18 = (bf16[96,6144]{1,0:T(8,128)(2,1)}, bf16[96,6144]{1,0:T(8,128)(2,1)}, u32[]{:S(2)}, u32[]{:S(2)}) collective-permute-start(bf16[96,6144]{1,0:T(8,128)(2,1)} %collective-permute-done.17.refs_10_.refs_14_.refs_18_), channel_id=1, source_target_pairs={{0,1},{1,0},{2,3},{3,2},{4,5},{5,4},{6,7},{7,6},{8,9},{9,8},{10,11... | collective-permute-start | bytes 3538952 | tf_op jit(solution)/shard_map/ppermute | solution.py:49
  73.5 1.0 copy-start.3
  74.5 26.5 %collective-permute-start.16 = (bf16[96,6144]{1,0:T(8,128)(2,1)S(1)}, bf16[96,6144]{1,0:T(8,128)(2,1)}, u32[]{:S(2)}, u32[]{:S(2)}) collective-permute-start(bf16[96,6144]{1,0:T(8,128)(2,1)S(1)} %collective-permute-done.15.refs_8_.refs_12_.refs_16_), channel_id=1, source_target_pairs={{0,1},{1,0},{2,3},{3,2},{4,5},{5,4},{6,7},{7,6},{8,9},{9,8},{10,11... | collective-permute-start | bytes 3538952 | tf_op jit(solution)/shard_map/ppermute | solution.py:49
  89.3 15.4 %collective-permute-start.20 = (bf16[96,6144]{1,0:T(8,128)(2,1)}, bf16[96,6144]{1,0:T(8,128)(2,1)}, u32[]{:S(2)}, u32[]{:S(2)}) collective-permute-start(bf16[96,6144]{1,0:T(8,128)(2,1)} %collective-permute-done.19.refs_16_.refs_20_), channel_id=1, source_target_pairs={{0,1},{1,0},{2,3},{3,2},{4,5},{5,4},{6,7},{7,6},{8,9},{9,8},{10,11... | collective-permute-start | bytes 3538952 | tf_op jit(solution)/shard_map/ppermute | solution.py:49
  89.3 16.5 %collective-permute-start.25 = (bf16[96,6144]{1,0:T(8,128)(2,1)}, bf16[96,6144]{1,0:T(8,128)(2,1)}, u32[]{:S(2)}, u32[]{:S(2)}) collective-permute-start(bf16[96,6144]{1,0:T(8,128)(2,1)} %collective-permute-done.23.refs_20_.refs_24_), channel_id=1, source_target_pairs={{0,6},{1,3},{2,0},{3,5},{4,2},{5,7},{6,4},{7,1},{8,14},{9,11},{10,... | collective-permute-start | bytes 3538952 | tf_op jit(solution)/shard_map/ppermute | solution.py:29
  98.6 21.8 %collective-permute-start.22 = (bf16[96,6144]{1,0:T(8,128)(2,1)}, bf16[96,6144]{1,0:T(8,128)(2,1)}, u32[]{:S(2)}, u32[]{:S(2)}) collective-permute-start(bf16[96,6144]{1,0:T(8,128)(2,1)} %collective-permute-done.21.refs_18_.refs_22_), channel_id=1, source_target_pairs={{0,1},{1,0},{2,3},{3,2},{4,5},{5,4},{6,7},{7,6},{8,9},{9,8},{10,11... | collective-permute-start | bytes 3538952 | tf_op jit(solution)/shard_map/ppermute | solution.py:49
  98.6 24.1 %collective-permute-start.24 = (bf16[96,6144]{1,0:T(8,128)(2,1)}, bf16[96,6144]{1,0:T(8,128)(2,1)}, u32[]{:S(2)}, u32[]{:S(2)}) collective-permute-start(bf16[96,6144]{1,0:T(8,128)(2,1)} %collective-permute-done.23.refs_20_.refs_24_), channel_id=1, source_target_pairs={{0,1},{1,0},{2,3},{3,2},{4,5},{5,4},{6,7},{7,6},{8,9},{9,8},{10,11... | collective-permute-start | bytes 3538952 | tf_op jit(solution)/shard_map/ppermute | solution.py:49
  101.0 34.4 %collective-permute-start.11 = (bf16[128,3072]{1,0:T(8,128)(2,1)}, bf16[128,3072]{1,0:T(8,128)(2,1)S(1)}, u32[]{:S(2)}, u32[]{:S(2)}) collective-permute-start(bf16[128,3072]{1,0:T(8,128)(2,1)} %collective-permute-done.9.refs_8_), channel_id=1, source_target_pairs={{0,96},{1,33},{32,0},{33,65},{64,32},{65,97},{96,64},{97,1},{2,98}... | collective-permute-start | bytes 2359304 | tf_op jit(solution)/shard_map/ppermute | solution.py:33
  104.7 30.7 %collective-permute-start.12 = (bf16[128,3072]{1,0:T(8,128)(2,1)}, bf16[128,3072]{1,0:T(8,128)(2,1)S(1)}, u32[]{:S(2)}, u32[]{:S(2)}) collective-permute-start(bf16[128,3072]{1,0:T(8,128)(2,1)} %copy-done.15), channel_id=1, source_target_pairs={{0,32},{1,97},{32,64},{33,1},{64,96},{65,33},{96,0},{97,65},{2,34}... | collective-permute-start | bytes 2359304 | tf_op jit(solution)/shard_map/ppermute | solution.py:33
  105.8 29.6 %collective-permute-start.26 = (bf16[96,6144]{1,0:T(8,128)(2,1)}, bf16[96,6144]{1,0:T(8,128)(2,1)S(1)}, u32[]{:S(2)}, u32[]{:S(2)}) collective-permute-start(bf16[96,6144]{1,0:T(8,128)(2,1)} %collective-permute-done.25.refs_26_), channel_id=1, source_target_pairs={{0,1},{1,0},{2,3},{3,2},{4,5},{5,4},{6,7},{7,6},{8,9},{9,8},{10,11... | collective-permute-start | bytes 3538952 | tf_op jit(solution)/shard_map/ppermute | solution.py:49
  106.4 1.3 copy-start.4
  107.6 1.0 copy-start.6
  108.6 1.0 copy-start.10
  109.6 10.7 %copy-start.18 = (f32[8,1,512]{2,1,0:T(1,128)S(1)}, f32[8,1,512]{2,1,0:T(1,128)}, u32[]{:S(2)}) copy-start(f32[8,1,512]{2,1,0:T(1,128)} %get-tuple-element.27.refs_12_.refs_8_.refs_5_) | copy-start | bytes 49156
  109.6 13.1 %copy-start.8 = (bf16[128,1536]{1,0:T(8,128)(2,1)S(1)}, bf16[128,1536]{1,0:T(8,128)(2,1)}, u32[]{:S(2)}) copy-start(bf16[128,1536]{1,0:T(8,128)(2,1)} %copy-done.7) | copy-start | bytes 1179652
  109.6 13.1 %copy-start.12 = (bf16[128,1536]{1,0:T(8,128)(2,1)S(1)}, bf16[128,1536]{1,0:T(8,128)(2,1)}, u32[]{:S(2)}) copy-start(bf16[128,1536]{1,0:T(8,128)(2,1)} %copy-done.11) | copy-start | bytes 1179652
  109.6 13.1 %copy-start.14 = (bf16[128,1536]{1,0:T(8,128)(2,1)S(1)}, bf16[128,1536]{1,0:T(8,128)(2,1)}, u32[]{:S(2)}) copy-start(bf16[128,1536]{1,0:T(8,128)(2,1)} %copy-done.13) | copy-start | bytes 1179652
  120.4 31.5 %collective-permute-start.28 = (f32[8,1,512]{2,1,0:T(1,128)S(1)}, f32[8,1,512]{2,1,0:T(1,128)S(1)}, u32[]{:S(2)}, u32[]{:S(2)}) collective-permute-start(f32[8,1,512]{2,1,0:T(1,128)S(1)} %copy-done.18), channel_id=1, source_target_pairs={{0,24},{8,16},{16,8},{24,0},{1,25},{9,17},{17,9},{25,1},{2,26},{10... | collective-permute-start | bytes 49160 | tf_op jit(solution)/shard_map/ppermute | solution.py:41
  122.7 13.7 %copy-start.16 = (bf16[128,3072]{1,0:T(8,128)(2,1)S(1)}, bf16[128,3072]{1,0:T(8,128)(2,1)}, u32[]{:S(2)}) copy-start(bf16[128,3072]{1,0:T(8,128)(2,1)} %copy-done.15) | copy-start | bytes 2359300
  135.4 1.0 copy-start.17
  151.9 0.6 copy-start.19
  155.7 51.9 %collective-permute-start.29 = (bf16[4,128,512]{2,1,0:T(8,128)(2,1)}, bf16[4,128,512]{2,1,0:T(8,128)(2,1)S(1)}, u32[]{:S(2)}, u32[]{:S(2)}) collective-permute-start(bf16[4,128,512]{2,1,0:T(8,128)(2,1)} %intra.3), channel_id=1, source_target_pairs={{0,24},{8,16},{16,8},{24,0},{1,25},{9,17},{17,9},{25,1},{2,26},{10... | collective-permute-start | bytes 1572872 | tf_op jit(solution)/shard_map/ppermute | solution.py:41
  156.8 50.9 %collective-permute-start.27 = (bf16[4,128,512]{2,1,0:T(8,128)(2,1)}, bf16[4,128,512]{2,1,0:T(8,128)(2,1)S(1)}, u32[]{:S(2)}, u32[]{:S(2)}) collective-permute-start(bf16[4,128,512]{2,1,0:T(8,128)(2,1)} %get-tuple-element.26), channel_id=1, source_target_pairs={{0,24},{8,16},{16,8},{24,0},{1,25},{9,17},{17,9},{25,1},{2,26},{10... | collective-permute-start | bytes 1572872 | tf_op jit(solution)/shard_map/ppermute | solution.py:41
  159.0 23.2 %all-to-all-start = ((f32[32,1,128]{2,1,0:T(1,128)}), f32[32,1,128]{2,1,0:T(1,128)S(1)}, u32[]{:S(2)}, u32[]{:S(2)}) async-start(f32[32,1,128]{2,1,0:T(1,128)} %get-tuple-element.30), calls=%async_computation | async-start | bytes 32768 | tf_op jit(solution)/shard_map/all_to_all | solution.py:45
  195.0 12.7 %all-to-all-start.2 = ((bf16[32,32,128]{2,1,0:T(8,128)(2,1)}), bf16[32,32,128]{2,1,0:T(8,128)(2,1)S(1)}, u32[]{:S(2)}, u32[]{:S(2)}) async-start(bf16[32,32,128]{2,1,0:T(8,128)(2,1)} %carries.1), calls=%async_computation.2 | async-start | bytes 524288 | tf_op jit(solution)/shard_map/all_to_all | solution.py:45

commit v7 on v6

--- a/solution.py
+++ b/solution.py
@@ -157,6 +157,9 @@
         in_specs.append(pl.BlockSpec(memory_space=pl.ANY))
         aliases = {len(args): 0}
         args.append(held)
+    need = 2 * 2 * KB * (TOK + 4 * 128 * len(cuts) + UNIT * len(units))
+    need += sum(len(members) * UNIT * TOK * 4 for _, members, _, _ in jobs)
+    need += (16 * UNIT + TOK) * TOK * 4 if after else 0
     products = sum(len(members) * (last + 1 - first) for _, members, first, last in jobs) * UNIT * TOK
     return pl.pallas_call(
         kernel,
@@ -169,7 +172,7 @@
         ),
         out_shape=out_shape,
         input_output_aliases=aliases,
-        compiler_params=pltpu.CompilerParams(vmem_limit_bytes=44 * 2**20),
+        compiler_params=pltpu.CompilerParams(vmem_limit_bytes=need + 3 * 2**20),
         cost_estimate=pl.CostEstimate(
             flops=2 * products * KB,
             bytes_accessed=2 * DIM * len(units) * UNIT,

time: 213 us -> 220 us (1.033)
  local copies, waits for them, and re-layouts: 10.8 us -> 18.8 us
    unnamed x44 -> x66, local copies, waits for them, and re-layouts: 8.22 us -> 16.2 us
  transfers between devices with their start and end apart: 32 -> 32, of which waited for: 12 -> 11; matrix products, arithmetic and copies ran while one was open for 1% -> 1% of each run, Pallas kernels for 23% -> 22%
where the time goes in v7:
time: 220 us; the launch traced here: 218 us
  waiting for transfers between devices  86.5 us (39%)
  Pallas kernels  55.1 us (25%)
  starting transfers between devices  45.8 us (21%)
  local copies, waits for them, and re-layouts  18.8 us (9%)
  blocking collectives  11.3 us (5%)
    pallas_call x3, Pallas kernels, project(): pl.pallas_call(kernel, grid_spec=pltpu.PrefetchScalarGridSpec(num_scalar_...  38.4 us
    ppermute x6, waiting for transfers between devices, z_out(): return lax.ppermute(v, ('zh', 'zl'), [(i, 3 - i) for i in range(4)])  23.3 us
    all_to_all x2, waiting for transfers between devices, exchange(): return lax.all_to_all(v, axes, 0, 0, tiled=True)  22 us
    ppermute x9, waiting for transfers between devices, x_move(): return lax.ppermute(v, ('x', 'c'), ring_pairs(step))  16.8 us
    unnamed x66, local copies, waits for them, and re-layouts  16.2 us
    ppermute x5, waiting for transfers between devices, y_move(): return lax.ppermute(v, ('y', 'c'), ring_pairs(step))  14.9 us
    ppermute x6, starting transfers between devices, z_out(): return lax.ppermute(v, ('zh', 'zl'), [(i, 3 - i) for i in range(4)])  13.3 us
    ppermute x9, starting transfers between devices, x_move(): return lax.ppermute(v, ('x', 'c'), ring_pairs(step))  12.7 us
  transfers between devices with their start and end apart: 32, of which 11 were waited for; matrix products, arithmetic and copies ran while one was open for 1% of the time, Pallas kernels for 22%

profile of v7, /device:TPU:0, one launch (start us, length us, event | category | flops | bytes accessed | tf_op | source)
XLA Modules:
  0.0 218.3 jit_solution(15443669823438168890)
XLA Ops:
  0.0 1.3 constant_dynamic-slice_fusion.1
  1.3 4.2 %collective-permute-start.1 = (bf16[128,1536]{1,0:T(8,128)(2,1)S(1)}, bf16[128,1536]{1,0:T(8,128)(2,1)S(1)}, u32[]{:S(2)}, u32[]{:S(2)}) collective-permute-start(bf16[128,1536]{1,0:T(8,128)(2,1)S(1)} %get-tuple-element.32), channel_id=1, source_target_pairs={{0,24},{8,16},{16,8},{24,0},{1,25},{9,17},{17,9},{25,1},{2,26},{10... | collective-permute-start | bytes 1179656 | tf_op jit(solution)/shard_map/ppermute | solution.py:41
  5.5 0.1 collective-permute-start.5
  5.6 9.9 %collective-permute-done.1.refs_0_ = bf16[128,1536]{1,0:T(8,128)(2,1)S(1)} collective-permute-done((bf16[128,1536]{1,0:T(8,128)(2,1)S(1)}, bf16[128,1536]{1,0:T(8,128)(2,1)S(1)}, u32[]{:S(2)}, u32[]{:S(2)}) %collective-permute-start.1) | collective-permute-done | bytes 393248 | tf_op jit(solution)/shard_map/ppermute | solution.py:41
  15.5 1.5 collective-permute-start.2
  17.0 1.7 collective-permute-start.3
  18.7 4.3 %collective-permute-done.5.refs_4_ = bf16[128,1536]{1,0:T(8,128)(2,1)S(1)} collective-permute-done((bf16[128,1536]{1,0:T(8,128)(2,1)S(1)}, bf16[128,1536]{1,0:T(8,128)(2,1)S(1)}, u32[]{:S(2)}, u32[]{:S(2)}) %collective-permute-start.5) | collective-permute-done | bytes 393248 | tf_op jit(solution)/shard_map/ppermute | solution.py:41
  23.1 1.5 collective-permute-start.6
  24.6 1.6 collective-permute-start
  26.1 1.7 collective-permute-start.7
  27.9 1.2 constant_dynamic-slice_fusion
  29.1 3.0 %collective-permute-start.9 = (bf16[128,3072]{1,0:T(8,128)(2,1)S(1)}, bf16[128,3072]{1,0:T(8,128)(2,1)S(1)}, u32[]{:S(2)}, u32[]{:S(2)}) collective-permute-start(bf16[128,3072]{1,0:T(8,128)(2,1)S(1)} %constant_dynamic-slice_fusion), channel_id=1, source_target_pairs={{0,24},{8,16},{16,8},{24,0},{1,25},{9,17},{17,9},{25,1},{2,26},{10... | collective-permute-start | bytes 2359304 | tf_op jit(solution)/shard_map/ppermute | solution.py:41
  32.1 0.8 copy-done.14
  32.9 1.4 collective-permute-done.6.refs_5_
  34.3 5.3 %collective-permute-start.15 = (bf16[96,6144]{1,0:T(8,128)(2,1)S(1)}, bf16[96,6144]{1,0:T(8,128)(2,1)}, u32[]{:S(2)}, u32[]{:S(2)}) collective-permute-start(bf16[96,6144]{1,0:T(8,128)(2,1)S(1)} %bitcast.24), channel_id=1, source_target_pairs={{0,6},{1,3},{2,0},{3,5},{4,2},{5,7},{6,4},{7,1},{8,14},{9,11},{10,... | collective-permute-start | bytes 3538952 | tf_op jit(solution)/shard_map/ppermute | solution.py:29
  39.6 0.7 copy-done.18
  40.3 9.1 %collective-permute-done.9.refs_8_ = bf16[128,3072]{1,0:T(8,128)(2,1)S(1)} collective-permute-done((bf16[128,3072]{1,0:T(8,128)(2,1)S(1)}, bf16[128,3072]{1,0:T(8,128)(2,1)S(1)}, u32[]{:S(2)}, u32[]{:S(2)}) %collective-permute-start.9) | collective-permute-done | bytes 786464 | tf_op jit(solution)/shard_map/ppermute | solution.py:41
  49.5 0.9 copy-done.22
  50.4 0.5 collective-permute-start.4
  50.8 0.1 stack.83.s_ref
  50.9 1.6 collective-permute-start.10
  52.5 0.5 broadcast_select_fusion.n_ref
  53.0 6.6 %collective-permute-done.4.refs_3_ = bf16[128,1536]{1,0:T(8,128)(2,1)} collective-permute-done((bf16[128,1536]{1,0:T(8,128)(2,1)}, bf16[128,1536]{1,0:T(8,128)(2,1)}, u32[]{:S(2)}, u32[]{:S(2)}) %collective-permute-start.4) | collective-permute-done | bytes 393248 | tf_op jit(solution)/shard_map/ppermute | solution.py:33
  59.7 0.2 collective-permute-done.17.refs_10_.refs_14_.refs_18_
  59.9 3.2 %collective-permute-start.23 = (bf16[96,6144]{1,0:T(8,128)(2,1)S(1)}, bf16[96,6144]{1,0:T(8,128)(2,1)}, u32[]{:S(2)}, u32[]{:S(2)}) collective-permute-start(bf16[96,6144]{1,0:T(8,128)(2,1)S(1)} %collective-permute-done.17.refs_10_.refs_14_.refs_18_), channel_id=1, source_target_pairs={{0,6},{1,3},{2,0},{3,5},{4,2},{5,7},{6,4},{7,1},{8,14},{9,11},{10,... | collective-permute-start | bytes 3538952 | tf_op jit(solution)/shard_map/ppermute | solution.py:29
  63.1 0.5 collective-permute-start.8
  63.6 8.7 %collective-permute-done.8.refs_7_ = bf16[128,1536]{1,0:T(8,128)(2,1)S(1)} collective-permute-done((bf16[128,1536]{1,0:T(8,128)(2,1)}, bf16[128,1536]{1,0:T(8,128)(2,1)S(1)}, u32[]{:S(2)}, u32[]{:S(2)}) %collective-permute-start.8) | collective-permute-done | bytes 393248 | tf_op jit(solution)/shard_map/ppermute | solution.py:33
  72.3 0.7 copy-done.20
  73.0 0.3 collective-permute-start.21
  73.4 1.1 copy-done.3
  74.4 0.4 collective-permute-start.16
  74.9 14.9 %collective-permute-done.19.refs_16_.refs_20_ = bf16[96,6144]{1,0:T(8,128)(2,1)} collective-permute-done((bf16[96,6144]{1,0:T(8,128)(2,1)S(1)}, bf16[96,6144]{1,0:T(8,128)(2,1)}, u32[]{:S(2)}, u32[]{:S(2)}) %collective-permute-start.19) | collective-permute-done | bytes 1179680 | tf_op jit(solution)/shard_map/ppermute | solution.py:29
  89.8 0.3 collective-permute-start.25
  90.1 9.2 %collective-permute-done.21.refs_18_.refs_22_ = bf16[96,6144]{1,0:T(8,128)(2,1)} collective-permute-done((bf16[96,6144]{1,0:T(8,128)(2,1)S(1)}, bf16[96,6144]{1,0:T(8,128)(2,1)}, u32[]{:S(2)}, u32[]{:S(2)}) %collective-permute-start.21) | collective-permute-done | bytes 1179680 | tf_op jit(solution)/shard_map/ppermute | solution.py:37
  99.4 1.0 copy-done.6
  100.4 0.5 collective-permute-start.24
  100.9 1.9 rates.1
  102.8 3.7 %collective-permute-start.11 = (bf16[128,3072]{1,0:T(8,128)(2,1)}, bf16[128,3072]{1,0:T(8,128)(2,1)S(1)}, u32[]{:S(2)}, u32[]{:S(2)}) collective-permute-start(bf16[128,3072]{1,0:T(8,128)(2,1)} %copy-done.22), channel_id=1, source_target_pairs={{0,96},{1,33},{32,0},{33,65},{64,32},{65,97},{96,64},{97,1},{2,98}... | collective-permute-start | bytes 2359304 | tf_op jit(solution)/shard_map/ppermute | solution.py:33
  106.5 0.4 collective-permute-start.26
  106.9 2.8 %copy-done.1 = bf16[512,6144]{1,0:T(8,128)(2,1)S(1)} copy-done((bf16[512,6144]{1,0:T(8,128)(2,1)S(1)}, bf16[512,6144]{1,0:T(8,128)(2,1)}, u32[]{:S(2)}) %copy-start.1) | copy-done | bytes 6291480
  109.7 1.3 copy-done.4
  111.0 1.3 copy-done.7
  112.3 1.0 copy-done.10
  113.3 1.0 copy-done.15
  114.3 11.3 %project.3 = (bf16[1536,512]{1,0:T(8,128)(2,1)S(1)}, f32[768,512]{1,0:T(8,128)S(1)}) custom-call(s32[20]{0:T(128)S(1)} %stack.83.s_ref, bf16[512,6144]{1,0:T(8,128)(2,1)S(1)} %copy-done.1, bf16[128,1536]{1,0:T(8,128)(2,1)S(1)} %copy-done.10, bf16[128,1536]{1,0:T(8,128)(2,1)} %collective-permute-done.2.refs_1_, bf16[128,1536]{1,0:T(8,128)(2,1)S(1)} %copy-done.15, ...), custom_call_target="tpu_custom_call" | custom-call | flops 6039797760 | bytes 9437184 | tf_op jit(solution)/shard_map/project/pallas_call | solution.py:164
  125.6 2.7 %collective-permute-start.28 = (f32[8,1,512]{2,1,0:T(1,128)S(1)}, f32[8,1,512]{2,1,0:T(1,128)S(1)}, u32[]{:S(2)}, u32[]{:S(2)}) collective-permute-start(f32[8,1,512]{2,1,0:T(1,128)S(1)} %copy-done.29), channel_id=1, source_target_pairs={{0,24},{8,16},{16,8},{24,0},{1,25},{9,17},{17,9},{25,1},{2,26},{10... | collective-permute-start | bytes 49160 | tf_op jit(solution)/shard_map/ppermute | solution.py:41
  128.4 12.4 %project.4 = (bf16[1536,512]{1,0:T(8,128)(2,1)S(1)}, f32[576,512]{1,0:T(8,128)S(1)}, f32[768,512]{1,0:T(8,128)S(1)}) custom-call(s32[20]{0:T(128)S(1)} %stack.83.s_ref, bf16[512,6144]{1,0:T(8,128)(2,1)} %x_ref.5, bf16[128,1536]{1,0:T(8,128)(2,1)S(1)} %copy-done.10, ...), custom_call_target="tpu_custom_call", output_to_operand_aliasing={{0}: (25, {})} | custom-call | flops 6643777536 | bytes 16515072 | tf_op jit(solution)/shard_map/project/pallas_call | solution.py:164
  140.8 1.2 copy-done
  142.0 1.0 copy-done.28
  143.0 14.7 %project.5 = (bf16[1536,512]{1,0:T(8,128)(2,1)}, bf16[1536,512]{1,0:T(8,128)(2,1)}, bf16[4,128,512]{2,1,0:T(8,128)(2,1)S(1)}) custom-call(s32[20]{0:T(128)S(1)} %stack.83.s_ref, bf16[512,6144]{1,0:T(8,128)(2,1)} %x_ref.5, bf16[128,1536]{1,0:T(8,128)(2,1)S(1)} %copy-done.11, ...), custom_call_target="tpu_custom_call", output_to_operand_aliasing={{0}: (32, {})} | custom-call | flops 6643777536 | bytes 18874368 | tf_op jit(solution)/shard_map/project/pallas_call | solution.py:164
  157.8 0.8 copy-done.26
  158.6 0.6 copy-done.30
  159.2 3.3 %intra.3 = bf16[4,128,512]{2,1,0:T(8,128)(2,1)} custom-call(s32[1]{0:T(128)} %bitcast.z_ref, bf16[1536,512]{1,0:T(8,128)(2,1)} %get-tuple-element.28.refs_0_.refs_1_.refs_2_.refs_3_.refs_4_.refs_5_.refs_6_.refs_7_.refs_8_.refs_9_.refs_10_.refs_11_.refs_12_.refs_13_.refs_14_.refs_15_.refs_16_, ...), custom_call_target="tpu_custom_call" | custom-call | tf_op jit(solution)/shard_map/intra/pallas_call | solution.py:275
  162.5 0.6 collective-permute-start.29
  163.1 2.7 %collective-permute-start.27 = (bf16[4,128,512]{2,1,0:T(8,128)(2,1)S(1)}, bf16[4,128,512]{2,1,0:T(8,128)(2,1)S(1)}, u32[]{:S(2)}, u32[]{:S(2)}) collective-permute-start(bf16[4,128,512]{2,1,0:T(8,128)(2,1)S(1)} %copy-done.27), channel_id=1, source_target_pairs={{0,24},{8,16},{16,8},{24,0},{1,25},{9,17},{17,9},{25,1},{2,26},{10... | collective-permute-start | bytes 1572872 | tf_op jit(solution)/shard_map/ppermute | solution.py:41
  165.7 3.8 %all-to-all-start = ((f32[32,1,128]{2,1,0:T(1,128)}), f32[32,1,128]{2,1,0:T(1,128)S(1)}, u32[]{:S(2)}, u32[]{:S(2)}) async-start(f32[32,1,128]{2,1,0:T(1,128)} %get-tuple-element.30), calls=%async_computation | async-start | bytes 32768 | tf_op jit(solution)/shard_map/all_to_all | solution.py:45
  169.6 3.1 %states.1 = bf16[16,2,32,128]{3,2,1,0:T(8,128)(2,1)} custom-call(s32[1]{0:T(128)} %bitcast.z_ref, bf16[1536,512]{1,0:T(8,128)(2,1)} %get-tuple-element.25.refs_0_.refs_1_.refs_2_.refs_3_.refs_4_.refs_5_.refs_6_.refs_7_.refs_8_.refs_9_.refs_10_.refs_11_, ...), custom_call_target="tpu_custom_call" | custom-call | tf_op jit(solution)/shard_map/states/pallas_call | solution.py:242
  172.7 16.6 %all-to-all-done.d_ref = f32[32,1,128]{2,1,0:T(1,128)S(1)} async-done(((f32[32,1,128]{2,1,0:T(1,128)}), f32[32,1,128]{2,1,0:T(1,128)S(1)}, u32[]{:S(2)}, u32[]{:S(2)}) %all-to-all-start) | async-done | bytes 16416 | tf_op jit(solution)/shard_map/all_to_all | solution.py:45
  189.3 11.3 %all_to_all.15.s_ref = bf16[16,2,32,128]{3,2,1,0:T(8,128)(2,1)S(1)} all-to-all(bf16[16,2,32,128]{3,2,1,0:T(8,128)(2,1)} %states.1), channel_id=1, replica_groups=mesh['x'=4,'zh'=2,'zl'=2,'y'=4,'c'=2] {'zl','y','c'}, dimensions={0} | all-to-all | bytes 524288 | tf_op jit(solution)/shard_map/all_to_all | solution.py:45
  200.7 1.4 carries.1
  202.1 3.9 %all-to-all-start.2 = ((bf16[32,32,128]{2,1,0:T(8,128)(2,1)}), bf16[32,32,128]{2,1,0:T(8,128)(2,1)S(1)}, u32[]{:S(2)}, u32[]{:S(2)}) async-start(bf16[32,32,128]{2,1,0:T(8,128)(2,1)} %carries.1), calls=%async_computation.2 | async-start | bytes 524288 | tf_op jit(solution)/shard_map/all_to_all | solution.py:45
  206.0 3.5 %intra.2.refs_6_ = f32[4,128,512]{2,1,0:T(8,128)} custom-call(s32[1]{0:T(128)} %bitcast.z_ref, bf16[1536,512]{1,0:T(8,128)(2,1)} %get-tuple-element.25.refs_0_.refs_1_.refs_2_.refs_3_.refs_4_.refs_5_.refs_6_.refs_7_.refs_8_.refs_9_.refs_10_.refs_11_, ...), custom_call_target="tpu_custom_call" | custom-call | tf_op jit(solution)/shard_map/intra/pallas_call | solution.py:275
  209.4 5.3 %all-to-all-done.2.refs_8_ = bf16[32,32,128]{2,1,0:T(8,128)(2,1)S(1)} async-done(((bf16[32,32,128]{2,1,0:T(8,128)(2,1)}), bf16[32,32,128]{2,1,0:T(8,128)(2,1)S(1)}, u32[]{:S(2)}, u32[]{:S(2)}) %all-to-all-start.2) | async-done | bytes 262176 | tf_op jit(solution)/shard_map/all_to_all | solution.py:45
  214.8 3.5 %finish.1 = bf16[512,1024]{1,0:T(8,128)(2,1)} custom-call(s32[1]{0:T(128)} %bitcast.z_ref, bf16[1536,512]{1,0:T(8,128)(2,1)} %get-tuple-element.25.refs_0_.refs_1_.refs_2_.refs_3_.refs_4_.refs_5_.refs_6_.refs_7_.refs_8_.refs_9_.refs_10_.refs_11_, ...), custom_call_target="tpu_custom_call" | custom-call | tf_op jit(solution)/shard_map/finish/pallas_call | solution.py:319
  (80 shorter events, 0.2 us)
Async XLA Ops:
  0.0 24.6 %copy-start.2 = (bf16[6144,96]{0,1:T(8,128)(2,1)S(1)}, bf16[6144,96]{0,1:T(8,128)(2,1)}, u32[]{:S(2)}) copy-start(bf16[6144,96]{0,1:T(8,128)(2,1)} %param.7) | copy-start | bytes 3538948
  1.3 51.2 %copy-start.31 = (s32[8]{0:T(128)S(1)}, s32[8]{0:T(128)}, u32[]{:S(2)}) copy-start(s32[8]{0:T(128)} %constant.101.clone) | copy-start | bytes 100
  1.3 51.2 %copy-start.32 = (s32[8]{0:T(128)S(1)}, s32[8]{0:T(128)}, u32[]{:S(2)}) copy-start(s32[8]{0:T(128)} %constant.102.clone) | copy-start | bytes 100
  1.3 14.2 %collective-permute-start.1 = (bf16[128,1536]{1,0:T(8,128)(2,1)S(1)}, bf16[128,1536]{1,0:T(8,128)(2,1)S(1)}, u32[]{:S(2)}, u32[]{:S(2)}) collective-permute-start(bf16[128,1536]{1,0:T(8,128)(2,1)S(1)} %get-tuple-element.32), channel_id=1, source_target_pairs={{0,24},{8,16},{16,8},{24,0},{1,25},{9,17},{17,9},{25,1},{2,26},{10... | collective-permute-start | bytes 1179656 | tf_op jit(solution)/shard_map/ppermute | solution.py:41
  5.5 17.5 %collective-permute-start.5 = (bf16[128,1536]{1,0:T(8,128)(2,1)S(1)}, bf16[128,1536]{1,0:T(8,128)(2,1)S(1)}, u32[]{:S(2)}, u32[]{:S(2)}) collective-permute-start(bf16[128,1536]{1,0:T(8,128)(2,1)S(1)} %get-tuple-element.31), channel_id=1, source_target_pairs={{0,24},{8,16},{16,8},{24,0},{1,25},{9,17},{17,9},{25,1},{2,26},{10... | collective-permute-start | bytes 1179656 | tf_op jit(solution)/shard_map/ppermute | solution.py:41
  15.5 24.1 %copy-start.9 = (bf16[128,1536]{1,0:T(8,128)(2,1)}, bf16[128,1536]{1,0:T(8,128)(2,1)S(1)}, u32[]{:S(2)}) copy-start(bf16[128,1536]{1,0:T(8,128)(2,1)S(1)} %collective-permute-done.1.refs_0_) | copy-start | bytes 1179652
  15.5 13.6 %collective-permute-start.2 = (bf16[128,1536]{1,0:T(8,128)(2,1)S(1)}, bf16[128,1536]{1,0:T(8,128)(2,1)}, u32[]{:S(2)}, u32[]{:S(2)}) collective-permute-start(bf16[128,1536]{1,0:T(8,128)(2,1)S(1)} %collective-permute-done.1.refs_0_), channel_id=1, source_target_pairs={{0,32},{1,97},{32,64},{33,1},{64,96},{65,33},{96,0},{97,65},{2,34}... | collective-permute-start | bytes 1179656 | tf_op jit(solution)/shard_map/ppermute | solution.py:33
  17.0 15.1 %collective-permute-start.3 = (bf16[128,1536]{1,0:T(8,128)(2,1)S(1)}, bf16[128,1536]{1,0:T(8,128)(2,1)S(1)}, u32[]{:S(2)}, u32[]{:S(2)}) collective-permute-start(bf16[128,1536]{1,0:T(8,128)(2,1)S(1)} %collective-permute-done.1.refs_0_), channel_id=1, source_target_pairs={{0,96},{1,33},{32,0},{33,65},{64,32},{65,97},{96,64},{97,1},{2,98}... | collective-permute-start | bytes 1179656 | tf_op jit(solution)/shard_map/ppermute | solution.py:33
  23.1 16.5 %copy-start.12 = (bf16[128,1536]{1,0:T(8,128)(2,1)}, bf16[128,1536]{1,0:T(8,128)(2,1)S(1)}, u32[]{:S(2)}) copy-start(bf16[128,1536]{1,0:T(8,128)(2,1)S(1)} %collective-permute-done.5.refs_4_) | copy-start | bytes 1179652
  23.1 11.2 %collective-permute-start.6 = (bf16[128,1536]{1,0:T(8,128)(2,1)S(1)}, bf16[128,1536]{1,0:T(8,128)(2,1)S(1)}, u32[]{:S(2)}, u32[]{:S(2)}) collective-permute-start(bf16[128,1536]{1,0:T(8,128)(2,1)S(1)} %collective-permute-done.5.refs_4_), channel_id=1, source_target_pairs={{0,32},{1,97},{32,64},{33,1},{64,96},{65,33},{96,0},{97,65},{2,34}... | collective-permute-start | bytes 1179656 | tf_op jit(solution)/shard_map/ppermute | solution.py:33
  24.6 26.4 %collective-permute-start = (bf16[96,6144]{1,0:T(8,128)(2,1)S(1)}, bf16[96,6144]{1,0:T(8,128)(2,1)S(1)}, u32[]{:S(2)}, u32[]{:S(2)}) collective-permute-start(bf16[96,6144]{1,0:T(8,128)(2,1)S(1)} %bitcast.22), channel_id=1, source_target_pairs={{0,2},{1,7},{2,4},{3,1},{4,6},{5,3},{6,0},{7,5},{8,10},{9,15},{10,... | collective-permute-start | bytes 3538952 | tf_op jit(solution)/shard_map/ppermute | solution.py:29
  26.1 13.5 %collective-permute-start.7 = (bf16[128,1536]{1,0:T(8,128)(2,1)S(1)}, bf16[128,1536]{1,0:T(8,128)(2,1)S(1)}, u32[]{:S(2)}, u32[]{:S(2)}) collective-permute-start(bf16[128,1536]{1,0:T(8,128)(2,1)S(1)} %collective-permute-done.5.refs_4_), channel_id=1, source_target_pairs={{0,96},{1,33},{32,0},{33,65},{64,32},{65,97},{96,64},{97,1},{2,98}... | collective-permute-start | bytes 1179656 | tf_op jit(solution)/shard_map/ppermute | solution.py:33
  29.1 20.4 %collective-permute-start.9 = (bf16[128,3072]{1,0:T(8,128)(2,1)S(1)}, bf16[128,3072]{1,0:T(8,128)(2,1)S(1)}, u32[]{:S(2)}, u32[]{:S(2)}) collective-permute-start(bf16[128,3072]{1,0:T(8,128)(2,1)S(1)} %constant_dynamic-slice_fusion), channel_id=1, source_target_pairs={{0,24},{8,16},{16,8},{24,0},{1,25},{9,17},{17,9},{25,1},{2,26},{10... | collective-permute-start | bytes 2359304 | tf_op jit(solution)/shard_map/ppermute | solution.py:41
  32.1 0.8 copy-start.14
  32.9 27.0 %collective-permute-start.17 = (bf16[96,6144]{1,0:T(8,128)(2,1)S(1)}, bf16[96,6144]{1,0:T(8,128)(2,1)S(1)}, u32[]{:S(2)}, u32[]{:S(2)}) collective-permute-start(bf16[96,6144]{1,0:T(8,128)(2,1)S(1)} %bitcast.23), channel_id=1, source_target_pairs={{0,8},{8,0},{1,9},{9,1},{2,10},{10,2},{3,11},{11,3},{4,12},{12,4},... | collective-permute-start | bytes 3538952 | tf_op jit(solution)/shard_map/ppermute | solution.py:37
  34.3 6.1 %copy-start.16 = (bf16[128,1536]{1,0:T(8,128)(2,1)}, bf16[128,1536]{1,0:T(8,128)(2,1)S(1)}, u32[]{:S(2)}) copy-start(bf16[128,1536]{1,0:T(8,128)(2,1)S(1)} %collective-permute-done.6.refs_5_) | copy-start | bytes 1179652
  34.3 25.6 %collective-permute-start.15 = (bf16[96,6144]{1,0:T(8,128)(2,1)S(1)}, bf16[96,6144]{1,0:T(8,128)(2,1)}, u32[]{:S(2)}, u32[]{:S(2)}) collective-permute-start(bf16[96,6144]{1,0:T(8,128)(2,1)S(1)} %bitcast.24), channel_id=1, source_target_pairs={{0,6},{1,3},{2,0},{3,5},{4,2},{5,7},{6,4},{7,1},{8,14},{9,11},{10,... | collective-permute-start | bytes 3538952 | tf_op jit(solution)/shard_map/ppermute | solution.py:29
  39.6 0.7 copy-start.18
  40.3 22.7 %collective-permute-start.13 = (bf16[96,6144]{1,0:T(8,128)(2,1)S(1)}, bf16[96,6144]{1,0:T(8,128)(2,1)}, u32[]{:S(2)}, u32[]{:S(2)}) collective-permute-start(bf16[96,6144]{1,0:T(8,128)(2,1)S(1)} %bitcast.25), channel_id=1, source_target_pairs={{0,1},{1,0},{2,3},{3,2},{4,5},{5,4},{6,7},{7,6},{8,9},{9,8},{10,11... | collective-permute-start | bytes 3538952 | tf_op jit(solution)/shard_map/ppermute | solution.py:49
  49.5 0.9 copy-start.22
  50.4 9.3 %collective-permute-start.4 = (bf16[128,1536]{1,0:T(8,128)(2,1)}, bf16[128,1536]{1,0:T(8,128)(2,1)}, u32[]{:S(2)}, u32[]{:S(2)}) collective-permute-start(bf16[128,1536]{1,0:T(8,128)(2,1)} %collective-permute-done.2.refs_1_), channel_id=1, source_target_pairs={{0,32},{1,97},{32,64},{33,1},{64,96},{65,33},{96,0},{97,65},{2,34}... | collective-permute-start | bytes 1179656 | tf_op jit(solution)/shard_map/ppermute | solution.py:33
  50.9 22.4 %collective-permute-start.10 = (bf16[128,3072]{1,0:T(8,128)(2,1)}, bf16[128,3072]{1,0:T(8,128)(2,1)S(1)}, u32[]{:S(2)}, u32[]{:S(2)}) collective-permute-start(bf16[128,3072]{1,0:T(8,128)(2,1)} %copy-done.22), channel_id=1, source_target_pairs={{0,32},{1,97},{32,64},{33,1},{64,96},{65,33},{96,0},{97,65},{2,34}... | collective-permute-start | bytes 2359304 | tf_op jit(solution)/shard_map/ppermute | solution.py:33
  59.7 13.7 %collective-permute-start.14 = (bf16[96,6144]{1,0:T(8,128)(2,1)S(1)}, bf16[96,6144]{1,0:T(8,128)(2,1)S(1)}, u32[]{:S(2)}, u32[]{:S(2)}) collective-permute-start(bf16[96,6144]{1,0:T(8,128)(2,1)S(1)} %collective-permute-done.refs_6_.refs_10_.refs_14_), channel_id=1, source_target_pairs={{0,1},{1,0},{2,3},{3,2},{4,5},{5,4},{6,7},{7,6},{8,9},{9,8},{10,11... | collective-permute-start | bytes 3538952 | tf_op jit(solution)/shard_map/ppermute | solution.py:49
  59.8 30.0 %collective-permute-start.19 = (bf16[96,6144]{1,0:T(8,128)(2,1)S(1)}, bf16[96,6144]{1,0:T(8,128)(2,1)}, u32[]{:S(2)}, u32[]{:S(2)}) collective-permute-start(bf16[96,6144]{1,0:T(8,128)(2,1)S(1)} %collective-permute-done.refs_6_.refs_10_.refs_14_), channel_id=1, source_target_pairs={{0,2},{1,7},{2,4},{3,1},{4,6},{5,3},{6,0},{7,5},{8,10},{9,15},{10,... | collective-permute-start | bytes 3538952 | tf_op jit(solution)/shard_map/ppermute | solution.py:29
  59.9 30.0 %collective-permute-start.23 = (bf16[96,6144]{1,0:T(8,128)(2,1)S(1)}, bf16[96,6144]{1,0:T(8,128)(2,1)}, u32[]{:S(2)}, u32[]{:S(2)}) collective-permute-start(bf16[96,6144]{1,0:T(8,128)(2,1)S(1)} %collective-permute-done.17.refs_10_.refs_14_.refs_18_), channel_id=1, source_target_pairs={{0,6},{1,3},{2,0},{3,5},{4,2},{5,7},{6,4},{7,1},{8,14},{9,11},{10,... | collective-permute-start | bytes 3538952 | tf_op jit(solution)/shard_map/ppermute | solution.py:29
  63.1 9.2 %collective-permute-start.8 = (bf16[128,1536]{1,0:T(8,128)(2,1)}, bf16[128,1536]{1,0:T(8,128)(2,1)S(1)}, u32[]{:S(2)}, u32[]{:S(2)}) collective-permute-start(bf16[128,1536]{1,0:T(8,128)(2,1)} %copy-done.16), channel_id=1, source_target_pairs={{0,32},{1,97},{32,64},{33,1},{64,96},{65,33},{96,0},{97,65},{2,34}... | collective-permute-start | bytes 1179656 | tf_op jit(solution)/shard_map/ppermute | solution.py:33
  72.3 0.8 copy-start.20
  73.0 26.3 %collective-permute-start.21 = (bf16[96,6144]{1,0:T(8,128)(2,1)S(1)}, bf16[96,6144]{1,0:T(8,128)(2,1)}, u32[]{:S(2)}, u32[]{:S(2)}) collective-permute-start(bf16[96,6144]{1,0:T(8,128)(2,1)S(1)} %collective-permute-done.refs_6_.refs_10_.refs_14_), channel_id=1, source_target_pairs={{0,8},{8,0},{1,9},{9,1},{2,10},{10,2},{3,11},{11,3},{4,12},{12,4},... | collective-permute-start | bytes 3538952 | tf_op jit(solution)/shard_map/ppermute | solution.py:37
  73.3 26.0 %copy-start.24 = (bf16[128,3072]{1,0:T(8,128)(2,1)}, bf16[128,3072]{1,0:T(8,128)(2,1)S(1)}, u32[]{:S(2)}) copy-start(bf16[128,3072]{1,0:T(8,128)(2,1)S(1)} %collective-permute-done.10.refs_9_) | copy-start | bytes 2359300
  73.3 26.0 %collective-permute-start.18 = (bf16[96,6144]{1,0:T(8,128)(2,1)S(1)}, bf16[96,6144]{1,0:T(8,128)(2,1)S(1)}, u32[]{:S(2)}, u32[]{:S(2)}) collective-permute-start(bf16[96,6144]{1,0:T(8,128)(2,1)S(1)} %collective-permute-done.17.refs_10_.refs_14_.refs_18_), channel_id=1, source_target_pairs={{0,1},{1,0},{2,3},{3,2},{4,5},{5,4},{6,7},{7,6},{8,9},{9,8},{10,11... | collective-permute-start | bytes 3538952 | tf_op jit(solution)/shard_map/ppermute | solution.py:49
  73.3 1.1 copy-start.3
  74.4 28.3 %collective-permute-start.16 = (bf16[96,6144]{1,0:T(8,128)(2,1)}, bf16[96,6144]{1,0:T(8,128)(2,1)}, u32[]{:S(2)}, u32[]{:S(2)}) collective-permute-start(bf16[96,6144]{1,0:T(8,128)(2,1)} %collective-permute-done.15.refs_8_.refs_12_.refs_16_), channel_id=1, source_target_pairs={{0,1},{1,0},{2,3},{3,2},{4,5},{5,4},{6,7},{7,6},{8,9},{9,8},{10,11... | collective-permute-start | bytes 3538952 | tf_op jit(solution)/shard_map/ppermute | solution.py:49
  89.8 16.6 %collective-permute-start.20 = (bf16[96,6144]{1,0:T(8,128)(2,1)}, bf16[96,6144]{1,0:T(8,128)(2,1)}, u32[]{:S(2)}, u32[]{:S(2)}) collective-permute-start(bf16[96,6144]{1,0:T(8,128)(2,1)} %collective-permute-done.19.refs_16_.refs_20_), channel_id=1, source_target_pairs={{0,1},{1,0},{2,3},{3,2},{4,5},{5,4},{6,7},{7,6},{8,9},{9,8},{10,11... | collective-permute-start | bytes 3538952 | tf_op jit(solution)/shard_map/ppermute | solution.py:49
  89.8 16.6 %collective-permute-start.25 = (bf16[96,6144]{1,0:T(8,128)(2,1)}, bf16[96,6144]{1,0:T(8,128)(2,1)}, u32[]{:S(2)}, u32[]{:S(2)}) collective-permute-start(bf16[96,6144]{1,0:T(8,128)(2,1)} %collective-permute-done.23.refs_20_.refs_24_), channel_id=1, source_target_pairs={{0,6},{1,3},{2,0},{3,5},{4,2},{5,7},{6,4},{7,1},{8,14},{9,11},{10,... | collective-permute-start | bytes 3538952 | tf_op jit(solution)/shard_map/ppermute | solution.py:29
  99.4 26.2 %collective-permute-start.22 = (bf16[96,6144]{1,0:T(8,128)(2,1)}, bf16[96,6144]{1,0:T(8,128)(2,1)}, u32[]{:S(2)}, u32[]{:S(2)}) collective-permute-start(bf16[96,6144]{1,0:T(8,128)(2,1)} %collective-permute-done.21.refs_18_.refs_22_), channel_id=1, source_target_pairs={{0,1},{1,0},{2,3},{3,2},{4,5},{5,4},{6,7},{7,6},{8,9},{9,8},{10,11... | collective-permute-start | bytes 3538952 | tf_op jit(solution)/shard_map/ppermute | solution.py:49
  99.4 1.0 copy-start.6
  100.4 27.9 %collective-permute-start.24 = (bf16[96,6144]{1,0:T(8,128)(2,1)}, bf16[96,6144]{1,0:T(8,128)(2,1)}, u32[]{:S(2)}, u32[]{:S(2)}) collective-permute-start(bf16[96,6144]{1,0:T(8,128)(2,1)} %collective-permute-done.23.refs_20_.refs_24_), channel_id=1, source_target_pairs={{0,1},{1,0},{2,3},{3,2},{4,5},{5,4},{6,7},{7,6},{8,9},{9,8},{10,11... | collective-permute-start | bytes 3538952 | tf_op jit(solution)/shard_map/ppermute | solution.py:49
  102.8 39.2 %collective-permute-start.11 = (bf16[128,3072]{1,0:T(8,128)(2,1)}, bf16[128,3072]{1,0:T(8,128)(2,1)S(1)}, u32[]{:S(2)}, u32[]{:S(2)}) collective-permute-start(bf16[128,3072]{1,0:T(8,128)(2,1)} %copy-done.22), channel_id=1, source_target_pairs={{0,96},{1,33},{32,0},{33,65},{64,32},{65,97},{96,64},{97,1},{2,98}... | collective-permute-start | bytes 2359304 | tf_op jit(solution)/shard_map/ppermute | solution.py:33
  106.5 35.5 %collective-permute-start.12 = (bf16[128,3072]{1,0:T(8,128)(2,1)}, bf16[128,3072]{1,0:T(8,128)(2,1)S(1)}, u32[]{:S(2)}, u32[]{:S(2)}) collective-permute-start(bf16[128,3072]{1,0:T(8,128)(2,1)} %copy-done.24), channel_id=1, source_target_pairs={{0,32},{1,97},{32,64},{33,1},{64,96},{65,33},{96,0},{97,65},{2,34}... | collective-permute-start | bytes 2359304 | tf_op jit(solution)/shard_map/ppermute | solution.py:33
  106.5 35.5 %collective-permute-start.26 = (bf16[96,6144]{1,0:T(8,128)(2,1)}, bf16[96,6144]{1,0:T(8,128)(2,1)S(1)}, u32[]{:S(2)}, u32[]{:S(2)}) collective-permute-start(bf16[96,6144]{1,0:T(8,128)(2,1)} %collective-permute-done.25.refs_26_), channel_id=1, source_target_pairs={{0,1},{1,0},{2,3},{3,2},{4,5},{5,4},{6,7},{7,6},{8,9},{9,8},{10,11... | collective-permute-start | bytes 3538952 | tf_op jit(solution)/shard_map/ppermute | solution.py:49
  106.9 2.8 %copy-start.1 = (bf16[512,6144]{1,0:T(8,128)(2,1)S(1)}, bf16[512,6144]{1,0:T(8,128)(2,1)}, u32[]{:S(2)}) copy-start(bf16[512,6144]{1,0:T(8,128)(2,1)} %x_ref.5) | copy-start | bytes 18874372
  109.7 1.3 copy-start.4
  111.0 1.3 copy-start.7
  112.3 1.0 copy-start.10
  113.3 1.0 copy-start.15
  114.3 11.3 %copy-start.29 = (f32[8,1,512]{2,1,0:T(1,128)S(1)}, f32[8,1,512]{2,1,0:T(1,128)}, u32[]{:S(2)}) copy-start(f32[8,1,512]{2,1,0:T(1,128)} %get-tuple-element.27.refs_12_.refs_8_.refs_5_) | copy-start | bytes 49156
  114.3 14.1 %copy-start.5 = (bf16[96,6144]{1,0:T(8,128)(2,1)S(1)}, bf16[96,6144]{1,0:T(8,128)(2,1)}, u32[]{:S(2)}) copy-start(bf16[96,6144]{1,0:T(8,128)(2,1)} %copy-done.3) | copy-start | bytes 3538948
  114.3 14.1 %copy-start.8 = (bf16[96,6144]{1,0:T(8,128)(2,1)S(1)}, bf16[96,6144]{1,0:T(8,128)(2,1)}, u32[]{:S(2)}) copy-start(bf16[96,6144]{1,0:T(8,128)(2,1)} %copy-done.6) | copy-start | bytes 3538948
  114.3 14.1 %copy-start.13 = (bf16[128,1536]{1,0:T(8,128)(2,1)S(1)}, bf16[128,1536]{1,0:T(8,128)(2,1)}, u32[]{:S(2)}) copy-start(bf16[128,1536]{1,0:T(8,128)(2,1)} %copy-done.12) | copy-start | bytes 1179652
  114.3 14.1 %copy-start.17 = (bf16[128,1536]{1,0:T(8,128)(2,1)S(1)}, bf16[128,1536]{1,0:T(8,128)(2,1)}, u32[]{:S(2)}) copy-start(bf16[128,1536]{1,0:T(8,128)(2,1)} %copy-done.16) | copy-start | bytes 1179652
  114.3 14.1 %copy-start.19 = (bf16[128,1536]{1,0:T(8,128)(2,1)S(1)}, bf16[128,1536]{1,0:T(8,128)(2,1)}, u32[]{:S(2)}) copy-start(bf16[128,1536]{1,0:T(8,128)(2,1)} %copy-done.18) | copy-start | bytes 1179652
  114.3 14.1 %copy-start.21 = (bf16[128,1536]{1,0:T(8,128)(2,1)S(1)}, bf16[128,1536]{1,0:T(8,128)(2,1)}, u32[]{:S(2)}) copy-start(bf16[128,1536]{1,0:T(8,128)(2,1)} %copy-done.20) | copy-start | bytes 1179652
  125.6 33.0 %collective-permute-start.28 = (f32[8,1,512]{2,1,0:T(1,128)S(1)}, f32[8,1,512]{2,1,0:T(1,128)S(1)}, u32[]{:S(2)}, u32[]{:S(2)}) collective-permute-start(f32[8,1,512]{2,1,0:T(1,128)S(1)} %copy-done.29), channel_id=1, source_target_pairs={{0,24},{8,16},{16,8},{24,0},{1,25},{9,17},{17,9},{25,1},{2,26},{10... | collective-permute-start | bytes 49160 | tf_op jit(solution)/shard_map/ppermute | solution.py:41
  128.4 14.6 %copy-start.11 = (bf16[128,1536]{1,0:T(8,128)(2,1)S(1)}, bf16[128,1536]{1,0:T(8,128)(2,1)}, u32[]{:S(2)}) copy-start(bf16[128,1536]{1,0:T(8,128)(2,1)} %copy-done.9) | copy-start | bytes 1179652
  128.4 14.6 %copy-start.23 = (bf16[128,3072]{1,0:T(8,128)(2,1)S(1)}, bf16[128,3072]{1,0:T(8,128)(2,1)}, u32[]{:S(2)}) copy-start(bf16[128,3072]{1,0:T(8,128)(2,1)} %copy-done.22) | copy-start | bytes 2359300
  128.4 14.6 %copy-start.25 = (bf16[128,3072]{1,0:T(8,128)(2,1)S(1)}, bf16[128,3072]{1,0:T(8,128)(2,1)}, u32[]{:S(2)}) copy-start(bf16[128,3072]{1,0:T(8,128)(2,1)} %copy-done.24) | copy-start | bytes 2359300
  140.8 1.2 copy-start
  142.0 1.0 copy-start.28
  157.8 0.8 copy-start.26
  159.2 3.9 %copy-start.27 = (bf16[4,128,512]{2,1,0:T(8,128)(2,1)S(1)}, bf16[4,128,512]{2,1,0:T(8,128)(2,1)}, u32[]{:S(2)}) copy-start(bf16[4,128,512]{2,1,0:T(8,128)(2,1)} %copy-done.26) | copy-start | bytes 1572868
  162.5 52.3 %collective-permute-start.29 = (bf16[4,128,512]{2,1,0:T(8,128)(2,1)}, bf16[4,128,512]{2,1,0:T(8,128)(2,1)S(1)}, u32[]{:S(2)}, u32[]{:S(2)}) collective-permute-start(bf16[4,128,512]{2,1,0:T(8,128)(2,1)} %intra.3), channel_id=1, source_target_pairs={{0,24},{8,16},{16,8},{24,0},{1,25},{9,17},{17,9},{25,1},{2,26},{10... | collective-permute-start | bytes 1572872 | tf_op jit(solution)/shard_map/ppermute | solution.py:41
  163.1 51.7 %collective-permute-start.27 = (bf16[4,128,512]{2,1,0:T(8,128)(2,1)S(1)}, bf16[4,128,512]{2,1,0:T(8,128)(2,1)S(1)}, u32[]{:S(2)}, u32[]{:S(2)}) collective-permute-start(bf16[4,128,512]{2,1,0:T(8,128)(2,1)S(1)} %copy-done.27), channel_id=1, source_target_pairs={{0,24},{8,16},{16,8},{24,0},{1,25},{9,17},{17,9},{25,1},{2,26},{10... | collective-permute-start | bytes 1572872 | tf_op jit(solution)/shard_map/ppermute | solution.py:41
  165.7 23.6 %all-to-all-start = ((f32[32,1,128]{2,1,0:T(1,128)}), f32[32,1,128]{2,1,0:T(1,128)S(1)}, u32[]{:S(2)}, u32[]{:S(2)}) async-start(f32[32,1,128]{2,1,0:T(1,128)} %get-tuple-element.30), calls=%async_computation | async-start | bytes 32768 | tf_op jit(solution)/shard_map/all_to_all | solution.py:45
  202.1 12.7 %all-to-all-start.2 = ((bf16[32,32,128]{2,1,0:T(8,128)(2,1)}), bf16[32,32,128]{2,1,0:T(8,128)(2,1)S(1)}, u32[]{:S(2)}, u32[]{:S(2)}) async-start(bf16[32,32,128]{2,1,0:T(8,128)(2,1)} %carries.1), calls=%async_computation.2 | async-start | bytes 524288 | tf_op jit(solution)/shard_map/all_to_all | solution.py:45
  (1 other events, 0.6 us)
